TPU v7x, 32 devices: a whole 2x2x4 slice. The times are simulated.
32 devices in a mesh: ha: 4 (over y, x), ba: 8 (over z, core).
Axes of the slice: x: 2, y: 2, z: 4, core: 2. Of those that a mesh axis runs over, the one named last changes fastest.
Arguments:
- images_in: bfloat16 [64, 32, 32, 1024], P('ba', 'ha'), may hold values from -6 to 6
- reduce_w: bfloat16 [1024, 1024], replicated, may hold values from -0.1875 to 0.1875
- gain_one: float32 [1024], replicated, may hold values from 0.1 to 1.9
- shift_one: float32 [1024], replicated, may hold values from -2 to 2
- group_w: bfloat16 [3, 3, 32, 1024], replicated, may hold values from -0.375 to 0.375
- gain_two: float32 [1024], replicated, may hold values from 0.1 to 1.9
- shift_two: float32 [1024], replicated, may hold values from -2 to 2
- expand_w: bfloat16 [1024, 2048], replicated, may hold values from -0.1875 to 0.1875
- gain_three: float32 [2048], replicated, may hold values from 0.1 to 1.9
- shift_three: float32 [2048], replicated, may hold values from -2 to 2
- proj_w: bfloat16 [1024, 2048], replicated, may hold values from -0.1875 to 0.1875
- gain_proj: float32 [2048], replicated, may hold values from 0.1 to 1.9
- shift_proj: float32 [2048], replicated, may hold values from -2 to 2
- valid_mask: int32 [64], P('ba'), may hold values from 0 to 1, as said below
- cotangent: bfloat16 [64, 16, 16, 2048], P('ba', 'ha'), may hold values from -6 to 6
Outputs:
- output: bfloat16 [64, 16, 16, 2048], P('ba', 'ha')
- grad_images: bfloat16 [64, 32, 32, 1024], P('ba', 'ha')
- grad_reduce: float32 [1024, 1024], replicated
- grad_gain_one: float32 [1024], replicated
- grad_shift_one: float32 [1024], replicated
- grad_group: float32 [3, 3, 32, 1024], replicated
- grad_gain_two: float32 [1024], replicated
- grad_shift_two: float32 [1024], replicated
- grad_expand: float32 [1024, 2048], replicated
- grad_gain_three: float32 [2048], replicated
- grad_shift_three: float32 [2048], replicated
- grad_proj: float32 [1024, 2048], replicated
- grad_gain_proj: float32 [2048], replicated
- grad_shift_proj: float32 [2048], replicated
Inputs may be any that keep to these rules, and one draw needn't show every extreme that they name: `valid_mask`: in each aligned block of 8 images (the images of one index of ba) the valid images come first; a block holds 8, 4, 2 or 1 valid images, and at least one block holds 8.
All inputs are finite; a program needn't handle non-finite values.
Results may differ from a plain program's by a relative error of at most 0.0087.
Values may be sent and summed in bfloat16 or wider, within the bound.
No kernel may reach another device: no remote copies, remote signals or barrier semaphores. Data moves between devices by JAX's collectives and lax.ppermute only.
A program may use at most 256 MiB of HBM per device.

v0:
```python
import jax
import jax.numpy as jnp
from jax import lax
from jax.sharding import PartitionSpec as P

GROUPS = 32
GW = 32


EPS = 1e-05


def shifted(value, axis, by):
    peers = lax.axis_size(axis)
    pairs = [(i, i + by) for i in range(peers) if 0 <= i + by < peers]
    return lax.ppermute(value, axis, pairs)


def silu_slope(values):
    logistic = jax.nn.sigmoid(values)
    return logistic * (1.0 + values * (1.0 - logistic))


def channel_sums(values):
    return jnp.sum(values, axis=(0, 1, 2))


def split_like(vector, extents):
    pieces = []
    offset = 0
    for extent in extents:
        pieces.append(vector[offset : offset + extent])
        offset += extent
    return pieces


def moments(activations, weight, local_count):
    extents = [member.shape[-1] for member in activations]
    totals, count_of = lax.psum(
        (jnp.concatenate([channel_sums(member * weight) for member in activations]), local_count),
        ("ha", "ba"),
    )
    means = split_like(totals / count_of, extents)
    centred = [member - mean_of for member, mean_of in zip(activations, means)]
    spread = lax.psum(
        jnp.concatenate([channel_sums(member * member * weight) for member in centred]),
        ("ha", "ba"),
    )
    variance = spread / count_of
    inv_std = split_like(lax.rsqrt(variance + EPS), extents)
    normed = [member * scale for member, scale in zip(centred, inv_std)]
    return (normed, inv_std, count_of)


def norm_back(upstreams, normed, inv_std, gain_list, weight, count_of):
    extents = [member.shape[-1] for member in upstreams]
    shift_sums, gain_sums = lax.psum(
        (
            jnp.concatenate([channel_sums(member) for member in upstreams]),
            jnp.concatenate(
                [channel_sums(member * other) for member, other in zip(upstreams, normed)]
            ),
        ),
        ("ha", "ba"),
    )
    shift_grads = split_like(shift_sums, extents)
    gain_grads = split_like(gain_sums, extents)
    results = []
    for position in range(len(upstreams)):
        adjusted = (
            upstreams[position]
            - weight * (shift_grads[position] + normed[position] * gain_grads[position]) / count_of
        )
        results.append((gain_list[position] * inv_std[position] * adjusted).astype(jnp.bfloat16))
    return (results, gain_grads, shift_grads)


def window_at(padded, row_tap, col_tap, rows_out, cols_out):
    return padded[:, row_tap : row_tap + 2 * rows_out : 2, col_tap : col_tap + 2 * cols_out : 2]


def by_group(values):
    return values.reshape(values.shape[:3] + (GROUPS, GW))


def pad_along(values, axis, before, after):
    widths = [(0, 0)] * values.ndim
    widths[axis] = (before, after)
    return jnp.pad(values, widths)


def weave(even_part, odd_part, axis):
    extent = odd_part.shape[axis]
    head = lax.slice_in_dim(even_part, 0, extent, axis=axis)
    tail = lax.slice_in_dim(even_part, extent, extent + 1, axis=axis)
    paired = jnp.stack([head, odd_part], axis=axis + 1)
    shape_of = list(odd_part.shape)
    shape_of[axis] = 2 * extent
    return jnp.concatenate([paired.reshape(shape_of), tail], axis=axis)


def per_device(
    images_in,
    reduce_w,
    gain_one,
    shift_one,
    group_w,
    gain_two,
    shift_two,
    expand_w,
    gain_three,
    shift_three,
    proj_w,
    gain_proj,
    shift_proj,
    valid_mask,
    cotangent,
):
    weight = valid_mask.astype(jnp.float32)[:, None, None, None]
    n_images, rows_in, cols_in, chans_in = images_in.shape
    rows_out = rows_in // 2
    cols_out = cols_in // 2
    mid_width = reduce_w.shape[1]
    reduced = jnp.einsum("nhwc,cd->nhwd", images_in, reduce_w, preferred_element_type=jnp.float32)
    normed_one, inv_one, count_in = moments(
        [reduced], weight, jnp.sum(weight) * float(rows_in * cols_in)
    )
    pre_one = normed_one[0] * gain_one + shift_one
    hidden_one = jax.nn.silu(pre_one).astype(jnp.bfloat16)
    from_above = shifted(hidden_one[:, -1:], "ha", 1)
    padded = jnp.pad(
        jnp.concatenate([from_above, hidden_one], axis=1), ((0, 0), (0, 0), (1, 0), (0, 0))
    )
    grouped = jnp.zeros((n_images, rows_out, cols_out, GROUPS, GW), jnp.float32)
    for row_tap in range(3):
        for col_tap in range(3):
            kernel = group_w[row_tap, col_tap].reshape(GW, GROUPS, GW)
            grouped = grouped + jnp.einsum(
                "nhwgc,cgj->nhwgj",
                by_group(window_at(padded, row_tap, col_tap, rows_out, cols_out)),
                kernel,
                preferred_element_type=jnp.float32,
            )
    grouped = grouped.reshape(n_images, rows_out, cols_out, mid_width)
    normed_two, inv_two, count_out = moments(
        [grouped], weight, jnp.sum(weight) * float(rows_out * cols_out)
    )
    pre_two = normed_two[0] * gain_two + shift_two
    hidden_two = jax.nn.silu(pre_two).astype(jnp.bfloat16)
    expanded = jnp.einsum("nhwc,cd->nhwd", hidden_two, expand_w, preferred_element_type=jnp.float32)
    sampled = images_in[:, ::2, ::2]
    projected = jnp.einsum("nhwc,cd->nhwd", sampled, proj_w, preferred_element_type=jnp.float32)
    normed_out, inv_out, count_out = moments(
        [expanded, projected], weight, jnp.sum(weight) * float(rows_out * cols_out)
    )
    summed = normed_out[0] * gain_three + shift_three + normed_out[1] * gain_proj + shift_proj
    output = (jax.nn.silu(summed) * weight).astype(jnp.bfloat16)
    upstream = cotangent.astype(jnp.float32) * weight * silu_slope(summed)
    grads_out, gains_out, shifts_out = norm_back(
        [upstream, upstream], normed_out, inv_out, [gain_three, gain_proj], weight, count_out
    )
    d_expanded, d_projected = (grads_out[0], grads_out[1])
    grad_expand = jnp.einsum(
        "nhwc,nhwd->cd", hidden_two, d_expanded, preferred_element_type=jnp.float32
    )
    grad_proj = jnp.einsum(
        "nhwc,nhwd->cd", sampled, d_projected, preferred_element_type=jnp.float32
    )
    back_two = jnp.einsum("nhwd,cd->nhwc", d_expanded, expand_w, preferred_element_type=jnp.float32)
    back_side = jnp.einsum("nhwd,cd->nhwc", d_projected, proj_w, preferred_element_type=jnp.float32)
    grads_two, gains_two, shifts_two = norm_back(
        [back_two * silu_slope(pre_two)], normed_two, inv_two, [gain_two], weight, count_out
    )
    d_grouped = by_group(grads_two[0])
    kernel_grads = []
    row_lines = []
    for row_tap in range(3):
        tap_pieces = []
        for col_tap in range(3):
            kernel = group_w[row_tap, col_tap].reshape(GW, GROUPS, GW)
            window = by_group(window_at(padded, row_tap, col_tap, rows_out, cols_out))
            kernel_grads.append(
                jnp.einsum(
                    "nhwgc,nhwgj->cgj", window, d_grouped, preferred_element_type=jnp.float32
                ).reshape(GW, mid_width)
            )
            tap_pieces.append(
                jnp.einsum(
                    "nhwgj,cgj->nhwgc", d_grouped, kernel, preferred_element_type=jnp.float32
                ).reshape(n_images, rows_out, cols_out, mid_width)
            )
        col_even = pad_along(tap_pieces[0], 2, 0, 1) + pad_along(tap_pieces[2], 2, 1, 0)
        row_lines.append(weave(col_even, tap_pieces[1], 2))
    row_even = pad_along(row_lines[0], 1, 0, 1) + pad_along(row_lines[2], 1, 1, 0)
    back_pad = weave(row_even, row_lines[1], 1)
    grad_group = jnp.stack(kernel_grads).reshape(3, 3, GW, mid_width)
    from_below = shifted(back_pad[:, 0:1, 1:].astype(jnp.bfloat16), "ha", -1).astype(jnp.float32)
    back_one = back_pad[:, 1:, 1:]
    back_one = jnp.concatenate([back_one[:, :-1], back_one[:, -1:] + from_below], axis=1)
    grads_one, gains_one, shifts_one = norm_back(
        [back_one * silu_slope(pre_one)], normed_one, inv_one, [gain_one], weight, count_in
    )
    d_reduced = grads_one[0]
    grad_reduce = jnp.einsum(
        "nhwc,nhwd->cd", images_in, d_reduced, preferred_element_type=jnp.float32
    )
    back_in = jnp.einsum("nhwd,cd->nhwc", d_reduced, reduce_w, preferred_element_type=jnp.float32)
    zeros_side = jnp.zeros_like(back_side)
    side_row = weave(pad_along(back_side, 2, 0, 1), zeros_side, 2)[:, :, :cols_in]
    side_full = weave(pad_along(side_row, 1, 0, 1), jnp.zeros_like(side_row), 1)[:, :rows_in]
    grad_images = (back_in + side_full).astype(jnp.bfloat16)
    parts = (
        lax.psum_scatter(grad_reduce.reshape(-1), ("ha", "ba"), scatter_dimension=0, tiled=True),
        lax.psum_scatter(grad_group.reshape(-1), ("ha", "ba"), scatter_dimension=0, tiled=True),
        lax.psum_scatter(grad_expand.reshape(-1), ("ha", "ba"), scatter_dimension=0, tiled=True),
        lax.psum_scatter(grad_proj.reshape(-1), ("ha", "ba"), scatter_dimension=0, tiled=True),
    )
    wholes = (
        lax.all_gather(parts[0].astype(jnp.bfloat16), ("ha", "ba"), axis=0, tiled=True).astype(
            jnp.float32
        ),
        lax.all_gather(parts[1].astype(jnp.bfloat16), ("ha", "ba"), axis=0, tiled=True).astype(
            jnp.float32
        ),
        lax.all_gather(parts[2].astype(jnp.bfloat16), ("ha", "ba"), axis=0, tiled=True).astype(
            jnp.float32
        ),
        lax.all_gather(parts[3].astype(jnp.bfloat16), ("ha", "ba"), axis=0, tiled=True).astype(
            jnp.float32
        ),
    )
    grad_reduce = wholes[0].reshape(grad_reduce.shape)
    grad_group = wholes[1].reshape(grad_group.shape)
    grad_expand = wholes[2].reshape(grad_expand.shape)
    grad_proj = wholes[3].reshape(grad_proj.shape)
    return (
        output,
        grad_images,
        grad_reduce,
        gains_one[0],
        shifts_one[0],
        grad_group,
        gains_two[0],
        shifts_two[0],
        grad_expand,
        gains_out[0],
        shifts_out[0],
        grad_proj,
        gains_out[1],
        shifts_out[1],
    )


def solution(mesh):
    return jax.shard_map(
        per_device,
        mesh=mesh,
        in_specs=(
            P("ba", "ha", None, None),
            P(),
            P(),
            P(),
            P(),
            P(),
            P(),
            P(),
            P(),
            P(),
            P(),
            P(),
            P(),
            P("ba"),
            P("ba", "ha", None, None),
        ),
        out_specs=(
            P("ba", "ha", None, None),
            P("ba", "ha", None, None),
            P(),
            P(),
            P(),
            P(),
            P(),
            P(),
            P(),
            P(),
            P(),
            P(),
            P(),
            P(),
        ),
        check_vma=False,
    )
```

profile of v0, /device:TPU:0, one launch (start us, length us, event | category | flops | bytes accessed | tf_op | source)
XLA Modules:
  0.0 1792.0 jit_solution(14944887087584480981)
XLA Ops:
  10.0 9.0 multiply_reduce_fusion.4
  18.9 42.0 %all-reduce.20 = (f32[1024]{0:T(1024)S(1)}, f32[]{:T(128)}) all-reduce(f32[1024]{0:T(1024)S(1)} %get-tuple-element.67, f32[]{:T(128)S(6)} %mul.307), channel_id=1, replica_groups=mesh['ha'=4,'ba'=8] {'ha','ba'}, use_global_device_ids=true, to_apply=%region_1.0 | all-reduce | flops 1025 | bytes 8200 | tf_op jit(solution)/shard_map/psum | solution.py:39
  66.3 40.4 %psum.103 = f32[1024]{0:T(1024)S(1)} all-reduce(f32[1024]{0:T(1024)S(1)} %multiply_reduce_fusion.3), channel_id=1, replica_groups=mesh['ha'=4,'ba'=8] {'ha','ba'}, use_global_device_ids=true, to_apply=%region_5.0 | all-reduce | flops 1024 | bytes 8192 | tf_op jit(solution)/shard_map/psum | solution.py:45
  121.0 15.3 slice.161
  161.4 17.4 slice.157
  178.8 17.4 slice.155
  196.2 17.9 slice.153
  214.0 17.5 slice.151
  231.5 17.4 slice.149
  248.9 17.7 slice.147
  266.7 17.5 slice.145
  284.1 17.5 slice.143
  301.6 15.6 slice.159
  348.4 17.8 reshape.172
  426.8 24.1 %multiply_reduce_fusion.2 = (f32[32,32]{1,0:T(8,128)S(1)}, f32[8,4,16,32,32]{4,2,1,0,3:T(8,128)}) fusion(f32[8]{0:T(128)S(1)} %convert_element_type.67, bf16[32,32,32,1,1]{2,1,0,4,3:T(8,128)(2,1)S(1)} %bitcast.259, bf16[8,4,16,32,32]{4,3,2,1,0:T(8,128)(2,1)} %reshape.178, f32[32,8,4,16,32]{4,3,2,1,0:T(8,128)S(1)} %fusion.35, ...), kind=kOutput, calls=%fused_computation.10 | convolution fusion | flops 38796288 | bytes 19992608 | tf_op jit(solution)/shard_map/nhwgc,cgj->nhwgj/dot_general | solution.py:138
  451.0 38.4 %all-reduce.19 = (f32[1024]{0:T(1024)S(1)}, f32[]{:T(128)}) all-reduce(f32[1024]{0:T(1024)S(1)} %reduce_sum.164, f32[]{:T(128)S(6)} %mul.317), channel_id=1, replica_groups=mesh['ha'=4,'ba'=8] {'ha','ba'}, use_global_device_ids=true, to_apply=%region_7.8 | all-reduce | flops 1025 | bytes 8200 | tf_op jit(solution)/shard_map/psum | solution.py:39
  490.2 11.7 copy.189
  503.6 40.4 %psum.106 = f32[1024]{0:T(1024)S(1)} all-reduce(f32[1024]{0:T(1024)S(1)} %reduce_sum.166), channel_id=1, replica_groups=mesh['ha'=4,'ba'=8] {'ha','ba'}, use_global_device_ids=true, to_apply=%region_10.11 | all-reduce | flops 1024 | bytes 8192 | tf_op jit(solution)/shard_map/psum | solution.py:45
  552.4 8.9 multiply_reduce_fusion.10
  561.3 40.2 %psum.107 = f32[4096]{0:T(1024)S(1)} all-reduce(f32[4096]{0:T(1024)S(1)} %pad_maximum_fusion.4), channel_id=1, replica_groups=mesh['ha'=4,'ba'=8] {'ha','ba'}, use_global_device_ids=true, to_apply=%region_13.14 | all-reduce | flops 4096 | bytes 32768 | tf_op jit(solution)/shard_map/psum | solution.py:39
  607.0 40.3 %psum.108 = f32[4096]{0:T(1024)S(1)} all-reduce(f32[4096]{0:T(1024)S(1)} %pad_maximum_fusion.5), channel_id=1, replica_groups=mesh['ha'=4,'ba'=8] {'ha','ba'}, use_global_device_ids=true, to_apply=%region_16.17 | all-reduce | flops 4096 | bytes 32768 | tf_op jit(solution)/shard_map/psum | solution.py:45
  648.0 8.1 fusion.113
  656.1 40.1 %all-reduce.18 = (f32[4096]{0:T(1024)S(1)}, f32[4096]{0:T(1024)S(1)}) all-reduce(f32[4096]{0:T(1024)S(1)} %get-tuple-element.74, f32[4096]{0:T(1024)S(1)} %get-tuple-element.73), channel_id=1, replica_groups=mesh['ha'=4,'ba'=8] {'ha','ba'}, use_global_device_ids=true, to_apply=%region_21.22 | all-reduce | flops 8192 | bytes 65536 | tf_op jit(solution)/shard_map/psum | solution.py:57
  714.4 40.2 %all-reduce.17 = (f32[1024]{0:T(1024)S(1)}, f32[1024]{0:T(1024)S(1)}) all-reduce(f32[1024]{0:T(1024)S(1)} %get-tuple-element.20, f32[1024]{0:T(1024)S(1)} %get-tuple-element.19), channel_id=1, replica_groups=mesh['ha'=4,'ba'=8] {'ha','ba'}, use_global_device_ids=true, to_apply=%region_25.26 | all-reduce | flops 2048 | bytes 16384 | tf_op jit(solution)/shard_map/psum | solution.py:57
  762.6 10.7 fusion.28
  844.6 8.2 copy.214
  860.6 11.6 copy.217
  872.2 8.1 reshape.188
  899.3 8.3 copy.192
  915.3 11.5 copy.195
  953.7 8.6 copy.203
  970.0 11.5 copy.206
  993.8 11.6 copy.220
  1022.7 8.2 copy.198
  1030.9 7.9 stack_reshape.36
  1048.3 8.2 copy.209
  1056.5 8.1 stack_reshape.37
  1092.1 8.6 slice.194
  1133.9 9.4 copy.260
  1143.4 8.9 copy.335
  1153.9 8.5 fusion.112
  1162.4 42.0 %all-reduce.16 = (f32[1024]{0:T(1024)S(1)}, f32[1024]{0:T(1024)S(1)}) all-reduce(f32[1024]{0:T(1024)S(1)} %get-tuple-element.15, f32[1024]{0:T(1024)S(1)} %get-tuple-element.14), channel_id=1, replica_groups=mesh['ha'=4,'ba'=8] {'ha','ba'}, use_global_device_ids=true, to_apply=%region_29.30 | all-reduce | flops 2048 | bytes 16384 | tf_op jit(solution)/shard_map/psum | solution.py:57
  1204.5 8.0 multiply_convert_fusion
  1231.2 361.0 %all-reduce.22 = (bf16[1048576]{0:T(1024)(128)(2,1)}, bf16[294912]{0:T(1024)(128)(2,1)}, bf16[2097152]{0:T(1024)(128)(2,1)}, bf16[2097152]{0:T(1024)(128)(2,1)}) all-reduce(f32[1048576]{0:T(1024)} %bitcast.254, f32[294912]{0:T(1024)S(1)} %bitcast.258, f32[2097152]{0:T(1024)} %bitcast.240, ...), channel_id=2, replica_groups=mesh['ha'=4,'ba'=8] {'ha','ba'}, use_global_device_ids=true, to_apply=%region_30.31.clone | all-reduce | flops 5537792 | bytes 33226752
  1611.3 42.9 %all_gather.13 = bf16[294912]{0:T(1024)(128)(2,1)S(1)} all-gather(bf16[9216]{0:T(1024)(128)(2,1)S(1)} %dynamic-slice.11), channel_id=1, replica_groups=mesh['ha'=4,'ba'=8] {'ha','ba'}, dimensions={0}, use_global_device_ids=true | all-gather | bytes 608256 | tf_op jit(solution)/shard_map/all_gather | solution.py:222
  1655.4 9.6 add_convert_fusion
  1669.5 44.3 %all-gather.6.cloned.1.call-done = bf16[2097152]{0:T(1024)(128)(2,1)} async-done(((bf16[65536]{0:T(1024)(128)(2,1)}), bf16[2097152]{0:T(1024)(128)(2,1)}) %all-gather.6.cloned.1.call-update) | async-done | bytes 4194320 | tf_op jit(solution)/shard_map/all_gather | solution.py:225
  1721.6 55.9 %all-gather.8.cloned.1.call-done = bf16[2097152]{0:T(1024)(128)(2,1)} async-done(((bf16[65536]{0:T(1024)(128)(2,1)}), bf16[2097152]{0:T(1024)(128)(2,1)}) %all-gather.8.cloned.1.call-update) | async-done | bytes 4194320 | tf_op jit(solution)/shard_map/all_gather | solution.py:228
  (338 shorter events, 481.0 us)
Async XLA Ops:
  7.2 1657.8 %all-gather.4.cloned.1.call-start = ((), (), s32[]{:S(2)}) async-start(), calls=%async_computation | async-start | bytes 2162688 | tf_op jit(solution)/shard_map/all_gather | solution.py:219
  8.0 746.6 %copy-start.64 = (f32[8]{0:T(128)}, f32[8]{0:T(128)S(1)}, u32[]{:S(2)}) copy-start(f32[8]{0:T(128)S(1)} %convert_element_type.67) | copy-start | bytes 100
  61.6 46.3 %copy-start.58 = (f32[1024]{0:T(1024)}, f32[1024]{0:T(1024)S(1)}, u32[]{:S(2)}) copy-start(f32[1024]{0:T(1024)S(1)} %broadcast_divide_fusion.2) | copy-start | bytes 12292
  61.6 45.1 %copy-start.62 = (f32[1024]{0:T(1024)S(1)}, f32[1024]{0:T(1024)}, u32[]{:S(2)}) copy-start(f32[1024]{0:T(1024)} %param.17) | copy-start | bytes 12292
  61.6 46.3 %copy-start.72 = (f32[1024]{0:T(1024)S(1)}, f32[1024]{0:T(1024)}, u32[]{:S(2)}) copy-start(f32[1024]{0:T(1024)} %param.18) | copy-start | bytes 12292
  115.6 40.1 %collective-permute-start = (bf16[8,1,32,1024]{3,2,1,0:T(8,128)(2,1)}, bf16[8,1,32,1024]{3,2,1,0:T(8,128)(2,1)}, u32[]{:S(2)}, u32[]{:S(2)}) collective-permute-start(bf16[8,1,32,1024]{3,2,1,0:T(8,128)(2,1)} %slice.180), channel_id=1, source_target_pairs={{0,8},{8,16},{16,24},{1,9},{9,17},{17,25},{2,10},{10,18},{18,26},{... | collective-permute-start | bytes 1572872 | tf_op jit(solution)/shard_map/ppermute | solution.py:16
  136.3 19.4 %copy-start.49 = (bf16[8,4,16,1024]{3,2,1,0:T(8,128)(2,1)}, bf16[8,4,16,1024]{3,2,1,0:T(8,128)(2,1)S(1)}, u32[]{:S(2)}) copy-start(bf16[8,4,16,1024]{3,2,1,0:T(8,128)(2,1)S(1)} %slice.161) | copy-start | bytes 3145732
  148.3 278.5 %copy-start.31 = (bf16[32,32,32]{2,1,0:T(8,128)(2,1)}, bf16[32,32,32]{2,1,0:T(8,128)(2,1)S(1)}, u32[]{:S(2)}) copy-start(bf16[32,32,32]{2,1,0:T(8,128)(2,1)S(1)} %reshape_squeeze.44) | copy-start | bytes 196612
  490.2 11.7 copy-start.4
  544.0 7.7 copy-start.81
  544.0 8.4 copy-start.83
  602.2 45.7 %copy-start.70 = (f32[2048]{0:T(1024)S(1)}, f32[2048]{0:T(1024)}, u32[]{:S(2)}) copy-start(f32[2048]{0:T(1024)} %param.23) | copy-start | bytes 24580
  602.3 45.7 %copy-start.71 = (f32[2048]{0:T(1024)S(1)}, f32[2048]{0:T(1024)}, u32[]{:S(2)}) copy-start(f32[2048]{0:T(1024)} %param.26) | copy-start | bytes 24580
  602.3 45.7 %copy-start.75 = (f32[2048]{0:T(1024)S(1)}, f32[2048]{0:T(1024)}, u32[]{:S(2)}) copy-start(f32[2048]{0:T(1024)} %param.27) | copy-start | bytes 24580
  602.3 45.7 %copy-start.76 = (f32[2048]{0:T(1024)S(1)}, f32[2048]{0:T(1024)}, u32[]{:S(2)}) copy-start(f32[2048]{0:T(1024)} %param.24) | copy-start | bytes 24580
  696.2 7.8 copy-start.66
  696.2 7.8 copy-start.67
  696.2 7.8 copy-start.68
  696.3 7.8 copy-start.69
  696.3 7.8 copy-start.29
  754.6 8.0 copy-start.77
  754.6 8.0 copy-start.78
  762.6 10.7 copy-start.1
  762.6 10.7 copy-start.25
  787.7 7.5 copy-start.18
  816.7 7.5 copy-start.19
  1092.1 10.9 slice-start.6
  1092.1 10.9 slice-start.7
  1122.1 30.1 %collective-permute-start.1 = (bf16[8,1,32,1024]{3,2,1,0:T(8,128)(2,1)}, bf16[8,1,32,1024]{3,2,1,0:T(8,128)(2,1)}, u32[]{:S(2)}, u32[]{:S(2)}) collective-permute-start(bf16[8,1,32,1024]{3,2,1,0:T(8,128)(2,1)} %slice.228), channel_id=1, source_target_pairs={{8,0},{16,8},{24,16},{9,1},{17,9},{25,17},{10,2},{18,10},{26,18},{... | collective-permute-start | bytes 1572872 | tf_op jit(solution)/shard_map/ppermute | solution.py:16
  1123.4 7.8 copy-start.55
  1123.4 7.8 copy-start.56
  1123.4 7.8 copy-start.54
  1123.5 7.8 copy-start.53
  1123.5 7.8 copy-start.52
  1123.5 7.9 copy-start.51
  1143.3 10.5 slice-start
  1143.3 10.5 slice-start.1
  1143.3 10.5 copy-start.59
  1143.3 10.6 copy-start.61
  1143.3 10.6 copy-start.63
  1143.3 10.6 copy-start.73
  1153.9 50.6 %copy-start.65 = (f32[8]{0:T(128)S(1)}, f32[8]{0:T(128)}, u32[]{:S(2)}) copy-start(f32[8]{0:T(128)} %copy-done.64) | copy-start | bytes 100
  1153.9 50.5 %copy-start.74 = (f32[1024]{0:T(1024)S(1)}, f32[1024]{0:T(1024)}, u32[]{:S(2)}) copy-start(f32[1024]{0:T(1024)} %get-tuple-element.39) | copy-start | bytes 12292
  1204.5 8.1 copy-start.79
  1204.5 8.1 copy-start.80
  1204.5 10.1 copy-start.57
  1593.7 120.1 %all-gather.6.cloned.1.call-start = ((), (), s32[]{:S(2)}) async-start(), calls=%async_computation.1 | async-start | bytes 4325376 | tf_op jit(solution)/shard_map/all_gather | solution.py:225
  1595.3 182.2 %all-gather.8.cloned.1.call-start = ((), (), s32[]{:S(2)}) async-start(), calls=%async_computation.2 | async-start | bytes 4325376 | tf_op jit(solution)/shard_map/all_gather | solution.py:228
  (49 other events, 250.0 us)
Sparse Core Ops, SparseCore 0:
  1593.8 55.8 all-gather.3
  1652.7 60.9 all-gather.5
  1716.8 60.6 all-gather.7
where the time goes:
time: 1810 us; the launch traced here: 1790 us
  blocking collectives  768 us (42%)
  local copies, waits for them, and re-layouts  562 us (31%)
  matrix products  240 us (13%)
  waiting for transfers between devices  100 us (6%)
  other arithmetic  98.4 us (5%)
    unnamed x1, blocking collectives  361 us
    slice x9, local copies, waits for them, and re-layouts, window_at(): padded[:, row_tap:row_tap + 2 * rows_out:2, col_tap:col_tap + 2 * cols_ou...  156 us
    psum x3, blocking collectives, norm_back(): lax.psum((jnp.concatenate([channel_sums(member) for member in upstreams])...  122 us
    psum x3, blocking collectives, moments(): lax.psum(jnp.concatenate([channel_sums(member * member * weight) for memb...  121 us
    psum x3, blocking collectives, moments(): lax.psum((jnp.concatenate([channel_sums(member * weight) for member in ac...  121 us
    transpose x9, local copies, waits for them, and re-layouts, per_device(): jnp.einsum('nhwgj,cgj->nhwgc', d_grouped, kernel, preferred_element_type=...  87.8 us
    reshape x10, local copies, waits for them, and re-layouts, by_group(): return values.reshape(values.shape[:3] + (GROUPS, GW))  70.1 us
    dot_general x9, matrix products, per_device(): jnp.einsum('nhwgc,nhwgj->cgj', window, d_grouped, preferred_element_type=...  68.5 us
  transfers between devices with their start and end apart: 5, of which 2 were waited for; matrix products, arithmetic and copies ran while one was open for 6% of the time, Pallas kernels for 0%

commit v1 on v0

--- a/solution.py
+++ b/solution.py
@@ -1,6 +1,8 @@
 import jax
 import jax.numpy as jnp
 from jax import lax
+from jax.experimental import pallas as pl
+from jax.experimental.pallas import tpu as pltpu
 from jax.sharding import PartitionSpec as P
 
 GROUPS = 32
@@ -34,37 +36,149 @@
     return pieces
 
 
+def exchange(value, axis, mask):
+    peers = lax.axis_size(axis)
+    return lax.ppermute(value, axis, [(i, i ^ mask) for i in range(peers)])
+
+
+def sum_plan():
+    rounds = []
+    for axis in ("ba", "ha"):
+        bits = [1 << b for b in range(lax.axis_size(axis).bit_length() - 1)]
+        if axis == "ba" and bits:
+            rounds.append((axis, bits[:1]))
+            bits = bits[1:]
+        while bits:
+            rounds.append((axis, bits[:2]))
+            bits = bits[2:]
+    return rounds
+
+
+def meet(value, axis, masks):
+    offsets = [0]
+    for mask in masks:
+        offsets = offsets + [o ^ mask for o in offsets]
+    return [value] + [exchange(value, axis, o) for o in offsets[1:]]
+
+
+def mesh_sum(value):
+    for axis, masks in sum_plan():
+        parts = meet(value, axis, masks)
+        while len(parts) > 1:
+            parts = [parts[i] + parts[i + 1] for i in range(0, len(parts), 2)]
+        value = parts[0]
+    return value
+
+
+def merge(one, two):
+    count = one[0] + two[0]
+    gap = two[1] - one[1]
+    mean = (one[0] * one[1] + two[0] * two[1]) / count
+    return (count, mean, one[2] + two[2] + gap * gap * (one[0] * two[0] / count))
+
+
+def mesh_moments(count, mean, spread):
+    width = mean.shape[0]
+    state = (count, mean, spread)
+    for axis, masks in sum_plan():
+        packed = jnp.stack([jnp.broadcast_to(state[0], (width,)), state[1], state[2]])
+        parts = [state] + [(p[0], p[1], p[2]) for p in meet(packed, axis, masks)[1:]]
+        while len(parts) > 1:
+            parts = [merge(parts[i], parts[i + 1]) for i in range(0, len(parts), 2)]
+        state = parts[0]
+    return state
+
+
+CUTS = (("ba", 1), ("ha", 1), ("ha", 2), ("ba", 2), ("ba", 4))
+PARTS = 32
+
+
+def own_part(cuts):
+    index = jnp.int32(0)
+    for axis, mask in cuts:
+        bit = jnp.bitwise_and(lax.axis_index(axis), mask) // mask
+        index = index * 2 + bit.astype(jnp.int32)
+    return index
+
+
+def pack_kernel(own_ref, value_ref, out_ref):
+    out_ref[...] = value_ref[...].astype(out_ref.dtype)
+
+
+def relabel(value, own, dtype):
+    parts, rows, cols = value.shape
+    spec = pltpu.PrefetchScalarGridSpec(
+        num_scalar_prefetch=1,
+        grid=(parts,),
+        in_specs=[pl.BlockSpec((None, rows, cols), lambda j, own: (jnp.bitwise_xor(j, own[0]), 0, 0))],
+        out_specs=pl.BlockSpec((None, rows, cols), lambda j, own: (j, 0, 0)),
+    )
+    return pl.pallas_call(
+        pack_kernel,
+        grid_spec=spec,
+        out_shape=jax.ShapeDtypeStruct(value.shape, dtype),
+    )(own.reshape(1), value)
+
+
+def add_low(one, two):
+    return (one.astype(jnp.float32) + two.astype(jnp.float32)).astype(jnp.bfloat16)
+
+
+def scatter_sum(blocks, cuts):
+    for axis, mask in cuts:
+        half = blocks.shape[0] // 2
+        got = exchange(blocks[half:], axis, mask)
+        blocks = add_low(blocks[:half], got)
+    spare = 8
+    while spare < lax.axis_size("ba"):
+        blocks = add_low(blocks, exchange(blocks, "ba", spare))
+        spare *= 2
+    return blocks
+
+
+def gather_all(part, cuts):
+    blocks = part
+    for axis, mask in reversed(cuts):
+        blocks = jnp.concatenate([blocks, exchange(blocks, axis, mask)], axis=0)
+    return blocks
+
+
+def total_gradient(value, cuts):
+    own = own_part(cuts)
+    part = scatter_sum(relabel(value, own, jnp.bfloat16), cuts)
+    return relabel(gather_all(part, cuts), own, jnp.float32)
+
+
 def moments(activations, weight, local_count):
     extents = [member.shape[-1] for member in activations]
-    totals, count_of = lax.psum(
-        (jnp.concatenate([channel_sums(member * weight) for member in activations]), local_count),
-        ("ha", "ba"),
-    )
-    means = split_like(totals / count_of, extents)
-    centred = [member - mean_of for member, mean_of in zip(activations, means)]
-    spread = lax.psum(
-        jnp.concatenate([channel_sums(member * member * weight) for member in centred]),
-        ("ha", "ba"),
-    )
-    variance = spread / count_of
-    inv_std = split_like(lax.rsqrt(variance + EPS), extents)
+    means = [channel_sums(member * weight) / local_count for member in activations]
+    spreads = [
+        channel_sums((member - mean) * (member - mean) * weight)
+        for member, mean in zip(activations, means)
+    ]
+    count, mean, spread = mesh_moments(local_count, jnp.concatenate(means), jnp.concatenate(spreads))
+    if jnp.ndim(count):
+        count = count[0]
+    inv_std = split_like(lax.rsqrt(spread / count + EPS), extents)
+    centred = [member - m for member, m in zip(activations, split_like(mean, extents))]
     normed = [member * scale for member, scale in zip(centred, inv_std)]
-    return (normed, inv_std, count_of)
+    return (normed, inv_std, count)
 
 
 def norm_back(upstreams, normed, inv_std, gain_list, weight, count_of):
     extents = [member.shape[-1] for member in upstreams]
-    shift_sums, gain_sums = lax.psum(
-        (
-            jnp.concatenate([channel_sums(member) for member in upstreams]),
-            jnp.concatenate(
-                [channel_sums(member * other) for member, other in zip(upstreams, normed)]
-            ),
-        ),
-        ("ha", "ba"),
-    )
-    shift_grads = split_like(shift_sums, extents)
-    gain_grads = split_like(gain_sums, extents)
+    sums = mesh_sum(
+        jnp.stack(
+            [
+                jnp.concatenate([channel_sums(member) for member in upstreams]),
+                jnp.concatenate(
+                    [channel_sums(member * other) for member, other in zip(upstreams, normed)]
+                ),
+            ]
+        )
+    )
+    shift_grads = split_like(sums[0], extents)
+    gain_grads = split_like(sums[1], extents)
     results = []
     for position in range(len(upstreams)):
         adjusted = (
@@ -209,30 +323,15 @@
     side_row = weave(pad_along(back_side, 2, 0, 1), zeros_side, 2)[:, :, :cols_in]
     side_full = weave(pad_along(side_row, 1, 0, 1), jnp.zeros_like(side_row), 1)[:, :rows_in]
     grad_images = (back_in + side_full).astype(jnp.bfloat16)
-    parts = (
-        lax.psum_scatter(grad_reduce.reshape(-1), ("ha", "ba"), scatter_dimension=0, tiled=True),
-        lax.psum_scatter(grad_group.reshape(-1), ("ha", "ba"), scatter_dimension=0, tiled=True),
-        lax.psum_scatter(grad_expand.reshape(-1), ("ha", "ba"), scatter_dimension=0, tiled=True),
-        lax.psum_scatter(grad_proj.reshape(-1), ("ha", "ba"), scatter_dimension=0, tiled=True),
-    )
-    wholes = (
-        lax.all_gather(parts[0].astype(jnp.bfloat16), ("ha", "ba"), axis=0, tiled=True).astype(
-            jnp.float32
-        ),
-        lax.all_gather(parts[1].astype(jnp.bfloat16), ("ha", "ba"), axis=0, tiled=True).astype(
-            jnp.float32
-        ),
-        lax.all_gather(parts[2].astype(jnp.bfloat16), ("ha", "ba"), axis=0, tiled=True).astype(
-            jnp.float32
-        ),
-        lax.all_gather(parts[3].astype(jnp.bfloat16), ("ha", "ba"), axis=0, tiled=True).astype(
-            jnp.float32
-        ),
-    )
-    grad_reduce = wholes[0].reshape(grad_reduce.shape)
-    grad_group = wholes[1].reshape(grad_group.shape)
-    grad_expand = wholes[2].reshape(grad_expand.shape)
-    grad_proj = wholes[3].reshape(grad_proj.shape)
+    swapped = (CUTS[0], CUTS[2], CUTS[1], CUTS[3], CUTS[4])
+    mid = grad_reduce.shape[1]
+    wide = grad_expand.shape[1]
+    grad_expand = total_gradient(grad_expand.reshape(PARTS, -1, wide), CUTS).reshape(grad_expand.shape)
+    grad_proj = total_gradient(grad_proj.reshape(PARTS, -1, wide), swapped).reshape(grad_proj.shape)
+    taps = jnp.transpose(grad_group.reshape(9, GW, mid), (1, 0, 2))
+    taps = total_gradient(taps, swapped)
+    grad_group = jnp.transpose(taps, (1, 0, 2)).reshape(grad_group.shape)
+    grad_reduce = total_gradient(grad_reduce.reshape(PARTS, -1, mid), CUTS).reshape(grad_reduce.shape)
     return (
         output,
         grad_images,

time: 1810 us -> 1240 us (0.69)
  blocking collectives: 768 us -> 0 us
  Pallas kernels: 0 us -> 140 us
  starting transfers between devices: 6.73 us -> 91.1 us
  local copies, waits for them, and re-layouts: 562 us -> 525 us
  waiting for transfers between devices: 100 us -> 126 us
    psum x9 -> x0, blocking collectives: 364 us -> none  [the longest x3 122 us: norm_back(): lax.psum((jnp.concatenate([channel_sums(member) for member in upstreams])...]
    unnamed x1 -> x0, blocking collectives: 361 us -> none
    pallas_call x0 -> x8, Pallas kernels: none -> 140 us  [relabel(): pl.pallas_call(pack_kernel, grid_spec=spec, out_shape=jax.ShapeDtypeStruc...]
    ppermute x0 -> x82, waiting for transfers between devices: none -> 126 us  [exchange(): return lax.ppermute(value, axis, [(i, i ^ mask) for i in range(peers)])]
    all_gather x3 -> x0, waiting for transfers between devices: 100 us -> none  [the longest x1 55.9 us: per_device(): lax.all_gather(parts[3].astype(jnp.bfloat16), ('ha', 'ba'), axis=0, tiled...]
    ppermute x0 -> x82, starting transfers between devices: none -> 86.9 us  [exchange(): return lax.ppermute(value, axis, [(i, i ^ mask) for i in range(peers)])]
    all_gather x1 -> x0, blocking collectives: 42.9 us -> none  [per_device(): lax.all_gather(parts[1].astype(jnp.bfloat16), ('ha', 'ba'), axis=0, tiled...]
    reshape x4 -> x0, local copies, waits for them, and re-layouts: 21.3 us -> none  [the longest x1 7.79 us: per_device(): grad_expand = wholes[2].reshape(grad_expand.shape)]
  transfers between devices with their start and end apart: 5 -> 84, of which waited for: 2 -> 51; matrix products, arithmetic and copies ran while one was open for 6% -> 14% of each run, Pallas kernels for 0% -> 10%
where the time goes in v1:
time: 1240 us; the launch traced here: 1220 us
  local copies, waits for them, and re-layouts  525 us (42%)
  matrix products  238 us (19%)
  Pallas kernels  140 us (11%)
  waiting for transfers between devices  126 us (10%)
  other arithmetic  94.6 us (8%)
  starting transfers between devices  91.1 us (7%)
    slice x9, local copies, waits for them, and re-layouts, window_at(): padded[:, row_tap:row_tap + 2 * rows_out:2, col_tap:col_tap + 2 * cols_ou...  156 us
    pallas_call x8, Pallas kernels, relabel(): pl.pallas_call(pack_kernel, grid_spec=spec, out_shape=jax.ShapeDtypeStruc...  140 us
    ppermute x82, waiting for transfers between devices, exchange(): return lax.ppermute(value, axis, [(i, i ^ mask) for i in range(peers)])  126 us
    transpose x9, local copies, waits for them, and re-layouts, per_device(): jnp.einsum('nhwgj,cgj->nhwgc', d_grouped, kernel, preferred_element_type=...  88.3 us
    ppermute x82, starting transfers between devices, exchange(): return lax.ppermute(value, axis, [(i, i ^ mask) for i in range(peers)])  86.9 us
    dot_general x9, matrix products, per_device(): jnp.einsum('nhwgc,nhwgj->cgj', window, d_grouped, preferred_element_type=...  71.7 us
    dot_general x9, matrix products, per_device(): jnp.einsum('nhwgc,cgj->nhwgj', by_group(window_at(padded, row_tap, col_ta...  68 us
    reshape x10, local copies, waits for them, and re-layouts, by_group(): return values.reshape(values.shape[:3] + (GROUPS, GW))  59 us
  transfers between devices with their start and end apart: 84, of which 51 were waited for; matrix products, arithmetic and copies ran while one was open for 14% of the time, Pallas kernels for 10%

profile of v1, /device:TPU:0, one launch (start us, length us, event | category | flops | bytes accessed | tf_op | source)
XLA Modules:
  0.0 1220.2 jit_solution(7650363211608857786)
XLA Ops:
  59.5 17.4 %slice.519 = bf16[8,4,16,1024]{3,2,1,0:T(8,128)(2,1)} slice(bf16[8,9,33,1024]{3,2,1,0:T(8,128)(2,1)} %fusion.3), slice={[0:8:1], [2:9:2], [1:33:2], [0:1024:1]} | slice | bytes 2097152 | tf_op jit(solution)/shard_map/slice | solution.py:193
  77.0 17.4 %slice.517 = bf16[8,4,16,1024]{3,2,1,0:T(8,128)(2,1)} slice(bf16[8,9,33,1024]{3,2,1,0:T(8,128)(2,1)} %fusion.3), slice={[0:8:1], [2:9:2], [0:32:2], [0:1024:1]} | slice | bytes 2097152 | tf_op jit(solution)/shard_map/slice | solution.py:193
  94.4 17.9 %slice.515 = bf16[8,4,16,1024]{3,2,1,0:T(8,128)(2,1)} slice(bf16[8,9,33,1024]{3,2,1,0:T(8,128)(2,1)} %fusion.3), slice={[0:8:1], [1:9:2], [2:33:2], [0:1024:1]} | slice | bytes 2097152 | tf_op jit(solution)/shard_map/slice | solution.py:193
  112.2 17.6 %slice.513 = bf16[8,4,16,1024]{3,2,1,0:T(8,128)(2,1)} slice(bf16[8,9,33,1024]{3,2,1,0:T(8,128)(2,1)} %fusion.3), slice={[0:8:1], [1:9:2], [1:33:2], [0:1024:1]} | slice | bytes 2097152 | tf_op jit(solution)/shard_map/slice | solution.py:193
  129.8 17.6 %slice.511 = bf16[8,4,16,1024]{3,2,1,0:T(8,128)(2,1)} slice(bf16[8,9,33,1024]{3,2,1,0:T(8,128)(2,1)} %fusion.3), slice={[0:8:1], [1:9:2], [0:32:2], [0:1024:1]} | slice | bytes 2097152 | tf_op jit(solution)/shard_map/slice | solution.py:193
  147.4 17.8 %slice.509 = bf16[8,4,16,1024]{3,2,1,0:T(8,128)(2,1)} slice(bf16[8,9,33,1024]{3,2,1,0:T(8,128)(2,1)} %fusion.3), slice={[0:8:1], [0:8:2], [2:33:2], [0:1024:1]} | slice | bytes 2097152 | tf_op jit(solution)/shard_map/slice | solution.py:193
  165.1 17.4 %slice.507 = bf16[8,4,16,1024]{3,2,1,0:T(8,128)(2,1)} slice(bf16[8,9,33,1024]{3,2,1,0:T(8,128)(2,1)} %fusion.3), slice={[0:8:1], [0:8:2], [1:33:2], [0:1024:1]} | slice | bytes 2097152 | tf_op jit(solution)/shard_map/slice | solution.py:193
  182.5 17.4 %slice.505 = bf16[8,4,16,1024]{3,2,1,0:T(8,128)(2,1)} slice(bf16[8,9,33,1024]{3,2,1,0:T(8,128)(2,1)} %fusion.3), slice={[0:8:1], [0:8:2], [0:32:2], [0:1024:1]} | slice | bytes 2097152 | tf_op jit(solution)/shard_map/slice | solution.py:193
  200.0 15.6 %slice.521 = bf16[8,4,16,1024]{3,2,1,0:T(8,128)(2,1)S(1)} slice(bf16[8,9,33,1024]{3,2,1,0:T(8,128)(2,1)} %fusion.3), slice={[0:8:1], [2:9:2], [2:33:2], [0:1024:1]} | slice | bytes 2097152 | tf_op jit(solution)/shard_map/slice | solution.py:193
  314.2 24.1 %multiply_reduce_fusion.2 = (f32[32,32]{1,0:T(8,128)S(1)}, f32[8,4,16,32,32]{4,2,1,0,3:T(8,128)}) fusion(f32[8]{0:T(128)S(1)} %convert_element_type.231, bf16[32,32,32,1,1]{2,1,0,4,3:T(8,128)(2,1)S(1)} %bitcast.351, bf16[8,4,16,32,32]{4,3,2,1,0:T(8,128)(2,1)} %reshape.943, f32[32,8,4,16,32]{4,3,2,1,0:T(8,128)S(1)} %fusion.36, ...), kind=kOutput, calls=%fused_computation.10 | convolution fusion | flops 38796288 | bytes 19992608 | tf_op jit(solution)/shard_map/nhwgc,cgj->nhwgj/dot_general | solution.py:252
  348.3 15.5 %slice.545 = bf16[8,4,16,1024]{3,2,1,0:T(8,128)(2,1)S(1)} slice(bf16[8,8,32,1024]{3,2,1,0:T(8,128)(2,1)} %param.15), slice={[0:8:1], [0:8:2], [0:32:2], [0:1024:1]} | slice | bytes 2097152 | tf_op jit(solution)/shard_map/slice | solution.py:265
  372.2 11.6 copy.109
  383.8 7.9 reshape.944
  483.9 10.7 fusion.29
  509.1 7.5 fusion.23
  558.5 8.6 copy.134
  567.1 7.7 reshape.952
  574.9 11.6 copy.137
  586.5 7.8 reshape.953
  613.4 8.4 copy.112
  621.8 7.7 reshape.946
  629.6 11.6 copy.115
  641.2 8.1 reshape.947
  668.3 8.4 copy.123
  676.7 7.7 reshape.949
  684.4 11.6 copy.126
  696.0 7.7 reshape.950
  708.1 11.6 copy.140
  719.8 8.1 stack_reshape.38
  737.2 8.2 copy.118
  745.5 7.8 stack_reshape.36
  762.8 8.2 copy.129
  771.0 7.9 stack_reshape.37
  806.4 8.7 slice.710
  826.5 10.5 fusion.13
  845.7 16.4 %shard_map.256 = bf16[32,9,1024]{2,1,0:T(8,128)(2,1)} custom-call(s32[1]{0:T(128)} %bitcast.137.own_ref, f32[32,9,1024]{2,1,0:T(8,128)} %bitcast.347), custom_call_target="tpu_custom_call" | custom-call | tf_op jit(solution)/shard_map/pallas_call | solution.py:116
  864.8 8.0 fusion.117
  904.1 17.6 %shard_map.254 = bf16[32,32,1024]{2,1,0:T(8,128)(2,1)} custom-call(s32[1]{0:T(128)} %bitcast.131.own_ref, f32[32,32,1024]{2,1,0:T(8,128)} %bitcast.350), custom_call_target="tpu_custom_call" | custom-call | tf_op jit(solution)/shard_map/pallas_call | solution.py:116
  924.0 7.6 fusion.64
  931.6 18.5 %shard_map.260 = bf16[32,32,2048]{2,1,0:T(8,128)(2,1)} custom-call(s32[1]{0:T(128)} %bitcast.137.own_ref, f32[32,32,2048]{2,1,0:T(8,128)} %bitcast.346), custom_call_target="tpu_custom_call" | custom-call | tf_op jit(solution)/shard_map/pallas_call | solution.py:116
  955.0 10.0 convolution_bitcast_fusion.value_ref
  965.1 18.5 %shard_map.258 = bf16[32,32,2048]{2,1,0:T(8,128)(2,1)} custom-call(s32[1]{0:T(128)} %bitcast.131.own_ref, f32[32,32,2048]{2,1,0:T(8,128)} %convolution_bitcast_fusion.value_ref), custom_call_target="tpu_custom_call" | custom-call | tf_op jit(solution)/shard_map/pallas_call | solution.py:116
  1053.7 7.6 collective-permute-done.76
  1098.6 7.4 collective-permute-done.81
  1138.5 15.5 %shard_map.257 = f32[32,9,1024]{2,1,0:T(8,128)} custom-call(s32[1]{0:T(128)} %bitcast.137.own_ref, bf16[32,9,1024]{2,1,0:T(8,128)(2,1)} %copy-done.57), custom_call_target="tpu_custom_call" | custom-call | tf_op jit(solution)/shard_map/pallas_call | solution.py:116
  1159.5 16.9 %shard_map.255 = f32[32,32,1024]{2,1,0:T(8,128)} custom-call(s32[1]{0:T(128)} %bitcast.131.own_ref, bf16[32,32,1024]{2,1,0:T(8,128)(2,1)} %constant_dynamic-update-slice_fusion.5.value_ref), custom_call_target="tpu_custom_call" | custom-call | tf_op jit(solution)/shard_map/pallas_call | solution.py:116
  1179.6 18.5 %shard_map.261 = f32[32,32,2048]{2,1,0:T(8,128)} custom-call(s32[1]{0:T(128)} %bitcast.137.own_ref, bf16[32,32,2048]{2,1,0:T(8,128)(2,1)} %constant_dynamic-update-slice_fusion.38.value_ref), custom_call_target="tpu_custom_call" | custom-call | tf_op jit(solution)/shard_map/pallas_call | solution.py:116
  1201.3 18.5 %shard_map.259 = f32[32,32,2048]{2,1,0:T(8,128)} custom-call(s32[1]{0:T(128)} %bitcast.131.own_ref, bf16[32,32,2048]{2,1,0:T(8,128)(2,1)} %constant_dynamic-update-slice_fusion.27.value_ref), custom_call_target="tpu_custom_call" | custom-call | tf_op jit(solution)/shard_map/pallas_call | solution.py:116
  (609 shorter events, 623.4 us)
Async XLA Ops:
  38.6 13.7 %collective-permute-start.7 = (bf16[8,1,32,1024]{3,2,1,0:T(8,128)(2,1)S(1)}, bf16[8,1,32,1024]{3,2,1,0:T(8,128)(2,1)S(1)}, u32[]{:S(2)}, u32[]{:S(2)}) collective-permute-start(bf16[8,1,32,1024]{3,2,1,0:T(8,128)(2,1)S(1)} %slice.651), channel_id=1, source_target_pairs={{0,8},{8,16},{16,24},{1,9},{9,17},{17,25},{2,10},{10,18},{18,26},{... | collective-permute-start | bytes 1572872 | tf_op jit(solution)/shard_map/ppermute | solution.py:18
  344.7 19.1 %collective-permute-start.10 = (f32[3,1024]{1,0:T(4,128)S(1)}, f32[3,1024]{1,0:T(4,128)S(1)}, u32[]{:S(2)}, u32[]{:S(2)}) collective-permute-start(f32[3,1024]{1,0:T(4,128)S(1)} %pad_maximum_fusion.24), channel_id=1, source_target_pairs={{0,4},{1,5},{2,6},{3,7},{4,0},{5,1},{6,2},{7,3},{8,12},{9,13},{10,... | collective-permute-start | bytes 36872 | tf_op jit(solution)/shard_map/ppermute | solution.py:41
  344.8 19.0 %collective-permute-start.11 = (f32[3,1024]{1,0:T(4,128)S(1)}, f32[3,1024]{1,0:T(4,128)S(1)}, u32[]{:S(2)}, u32[]{:S(2)}) collective-permute-start(f32[3,1024]{1,0:T(4,128)S(1)} %pad_maximum_fusion.24), channel_id=1, source_target_pairs={{0,6},{1,7},{2,4},{3,5},{4,2},{5,3},{6,0},{7,1},{8,14},{9,15},{10,... | collective-permute-start | bytes 36872 | tf_op jit(solution)/shard_map/ppermute | solution.py:41
  345.8 18.0 %collective-permute-start.9 = (f32[3,1024]{1,0:T(4,128)S(1)}, f32[3,1024]{1,0:T(4,128)S(1)}, u32[]{:S(2)}, u32[]{:S(2)}) collective-permute-start(f32[3,1024]{1,0:T(4,128)S(1)} %pad_maximum_fusion.24), channel_id=1, source_target_pairs={{0,2},{1,3},{2,0},{3,1},{4,6},{5,7},{6,4},{7,5},{8,10},{9,11},{10,... | collective-permute-start | bytes 36872 | tf_op jit(solution)/shard_map/ppermute | solution.py:41
  364.0 29.9 %collective-permute-start.12 = (f32[3,1024]{1,0:T(4,128)S(1)}, f32[3,1024]{1,0:T(4,128)S(1)}, u32[]{:S(2)}, u32[]{:S(2)}) collective-permute-start(f32[3,1024]{1,0:T(4,128)S(1)} %pad_maximum_fusion.25), channel_id=1, source_target_pairs={{0,8},{8,0},{16,24},{24,16},{1,9},{9,1},{17,25},{25,17},{2,10},{10... | collective-permute-start | bytes 36872 | tf_op jit(solution)/shard_map/ppermute | solution.py:41
  407.8 8.6 collective-permute-start.17
  409.3 7.2 collective-permute-start.18
  434.8 5.7 collective-permute-start.25
  465.8 10.1 collective-permute-start.33
  466.8 9.0 collective-permute-start.34
  468.4 7.5 collective-permute-start.35
  824.7 38.5 %collective-permute-start.36 = (bf16[8,1,32,1024]{3,2,1,0:T(8,128)(2,1)}, bf16[8,1,32,1024]{3,2,1,0:T(8,128)(2,1)S(1)}, u32[]{:S(2)}, u32[]{:S(2)}) collective-permute-start(bf16[8,1,32,1024]{3,2,1,0:T(8,128)(2,1)} %slice.959), channel_id=1, source_target_pairs={{8,0},{16,8},{24,16},{9,1},{17,9},{25,17},{10,2},{18,10},{26,18},{... | collective-permute-start | bytes 1572872 | tf_op jit(solution)/shard_map/ppermute | solution.py:18
  863.2 18.4 %collective-permute-start.54 = (bf16[16,9,1024]{2,1,0:T(8,128)(2,1)S(1)}, bf16[16,9,1024]{2,1,0:T(8,128)(2,1)S(1)}, u32[]{:S(2)}, u32[]{:S(2)}) collective-permute-start(bf16[16,9,1024]{2,1,0:T(8,128)(2,1)S(1)} %slice.728), channel_id=1, source_target_pairs={{0,1},{1,0},{2,3},{3,2},{4,5},{5,4},{6,7},{7,6},{8,9},{9,8},{10,11... | collective-permute-start | bytes 884744 | tf_op jit(solution)/shard_map/ppermute | solution.py:41
  877.1 7.8 collective-permute-start.38
  877.2 7.8 collective-permute-start.39
  881.8 8.9 collective-permute-start.55
  885.1 7.4 collective-permute-start.41
  890.8 63.1 %collective-permute-start.56 = (bf16[4,9,1024]{2,1,0:T(8,128)(2,1)S(1)}, bf16[4,9,1024]{2,1,0:T(8,128)(2,1)}, u32[]{:S(2)}, u32[]{:S(2)}) collective-permute-start(bf16[4,9,1024]{2,1,0:T(8,128)(2,1)S(1)} %slice.732), channel_id=1, source_target_pairs={{0,8},{8,0},{16,24},{24,16},{1,9},{9,1},{17,25},{25,17},{2,10},{10... | collective-permute-start | bytes 221192 | tf_op jit(solution)/shard_map/ppermute | solution.py:41
  924.0 69.6 %collective-permute-start.44 = (bf16[16,32,1024]{2,1,0:T(8,128)(2,1)}, bf16[16,32,1024]{2,1,0:T(8,128)(2,1)S(1)}, u32[]{:S(2)}, u32[]{:S(2)}) collective-permute-start(bf16[16,32,1024]{2,1,0:T(8,128)(2,1)} %slice.718), channel_id=1, source_target_pairs={{0,1},{1,0},{2,3},{3,2},{4,5},{5,4},{6,7},{7,6},{8,9},{9,8},{10,11... | collective-permute-start | bytes 3145736 | tf_op jit(solution)/shard_map/ppermute | solution.py:41
  953.5 65.1 %collective-permute-start.74 = (bf16[16,32,2048]{2,1,0:T(8,128)(2,1)}, bf16[16,32,2048]{2,1,0:T(8,128)(2,1)}, u32[]{:S(2)}, u32[]{:S(2)}) collective-permute-start(bf16[16,32,2048]{2,1,0:T(8,128)(2,1)} %slice.748), channel_id=1, source_target_pairs={{0,1},{1,0},{2,3},{3,2},{4,5},{5,4},{6,7},{7,6},{8,9},{9,8},{10,11... | collective-permute-start | bytes 6291464 | tf_op jit(solution)/shard_map/ppermute | solution.py:41
  954.9 36.1 %collective-permute-start.57 = (bf16[2,9,1024]{2,1,0:T(8,128)(2,1)S(1)}, bf16[2,9,1024]{2,1,0:T(8,128)(2,1)S(1)}, u32[]{:S(2)}, u32[]{:S(2)}) collective-permute-start(bf16[2,9,1024]{2,1,0:T(8,128)(2,1)S(1)} %slice.734), channel_id=1, source_target_pairs={{0,2},{1,3},{2,0},{3,1},{4,6},{5,7},{6,4},{7,5},{8,10},{9,11},{10,... | collective-permute-start | bytes 110600 | tf_op jit(solution)/shard_map/ppermute | solution.py:41
  985.5 38.6 %collective-permute-start.64 = (bf16[16,32,2048]{2,1,0:T(8,128)(2,1)S(1)}, bf16[16,32,2048]{2,1,0:T(8,128)(2,1)S(1)}, u32[]{:S(2)}, u32[]{:S(2)}) collective-permute-start(bf16[16,32,2048]{2,1,0:T(8,128)(2,1)S(1)} %slice.738), channel_id=1, source_target_pairs={{0,1},{1,0},{2,3},{3,2},{4,5},{5,4},{6,7},{7,6},{8,9},{9,8},{10,11... | collective-permute-start | bytes 6291464 | tf_op jit(solution)/shard_map/ppermute | solution.py:41
  994.0 14.8 %collective-permute-start.45 = (bf16[8,32,1024]{2,1,0:T(8,128)(2,1)S(1)}, bf16[8,32,1024]{2,1,0:T(8,128)(2,1)S(1)}, u32[]{:S(2)}, u32[]{:S(2)}) collective-permute-start(bf16[8,32,1024]{2,1,0:T(8,128)(2,1)S(1)} %slice.720), channel_id=1, source_target_pairs={{0,8},{8,0},{16,24},{24,16},{1,9},{9,1},{17,25},{25,17},{2,10},{10... | collective-permute-start | bytes 1572872 | tf_op jit(solution)/shard_map/ppermute | solution.py:41
  1005.2 5.6 collective-permute-start.61
  1009.1 9.3 collective-permute-start.46
  1010.8 19.1 %collective-permute-start.62 = (bf16[8,9,1024]{2,1,0:T(8,128)(2,1)S(1)}, bf16[8,9,1024]{2,1,0:T(8,128)(2,1)S(1)}, u32[]{:S(2)}, u32[]{:S(2)}) collective-permute-start(bf16[8,9,1024]{2,1,0:T(8,128)(2,1)S(1)} %pad_maximum_fusion.10), channel_id=1, source_target_pairs={{0,16},{8,24},{16,0},{24,8},{1,17},{9,25},{17,1},{25,9},{2,18},{10... | collective-permute-start | bytes 442376 | tf_op jit(solution)/shard_map/ppermute | solution.py:41
  1021.2 26.2 %collective-permute-start.75 = (bf16[8,32,2048]{2,1,0:T(8,128)(2,1)S(1)}, bf16[8,32,2048]{2,1,0:T(8,128)(2,1)S(1)}, u32[]{:S(2)}, u32[]{:S(2)}) collective-permute-start(bf16[8,32,2048]{2,1,0:T(8,128)(2,1)S(1)} %slice.750), channel_id=1, source_target_pairs={{0,16},{8,24},{16,0},{24,8},{1,17},{9,25},{17,1},{25,9},{2,18},{10... | collective-permute-start | bytes 3145736 | tf_op jit(solution)/shard_map/ppermute | solution.py:41
  1025.0 23.5 %collective-permute-start.65 = (bf16[8,32,2048]{2,1,0:T(8,128)(2,1)S(1)}, bf16[8,32,2048]{2,1,0:T(8,128)(2,1)S(1)}, u32[]{:S(2)}, u32[]{:S(2)}) collective-permute-start(bf16[8,32,2048]{2,1,0:T(8,128)(2,1)S(1)} %slice.740), channel_id=1, source_target_pairs={{0,8},{8,0},{16,24},{24,16},{1,9},{9,1},{17,25},{25,17},{2,10},{10... | collective-permute-start | bytes 3145736 | tf_op jit(solution)/shard_map/ppermute | solution.py:41
  1030.0 107.5 %collective-permute-start.63 = (bf16[16,9,1024]{2,1,0:T(8,128)(2,1)S(1)}, bf16[16,9,1024]{2,1,0:T(8,128)(2,1)S(1)}, u32[]{:S(2)}, u32[]{:S(2)}) collective-permute-start(bf16[16,9,1024]{2,1,0:T(8,128)(2,1)S(1)} %get-tuple-element.111), channel_id=1, source_target_pairs={{0,1},{1,0},{2,3},{3,2},{4,5},{5,4},{6,7},{7,6},{8,9},{9,8},{10,11... | collective-permute-start | bytes 884744 | tf_op jit(solution)/shard_map/ppermute | solution.py:41
  1040.1 12.9 %collective-permute-start.51 = (bf16[4,32,1024]{2,1,0:T(8,128)(2,1)S(1)}, bf16[4,32,1024]{2,1,0:T(8,128)(2,1)S(1)}, u32[]{:S(2)}, u32[]{:S(2)}) collective-permute-start(bf16[4,32,1024]{2,1,0:T(8,128)(2,1)S(1)} %pad_maximum_fusion.9), channel_id=1, source_target_pairs={{0,16},{8,24},{16,0},{24,8},{1,17},{9,25},{17,1},{25,9},{2,18},{10... | collective-permute-start | bytes 786440 | tf_op jit(solution)/shard_map/ppermute | solution.py:41
  1047.9 13.4 %collective-permute-start.76 = (bf16[4,32,2048]{2,1,0:T(8,128)(2,1)S(1)}, bf16[4,32,2048]{2,1,0:T(8,128)(2,1)S(1)}, u32[]{:S(2)}, u32[]{:S(2)}) collective-permute-start(bf16[4,32,2048]{2,1,0:T(8,128)(2,1)S(1)} %slice.752), channel_id=1, source_target_pairs={{0,8},{8,0},{16,24},{24,16},{1,9},{9,1},{17,25},{25,17},{2,10},{10... | collective-permute-start | bytes 1572872 | tf_op jit(solution)/shard_map/ppermute | solution.py:41
  1049.0 13.9 %collective-permute-start.66 = (bf16[4,32,2048]{2,1,0:T(8,128)(2,1)S(1)}, bf16[4,32,2048]{2,1,0:T(8,128)(2,1)S(1)}, u32[]{:S(2)}, u32[]{:S(2)}) collective-permute-start(bf16[4,32,2048]{2,1,0:T(8,128)(2,1)S(1)} %slice.742), channel_id=1, source_target_pairs={{0,16},{8,24},{16,0},{24,8},{1,17},{9,25},{17,1},{25,9},{2,18},{10... | collective-permute-start | bytes 1572872 | tf_op jit(solution)/shard_map/ppermute | solution.py:41
  1053.1 76.2 %collective-permute-start.52 = (bf16[8,32,1024]{2,1,0:T(8,128)(2,1)S(1)}, bf16[8,32,1024]{2,1,0:T(8,128)(2,1)S(1)}, u32[]{:S(2)}, u32[]{:S(2)}) collective-permute-start(bf16[8,32,1024]{2,1,0:T(8,128)(2,1)S(1)} %pad_maximum_fusion.6), channel_id=1, source_target_pairs={{0,8},{8,0},{16,24},{24,16},{1,9},{9,1},{17,25},{25,17},{2,10},{10... | collective-permute-start | bytes 1572872 | tf_op jit(solution)/shard_map/ppermute | solution.py:41
  1061.5 6.8 collective-permute-start.77
  1063.0 11.8 collective-permute-start.67
  1068.3 8.7 collective-permute-start.78
  1074.8 7.4 collective-permute-start.68
  1077.8 6.4 collective-permute-start.79
  1083.0 7.0 collective-permute-start.69
  1084.3 8.1 collective-permute-start.80
  1090.0 6.4 collective-permute-start.70
  1092.4 13.6 %collective-permute-start.81 = (bf16[4,32,2048]{2,1,0:T(8,128)(2,1)S(1)}, bf16[4,32,2048]{2,1,0:T(8,128)(2,1)S(1)}, u32[]{:S(2)}, u32[]{:S(2)}) collective-permute-start(bf16[4,32,2048]{2,1,0:T(8,128)(2,1)S(1)} %pad_maximum_fusion.8), channel_id=1, source_target_pairs={{0,8},{8,0},{16,24},{24,16},{1,9},{9,1},{17,25},{25,17},{2,10},{10... | collective-permute-start | bytes 1572872 | tf_op jit(solution)/shard_map/ppermute | solution.py:41
  1096.4 14.5 %collective-permute-start.71 = (bf16[4,32,2048]{2,1,0:T(8,128)(2,1)S(1)}, bf16[4,32,2048]{2,1,0:T(8,128)(2,1)S(1)}, u32[]{:S(2)}, u32[]{:S(2)}) collective-permute-start(bf16[4,32,2048]{2,1,0:T(8,128)(2,1)S(1)} %pad_maximum_fusion.7), channel_id=1, source_target_pairs={{0,16},{8,24},{16,0},{24,8},{1,17},{9,25},{17,1},{25,9},{2,18},{10... | collective-permute-start | bytes 1572872 | tf_op jit(solution)/shard_map/ppermute | solution.py:41
  1106.1 16.1 %collective-permute-start.82 = (bf16[8,32,2048]{2,1,0:T(8,128)(2,1)S(1)}, bf16[8,32,2048]{2,1,0:T(8,128)(2,1)S(1)}, u32[]{:S(2)}, u32[]{:S(2)}) collective-permute-start(bf16[8,32,2048]{2,1,0:T(8,128)(2,1)S(1)} %pad_maximum_fusion.5), channel_id=1, source_target_pairs={{0,16},{8,24},{16,0},{24,8},{1,17},{9,25},{17,1},{25,9},{2,18},{10... | collective-permute-start | bytes 3145736 | tf_op jit(solution)/shard_map/ppermute | solution.py:41
  1111.3 14.9 %collective-permute-start.72 = (bf16[8,32,2048]{2,1,0:T(8,128)(2,1)S(1)}, bf16[8,32,2048]{2,1,0:T(8,128)(2,1)S(1)}, u32[]{:S(2)}, u32[]{:S(2)}) collective-permute-start(bf16[8,32,2048]{2,1,0:T(8,128)(2,1)S(1)} %pad_maximum_fusion.4), channel_id=1, source_target_pairs={{0,8},{8,0},{16,24},{24,16},{1,9},{9,1},{17,25},{25,17},{2,10},{10... | collective-permute-start | bytes 3145736 | tf_op jit(solution)/shard_map/ppermute | solution.py:41
  1123.7 52.7 %collective-permute-start.83 = (bf16[16,32,2048]{2,1,0:T(8,128)(2,1)}, bf16[16,32,2048]{2,1,0:T(8,128)(2,1)}, u32[]{:S(2)}, u32[]{:S(2)}) collective-permute-start(bf16[16,32,2048]{2,1,0:T(8,128)(2,1)} %get-tuple-element.88), channel_id=1, source_target_pairs={{0,1},{1,0},{2,3},{3,2},{4,5},{5,4},{6,7},{7,6},{8,9},{9,8},{10,11... | collective-permute-start | bytes 6291464 | tf_op jit(solution)/shard_map/ppermute | solution.py:41
  1127.7 70.4 %collective-permute-start.73 = (bf16[16,32,2048]{2,1,0:T(8,128)(2,1)}, bf16[16,32,2048]{2,1,0:T(8,128)(2,1)}, u32[]{:S(2)}, u32[]{:S(2)}) collective-permute-start(bf16[16,32,2048]{2,1,0:T(8,128)(2,1)} %get-tuple-element.90), channel_id=1, source_target_pairs={{0,1},{1,0},{2,3},{3,2},{4,5},{5,4},{6,7},{7,6},{8,9},{9,8},{10,11... | collective-permute-start | bytes 6291464 | tf_op jit(solution)/shard_map/ppermute | solution.py:41
  1130.4 26.8 %collective-permute-start.53 = (bf16[16,32,1024]{2,1,0:T(8,128)(2,1)}, bf16[16,32,1024]{2,1,0:T(8,128)(2,1)}, u32[]{:S(2)}, u32[]{:S(2)}) collective-permute-start(bf16[16,32,1024]{2,1,0:T(8,128)(2,1)} %get-tuple-element.105), channel_id=1, source_target_pairs={{0,1},{1,0},{2,3},{3,2},{4,5},{5,4},{6,7},{7,6},{8,9},{9,8},{10,11... | collective-permute-start | bytes 3145736 | tf_op jit(solution)/shard_map/ppermute | solution.py:41
  (133 other events, 1712.3 us)

commit v2 on v1

v2 whole, which is shorter than its diff:
```python
import functools

import jax
import jax.numpy as jnp
from jax import lax
from jax.experimental import pallas as pl
from jax.experimental.pallas import tpu as pltpu
from jax.sharding import PartitionSpec as P

GW = 32
EPS = 1e-05


def shifted(value, axis, by):
    peers = lax.axis_size(axis)
    pairs = [(i, i + by) for i in range(peers) if 0 <= i + by < peers]
    return lax.ppermute(value, axis, pairs)


def exchange(value, axis, mask):
    peers = lax.axis_size(axis)
    return lax.ppermute(value, axis, [(i, i ^ mask) for i in range(peers)])


def sum_plan():
    rounds = []
    for axis in ("ba", "ha"):
        bits = [1 << b for b in range(lax.axis_size(axis).bit_length() - 1)]
        if axis == "ba" and bits:
            rounds.append((axis, bits[:1]))
            bits = bits[1:]
        while bits:
            rounds.append((axis, bits[:2]))
            bits = bits[2:]
    return rounds


def meet(value, axis, masks):
    offsets = [0]
    for mask in masks:
        offsets = offsets + [o ^ mask for o in offsets]
    return [value] + [exchange(value, axis, o) for o in offsets[1:]]


def mesh_sum(value):
    for axis, masks in sum_plan():
        parts = meet(value, axis, masks)
        while len(parts) > 1:
            parts = [parts[i] + parts[i + 1] for i in range(0, len(parts), 2)]
        value = parts[0]
    return value


def merge(one, two, one_count, two_count):
    count = one_count + two_count
    gap = two[0] - one[0]
    mean = (one_count * one[0] + two_count * two[0]) / count
    return jnp.stack([mean, one[1] + two[1] + gap * gap * (one_count * two_count / count)])


def merge_parts(parts, counts):
    parts, counts = list(parts), list(counts)
    while len(parts) > 1:
        pairs = range(0, len(parts), 2)
        parts = [merge(parts[i], parts[i + 1], counts[i], counts[i + 1]) for i in pairs]
        counts = [counts[i] + counts[i + 1] for i in pairs]
    return parts[0], counts[0]


def first_moments(packed):
    rounds = []
    state = packed
    for axis, masks in sum_plan():
        parts = meet(state, axis, masks)
        counts = [part[0, 0] for part in parts]
        rounds.append(counts)
        merged, count = merge_parts([part[1:] for part in parts], counts)
        state = jnp.concatenate([jnp.full((1, merged.shape[1]), count), merged])
    return state[1:], state[0, 0], rounds


def mesh_moments(packed, rounds):
    for (axis, masks), counts in zip(sum_plan(), rounds):
        packed, _ = merge_parts(meet(packed, axis, masks), counts)
    return packed


CUTS = (("ba", 1), ("ha", 1), ("ha", 2), ("ba", 2), ("ba", 4))
PARTS = 32


def own_part(cuts):
    index = jnp.int32(0)
    for axis, mask in cuts:
        bit = jnp.bitwise_and(lax.axis_index(axis), mask) // mask
        index = index * 2 + bit.astype(jnp.int32)
    return index


def pack_kernel(own_ref, value_ref, out_ref):
    out_ref[...] = value_ref[...].astype(out_ref.dtype)


def relabel(value, own, dtype):
    parts, rows, cols = value.shape
    spec = pltpu.PrefetchScalarGridSpec(
        num_scalar_prefetch=1,
        grid=(parts,),
        in_specs=[pl.BlockSpec((None, rows, cols), lambda j, own: (jnp.bitwise_xor(j, own[0]), 0, 0))],
        out_specs=pl.BlockSpec((None, rows, cols), lambda j, own: (j, 0, 0)),
    )
    return pl.pallas_call(
        pack_kernel,
        grid_spec=spec,
        out_shape=jax.ShapeDtypeStruct(value.shape, dtype),
    )(own.reshape(1), value)


def add_low(one, two):
    return (one.astype(jnp.float32) + two.astype(jnp.float32)).astype(jnp.bfloat16)


def scatter_sum(blocks, cuts):
    for axis, mask in cuts:
        half = blocks.shape[0] // 2
        got = exchange(blocks[half:], axis, mask)
        blocks = add_low(blocks[:half], got)
    spare = 8
    while spare < lax.axis_size("ba"):
        blocks = add_low(blocks, exchange(blocks, "ba", spare))
        spare *= 2
    return blocks


def gather_all(part, cuts):
    blocks = part
    for axis, mask in reversed(cuts):
        blocks = jnp.concatenate([blocks, exchange(blocks, axis, mask)], axis=0)
    return blocks


def total_gradient(blocks, cuts, own):
    return relabel(gather_all(scatter_sum(blocks, cuts), cuts), own, jnp.float32)


LOW = jnp.bfloat16
WIDE = jnp.float32
TAPS = 3
SMEM = pltpu.SMEM


def dot(one, two):
    return jnp.dot(one, two, preferred_element_type=WIDE)


def dot_nt(one, two):
    return lax.dot_general(one, two, (((1,), (1,)), ((), ())), preferred_element_type=WIDE)


def dot_tn(one, two):
    return lax.dot_general(one, two, (((0,), (0,)), ((), ())), preferred_element_type=WIDE)


def iota(shape, axis):
    return lax.broadcasted_iota(jnp.int32, shape, axis)


def logistic(values):
    return 0.5 * jnp.tanh(0.5 * values) + 0.5


def fold(values):
    rows, width = values.shape
    return jnp.sum(values.reshape(rows // 8, 8, width), axis=0)


def close(partial):
    return jnp.sum(partial, axis=0, keepdims=True)


def spans(rows, size):
    return [slice(at, at + size) for at in range(0, rows, size)]


def widen(mask, width):
    return jnp.concatenate([mask] * (width // mask.shape[1]), axis=1)


def parity_order(image_rows, cols, axis=0):
    pixels = image_rows * cols
    quarter = pixels // 4
    half_cols = cols // 2
    place = iota((pixels, pixels), axis)
    source = iota((pixels, pixels), 1 - axis)
    plane = place // quarter
    inside = place % quarter
    row = 2 * (inside // half_cols) + plane // 2
    col = 2 * (inside % half_cols) + plane % 2
    return (source == row * cols + col).astype(WIDE).astype(LOW)


def halo_order(images, cols):
    count = images * cols
    half_cols = cols // 2
    place = iota((count, count), 0)
    source = iota((count, count), 1)
    parity = place // (count // 2)
    inside = place % (count // 2)
    image = inside // half_cols
    col = 2 * (inside % half_cols) + parity
    return (source == image * cols + col).astype(WIDE).astype(LOW)


def local_moments(ref, mask_ref, planes, plane_rows, count, size):
    width = ref.shape[1]
    total = jnp.zeros((8, width), WIDE)
    for plane in range(planes):
        for span in spans(plane_rows, size):
            at = slice(plane * plane_rows + span.start, plane * plane_rows + span.stop)
            total += fold(ref[at, :] * widen(mask_ref[span, :], width))
    mean = close(total) / count
    total = jnp.zeros((8, width), WIDE)
    for plane in range(planes):
        for span in spans(plane_rows, size):
            at = slice(plane * plane_rows + span.start, plane * plane_rows + span.stop)
            gap = ref[at, :] - mean
            total += fold(gap * gap * widen(mask_ref[span, :], width))
    return mean, close(total)


def reduce_kernel(dims, count_ref, x_ref, w_ref, mask_ref, planes_ref, reduced_ref, stats_ref):
    images, image_rows, cols = dims
    pixels = image_rows * cols
    quarter = pixels // 4
    plane_rows = images * quarter

    @pl.when(pl.program_id(0) == 0)
    def _():
        order = parity_order(image_rows, cols)
        for image in range(images):
            moved = dot(order, x_ref[image * pixels : (image + 1) * pixels, :]).astype(LOW)
            for plane in range(4):
                at = plane * plane_rows + image * quarter
                planes_ref[at : at + quarter, :] = moved[plane * quarter : (plane + 1) * quarter, :]

    for plane in range(4):
        at = slice(plane * plane_rows, (plane + 1) * plane_rows)
        reduced_ref[at, :] = dot(planes_ref[at, :], w_ref[...])
    count = count_ref[0] * float(pixels)
    mean, spread = local_moments(reduced_ref, mask_ref, 4, plane_rows, count, quarter)
    stats_ref[0:1, :] = jnp.full(mean.shape, count, WIDE)
    stats_ref[1:2, :] = mean
    stats_ref[2:3, :] = spread


def project_kernel(quarter, count_ref, x_ref, w_ref, mask_ref, out_ref, stats_ref):
    out_ref[...] = dot(x_ref[...], w_ref[...])
    count = count_ref[0] * float(quarter)
    mean, spread = local_moments(out_ref, mask_ref, 1, out_ref.shape[0], count, quarter)
    stats_ref[0:1, :] = mean
    stats_ref[1:2, :] = spread


def group_mask(width):
    return (iota((width, width), 0) // GW == iota((width, width), 1) // GW).astype(WIDE).astype(LOW)


def block_weights(w_ref, mask, tap):
    width = w_ref.shape[1]
    part = w_ref[tap * GW : (tap + 1) * GW, :]
    return jnp.concatenate([part] * (width // GW), axis=0) * mask


def shift_columns(values, cols, by):
    rows, width = values.shape
    moved = pltpu.roll(values, by % rows, 0)
    edge = 0 if by > 0 else cols - 1
    return jnp.where(iota((rows, width), 0) % cols == edge, 0.0, moved)


def activate(values, mean, scale, shift):
    normal = (values - mean) * scale + shift
    return normal * logistic(normal)


def windows(planes, odd, halves):
    even_even, even_odd, even_moved = planes
    images, deep, half_cols, width = odd[0].shape
    tall = deep - 1

    def part(ref, at):
        return ref[:, at : at + tall, :, :].reshape(images * tall * half_cols, width)

    result = []
    for row_tap in range(TAPS):
        if row_tap == 1:
            result += [even_moved[...], even_even[...], even_odd[...]]
        else:
            at = 0 if row_tap == 0 else 1
            result += [part(odd[2], at), part(odd[0], at), part(odd[1], at)]
    return result


def store_hidden(dims, get, halo, even, odd):
    images, tall, half_cols = dims
    quarter = tall * half_cols
    for image in range(images):
        at = slice(image * quarter, (image + 1) * quarter)
        even[0][at, :] = get(0, image).astype(LOW)
        values = get(1, image)
        even[1][at, :] = values.astype(LOW)
        even[2][at, :] = shift_columns(values, half_cols, 1).astype(LOW)
        values = get(2, image)
        width = values.shape[1]
        odd[0][image, 1:, :, :] = values.astype(LOW).reshape(tall, half_cols, width)
        values = get(3, image)
        odd[1][image, 1:, :, :] = values.astype(LOW).reshape(tall, half_cols, width)
        odd[2][image, 1:, :, :] = shift_columns(values, half_cols, 1).astype(LOW).reshape(tall, half_cols, width)
    width = halo[0].shape[1]
    odd[0][:, 0, :, :] = halo[0].astype(LOW).reshape(images, half_cols, width)
    odd[1][:, 0, :, :] = halo[1].astype(LOW).reshape(images, half_cols, width)
    odd[2][:, 0, :, :] = shift_columns(halo[1], half_cols, 1).astype(LOW).reshape(images, half_cols, width)


def window_scratch(images, tall, half_cols, width):
    flat = pltpu.VMEM((images * tall * half_cols, width), LOW)
    deep = pltpu.VMEM((images, tall + 1, half_cols, width), LOW)
    return [flat, flat, flat, deep, deep, deep]


def conv_kernel(
    dims,
    scalar_ref,
    reduced_ref,
    moments_ref,
    affine_ref,
    halo_ref,
    reduce_ref,
    group_ref,
    mask_ref,
    grouped_ref,
    stats_ref,
    edge_ref,
    moved_ref,
    *buffers,
):
    images, tall, half_cols = dims
    quarter = tall * half_cols
    plane_rows = images * quarter
    width = reduced_ref.shape[1]

    @pl.when(pl.program_id(0) == 0)
    def _():
        moved_ref[...] = dot(halo_order(images, 2 * half_cols), halo_ref[...]).astype(LOW)

    mean = moments_ref[0:1, :]
    scale = affine_ref[0:1, :] * lax.rsqrt(moments_ref[1:2, :] / scalar_ref[1] + EPS)
    shift = affine_ref[1:2, :]
    edge = activate(dot(moved_ref[...], reduce_ref[...]), mean, scale, shift) * scalar_ref[3]
    edge_ref[...] = edge.astype(LOW)
    half = edge.shape[0] // 2

    def get(plane, image):
        at = plane * plane_rows + image * quarter
        return activate(reduced_ref[at : at + quarter, :], mean, scale, shift)

    even, odd = buffers[:3], buffers[3:]
    store_hidden(dims, get, (edge[:half], edge[half:]), even, odd)
    mask = group_mask(width)
    total = None
    for tap, window in enumerate(windows(even, odd, half_cols)):
        term = dot(window, block_weights(group_ref, mask, tap))
        total = term if total is None else total + term
    grouped_ref[...] = total
    count = scalar_ref[0] * float(quarter)
    mean, spread = local_moments(grouped_ref, mask_ref, 1, plane_rows, count, quarter)
    stats_ref[0:1, :] = mean
    stats_ref[1:2, :] = spread


def expand_kernel(
    quarter, scalar_ref, grouped_ref, moments_ref, affine_ref, w_ref, mask_ref, hidden_ref, out_ref, stats_ref
):
    @pl.when(pl.program_id(0) == 0)
    def _():
        mean = moments_ref[0:1, :]
        scale = affine_ref[0:1, :] * lax.rsqrt(moments_ref[1:2, :] / scalar_ref[2] + EPS)
        for span in spans(grouped_ref.shape[0], 16):
            hidden_ref[span, :] = activate(grouped_ref[span, :], mean, scale, affine_ref[1:2, :]).astype(LOW)

    out_ref[...] = dot(hidden_ref[...], w_ref[...])
    count = scalar_ref[0] * float(quarter)
    mean, spread = local_moments(out_ref, mask_ref, 1, out_ref.shape[0], count, quarter)
    stats_ref[0:1, :] = mean
    stats_ref[1:2, :] = spread


def slope(values, gate):
    return gate * (1.0 + values * (1.0 - gate))


def tail_values(one, two, stats, affine, count):
    first = (one - stats[0:1, :]) * lax.rsqrt(stats[1:2, :] / count + EPS)
    second = (two - stats[2:3, :]) * lax.rsqrt(stats[3:4, :] / count + EPS)
    summed = first * affine[0:1, :] + affine[1:2, :] + second * affine[2:3, :] + affine[3:4, :]
    return first, second, summed


def output_kernel(
    size, scalar_ref, expanded_ref, projected_ref, stats_ref, affine_ref, cot_ref, mask_ref, out_ref, sums_ref
):
    rows, width = out_ref.shape
    totals = [jnp.zeros((8, width), WIDE) for _ in range(3)]
    stats = stats_ref[...]
    affine = affine_ref[...]
    for span in spans(rows, size):
        first, second, summed = tail_values(
            expanded_ref[span, :], projected_ref[span, :], stats, affine, scalar_ref[2]
        )
        valid = widen(mask_ref[span, :], width)
        gate = logistic(summed)
        out_ref[span, :] = (valid * (summed * gate)).astype(LOW)
        upstream = cot_ref[span, :].astype(WIDE) * valid * slope(summed, gate)
        totals[0] += fold(upstream)
        totals[1] += fold(upstream * first)
        totals[2] += fold(upstream * second)
    for at in range(3):
        sums_ref[at : at + 1, :] = close(totals[at])


def weights_kernel(
    size,
    scalar_ref,
    own_ref,
    expanded_ref,
    projected_ref,
    stats_ref,
    affine_ref,
    sums_ref,
    cot_ref,
    mask_ref,
    hidden_ref,
    sampled_ref,
    d_expanded_ref,
    d_projected_ref,
    grad_expand_ref,
    grad_proj_ref,
):
    rows, width = d_expanded_ref.shape
    stats = stats_ref[...]
    affine = affine_ref[...]
    count = scalar_ref[2]
    gain_one = affine[0:1, :] * lax.rsqrt(stats[1:2, :] / count + EPS)
    gain_two = affine[2:3, :] * lax.rsqrt(stats[3:4, :] / count + EPS)
    sums = sums_ref[...] / count
    for span in spans(rows, size):
        first, second, summed = tail_values(expanded_ref[span, :], projected_ref[span, :], stats, affine, count)
        valid = widen(mask_ref[span, :], width)
        upstream = cot_ref[span, :].astype(WIDE) * slope(summed, logistic(summed)) - sums[0:1, :]
        d_expanded_ref[span, :] = (valid * gain_one * (upstream - first * sums[1:2, :])).astype(LOW)
        d_projected_ref[span, :] = (valid * gain_two * (upstream - second * sums[2:3, :])).astype(LOW)
    relabel_store(dot_tn(sampled_ref[...], d_projected_ref[...]), grad_proj_ref, own_ref[1])
    relabel_store(dot_tn(hidden_ref[...], d_expanded_ref[...]), grad_expand_ref, own_ref[0])


def relabel_store(value, ref, own):
    parts, rows, _ = ref.shape
    for part in range(parts):
        ref[jnp.bitwise_xor(own, part)] = value[part * rows : (part + 1) * rows, :].astype(ref.dtype)


def back_two_kernel(size, scalar_ref, d_ref, w_ref, grouped_ref, moments_ref, affine_ref, out_ref, sums_ref):
    rows, width = out_ref.shape
    mean = moments_ref[0:1, :]
    inv = lax.rsqrt(moments_ref[1:2, :] / scalar_ref[2] + EPS)
    out_ref[...] = dot_nt(d_ref[...], w_ref[...])
    totals = [jnp.zeros((8, width), WIDE) for _ in range(2)]
    for span in spans(rows, size):
        normed = (grouped_ref[span, :] - mean) * inv
        before = normed * affine_ref[0:1, :] + affine_ref[1:2, :]
        grad = out_ref[span, :] * slope(before, logistic(before))
        out_ref[span, :] = grad
        totals[0] += fold(grad)
        totals[1] += fold(grad * normed)
    for at in range(2):
        sums_ref[at : at + 1, :] = close(totals[at])


def norm_back_values(grad, values, mean, inv, gain, sums):
    return gain * inv * (grad - (sums[0:1, :] + (values - mean) * inv * sums[1:2, :]))


def conv_back_kernel(
    dims,
    scalar_ref,
    own_ref,
    grad_ref,
    grouped_ref,
    below_grad_ref,
    below_grouped_ref,
    moments_two_ref,
    affine_two_ref,
    sums_two_ref,
    reduced_ref,
    edge_ref,
    moments_one_ref,
    affine_one_ref,
    group_ref,
    mask_ref,
    out_ref,
    sums_ref,
    grad_group_ref,
    *buffers,
):
    images, tall, half_cols = dims
    quarter = tall * half_cols
    plane_rows = images * quarter
    width = reduced_ref.shape[1]
    even, odd, below = buffers[:3], buffers[3:6], buffers[6:8]
    count_in, count_out = scalar_ref[1], scalar_ref[2]

    mean = moments_two_ref[0:1, :]
    inv = lax.rsqrt(moments_two_ref[1:2, :] / count_out + EPS)
    gain = affine_two_ref[0:1, :]
    sums = sums_two_ref[...] / count_out
    for image in range(images):
        at = slice(image * quarter, (image + 1) * quarter)
        values = norm_back_values(grad_ref[at, :], grouped_ref[at, :], mean, inv, gain, sums)
        values = values * widen(mask_ref[at, :], width)
        below[0][image, :tall, :, :] = values.astype(LOW).reshape(tall, half_cols, width)
        below[1][image, :tall, :, :] = (
            shift_columns(values, half_cols, -1).astype(LOW).reshape(tall, half_cols, width)
        )
        at = slice(image * half_cols, (image + 1) * half_cols)
        values = norm_back_values(
            below_grad_ref[at, :].astype(WIDE), below_grouped_ref[at, :].astype(WIDE), mean, inv, gain, sums
        )
        valid = mask_ref[image * quarter : image * quarter + half_cols, :]
        values = values * widen(valid, width) * scalar_ref[4]
        below[0][image, tall, :, :] = values.astype(LOW)
        below[1][image, tall, :, :] = shift_columns(values, half_cols, -1).astype(LOW)

    def part(ref, at):
        return ref[:, at : at + tall, :, :].reshape(plane_rows, width)

    mask = group_mask(width)
    weights = [block_weights(group_ref, mask, tap) for tap in range(TAPS * TAPS)]
    here, left = part(below[0], 0), part(below[1], 0)
    next_here, next_left = part(below[0], 1), part(below[1], 1)
    out_ref[0:plane_rows, :] = dot_nt(here, weights[4])
    out_ref[plane_rows : 2 * plane_rows, :] = dot_nt(here, weights[5]) + dot_nt(left, weights[3])
    out_ref[2 * plane_rows : 3 * plane_rows, :] = dot_nt(here, weights[7]) + dot_nt(next_here, weights[1])
    out_ref[3 * plane_rows : 4 * plane_rows, :] = (
        dot_nt(here, weights[8])
        + dot_nt(left, weights[6])
        + dot_nt(next_here, weights[2])
        + dot_nt(next_left, weights[0])
    )

    mean_one = moments_one_ref[0:1, :]
    inv_one = lax.rsqrt(moments_one_ref[1:2, :] / count_in + EPS)
    totals = [jnp.zeros((8, width), WIDE) for _ in range(2)]

    def get(plane, image):
        start = plane * plane_rows + image * quarter
        at = slice(start, start + quarter)
        normed = (reduced_ref[at, :] - mean_one) * inv_one
        before = normed * affine_one_ref[0:1, :] + affine_one_ref[1:2, :]
        gate = logistic(before)
        grad = out_ref[at, :] * slope(before, gate)
        out_ref[at, :] = grad
        totals[0] += fold(grad)
        totals[1] += fold(grad * normed)
        return before * gate

    half = edge_ref.shape[0] // 2
    edge = edge_ref[...].astype(WIDE)
    store_hidden(dims, get, (edge[:half], edge[half:]), even, odd)
    for at in range(2):
        sums_ref[at : at + 1, :] = close(totals[at])
    wide_mask = mask.astype(WIDE)
    pieces = []
    for window in windows(even, odd, half_cols):
        full = dot_tn(window, here) * wide_mask
        pieces.append(jnp.sum(full.reshape(width // GW, GW, width), axis=0))
    relabel_store(jnp.concatenate(pieces, axis=0), grad_group_ref, own_ref[1])


def reduced_back_kernel(
    size,
    scalar_ref,
    own_ref,
    grad_ref,
    reduced_ref,
    moments_ref,
    affine_ref,
    sums_ref,
    mask_ref,
    planes_ref,
    d_ref,
    grad_reduce_ref,
):
    rows, width = d_ref.shape
    plane_rows = mask_ref.shape[0]
    mean = moments_ref[0:1, :]
    inv = lax.rsqrt(moments_ref[1:2, :] / scalar_ref[1] + EPS)
    sums = sums_ref[...] / scalar_ref[1]
    for span in spans(rows, size):
        values = norm_back_values(grad_ref[span, :], reduced_ref[span, :], mean, inv, affine_ref[0:1, :], sums)
        at = span.start % plane_rows
        d_ref[span, :] = (values * widen(mask_ref[at : at + size, :], width)).astype(LOW)
    relabel_store(dot_tn(planes_ref[...], d_ref[...]), grad_reduce_ref, own_ref[0])


def images_back_kernel(dims, d_ref, w_ref, side_ref, proj_ref, out_ref, side_out, order_ref):
    image_rows, cols = dims
    pixels = image_rows * cols
    quarter = pixels // 4

    @pl.when(pl.program_id(0) == 0)
    def _():
        side_out[...] = dot_nt(side_ref[...], proj_ref[...])
        order_ref[...] = parity_order(image_rows, cols, 1)

    image = pl.program_id(0)
    values = dot_nt(d_ref[...].reshape(pixels, d_ref.shape[-1]), w_ref[...])
    first = values[:quarter] + side_out[pl.ds(pl.multiple_of(image * quarter, quarter), quarter), :]
    planes = jnp.concatenate([first, values[quarter:]], axis=0).astype(LOW)
    out_ref[...] = dot(order_ref[...], planes).astype(LOW)


def whole(shape):
    return pl.BlockSpec(shape, lambda i: (0,) * len(shape))


def wide_cols(rows, width):
    return pl.BlockSpec((rows, width), lambda i: (0, i))


SCALARS = pl.BlockSpec(memory_space=pltpu.SMEM)


def call(kernel, grid, in_specs, out_specs, out_shapes, cost, scratch=()):
    flops, moved = cost
    return pl.pallas_call(
        kernel,
        grid=(grid,),
        in_specs=in_specs,
        out_specs=out_specs,
        out_shape=[jax.ShapeDtypeStruct(shape, kind) for shape, kind in out_shapes],
        scratch_shapes=list(scratch),
        compiler_params=pltpu.CompilerParams(vmem_limit_bytes=56 * 1024 * 1024),
        cost_estimate=pl.CostEstimate(flops=flops, bytes_accessed=moved, transcendentals=0),
    )


def per_device(
    images_in,
    reduce_w,
    gain_one,
    shift_one,
    group_w,
    gain_two,
    shift_two,
    expand_w,
    gain_three,
    shift_three,
    proj_w,
    gain_proj,
    shift_proj,
    valid_mask,
    cotangent,
):
    images, image_rows, cols, chans = images_in.shape
    mid = reduce_w.shape[1]
    wide = expand_w.shape[1]
    tall, half_cols = image_rows // 2, cols // 2
    quarter = tall * half_cols
    rows = images * quarter
    pixels = images * image_rows * cols
    block = 256
    steps = mid // block
    strip = 512
    strips = wide // strip

    weight = valid_mask.astype(WIDE)
    local = jnp.sum(weight)
    local_one = local.reshape(1)
    mask = jnp.broadcast_to(weight[:, None, None], (images, quarter, 128)).reshape(rows, 128)
    row_index = lax.axis_index("ha")
    has_upper = (row_index > 0).astype(WIDE)
    has_lower = (row_index < lax.axis_size("ha") - 1).astype(WIDE)
    swapped = (CUTS[0], CUTS[2], CUTS[1], CUTS[3], CUTS[4])
    own_plain, own_swapped = own_part(CUTS), own_part(swapped)
    own = jnp.stack([own_plain, own_swapped])
    affine_one = jnp.stack([gain_one, shift_one])
    affine_two = jnp.stack([gain_two, shift_two])
    affine_out = jnp.stack([gain_three, shift_three, gain_proj, shift_proj])
    group_flat = group_w.reshape(TAPS * TAPS * GW, mid)

    halo_images = shifted(images_in[:, -1], "ha", 1).reshape(images * cols, chans)
    planes, reduced, stats = call(
        functools.partial(reduce_kernel, (images, image_rows, cols)),
        steps,
        [SCALARS, whole((pixels, chans)), wide_cols(chans, block), whole((rows, 128))],
        [whole((pixels, chans)), wide_cols(pixels, block), wide_cols(3, block)],
        [((pixels, chans), LOW), ((pixels, mid), WIDE), ((3, mid), WIDE)],
        (2 * pixels * chans * (mid + 256), 20 << 20),
    )(local_one, images_in.reshape(pixels, chans), reduce_w, mask)
    moments_one, count_in, rounds = first_moments(stats)
    projected, stats_proj = call(
        functools.partial(project_kernel, quarter),
        strips,
        [SCALARS, whole((rows, chans)), wide_cols(chans, strip), whole((rows, 128))],
        [wide_cols(rows, strip), wide_cols(2, strip)],
        [((rows, wide), WIDE), ((2, wide), WIDE)],
        (2 * rows * chans * wide, 10 << 20),
    )(local_one, planes, proj_w, mask)
    count_out = count_in / 4.0
    rounds = [[count / 4.0 for count in counts] for counts in rounds]
    scalars = jnp.stack([local, count_in, count_out, has_upper, has_lower])

    grouped, stats, edge = call(
        functools.partial(conv_kernel, (images, tall, half_cols)),
        steps,
        [
            SCALARS,
            wide_cols(pixels, block),
            wide_cols(2, block),
            wide_cols(2, block),
            whole((images * cols, chans)),
            wide_cols(chans, block),
            wide_cols(TAPS * TAPS * GW, block),
            whole((rows, 128)),
        ],
        [wide_cols(rows, block), wide_cols(2, block), wide_cols(images * cols, block)],
        [((rows, mid), WIDE), ((2, mid), WIDE), ((images * cols, mid), LOW)],
        (2 * rows * mid * 9 * 256, 14 << 20),
        [pltpu.VMEM((images * cols, chans), LOW)] + window_scratch(images, tall, half_cols, block),
    )(scalars, reduced, moments_one, affine_one, halo_images, reduce_w, group_flat, mask)
    below_grouped = shifted(
        grouped.reshape(images, tall, half_cols, mid)[:, 0].astype(LOW), "ha", -1
    ).reshape(images * half_cols, mid)
    merged = mesh_moments(jnp.concatenate([stats, stats_proj], axis=1), rounds)
    moments_two, moments_proj = merged[:, :mid], merged[:, mid:]

    hidden_two, expanded, stats = call(
        functools.partial(expand_kernel, quarter),
        strips,
        [
            SCALARS,
            whole((rows, mid)),
            whole((2, mid)),
            whole((2, mid)),
            wide_cols(mid, strip),
            whole((rows, 128)),
        ],
        [whole((rows, mid)), wide_cols(rows, strip), wide_cols(2, strip)],
        [((rows, mid), LOW), ((rows, wide), WIDE), ((2, wide), WIDE)],
        (2 * rows * mid * wide, 12 << 20),
    )(scalars, grouped, moments_two, affine_two, expand_w, mask)
    moments_out = jnp.concatenate([mesh_moments(stats, rounds), moments_proj])

    cot = cotangent.reshape(rows, wide)
    output, sums = call(
        functools.partial(output_kernel, 16),
        strips,
        [
            SCALARS,
            wide_cols(rows, strip),
            wide_cols(rows, strip),
            wide_cols(4, strip),
            wide_cols(4, strip),
            wide_cols(rows, strip),
            whole((rows, 128)),
        ],
        [wide_cols(rows, strip), wide_cols(3, strip)],
        [((rows, wide), LOW), ((3, wide), WIDE)],
        (20 * rows * wide, 12 << 20),
    )(scalars, expanded, projected, moments_out, affine_out, cot, mask)
    sums_out = mesh_sum(sums)

    parts_spec = pl.BlockSpec((PARTS, mid // PARTS, strip), lambda i: (0, 0, i))
    d_expanded, d_projected, parts_expand, parts_proj = call(
        functools.partial(weights_kernel, 16),
        strips,
        [
            SCALARS,
            SCALARS,
            wide_cols(rows, strip),
            wide_cols(rows, strip),
            wide_cols(4, strip),
            wide_cols(4, strip),
            wide_cols(3, strip),
            wide_cols(rows, strip),
            whole((rows, 128)),
            whole((rows, mid)),
            whole((rows, chans)),
        ],
        [wide_cols(rows, strip), wide_cols(rows, strip), parts_spec, parts_spec],
        [
            ((rows, wide), LOW),
            ((rows, wide), LOW),
            ((PARTS, mid // PARTS, wide), LOW),
            ((PARTS, chans // PARTS, wide), LOW),
        ],
        (4 * rows * mid * wide, 24 << 20),
    )(scalars, own, expanded, projected, moments_out, affine_out, sums_out, cot, mask, hidden_two, planes)

    grad_two, sums = call(
        functools.partial(back_two_kernel, 16),
        steps,
        [
            SCALARS,
            whole((rows, wide)),
            pl.BlockSpec((block, wide), lambda i: (i, 0)),
            wide_cols(rows, block),
            wide_cols(2, block),
            wide_cols(2, block),
        ],
        [wide_cols(rows, block), wide_cols(2, block)],
        [((rows, mid), WIDE), ((2, mid), WIDE)],
        (2 * rows * mid * wide, 10 << 20),
    )(scalars, d_expanded, expand_w, grouped, moments_two, affine_two)
    below_grad = shifted(
        grad_two.reshape(images, tall, half_cols, mid)[:, 0].astype(LOW), "ha", -1
    ).reshape(images * half_cols, mid)
    sums_two = mesh_sum(sums)

    deep = pltpu.VMEM((images, tall + 1, half_cols, block), LOW)
    grad_one, sums, parts_group = call(
        functools.partial(conv_back_kernel, (images, tall, half_cols)),
        steps,
        [
            SCALARS,
            SCALARS,
            wide_cols(rows, block),
            wide_cols(rows, block),
            wide_cols(images * half_cols, block),
            wide_cols(images * half_cols, block),
            wide_cols(2, block),
            wide_cols(2, block),
            wide_cols(2, block),
            wide_cols(pixels, block),
            wide_cols(images * cols, block),
            wide_cols(2, block),
            wide_cols(2, block),
            wide_cols(TAPS * TAPS * GW, block),
            whole((rows, 128)),
        ],
        [
            wide_cols(pixels, block),
            wide_cols(2, block),
            pl.BlockSpec((PARTS, TAPS * TAPS * GW // PARTS, block), lambda i: (0, 0, i)),
        ],
        [
            ((pixels, mid), WIDE),
            ((2, mid), WIDE),
            ((PARTS, TAPS * TAPS * GW // PARTS, mid), LOW),
        ],
        (4 * rows * mid * 9 * 256, 24 << 20),
        window_scratch(images, tall, half_cols, block) + [deep, deep],
    )(
        scalars,
        own,
        grad_two,
        grouped,
        below_grad,
        below_grouped,
        moments_two,
        affine_two,
        sums_two,
        reduced,
        edge,
        moments_one,
        affine_one,
        group_flat,
        mask,
    )
    sums_one = mesh_sum(sums)

    d_reduced, parts_reduce = call(
        functools.partial(reduced_back_kernel, 16),
        steps,
        [
            SCALARS,
            SCALARS,
            wide_cols(pixels, block),
            wide_cols(pixels, block),
            wide_cols(2, block),
            wide_cols(2, block),
            wide_cols(2, block),
            whole((rows, 128)),
            whole((pixels, chans)),
        ],
        [
            wide_cols(pixels, block),
            pl.BlockSpec((PARTS, chans // PARTS, block), lambda i: (0, 0, i)),
        ],
        [((pixels, mid), LOW), ((PARTS, chans // PARTS, mid), LOW)],
        (2 * pixels * mid * chans, 26 << 20),
    )(scalars, own, grad_one, reduced, moments_one, affine_one, sums_one, mask, planes)

    grad_images = call(
        functools.partial(images_back_kernel, (image_rows, cols)),
        images,
        [
            pl.BlockSpec((4, None, quarter, mid), lambda i: (0, i, 0, 0)),
            whole((chans, mid)),
            whole((rows, wide)),
            whole((chans, wide)),
        ],
        [pl.BlockSpec((None, image_rows * cols, chans), lambda i: (i, 0, 0))],
        [((images, image_rows * cols, chans), LOW)],
        (2 * pixels * mid * chans + 2 * rows * wide * chans, 16 << 20),
        [pltpu.VMEM((rows, chans), WIDE), pltpu.VMEM((image_rows * cols, image_rows * cols), LOW)],
    )(d_reduced.reshape(4, images, quarter, mid), reduce_w, d_projected, proj_w)[0]

    grad_expand = total_gradient(parts_expand, CUTS, own_plain)
    grad_proj = total_gradient(parts_proj, swapped, own_swapped)
    grad_group = total_gradient(parts_group, swapped, own_swapped)
    grad_reduce = total_gradient(parts_reduce, CUTS, own_plain)
    return (
        output.reshape(cotangent.shape),
        grad_images.reshape(images_in.shape),
        grad_reduce.reshape(reduce_w.shape),
        sums_one[1],
        sums_one[0],
        grad_group.reshape(group_w.shape),
        sums_two[1],
        sums_two[0],
        grad_expand.reshape(expand_w.shape),
        sums_out[1],
        sums_out[0],
        grad_proj.reshape(proj_w.shape),
        sums_out[2],
        sums_out[0],
    )


def solution(mesh):
    split = P("ba", "ha", None, None)
    rest = (P(),) * 12
    return jax.shard_map(
        per_device,
        mesh=mesh,
        in_specs=(split,) + rest + (P("ba"), split),
        out_specs=(split, split) + rest,
        check_vma=False,
    )
```

time: 1240 us -> 485 us (0.39); the launches traced: 1220 us -> 479 us
  local copies, waits for them, and re-layouts: 525 us -> 42.2 us
  matrix products: 238 us -> 0 us
  other arithmetic: 94.6 us -> 27 us
  Pallas kernels: 140 us -> 179 us
  between operations: 4.53 us -> 17.4 us
    dot_general x36 -> x0, matrix products: 238 us -> none  [the longest x9 71.7 us: per_device(): jnp.einsum('nhwgc,nhwgj->cgj', window, d_grouped, preferred_element_type=...]
    slice x24 -> x11, local copies, waits for them, and re-layouts: 185 us -> 6.68 us  [the longest x8 4.86 us: first_moments(): counts = [part[0, 0] for part in parts]]
    reshape x20 -> x1, local copies, waits for them, and re-layouts: 125 us -> 2.54 us  [per_device(): grad_group.reshape(group_w.shape)]
    pallas_call x0 -> x10, Pallas kernels: none -> 110 us  [the longest x1 15.4 us: per_device(): call(functools.partial(images_back_kernel, (image_rows, cols)), images, [...]
    transpose x10 -> x0, local copies, waits for them, and re-layouts: 91.6 us -> none  [the longest x9 88.3 us: per_device(): jnp.einsum('nhwgj,cgj->nhwgc', d_grouped, kernel, preferred_element_type=...]
    pallas_call x8 -> x4, Pallas kernels: 140 us -> 69.4 us  [relabel(): pl.pallas_call(pack_kernel, grid_spec=spec, out_shape=jax.ShapeDtypeStruc...]
    another operation x33 -> x1, local copies, waits for them, and re-layouts: 66.9 us -> 1.3 us  [per_device(): scalars = jnp.stack([local, count_in, count_out, has_upper, has_lower])]
    another operation x20 -> x11, other arithmetic: 29.3 us -> 5.05 us  [the longest x8 28.9 us: weave(): paired = jnp.stack([head, odd_part], axis=axis + 1)]
  transfers between devices with their start and end apart: 84 -> 85, of which waited for: 51 -> 46; matrix products, arithmetic and copies ran while one was open for 14% -> 11% of each run, Pallas kernels for 10% -> 18%
where the time goes in v2:
time: 485 us; the launch traced here: 479 us
  Pallas kernels  179 us (37%)
  waiting for transfers between devices  122 us (25%)
  starting transfers between devices  91.6 us (19%)
  local copies, waits for them, and re-layouts  42.2 us (9%)
  other arithmetic  27 us (6%)
  between operations  17.4 us (4%)
    ppermute x82, waiting for transfers between devices, exchange(): return lax.ppermute(value, axis, [(i, i ^ mask) for i in range(peers)])  122 us
    ppermute x82, starting transfers between devices, exchange(): return lax.ppermute(value, axis, [(i, i ^ mask) for i in range(peers)])  84.2 us
    pallas_call x4, Pallas kernels, relabel(): pl.pallas_call(pack_kernel, grid_spec=spec, out_shape=jax.ShapeDtypeStruc...  69.4 us
    pallas_call x1, Pallas kernels, per_device(): call(functools.partial(images_back_kernel, (image_rows, cols)), images, [...  15.4 us
    pallas_call x1, Pallas kernels, per_device(): call(functools.partial(conv_back_kernel, (images, tall, half_cols)), step...  14.5 us
    unnamed x68, local copies, waits for them, and re-layouts  14.5 us
    pallas_call x1, Pallas kernels, per_device(): call(functools.partial(reduced_back_kernel, 16), steps, [SCALARS, SCALARS...  13.6 us
    pallas_call x1, Pallas kernels, per_device(): call(functools.partial(weights_kernel, 16), strips, [SCALARS, SCALARS, wi...  13.6 us
  transfers between devices with their start and end apart: 85, of which 46 were waited for; matrix products, arithmetic and copies ran while one was open for 11% of the time, Pallas kernels for 18%

profile of v2, /device:TPU:0, one launch (start us, length us, event | category | flops | bytes accessed | tf_op | source)
XLA Modules:
  0.0 479.2 jit_solution(15766122932812539418)
XLA Ops:
  3.6 12.2 %shard_map.254 = (bf16[2048,1024]{1,0:T(8,128)(2,1)}, f32[2048,1024]{1,0:T(8,128)}, f32[3,1024]{1,0:T(4,128)}) custom-call(f32[1]{0:T(128)} %bitcast.count_ref, bf16[2048,1024]{1,0:T(8,128)(2,1)} %bitcast.64, bf16[1024,1024]{1,0:T(8,128)(2,1)} %w_ref.9, f32[512,128]{1,0:T(8,128)} %broadcast_in_dim.19.mask_ref), custom_call_target="tpu_custom_call" | custom-call | flops 5368709120 | bytes 20971520 | tf_op jit(solution)/shard_map/pallas_call | solution.py:702
  17.3 4.6 collective-permute-start.7
  26.3 2.1 add_divide_fusion.20
  28.4 3.7 collective-permute-start.3
  32.9 7.3 %shard_map.256 = (f32[512,2048]{1,0:T(8,128)}, f32[2,2048]{1,0:T(2,128)}) custom-call(f32[1]{0:T(128)} %bitcast.count_ref, bf16[2048,1024]{1,0:T(8,128)(2,1)} %get-tuple-element.42.x_ref.sampled_ref.planes_ref, bf16[1024,2048]{1,0:T(8,128)(2,1)} %proj_ref.1, f32[512,128]{1,0:T(8,128)} %broadcast_in_dim.19.mask_ref), custom_call_target="tpu_custom_call" | custom-call | flops 2147483648 | bytes 10485760 | tf_op jit(solution)/shard_map/pallas_call | solution.py:711
  48.2 2.6 collective-permute-start.5
  62.6 9.5 %shard_map.255 = (f32[512,1024]{1,0:T(8,128)}, f32[2,1024]{1,0:T(2,128)}, bf16[256,1024]{1,0:T(8,128)(2,1)}) custom-call(f32[5]{0:T(128)} %stack.105.scalar_ref, f32[2048,1024]{1,0:T(8,128)} %get-tuple-element.39.reduced_ref, f32[2,1024]{1,0:T(2,128)} %pad_maximum_fusion.21.moments_ref.moments_one_ref, ...), custom_call_target="tpu_custom_call" | custom-call | flops 2415919104 | bytes 14680064 | tf_op jit(solution)/shard_map/pallas_call | solution.py:723
  74.2 3.7 collective-permute-start.11
  90.4 7.6 %shard_map.257 = (bf16[512,1024]{1,0:T(8,128)(2,1)}, f32[512,2048]{1,0:T(8,128)}, f32[2,2048]{1,0:T(2,128)}) custom-call(f32[5]{0:T(128)} %stack.105.scalar_ref, f32[512,1024]{1,0:T(8,128)} %get-tuple-element.40.grouped_ref, f32[2,1024]{1,0:T(2,128)} %pad_maximum_fusion.20.moments_ref.moments_two_ref, ...), custom_call_target="tpu_custom_call" | custom-call | flops 2147483648 | bytes 12582912 | tf_op jit(solution)/shard_map/pallas_call | solution.py:747
  102.4 2.3 collective-permute-start.16
  113.7 8.4 %shard_map.258 = (bf16[512,2048]{1,0:T(8,128)(2,1)}, f32[3,2048]{1,0:T(4,128)}) custom-call(f32[5]{0:T(128)} %stack.105.scalar_ref, f32[512,2048]{1,0:T(8,128)} %get-tuple-element.44.expanded_ref, f32[512,2048]{1,0:T(8,128)} %get-tuple-element.45.projected_ref, f32[4,2048]{1,0:T(4,128)} %fusion.stats_ref, f32[4,2048]{1,0:T(4,128)} %pad_maximum_fusion.13.affine_ref, ...), custom_call_target="tpu_custom_call" | custom-call | flops 20971520 | bytes 12582912 | tf_op jit(solution)/shard_map/pallas_call | solution.py:765
  124.3 2.3 collective-permute-start.25
  139.1 13.6 %shard_map.259 = (bf16[512,2048]{1,0:T(8,128)(2,1)}, bf16[512,2048]{1,0:T(8,128)(2,1)}, bf16[32,32,2048]{2,1,0:T(8,128)(2,1)}, bf16[32,32,2048]{2,1,0:T(8,128)(2,1)}) custom-call(f32[5]{0:T(128)} %stack.105.scalar_ref, s32[2]{0:T(128)} %pad_add_fusion.own_ref, f32[512,2048]{1,0:T(8,128)} %get-tuple-element.44.expanded_ref, ...), custom_call_target="tpu_custom_call" | custom-call | flops 4294967296 | bytes 25165824 | tf_op jit(solution)/shard_map/pallas_call | solution.py:784
  152.7 7.7 %shard_map.260 = (f32[512,1024]{1,0:T(8,128)}, f32[2,1024]{1,0:T(2,128)}) custom-call(f32[5]{0:T(128)} %stack.105.scalar_ref, bf16[512,2048]{1,0:T(8,128)(2,1)} %get-tuple-element.50.d_ref, bf16[1024,2048]{1,0:T(8,128)(2,1)} %w_ref.8, f32[512,1024]{1,0:T(8,128)} %get-tuple-element.40.grouped_ref, f32[2,1024]{1,0:T(2,128)} %pad_maximum_fusion.20.moments_ref.moments_two_ref, ...), custom_call_target="tpu_custom_call" | custom-call | flops 2147483648 | bytes 10485760 | tf_op jit(solution)/shard_map/pallas_call | solution.py:810
  170.0 4.7 collective-permute-start.37
  175.9 4.4 collective-permute-done.37
  181.8 14.5 %shard_map.261 = (f32[2048,1024]{1,0:T(8,128)}, f32[2,1024]{1,0:T(2,128)}, bf16[32,9,1024]{2,1,0:T(8,128)(2,1)}) custom-call(f32[5]{0:T(128)} %stack.105.scalar_ref, s32[2]{0:T(128)} %pad_add_fusion.own_ref, f32[512,1024]{1,0:T(8,128)} %get-tuple-element.51.grad_ref, f32[512,1024]{1,0:T(8,128)} %get-tuple-element.40.grouped_ref, bf16[128,1024]{1,0:T(8,128)(2,1)} %bitcast.84, ...), custom_call_target="tpu_custom_call" | custom-call | flops 4831838208 | bytes 25165824 | tf_op jit(solution)/shard_map/pallas_call | solution.py:831
  200.2 2.6 collective-permute-start.39
  213.6 13.6 %shard_map.262 = (bf16[2048,1024]{1,0:T(8,128)(2,1)}, bf16[32,32,1024]{2,1,0:T(8,128)(2,1)}) custom-call(f32[5]{0:T(128)} %stack.105.scalar_ref, s32[2]{0:T(128)} %pad_add_fusion.own_ref, f32[2048,1024]{1,0:T(8,128)} %get-tuple-element.54.grad_ref, f32[2048,1024]{1,0:T(8,128)} %get-tuple-element.39.reduced_ref, ...), custom_call_target="tpu_custom_call" | custom-call | flops 4294967296 | bytes 27262976 | tf_op jit(solution)/shard_map/pallas_call | solution.py:882
  229.9 4.7 collective-permute-done.57
  239.1 2.1 collective-permute-start.59
  246.6 7.2 %collective-permute-done.46 = bf16[8,32,1024]{2,1,0:T(8,128)(2,1)S(1)} collective-permute-done((bf16[8,32,1024]{2,1,0:T(8,128)(2,1)S(1)}, bf16[8,32,1024]{2,1,0:T(8,128)(2,1)S(1)}, u32[]{:S(2)}, u32[]{:S(2)}) %collective-permute-start.46) | collective-permute-done | bytes 524320 | tf_op jit(solution)/shard_map/ppermute | solution.py:22
  257.0 3.4 collective-permute-done.61
  263.8 3.0 collective-permute-done.48
  269.8 3.0 collective-permute-done.49
  274.3 4.5 collective-permute-done.50
  280.8 3.1 collective-permute-done.51
  285.0 3.9 collective-permute-done.76
  291.0 4.0 collective-permute-done.66
  296.4 3.8 collective-permute-done.52
  301.3 4.2 collective-permute-done.77
  308.0 6.0 %collective-permute-done.78 = bf16[2,32,2048]{2,1,0:T(8,128)(2,1)S(1)} collective-permute-done((bf16[2,32,2048]{2,1,0:T(8,128)(2,1)S(1)}, bf16[2,32,2048]{2,1,0:T(8,128)(2,1)S(1)}, u32[]{:S(2)}, u32[]{:S(2)}) %collective-permute-start.78) | collective-permute-done | bytes 262176 | tf_op jit(solution)/shard_map/ppermute | solution.py:22
  314.6 4.7 collective-permute-done.68
  319.4 3.7 collective-permute-done.79
  323.8 2.5 collective-permute-done.69
  327.4 6.4 %collective-permute-done.70 = bf16[1,32,2048]{2,1,0:T(8,128)(2,1)S(1)} collective-permute-done((bf16[1,32,2048]{2,1,0:T(8,128)(2,1)S(1)}, bf16[1,32,2048]{2,1,0:T(8,128)(2,1)S(1)}, u32[]{:S(2)}, u32[]{:S(2)}) %collective-permute-start.70) | collective-permute-done | bytes 131104 | tf_op jit(solution)/shard_map/ppermute | solution.py:22
  336.1 4.2 collective-permute-done.71
  345.3 6.5 %collective-permute-done.72 = bf16[4,32,2048]{2,1,0:T(8,128)(2,1)S(1)} collective-permute-done((bf16[4,32,2048]{2,1,0:T(8,128)(2,1)S(1)}, bf16[4,32,2048]{2,1,0:T(8,128)(2,1)S(1)}, u32[]{:S(2)}, u32[]{:S(2)}) %collective-permute-start.72) | collective-permute-done | bytes 524320 | tf_op jit(solution)/shard_map/ppermute | solution.py:22
  353.0 5.1 %collective-permute-done.82 = bf16[4,32,2048]{2,1,0:T(8,128)(2,1)S(1)} collective-permute-done((bf16[4,32,2048]{2,1,0:T(8,128)(2,1)S(1)}, bf16[4,32,2048]{2,1,0:T(8,128)(2,1)S(1)}, u32[]{:S(2)}, u32[]{:S(2)}) %collective-permute-start.82) | collective-permute-done | bytes 524320 | tf_op jit(solution)/shard_map/ppermute | solution.py:22
  363.1 9.7 %collective-permute-done.73 = bf16[8,32,2048]{2,1,0:T(8,128)(2,1)S(1)} collective-permute-done((bf16[8,32,2048]{2,1,0:T(8,128)(2,1)S(1)}, bf16[8,32,2048]{2,1,0:T(8,128)(2,1)S(1)}, u32[]{:S(2)}, u32[]{:S(2)}) %collective-permute-start.73) | collective-permute-done | bytes 1048608 | tf_op jit(solution)/shard_map/ppermute | solution.py:22
  380.6 15.4 %shard_map.263 = bf16[8,256,1024]{2,1,0:T(8,128)(2,1)} custom-call(bf16[4,8,64,1024]{3,2,1,0:T(8,128)(2,1)} %bitcast.81, bf16[1024,1024]{1,0:T(8,128)(2,1)} %w_ref.9, bf16[512,2048]{1,0:T(8,128)(2,1)} %get-tuple-element.57.side_ref, bf16[1024,2048]{1,0:T(8,128)(2,1)} %proj_ref.1), custom_call_target="tpu_custom_call" | custom-call | flops 6442450944 | bytes 16777216 | tf_op jit(solution)/shard_map/pallas_call | solution.py:904
  397.7 15.5 %shard_map.265 = f32[32,9,1024]{2,1,0:T(8,128)} custom-call(s32[1]{0:T(128)} %bitcast.28.own_ref, bf16[32,9,1024]{2,1,0:T(8,128)(2,1)} %copy-done.7), custom_call_target="tpu_custom_call" | custom-call | tf_op jit(solution)/shard_map/pallas_call | solution.py:112
  413.1 2.5 reshape.100
  418.3 16.9 %shard_map.264 = f32[32,32,1024]{2,1,0:T(8,128)} custom-call(s32[1]{0:T(128)} %bitcast.27.own_ref, bf16[32,32,1024]{2,1,0:T(8,128)(2,1)} %copy-done.5), custom_call_target="tpu_custom_call" | custom-call | tf_op jit(solution)/shard_map/pallas_call | solution.py:112
  435.3 3.2 constant_dynamic-update-slice_fusion.29.value_ref
  438.4 18.5 %shard_map.266 = f32[32,32,2048]{2,1,0:T(8,128)} custom-call(s32[1]{0:T(128)} %bitcast.27.own_ref, bf16[32,32,2048]{2,1,0:T(8,128)(2,1)} %constant_dynamic-update-slice_fusion.29.value_ref), custom_call_target="tpu_custom_call" | custom-call | tf_op jit(solution)/shard_map/pallas_call | solution.py:112
  456.9 3.2 constant_dynamic-update-slice_fusion.40.value_ref
  460.1 18.5 %shard_map.267 = f32[32,32,2048]{2,1,0:T(8,128)} custom-call(s32[1]{0:T(128)} %bitcast.28.own_ref, bf16[32,32,2048]{2,1,0:T(8,128)(2,1)} %constant_dynamic-update-slice_fusion.40.value_ref), custom_call_target="tpu_custom_call" | custom-call | tf_op jit(solution)/shard_map/pallas_call | solution.py:112
  (327 shorter events, 145.1 us)
Async XLA Ops:
  15.8 7.4 %collective-permute-start = (f32[3,1024]{1,0:T(4,128)}, f32[3,1024]{1,0:T(4,128)S(1)}, u32[]{:S(2)}, u32[]{:S(2)}) collective-permute-start(f32[3,1024]{1,0:T(4,128)} %get-tuple-element.38), channel_id=1, source_target_pairs={{0,1},{1,0},{2,3},{3,2},{4,5},{5,4},{6,7},{7,6},{8,9},{9,8},{10,11... | collective-permute-start | bytes 36872 | tf_op jit(solution)/shard_map/ppermute | solution.py:22
  17.3 44.5 %collective-permute-start.7 = (bf16[8,32,1024]{2,1,0:T(8,128)(2,1)S(1)}, bf16[8,32,1024]{2,1,0:T(8,128)(2,1)S(1)}, u32[]{:S(2)}, u32[]{:S(2)}) collective-permute-start(bf16[8,32,1024]{2,1,0:T(8,128)(2,1)S(1)} %slice_bitcast_fusion), channel_id=1, source_target_pairs={{0,8},{8,16},{16,24},{1,9},{9,17},{17,25},{2,10},{10,18},{18,26},{... | collective-permute-start | bytes 1572872 | tf_op jit(solution)/shard_map/ppermute | solution.py:17
  28.4 11.8 %collective-permute-start.3 = (f32[3,1024]{1,0:T(4,128)S(1)}, f32[3,1024]{1,0:T(4,128)S(1)}, u32[]{:S(2)}, u32[]{:S(2)}) collective-permute-start(f32[3,1024]{1,0:T(4,128)S(1)} %pad_maximum_fusion.16), channel_id=1, source_target_pairs={{0,6},{1,7},{2,4},{3,5},{4,2},{5,3},{6,0},{7,1},{8,14},{9,15},{10,... | collective-permute-start | bytes 36872 | tf_op jit(solution)/shard_map/ppermute | solution.py:22
  32.1 8.6 %collective-permute-start.2 = (f32[3,1024]{1,0:T(4,128)S(1)}, f32[3,1024]{1,0:T(4,128)S(1)}, u32[]{:S(2)}, u32[]{:S(2)}) collective-permute-start(f32[3,1024]{1,0:T(4,128)S(1)} %pad_maximum_fusion.16), channel_id=1, source_target_pairs={{0,4},{1,5},{2,6},{3,7},{4,0},{5,1},{6,2},{7,3},{8,12},{9,13},{10,... | collective-permute-start | bytes 36872 | tf_op jit(solution)/shard_map/ppermute | solution.py:22
  32.1 11.7 %collective-permute-start.1 = (f32[3,1024]{1,0:T(4,128)S(1)}, f32[3,1024]{1,0:T(4,128)S(1)}, u32[]{:S(2)}, u32[]{:S(2)}) collective-permute-start(f32[3,1024]{1,0:T(4,128)S(1)} %pad_maximum_fusion.16), channel_id=1, source_target_pairs={{0,2},{1,3},{2,0},{3,1},{4,6},{5,7},{6,4},{7,5},{8,10},{9,11},{10,... | collective-permute-start | bytes 36872 | tf_op jit(solution)/shard_map/ppermute | solution.py:22
  74.2 6.5 %collective-permute-start.11 = (f32[2,3072]{1,0:T(2,128)S(1)}, f32[2,3072]{1,0:T(2,128)S(1)}, u32[]{:S(2)}, u32[]{:S(2)}) collective-permute-start(f32[2,3072]{1,0:T(2,128)S(1)} %pad_maximum_fusion.14), channel_id=1, source_target_pairs={{0,6},{1,7},{2,4},{3,5},{4,2},{5,3},{6,0},{7,1},{8,14},{9,15},{10,... | collective-permute-start | bytes 73736 | tf_op jit(solution)/shard_map/ppermute | solution.py:22
  82.8 6.1 %collective-permute-start.14 = (f32[2,3072]{1,0:T(2,128)S(1)}, f32[2,3072]{1,0:T(2,128)S(1)}, u32[]{:S(2)}, u32[]{:S(2)}) collective-permute-start(f32[2,3072]{1,0:T(2,128)S(1)} %pad_maximum_fusion.15), channel_id=1, source_target_pairs={{0,24},{8,16},{16,8},{24,0},{1,25},{9,17},{17,9},{25,1},{2,26},{10... | collective-permute-start | bytes 73736 | tf_op jit(solution)/shard_map/ppermute | solution.py:22
  100.3 5.7 %collective-permute-start.18 = (f32[2,2048]{1,0:T(2,128)S(1)}, f32[2,2048]{1,0:T(2,128)S(1)}, u32[]{:S(2)}, u32[]{:S(2)}) collective-permute-start(f32[2,2048]{1,0:T(2,128)S(1)} %pad_maximum_fusion.18), channel_id=1, source_target_pairs={{0,6},{1,7},{2,4},{3,5},{4,2},{5,3},{6,0},{7,1},{8,14},{9,15},{10,... | collective-permute-start | bytes 49160 | tf_op jit(solution)/shard_map/ppermute | solution.py:22
  124.3 6.1 %collective-permute-start.25 = (f32[3,2048]{1,0:T(4,128)S(1)}, f32[3,2048]{1,0:T(4,128)S(1)}, u32[]{:S(2)}, u32[]{:S(2)}) collective-permute-start(f32[3,2048]{1,0:T(4,128)S(1)} %add.625), channel_id=1, source_target_pairs={{0,6},{1,7},{2,4},{3,5},{4,2},{5,3},{6,0},{7,1},{8,14},{9,15},{10,... | collective-permute-start | bytes 73736 | tf_op jit(solution)/shard_map/ppermute | solution.py:22
  160.5 20.5 %collective-permute-start.30 = (bf16[8,16,1024]{2,1,0:T(8,128)(2,1)S(1)}, bf16[8,16,1024]{2,1,0:T(8,128)(2,1)S(1)}, u32[]{:S(2)}, u32[]{:S(2)}) collective-permute-start(bf16[8,16,1024]{2,1,0:T(8,128)(2,1)S(1)} %slice_bitcast_fusion.1), channel_id=1, source_target_pairs={{8,0},{16,8},{24,16},{9,1},{17,9},{25,17},{10,2},{18,10},{26,18},{... | collective-permute-start | bytes 786440 | tf_op jit(solution)/shard_map/ppermute | solution.py:17
  163.8 5.8 %collective-permute-start.34 = (f32[2,1024]{1,0:T(2,128)S(1)}, f32[2,1024]{1,0:T(2,128)S(1)}, u32[]{:S(2)}, u32[]{:S(2)}) collective-permute-start(f32[2,1024]{1,0:T(2,128)S(1)} %add.632), channel_id=1, source_target_pairs={{0,6},{1,7},{2,4},{3,5},{4,2},{5,3},{6,0},{7,1},{8,14},{9,15},{10,... | collective-permute-start | bytes 24584 | tf_op jit(solution)/shard_map/ppermute | solution.py:22
  168.3 12.7 %collective-permute-start.29 = (bf16[8,16,1024]{2,1,0:T(8,128)(2,1)S(1)}, bf16[8,16,1024]{2,1,0:T(8,128)(2,1)S(1)}, u32[]{:S(2)}, u32[]{:S(2)}) collective-permute-start(bf16[8,16,1024]{2,1,0:T(8,128)(2,1)S(1)} %slice_bitcast_fusion.2), channel_id=1, source_target_pairs={{8,0},{16,8},{24,16},{9,1},{17,9},{25,17},{10,2},{18,10},{26,18},{... | collective-permute-start | bytes 786440 | tf_op jit(solution)/shard_map/ppermute | solution.py:17
  170.0 10.3 %collective-permute-start.37 = (f32[2,1024]{1,0:T(2,128)S(1)}, f32[2,1024]{1,0:T(2,128)S(1)}, u32[]{:S(2)}, u32[]{:S(2)}) collective-permute-start(f32[2,1024]{1,0:T(2,128)S(1)} %add_add_fusion.5), channel_id=1, source_target_pairs={{0,24},{8,16},{16,8},{24,0},{1,25},{9,17},{17,9},{25,1},{2,26},{10... | collective-permute-start | bytes 24584 | tf_op jit(solution)/shard_map/ppermute | solution.py:22
  203.9 7.8 %collective-permute-start.55 = (bf16[16,9,1024]{2,1,0:T(8,128)(2,1)S(1)}, bf16[16,9,1024]{2,1,0:T(8,128)(2,1)S(1)}, u32[]{:S(2)}, u32[]{:S(2)}) collective-permute-start(bf16[16,9,1024]{2,1,0:T(8,128)(2,1)S(1)} %slice.452), channel_id=1, source_target_pairs={{0,1},{1,0},{2,3},{3,2},{4,5},{5,4},{6,7},{7,6},{8,9},{9,8},{10,11... | collective-permute-start | bytes 884744 | tf_op jit(solution)/shard_map/ppermute | solution.py:22
  213.0 15.6 %collective-permute-start.56 = (bf16[8,9,1024]{2,1,0:T(8,128)(2,1)S(1)}, bf16[8,9,1024]{2,1,0:T(8,128)(2,1)S(1)}, u32[]{:S(2)}, u32[]{:S(2)}) collective-permute-start(bf16[8,9,1024]{2,1,0:T(8,128)(2,1)S(1)} %slice.550), channel_id=1, source_target_pairs={{0,16},{8,24},{16,0},{24,8},{1,17},{9,25},{17,1},{25,9},{2,18},{10... | collective-permute-start | bytes 442376 | tf_op jit(solution)/shard_map/ppermute | solution.py:22
  228.5 12.7 %collective-permute-start.45 = (bf16[16,32,1024]{2,1,0:T(8,128)(2,1)S(1)}, bf16[16,32,1024]{2,1,0:T(8,128)(2,1)S(1)}, u32[]{:S(2)}, u32[]{:S(2)}) collective-permute-start(bf16[16,32,1024]{2,1,0:T(8,128)(2,1)S(1)} %slice.440), channel_id=1, source_target_pairs={{0,1},{1,0},{2,3},{3,2},{4,5},{5,4},{6,7},{7,6},{8,9},{9,8},{10,11... | collective-permute-start | bytes 3145736 | tf_op jit(solution)/shard_map/ppermute | solution.py:22
  228.7 6.0 %collective-permute-start.57 = (bf16[4,9,1024]{2,1,0:T(8,128)(2,1)S(1)}, bf16[4,9,1024]{2,1,0:T(8,128)(2,1)S(1)}, u32[]{:S(2)}, u32[]{:S(2)}) collective-permute-start(bf16[4,9,1024]{2,1,0:T(8,128)(2,1)S(1)} %slice.552), channel_id=1, source_target_pairs={{0,8},{8,0},{16,24},{24,16},{1,9},{9,1},{17,25},{25,17},{2,10},{10... | collective-permute-start | bytes 221192 | tf_op jit(solution)/shard_map/ppermute | solution.py:22
  229.7 32.2 %collective-permute-start.75 = (bf16[16,32,2048]{2,1,0:T(8,128)(2,1)S(1)}, bf16[16,32,2048]{2,1,0:T(8,128)(2,1)S(1)}, u32[]{:S(2)}, u32[]{:S(2)}) collective-permute-start(bf16[16,32,2048]{2,1,0:T(8,128)(2,1)S(1)} %slice.476), channel_id=1, source_target_pairs={{0,1},{1,0},{2,3},{3,2},{4,5},{5,4},{6,7},{7,6},{8,9},{9,8},{10,11... | collective-permute-start | bytes 6291464 | tf_op jit(solution)/shard_map/ppermute | solution.py:22
  237.5 30.2 %collective-permute-start.65 = (bf16[16,32,2048]{2,1,0:T(8,128)(2,1)S(1)}, bf16[16,32,2048]{2,1,0:T(8,128)(2,1)S(1)}, u32[]{:S(2)}, u32[]{:S(2)}) collective-permute-start(bf16[16,32,2048]{2,1,0:T(8,128)(2,1)S(1)} %slice.464), channel_id=1, source_target_pairs={{0,1},{1,0},{2,3},{3,2},{4,5},{5,4},{6,7},{7,6},{8,9},{9,8},{10,11... | collective-permute-start | bytes 6291464 | tf_op jit(solution)/shard_map/ppermute | solution.py:22
  241.6 12.2 %collective-permute-start.46 = (bf16[8,32,1024]{2,1,0:T(8,128)(2,1)S(1)}, bf16[8,32,1024]{2,1,0:T(8,128)(2,1)S(1)}, u32[]{:S(2)}, u32[]{:S(2)}) collective-permute-start(bf16[8,32,1024]{2,1,0:T(8,128)(2,1)S(1)} %slice.540), channel_id=1, source_target_pairs={{0,8},{8,0},{16,24},{24,16},{1,9},{9,1},{17,25},{25,17},{2,10},{10... | collective-permute-start | bytes 1572872 | tf_op jit(solution)/shard_map/ppermute | solution.py:22
  244.6 11.0 %collective-permute-start.60 = (bf16[1,9,1024]{2,1,0:T(8,128)(2,1)S(1)}, bf16[1,9,1024]{2,1,0:T(8,128)(2,1)S(1)}, u32[]{:S(2)}, u32[]{:S(2)}) collective-permute-start(bf16[1,9,1024]{2,1,0:T(8,128)(2,1)S(1)} %get-tuple-element.67), channel_id=1, source_target_pairs={{0,4},{1,5},{2,6},{3,7},{4,0},{5,1},{6,2},{7,3},{8,12},{9,13},{10,... | collective-permute-start | bytes 55304 | tf_op jit(solution)/shard_map/ppermute | solution.py:22
  254.0 6.9 %collective-permute-start.47 = (bf16[4,32,1024]{2,1,0:T(8,128)(2,1)S(1)}, bf16[4,32,1024]{2,1,0:T(8,128)(2,1)S(1)}, u32[]{:S(2)}, u32[]{:S(2)}) collective-permute-start(bf16[4,32,1024]{2,1,0:T(8,128)(2,1)S(1)} %slice.542), channel_id=1, source_target_pairs={{0,16},{8,24},{16,0},{24,8},{1,17},{9,25},{17,1},{25,9},{2,18},{10... | collective-permute-start | bytes 786440 | tf_op jit(solution)/shard_map/ppermute | solution.py:22
  260.4 18.5 %collective-permute-start.62 = (bf16[4,9,1024]{2,1,0:T(8,128)(2,1)S(1)}, bf16[4,9,1024]{2,1,0:T(8,128)(2,1)S(1)}, u32[]{:S(2)}, u32[]{:S(2)}) collective-permute-start(bf16[4,9,1024]{2,1,0:T(8,128)(2,1)S(1)} %pad_maximum_fusion.10), channel_id=1, source_target_pairs={{0,8},{8,0},{16,24},{24,16},{1,9},{9,1},{17,25},{25,17},{2,10},{10... | collective-permute-start | bytes 221192 | tf_op jit(solution)/shard_map/ppermute | solution.py:22
  261.1 5.7 %collective-permute-start.48 = (bf16[2,32,1024]{2,1,0:T(8,128)(2,1)S(1)}, bf16[2,32,1024]{2,1,0:T(8,128)(2,1)S(1)}, u32[]{:S(2)}, u32[]{:S(2)}) collective-permute-start(bf16[2,32,1024]{2,1,0:T(8,128)(2,1)S(1)} %slice.544), channel_id=1, source_target_pairs={{0,2},{1,3},{2,0},{3,1},{4,6},{5,7},{6,4},{7,5},{8,10},{9,11},{10,... | collective-permute-start | bytes 393224 | tf_op jit(solution)/shard_map/ppermute | solution.py:22
  262.8 26.2 %collective-permute-start.76 = (bf16[8,32,2048]{2,1,0:T(8,128)(2,1)S(1)}, bf16[8,32,2048]{2,1,0:T(8,128)(2,1)S(1)}, u32[]{:S(2)}, u32[]{:S(2)}) collective-permute-start(bf16[8,32,2048]{2,1,0:T(8,128)(2,1)S(1)} %slice.570), channel_id=1, source_target_pairs={{0,16},{8,24},{16,0},{24,8},{1,17},{9,25},{17,1},{25,9},{2,18},{10... | collective-permute-start | bytes 3145736 | tf_op jit(solution)/shard_map/ppermute | solution.py:22
  266.8 6.0 %collective-permute-start.49 = (bf16[1,32,1024]{2,1,0:T(8,128)(2,1)S(1)}, bf16[1,32,1024]{2,1,0:T(8,128)(2,1)S(1)}, u32[]{:S(2)}, u32[]{:S(2)}) collective-permute-start(bf16[1,32,1024]{2,1,0:T(8,128)(2,1)S(1)} %slice.546), channel_id=1, source_target_pairs={{0,4},{1,5},{2,6},{3,7},{4,0},{5,1},{6,2},{7,3},{8,12},{9,13},{10,... | collective-permute-start | bytes 196616 | tf_op jit(solution)/shard_map/ppermute | solution.py:22
  268.8 26.2 %collective-permute-start.66 = (bf16[8,32,2048]{2,1,0:T(8,128)(2,1)S(1)}, bf16[8,32,2048]{2,1,0:T(8,128)(2,1)S(1)}, u32[]{:S(2)}, u32[]{:S(2)}) collective-permute-start(bf16[8,32,2048]{2,1,0:T(8,128)(2,1)S(1)} %slice.560), channel_id=1, source_target_pairs={{0,8},{8,0},{16,24},{24,16},{1,9},{9,1},{17,25},{25,17},{2,10},{10... | collective-permute-start | bytes 3145736 | tf_op jit(solution)/shard_map/ppermute | solution.py:22
  279.0 100.4 %collective-permute-start.63 = (bf16[8,9,1024]{2,1,0:T(8,128)(2,1)S(1)}, bf16[8,9,1024]{2,1,0:T(8,128)(2,1)S(1)}, u32[]{:S(2)}, u32[]{:S(2)}) collective-permute-start(bf16[8,9,1024]{2,1,0:T(8,128)(2,1)S(1)} %pad_maximum_fusion.6), channel_id=1, source_target_pairs={{0,16},{8,24},{16,0},{24,8},{1,17},{9,25},{17,1},{25,9},{2,18},{10... | collective-permute-start | bytes 442376 | tf_op jit(solution)/shard_map/ppermute | solution.py:22
  283.9 16.3 %collective-permute-start.52 = (bf16[4,32,1024]{2,1,0:T(8,128)(2,1)S(1)}, bf16[4,32,1024]{2,1,0:T(8,128)(2,1)S(1)}, u32[]{:S(2)}, u32[]{:S(2)}) collective-permute-start(bf16[4,32,1024]{2,1,0:T(8,128)(2,1)S(1)} %pad_maximum_fusion.5), channel_id=1, source_target_pairs={{0,16},{8,24},{16,0},{24,8},{1,17},{9,25},{17,1},{25,9},{2,18},{10... | collective-permute-start | bytes 786440 | tf_op jit(solution)/shard_map/ppermute | solution.py:22
  289.4 16.1 %collective-permute-start.77 = (bf16[4,32,2048]{2,1,0:T(8,128)(2,1)S(1)}, bf16[4,32,2048]{2,1,0:T(8,128)(2,1)S(1)}, u32[]{:S(2)}, u32[]{:S(2)}) collective-permute-start(bf16[4,32,2048]{2,1,0:T(8,128)(2,1)S(1)} %slice.572), channel_id=1, source_target_pairs={{0,8},{8,0},{16,24},{24,16},{1,9},{9,1},{17,25},{25,17},{2,10},{10... | collective-permute-start | bytes 1572872 | tf_op jit(solution)/shard_map/ppermute | solution.py:22
  295.4 11.6 %collective-permute-start.67 = (bf16[4,32,2048]{2,1,0:T(8,128)(2,1)S(1)}, bf16[4,32,2048]{2,1,0:T(8,128)(2,1)S(1)}, u32[]{:S(2)}, u32[]{:S(2)}) collective-permute-start(bf16[4,32,2048]{2,1,0:T(8,128)(2,1)S(1)} %slice.562), channel_id=1, source_target_pairs={{0,16},{8,24},{16,0},{24,8},{1,17},{9,25},{17,1},{25,9},{2,18},{10... | collective-permute-start | bytes 1572872 | tf_op jit(solution)/shard_map/ppermute | solution.py:22
  300.2 78.2 %collective-permute-start.53 = (bf16[8,32,1024]{2,1,0:T(8,128)(2,1)S(1)}, bf16[8,32,1024]{2,1,0:T(8,128)(2,1)S(1)}, u32[]{:S(2)}, u32[]{:S(2)}) collective-permute-start(bf16[8,32,1024]{2,1,0:T(8,128)(2,1)S(1)} %pad_maximum_fusion.2), channel_id=1, source_target_pairs={{0,8},{8,0},{16,24},{24,16},{1,9},{9,1},{17,25},{25,17},{2,10},{10... | collective-permute-start | bytes 1572872 | tf_op jit(solution)/shard_map/ppermute | solution.py:22
  305.7 8.3 %collective-permute-start.78 = (bf16[2,32,2048]{2,1,0:T(8,128)(2,1)S(1)}, bf16[2,32,2048]{2,1,0:T(8,128)(2,1)S(1)}, u32[]{:S(2)}, u32[]{:S(2)}) collective-permute-start(bf16[2,32,2048]{2,1,0:T(8,128)(2,1)S(1)} %slice.574), channel_id=1, source_target_pairs={{0,2},{1,3},{2,0},{3,1},{4,6},{5,7},{6,4},{7,5},{8,10},{9,11},{10,... | collective-permute-start | bytes 786440 | tf_op jit(solution)/shard_map/ppermute | solution.py:22
  307.2 12.0 %collective-permute-start.68 = (bf16[2,32,2048]{2,1,0:T(8,128)(2,1)S(1)}, bf16[2,32,2048]{2,1,0:T(8,128)(2,1)S(1)}, u32[]{:S(2)}, u32[]{:S(2)}) collective-permute-start(bf16[2,32,2048]{2,1,0:T(8,128)(2,1)S(1)} %slice.564), channel_id=1, source_target_pairs={{0,2},{1,3},{2,0},{3,1},{4,6},{5,7},{6,4},{7,5},{8,10},{9,11},{10,... | collective-permute-start | bytes 786440 | tf_op jit(solution)/shard_map/ppermute | solution.py:22
  314.1 9.0 %collective-permute-start.79 = (bf16[1,32,2048]{2,1,0:T(8,128)(2,1)S(1)}, bf16[1,32,2048]{2,1,0:T(8,128)(2,1)S(1)}, u32[]{:S(2)}, u32[]{:S(2)}) collective-permute-start(bf16[1,32,2048]{2,1,0:T(8,128)(2,1)S(1)} %slice.576), channel_id=1, source_target_pairs={{0,4},{1,5},{2,6},{3,7},{4,0},{5,1},{6,2},{7,3},{8,12},{9,13},{10,... | collective-permute-start | bytes 393224 | tf_op jit(solution)/shard_map/ppermute | solution.py:22
  319.3 7.0 %collective-permute-start.69 = (bf16[1,32,2048]{2,1,0:T(8,128)(2,1)S(1)}, bf16[1,32,2048]{2,1,0:T(8,128)(2,1)S(1)}, u32[]{:S(2)}, u32[]{:S(2)}) collective-permute-start(bf16[1,32,2048]{2,1,0:T(8,128)(2,1)S(1)} %slice.566), channel_id=1, source_target_pairs={{0,4},{1,5},{2,6},{3,7},{4,0},{5,1},{6,2},{7,3},{8,12},{9,13},{10,... | collective-permute-start | bytes 393224 | tf_op jit(solution)/shard_map/ppermute | solution.py:22
  323.8 10.2 %collective-permute-start.80 = (bf16[1,32,2048]{2,1,0:T(8,128)(2,1)S(1)}, bf16[1,32,2048]{2,1,0:T(8,128)(2,1)S(1)}, u32[]{:S(2)}, u32[]{:S(2)}) collective-permute-start(bf16[1,32,2048]{2,1,0:T(8,128)(2,1)S(1)} %get-tuple-element.63), channel_id=1, source_target_pairs={{0,4},{1,5},{2,6},{3,7},{4,0},{5,1},{6,2},{7,3},{8,12},{9,13},{10,... | collective-permute-start | bytes 393224 | tf_op jit(solution)/shard_map/ppermute | solution.py:22
  327.0 6.8 %collective-permute-start.70 = (bf16[1,32,2048]{2,1,0:T(8,128)(2,1)S(1)}, bf16[1,32,2048]{2,1,0:T(8,128)(2,1)S(1)}, u32[]{:S(2)}, u32[]{:S(2)}) collective-permute-start(bf16[1,32,2048]{2,1,0:T(8,128)(2,1)S(1)} %get-tuple-element.65), channel_id=1, source_target_pairs={{0,4},{1,5},{2,6},{3,7},{4,0},{5,1},{6,2},{7,3},{8,12},{9,13},{10,... | collective-permute-start | bytes 393224 | tf_op jit(solution)/shard_map/ppermute | solution.py:22
  333.9 6.4 %collective-permute-start.71 = (bf16[2,32,2048]{2,1,0:T(8,128)(2,1)S(1)}, bf16[2,32,2048]{2,1,0:T(8,128)(2,1)S(1)}, u32[]{:S(2)}, u32[]{:S(2)}) collective-permute-start(bf16[2,32,2048]{2,1,0:T(8,128)(2,1)S(1)} %pad_maximum_fusion.7), channel_id=1, source_target_pairs={{0,2},{1,3},{2,0},{3,1},{4,6},{5,7},{6,4},{7,5},{8,10},{9,11},{10,... | collective-permute-start | bytes 786440 | tf_op jit(solution)/shard_map/ppermute | solution.py:22
  334.0 9.1 %collective-permute-start.81 = (bf16[2,32,2048]{2,1,0:T(8,128)(2,1)S(1)}, bf16[2,32,2048]{2,1,0:T(8,128)(2,1)S(1)}, u32[]{:S(2)}, u32[]{:S(2)}) collective-permute-start(bf16[2,32,2048]{2,1,0:T(8,128)(2,1)S(1)} %pad_maximum_fusion.8), channel_id=1, source_target_pairs={{0,2},{1,3},{2,0},{3,1},{4,6},{5,7},{6,4},{7,5},{8,10},{9,11},{10,... | collective-permute-start | bytes 786440 | tf_op jit(solution)/shard_map/ppermute | solution.py:22
  340.3 11.4 %collective-permute-start.72 = (bf16[4,32,2048]{2,1,0:T(8,128)(2,1)S(1)}, bf16[4,32,2048]{2,1,0:T(8,128)(2,1)S(1)}, u32[]{:S(2)}, u32[]{:S(2)}) collective-permute-start(bf16[4,32,2048]{2,1,0:T(8,128)(2,1)S(1)} %pad_maximum_fusion.3), channel_id=1, source_target_pairs={{0,16},{8,24},{16,0},{24,8},{1,17},{9,25},{17,1},{25,9},{2,18},{10... | collective-permute-start | bytes 1572872 | tf_op jit(solution)/shard_map/ppermute | solution.py:22
  343.2 14.9 %collective-permute-start.82 = (bf16[4,32,2048]{2,1,0:T(8,128)(2,1)S(1)}, bf16[4,32,2048]{2,1,0:T(8,128)(2,1)S(1)}, u32[]{:S(2)}, u32[]{:S(2)}) collective-permute-start(bf16[4,32,2048]{2,1,0:T(8,128)(2,1)S(1)} %pad_maximum_fusion.4), channel_id=1, source_target_pairs={{0,8},{8,0},{16,24},{24,16},{1,9},{9,1},{17,25},{25,17},{2,10},{10... | collective-permute-start | bytes 1572872 | tf_op jit(solution)/shard_map/ppermute | solution.py:22
  351.9 21.0 %collective-permute-start.73 = (bf16[8,32,2048]{2,1,0:T(8,128)(2,1)S(1)}, bf16[8,32,2048]{2,1,0:T(8,128)(2,1)S(1)}, u32[]{:S(2)}, u32[]{:S(2)}) collective-permute-start(bf16[8,32,2048]{2,1,0:T(8,128)(2,1)S(1)} %pad_maximum_fusion), channel_id=1, source_target_pairs={{0,8},{8,0},{16,24},{24,16},{1,9},{9,1},{17,25},{25,17},{2,10},{10... | collective-permute-start | bytes 3145736 | tf_op jit(solution)/shard_map/ppermute | solution.py:22
  358.2 15.8 %collective-permute-start.83 = (bf16[8,32,2048]{2,1,0:T(8,128)(2,1)S(1)}, bf16[8,32,2048]{2,1,0:T(8,128)(2,1)S(1)}, u32[]{:S(2)}, u32[]{:S(2)}) collective-permute-start(bf16[8,32,2048]{2,1,0:T(8,128)(2,1)S(1)} %pad_maximum_fusion.1), channel_id=1, source_target_pairs={{0,16},{8,24},{16,0},{24,8},{1,17},{9,25},{17,1},{25,9},{2,18},{10... | collective-permute-start | bytes 3145736 | tf_op jit(solution)/shard_map/ppermute | solution.py:22
  374.0 61.3 %collective-permute-start.74 = (bf16[16,32,2048]{2,1,0:T(8,128)(2,1)}, bf16[16,32,2048]{2,1,0:T(8,128)(2,1)}, u32[]{:S(2)}, u32[]{:S(2)}) collective-permute-start(bf16[16,32,2048]{2,1,0:T(8,128)(2,1)} %get-tuple-element.90), channel_id=1, source_target_pairs={{0,1},{1,0},{2,3},{3,2},{4,5},{5,4},{6,7},{7,6},{8,9},{9,8},{10,11... | collective-permute-start | bytes 6291464 | tf_op jit(solution)/shard_map/ppermute | solution.py:22
  375.3 81.6 %collective-permute-start.84 = (bf16[16,32,2048]{2,1,0:T(8,128)(2,1)}, bf16[16,32,2048]{2,1,0:T(8,128)(2,1)}, u32[]{:S(2)}, u32[]{:S(2)}) collective-permute-start(bf16[16,32,2048]{2,1,0:T(8,128)(2,1)} %get-tuple-element.88), channel_id=1, source_target_pairs={{0,1},{1,0},{2,3},{3,2},{4,5},{5,4},{6,7},{7,6},{8,9},{9,8},{10,11... | collective-permute-start | bytes 6291464 | tf_op jit(solution)/shard_map/ppermute | solution.py:22
  379.3 36.3 %collective-permute-start.54 = (bf16[16,32,1024]{2,1,0:T(8,128)(2,1)}, bf16[16,32,1024]{2,1,0:T(8,128)(2,1)}, u32[]{:S(2)}, u32[]{:S(2)}) collective-permute-start(bf16[16,32,1024]{2,1,0:T(8,128)(2,1)} %get-tuple-element.96), channel_id=1, source_target_pairs={{0,1},{1,0},{2,3},{3,2},{4,5},{5,4},{6,7},{7,6},{8,9},{9,8},{10,11... | collective-permute-start | bytes 3145736 | tf_op jit(solution)/shard_map/ppermute | solution.py:22
  380.2 16.5 %collective-permute-start.64 = (bf16[16,9,1024]{2,1,0:T(8,128)(2,1)}, bf16[16,9,1024]{2,1,0:T(8,128)(2,1)S(1)}, u32[]{:S(2)}, u32[]{:S(2)}) collective-permute-start(bf16[16,9,1024]{2,1,0:T(8,128)(2,1)} %get-tuple-element.102), channel_id=1, source_target_pairs={{0,1},{1,0},{2,3},{3,2},{4,5},{5,4},{6,7},{7,6},{8,9},{9,8},{10,11... | collective-permute-start | bytes 884744 | tf_op jit(solution)/shard_map/ppermute | solution.py:22
  (62 other events, 663.1 us)

commit v3 on v2

v3 whole, which is shorter than its diff:
```python
import functools
import math

import jax
import jax.numpy as jnp
from jax import lax
from jax.experimental import pallas as pl
from jax.experimental.pallas import tpu as pltpu
from jax.sharding import PartitionSpec as P

GW = 32
EPS = 1e-05
VMEM_LIMIT = 40 * 1024 * 1024


def shifted(value, axis, by):
    peers = lax.axis_size(axis)
    pairs = [(i, i + by) for i in range(peers) if 0 <= i + by < peers]
    return lax.ppermute(value, axis, pairs)


def exchange(value, axis, mask):
    peers = lax.axis_size(axis)
    return lax.ppermute(value, axis, [(i, i ^ mask) for i in range(peers)])


def sum_plan(axes):
    rounds = []
    for axis in axes:
        bits = [1 << b for b in range(lax.axis_size(axis).bit_length() - 1)]
        if axis == "ba" and bits:
            rounds.append((axis, bits[:1]))
            bits = bits[1:]
        while bits:
            rounds.append((axis, bits[:2]))
            bits = bits[2:]
    return rounds


def meet(value, axis, masks):
    offsets = [0]
    for mask in masks:
        offsets = offsets + [o ^ mask for o in offsets]
    return [value] + [exchange(value, axis, o) for o in offsets[1:]]


def add_round(value, axis, masks):
    parts = meet(value, axis, masks)
    while len(parts) > 1:
        parts = [parts[i] + parts[i + 1] for i in range(0, len(parts), 2)]
    return parts[0]


def mesh_sum(value, rounds):
    for axis, masks in rounds:
        value = add_round(value, axis, masks)
    return value


def merge(one, two):
    count = one[0] + two[0]
    gap = two[1] - one[1]
    return (
        count,
        (one[0] * one[1] + two[0] * two[1]) / count,
        one[2] + two[2] + gap * gap * (one[0] * two[0] / count),
        (one[0] * one[3] + two[0] * two[3]) / count,
    )


def mesh_moments(packed, rounds):
    for axis, masks in rounds:
        parts = [tuple(part) for part in meet(packed, axis, masks)]
        while len(parts) > 1:
            parts = [merge(parts[i], parts[i + 1]) for i in range(0, len(parts), 2)]
        packed = jnp.stack(parts[0])
    return packed


CUTS = (("ba", 1), ("ha", 1), ("ha", 2), ("ba", 2), ("ba", 4))
PARTS = 32


def own_part(cuts):
    index = jnp.int32(0)
    for axis, mask in cuts:
        bit = jnp.bitwise_and(lax.axis_index(axis), mask) // mask
        index = index * 2 + bit.astype(jnp.int32)
    return index


def spread_kernel(own_ref, low_ref, high_ref, *out_refs):
    half = low_ref.shape[0]
    rows = out_refs[0].shape[1]
    for part in range(2 * half):
        at = jnp.bitwise_xor(own_ref[0], part)
        ref = low_ref if part < half else high_ref
        out_refs[0][at] = ref[part % half, :rows, :].astype(jnp.float32)
        if len(out_refs) > 1:
            more = out_refs[1].shape[0]
            extra = ref[part % half, rows : rows + more, :].astype(jnp.float32)
            for row in range(more):
                out_refs[1][row, pl.ds(at, 1), :] = extra[row : row + 1, :]


def plain_order(low, high, own, rows, more):
    half, deep, cols = low.shape
    width = 512
    shapes = [(2 * half, rows)] + ([(more, 2 * half)] if more else [])
    block = pl.BlockSpec((half, deep, width), lambda i: (0, 0, i))
    return pl.pallas_call(
        spread_kernel,
        grid=(cols // width,),
        in_specs=[pl.BlockSpec(memory_space=pltpu.SMEM), block, block],
        out_specs=[pl.BlockSpec(shape + (width,), lambda i: (0, 0, i)) for shape in shapes],
        out_shape=[jax.ShapeDtypeStruct(shape + (cols,), jnp.float32) for shape in shapes],
        compiler_params=pltpu.CompilerParams(vmem_limit_bytes=VMEM_LIMIT),
        cost_estimate=pl.CostEstimate(flops=0, bytes_accessed=12 * low.size, transcendentals=0),
    )(own.reshape(1), low, high)


def add_low(one, two):
    return (one.astype(jnp.float32) + two.astype(jnp.float32)).astype(jnp.bfloat16)


def tie(*values):
    return lax.optimization_barrier(values)


class Gradient:
    def __init__(self, low, high, cuts, own):
        self.low, self.high, self.cuts, self.own = low, high, cuts, own
        self.blocks = None
        self.at = 0
        self.got = None

    def send(self):
        count = len(self.cuts)
        if self.at < count:
            self.got = exchange(self.high, *self.cuts[self.at])
        else:
            self.got = exchange(self.blocks, *self.cuts[2 * count - 1 - self.at])

    def take(self):
        count = len(self.cuts)
        if self.at < count:
            blocks = add_low(self.low, self.got)
            half = blocks.shape[0] // 2
            if half:
                self.low, self.high = blocks[:half], blocks[half:]
            else:
                spare = 8
                while spare < lax.axis_size("ba"):
                    blocks = add_low(blocks, exchange(blocks, "ba", spare))
                    spare *= 2
                self.blocks = blocks
        else:
            if self.at == 2 * count - 1:
                self.low, self.high = self.blocks, self.got
            else:
                self.blocks = jnp.concatenate([self.blocks, self.got], axis=0)
        self.got = None
        self.at += 1

    def step(self):
        self.take()
        if self.at < 2 * len(self.cuts):
            self.send()

    def finish(self, rows, more=0):
        return plain_order(self.low, self.high, self.own, rows, more)


def arrive(grads, *values):
    held = tie(*values, *[grad.got for grad in grads])
    for grad, got in zip(grads, held[len(values) :]):
        grad.got = got
    return held[: len(values)]


LOW = jnp.bfloat16
WIDE = jnp.float32
TAPS = 3
SMEM = pltpu.SMEM


def dot(one, two):
    return jnp.dot(one, two, preferred_element_type=WIDE)


def dot_nt(one, two):
    return lax.dot_general(one, two, (((1,), (1,)), ((), ())), preferred_element_type=WIDE)


def dot_tn(one, two):
    return lax.dot_general(one, two, (((0,), (0,)), ((), ())), preferred_element_type=WIDE)


def iota(shape, axis):
    return lax.broadcasted_iota(jnp.int32, shape, axis)


def logistic(values):
    return 0.5 * jnp.tanh(0.5 * values) + 0.5


def fold(values):
    rows, width = values.shape
    return jnp.sum(values.reshape(rows // 8, 8, width), axis=0)


def close(partial):
    return jnp.sum(partial, axis=0, keepdims=True)


def spans(rows, size):
    return [slice(at, at + size) for at in range(0, rows, size)]


def parity_order(image_rows, cols, axis=0):
    pixels = image_rows * cols
    quarter = pixels // 4
    half_cols = cols // 2
    place = iota((pixels, pixels), axis)
    source = iota((pixels, pixels), 1 - axis)
    plane = place // quarter
    inside = place % quarter
    row = 2 * (inside // half_cols) + plane // 2
    col = 2 * (inside % half_cols) + plane % 2
    return (source == row * cols + col).astype(WIDE).astype(LOW)


def halo_order(images, cols):
    count = images * cols
    half_cols = cols // 2
    place = iota((count, count), 0)
    source = iota((count, count), 1)
    parity = place // (count // 2)
    inside = place % (count // 2)
    image = inside // half_cols
    col = 2 * (inside % half_cols) + parity
    return (source == image * cols + col).astype(WIDE).astype(LOW)


def shifted_sums(ref, valid_ref, base, planes, images, quarter):
    width = ref.shape[1]
    total = jnp.zeros((8, width), WIDE)
    square = jnp.zeros((8, width), WIDE)
    for image in range(images):
        first = jnp.zeros((8, width), WIDE)
        second = jnp.zeros((8, width), WIDE)
        for plane in range(planes):
            at = (plane * images + image) * quarter
            gap = ref[at : at + quarter, :] - base
            first += fold(gap)
            second += fold(gap * gap)
        total += first * valid_ref[image]
        square += second * valid_ref[image]
    return close(total), close(square)


def moments_of(sums, base, count):
    offset = sums[0:1, :] / count
    variance = jnp.maximum(sums[1:2, :] / count - offset * offset, 0.0)
    return base + offset, lax.rsqrt(variance + EPS)


def row_of(values, w):
    return dot(jnp.broadcast_to(values, (16, values.shape[1])).astype(LOW), w)[0:1, :]


def reduce_kernel(dims, valid_ref, x_ref, w_ref, planes_ref, reduced_ref, stats_ref, sampled_ref):
    images, image_rows, cols = dims
    pixels = image_rows * cols
    quarter = pixels // 4
    plane_rows = images * quarter
    valid = valid_ref[0]
    for image in range(1, images):
        valid = valid + valid_ref[image]

    @pl.when(pl.program_id(0) == 0)
    def _():
        order = parity_order(image_rows, cols)
        total = jnp.zeros((8, x_ref.shape[1]), WIDE)
        for image in range(images):
            moved = dot(order, x_ref[image * pixels : (image + 1) * pixels, :])
            total += fold(moved[:quarter, :]) * valid_ref[image]
            moved = moved.astype(LOW)
            for plane in range(4):
                at = plane * plane_rows + image * quarter
                planes_ref[at : at + quarter, :] = moved[plane * quarter : (plane + 1) * quarter, :]
        sampled_ref[...] = close(total) / (valid * float(quarter))

    for plane in range(4):
        at = slice(plane * plane_rows, (plane + 1) * plane_rows)
        reduced_ref[at, :] = dot(planes_ref[at, :], w_ref[...])
    count = valid * float(pixels)
    base = reduced_ref[0:1, :]
    total, square = shifted_sums(reduced_ref, valid_ref, base, 4, images, quarter)
    stats_ref[0:1, :] = jnp.full(base.shape, count, WIDE)
    stats_ref[1:2, :] = base + total / count
    stats_ref[2:3, :] = jnp.maximum(square - total * (total / count), 0.0)


def turn_kernel(own_ref, value_ref, out_ref):
    parts, rows, _ = out_ref.shape
    turned = value_ref[...].T
    for part in range(parts):
        out_ref[jnp.bitwise_xor(own_ref[0], part)] = turned[part * rows : (part + 1) * rows, :]


def project_kernel(quarter, valid_ref, x_ref, w_ref, sampled_ref, out_ref, sums_ref):
    out_ref[...] = dot(x_ref[...], w_ref[...])
    base = row_of(sampled_ref[...], w_ref[...])
    images = out_ref.shape[0] // quarter
    total, square = shifted_sums(out_ref, valid_ref, base, 1, images, quarter)
    sums_ref[0:1, :] = total
    sums_ref[1:2, :] = square
    sums_ref[2:3, :] = base


def group_mask(width):
    return (iota((width, width), 0) // GW == iota((width, width), 1) // GW).astype(WIDE).astype(LOW)


def block_weights(w_ref, mask, tap):
    width = w_ref.shape[1]
    part = w_ref[tap * GW : (tap + 1) * GW, :]
    return jnp.concatenate([part] * (width // GW), axis=0) * mask


def shift_columns(values, cols, by):
    rows, width = values.shape
    moved = pltpu.roll(values, by % rows, 0)
    edge = 0 if by > 0 else cols - 1
    return jnp.where(iota((rows, width), 0) % cols == edge, 0.0, moved)


def activate(values, mean, scale, shift):
    normal = (values - mean) * scale + shift
    return normal * logistic(normal)


def windows(planes, odd, halves):
    even_even, even_odd, even_moved = planes
    images, deep, half_cols, width = odd[0].shape
    tall = deep - 1

    def part(ref, at):
        return ref[:, at : at + tall, :, :].reshape(images * tall * half_cols, width)

    result = []
    for row_tap in range(TAPS):
        if row_tap == 1:
            result += [even_moved[...], even_even[...], even_odd[...]]
        else:
            at = 0 if row_tap == 0 else 1
            result += [part(odd[2], at), part(odd[0], at), part(odd[1], at)]
    return result


def store_hidden(dims, get, halo, even, odd):
    images, tall, half_cols = dims
    quarter = tall * half_cols
    for image in range(images):
        at = slice(image * quarter, (image + 1) * quarter)
        even[0][at, :] = get(0, image).astype(LOW)
        values = get(1, image)
        even[1][at, :] = values.astype(LOW)
        even[2][at, :] = shift_columns(values, half_cols, 1).astype(LOW)
        values = get(2, image)
        width = values.shape[1]
        odd[0][image, 1:, :, :] = values.astype(LOW).reshape(tall, half_cols, width)
        values = get(3, image)
        odd[1][image, 1:, :, :] = values.astype(LOW).reshape(tall, half_cols, width)
        odd[2][image, 1:, :, :] = shift_columns(values, half_cols, 1).astype(LOW).reshape(tall, half_cols, width)
    width = halo[0].shape[1]
    odd[0][:, 0, :, :] = halo[0].astype(LOW).reshape(images, half_cols, width)
    odd[1][:, 0, :, :] = halo[1].astype(LOW).reshape(images, half_cols, width)
    odd[2][:, 0, :, :] = shift_columns(halo[1], half_cols, 1).astype(LOW).reshape(images, half_cols, width)


def window_scratch(images, tall, half_cols, width):
    flat = pltpu.VMEM((images * tall * half_cols, width), LOW)
    deep = pltpu.VMEM((images, tall + 1, half_cols, width), LOW)
    return [flat, flat, flat, deep, deep, deep]


def conv_kernel(
    dims,
    scalar_ref,
    valid_ref,
    reduced_ref,
    moments_ref,
    affine_ref,
    halo_ref,
    reduce_ref,
    group_ref,
    grouped_ref,
    sums_ref,
    base_ref,
    first_ref,
    edge_ref,
    moved_ref,
    *buffers,
):
    images, tall, half_cols = dims
    quarter = tall * half_cols
    plane_rows = images * quarter
    width = reduced_ref.shape[1]

    @pl.when(pl.program_id(0) == 0)
    def _():
        moved_ref[...] = dot(halo_order(images, 2 * half_cols), halo_ref[...]).astype(LOW)

    mean = moments_ref[0:1, :]
    scale = affine_ref[0:1, :] * lax.rsqrt(moments_ref[1:2, :] / scalar_ref[0] + EPS)
    shift = affine_ref[1:2, :]
    edge = activate(dot(moved_ref[...], reduce_ref[...]), mean, scale, shift) * scalar_ref[2]
    edge_ref[...] = edge.astype(LOW)
    half = edge.shape[0] // 2

    def get(plane, image):
        at = plane * plane_rows + image * quarter
        return activate(reduced_ref[at : at + quarter, :], mean, scale, shift)

    even, odd = buffers[:3], buffers[3:]
    store_hidden(dims, get, (edge[:half], edge[half:]), even, odd)
    mask = group_mask(width)
    total = None
    for tap, window in enumerate(windows(even, odd, half_cols)):
        term = dot(window, block_weights(group_ref, mask, tap))
        total = term if total is None else total + term
    grouped_ref[...] = total
    kernel = group_ref[0:GW, :].astype(WIDE)
    for tap in range(1, TAPS * TAPS):
        kernel = kernel + group_ref[tap * GW : (tap + 1) * GW, :].astype(WIDE)
    kernel = jnp.concatenate([kernel.astype(LOW)] * (width // GW), axis=0) * mask
    base = row_of(shift * logistic(shift), kernel)
    total, square = shifted_sums(grouped_ref, valid_ref, base, 1, images, quarter)
    sums_ref[0:1, :] = total
    sums_ref[1:2, :] = square
    base_ref[...] = base
    for image in range(images):
        at = image * quarter
        first_ref[image * half_cols : (image + 1) * half_cols, :] = grouped_ref[at : at + half_cols, :].astype(LOW)


def expand_kernel(
    quarter,
    scalar_ref,
    valid_ref,
    grouped_ref,
    sums_two_ref,
    base_two_ref,
    affine_ref,
    w_ref,
    side_ref,
    hidden_ref,
    out_ref,
    sums_ref,
    base_ref,
):
    shift = affine_ref[1:2, :]

    @pl.when(pl.program_id(0) == 0)
    def _():
        mean, inv = moments_of(sums_two_ref[...], base_two_ref[...], scalar_ref[1])
        scale = affine_ref[0:1, :] * inv
        for span in spans(grouped_ref.shape[0], 16):
            hidden_ref[span, :] = activate(grouped_ref[span, :], mean, scale, shift).astype(LOW)

    out_ref[...] = dot(hidden_ref[...], w_ref[...])
    base = row_of(shift * logistic(shift), w_ref[...])
    images = out_ref.shape[0] // quarter
    total, square = shifted_sums(out_ref, valid_ref, base, 1, images, quarter)
    sums_ref[0:1, :] = total
    sums_ref[1:2, :] = square
    sums_ref[2:4, :] = side_ref[0:2, :]
    base_ref[0:1, :] = base
    base_ref[1:2, :] = side_ref[2:3, :]


def slope(values, gate):
    return gate * (1.0 + values * (1.0 - gate))


def tail_moments(sums_ref, base_ref, count):
    return (
        *moments_of(sums_ref[0:2, :], base_ref[0:1, :], count),
        *moments_of(sums_ref[2:4, :], base_ref[1:2, :], count),
    )


def tail_values(one, two, moments, affine):
    first = (one - moments[0]) * moments[1]
    second = (two - moments[2]) * moments[3]
    summed = first * affine[0:1, :] + affine[1:2, :] + second * affine[2:3, :] + affine[3:4, :]
    return first, second, summed


def output_kernel(
    size,
    scalar_ref,
    valid_ref,
    expanded_ref,
    projected_ref,
    stats_ref,
    base_ref,
    affine_ref,
    cot_ref,
    out_ref,
    sums_ref,
):
    rows, width = out_ref.shape
    quarter = rows // valid_ref.shape[0]
    totals = [jnp.zeros((8, width), WIDE) for _ in range(3)]
    moments = tail_moments(stats_ref, base_ref, scalar_ref[1])
    affine = affine_ref[...]
    for span in spans(rows, size):
        first, second, summed = tail_values(expanded_ref[span, :], projected_ref[span, :], moments, affine)
        valid = valid_ref[span.start // quarter]
        gate = logistic(summed)
        out_ref[span, :] = (valid * (summed * gate)).astype(LOW)
        upstream = (cot_ref[span, :].astype(WIDE) * valid) * slope(summed, gate)
        totals[0] += fold(upstream)
        totals[1] += fold(upstream * first)
        totals[2] += fold(upstream * second)
    for at in range(3):
        sums_ref[at : at + 1, :] = close(totals[at])


def weights_kernel(
    size,
    scalar_ref,
    valid_ref,
    expanded_ref,
    projected_ref,
    stats_ref,
    base_ref,
    affine_ref,
    sums_ref,
    cot_ref,
    hidden_ref,
    sampled_ref,
    d_expanded_ref,
    d_projected_ref,
    expand_low_ref,
    expand_high_ref,
    proj_low_ref,
    proj_high_ref,
):
    rows, width = d_expanded_ref.shape
    quarter = rows // valid_ref.shape[0]
    count = scalar_ref[1]
    moments = tail_moments(stats_ref, base_ref, count)
    affine = affine_ref[...]
    gain_one = affine[0:1, :] * moments[1]
    gain_two = affine[2:3, :] * moments[3]
    sums = sums_ref[...] / count
    for span in spans(rows, size):
        first, second, summed = tail_values(expanded_ref[span, :], projected_ref[span, :], moments, affine)
        valid = valid_ref[span.start // quarter]
        upstream = cot_ref[span, :].astype(WIDE) * slope(summed, logistic(summed)) - sums[0:1, :]
        d_expanded_ref[span, :] = ((valid * gain_one) * (upstream - first * sums[1:2, :])).astype(LOW)
        d_projected_ref[span, :] = ((valid * gain_two) * (upstream - second * sums[2:3, :])).astype(LOW)
    store_halves(sampled_ref[...], d_projected_ref[...], proj_low_ref, proj_high_ref)
    store_halves(hidden_ref[...], d_expanded_ref[...], expand_low_ref, expand_high_ref)


def store_halves(turned, grads, low_ref, high_ref):
    half = low_ref.shape[0]
    for at, ref in ((0, low_ref), (half, high_ref)):
        left = turned[at : at + half].reshape(half * turned.shape[1], turned.shape[2])
        ref[...] = dot(left, grads).astype(LOW).reshape(ref.shape)


def back_two_kernel(
    size, dims, scalar_ref, d_ref, w_ref, grouped_ref, sums_two_ref, base_two_ref, affine_ref, out_ref, sums_ref, first_ref
):
    rows, width = out_ref.shape
    images, tall, half_cols = dims
    mean, inv = moments_of(sums_two_ref[...], base_two_ref[...], scalar_ref[1])
    out_ref[...] = dot_nt(d_ref[...], w_ref[...])
    totals = [jnp.zeros((8, width), WIDE) for _ in range(2)]
    for span in spans(rows, size):
        normed = (grouped_ref[span, :] - mean) * inv
        before = normed * affine_ref[0:1, :] + affine_ref[1:2, :]
        grad = out_ref[span, :] * slope(before, logistic(before))
        out_ref[span, :] = grad
        totals[0] += fold(grad)
        totals[1] += fold(grad * normed)
    for at in range(2):
        sums_ref[at : at + 1, :] = close(totals[at])
    for image in range(images):
        at = image * tall * half_cols
        first_ref[image * half_cols : (image + 1) * half_cols, :] = out_ref[at : at + half_cols, :].astype(LOW)


def side_kernel(d_ref, w_ref, out_ref):
    out_ref[...] = dot_nt(d_ref[...], w_ref[...])


def norm_back_values(grad, values, mean, inv, gain, sums):
    return gain * inv * (grad - (sums[0:1, :] + (values - mean) * inv * sums[1:2, :]))


def conv_back_kernel(
    dims,
    scalar_ref,
    own_ref,
    valid_ref,
    grad_ref,
    grouped_ref,
    below_grad_ref,
    below_grouped_ref,
    sums_two_ref,
    base_two_ref,
    affine_two_ref,
    grads_two_ref,
    reduced_ref,
    edge_ref,
    moments_one_ref,
    affine_one_ref,
    group_ref,
    out_ref,
    sums_ref,
    grad_group_ref,
    *buffers,
):
    images, tall, half_cols = dims
    quarter = tall * half_cols
    plane_rows = images * quarter
    width = reduced_ref.shape[1]
    even, odd, below = buffers[:3], buffers[3:6], buffers[6:8]
    count_in, count_out = scalar_ref[0], scalar_ref[1]

    mean, inv = moments_of(sums_two_ref[...], base_two_ref[...], count_out)
    gain = affine_two_ref[0:1, :]
    sums = grads_two_ref[...] / count_out
    for image in range(images):
        at = slice(image * quarter, (image + 1) * quarter)
        values = norm_back_values(grad_ref[at, :], grouped_ref[at, :], mean, inv, gain, sums)
        values = values * valid_ref[image]
        below[0][image, :tall, :, :] = values.astype(LOW).reshape(tall, half_cols, width)
        below[1][image, :tall, :, :] = (
            shift_columns(values, half_cols, -1).astype(LOW).reshape(tall, half_cols, width)
        )
        at = slice(image * half_cols, (image + 1) * half_cols)
        values = norm_back_values(
            below_grad_ref[at, :].astype(WIDE), below_grouped_ref[at, :].astype(WIDE), mean, inv, gain, sums
        )
        values = values * (valid_ref[image] * scalar_ref[3])
        below[0][image, tall, :, :] = values.astype(LOW)
        below[1][image, tall, :, :] = shift_columns(values, half_cols, -1).astype(LOW)

    def part(ref, at):
        return ref[:, at : at + tall, :, :].reshape(plane_rows, width)

    mask = group_mask(width)
    weights = [block_weights(group_ref, mask, tap) for tap in range(TAPS * TAPS)]
    here, left = part(below[0], 0), part(below[1], 0)
    next_here, next_left = part(below[0], 1), part(below[1], 1)
    out_ref[0:plane_rows, :] = dot_nt(here, weights[4])
    out_ref[plane_rows : 2 * plane_rows, :] = dot_nt(here, weights[5]) + dot_nt(left, weights[3])
    out_ref[2 * plane_rows : 3 * plane_rows, :] = dot_nt(here, weights[7]) + dot_nt(next_here, weights[1])
    out_ref[3 * plane_rows : 4 * plane_rows, :] = (
        dot_nt(here, weights[8])
        + dot_nt(left, weights[6])
        + dot_nt(next_here, weights[2])
        + dot_nt(next_left, weights[0])
    )

    mean_one = moments_one_ref[0:1, :]
    inv_one = lax.rsqrt(moments_one_ref[1:2, :] / count_in + EPS)
    totals = [jnp.zeros((8, width), WIDE) for _ in range(2)]

    def get(plane, image):
        start = plane * plane_rows + image * quarter
        at = slice(start, start + quarter)
        normed = (reduced_ref[at, :] - mean_one) * inv_one
        before = normed * affine_one_ref[0:1, :] + affine_one_ref[1:2, :]
        gate = logistic(before)
        grad = out_ref[at, :] * slope(before, gate)
        out_ref[at, :] = grad
        totals[0] += fold(grad)
        totals[1] += fold(grad * normed)
        return before * gate

    half = edge_ref.shape[0] // 2
    edge = edge_ref[...].astype(WIDE)
    store_hidden(dims, get, (edge[:half], edge[half:]), even, odd)
    for at in range(2):
        sums_ref[at : at + 1, :] = close(totals[at])
    turned = here.T
    picked = jnp.bitwise_xor(iota((GW, width), 0), own_ref[0])
    one_hot = (iota((GW, width), 1) % GW == picked).astype(WIDE).astype(LOW)
    for tap, window in enumerate(windows(even, odd, half_cols)):
        full = dot(turned, window).astype(LOW) * mask
        grad_group_ref[tap] = dot_nt(one_hot, full).astype(LOW)


def reduced_back_kernel(
    size,
    scalar_ref,
    valid_ref,
    grad_ref,
    reduced_ref,
    moments_ref,
    affine_ref,
    sums_ref,
    *refs,
):
    planes_refs, (d_ref, low_ref, high_ref) = refs[:4], refs[4:]
    rows, width = d_ref.shape
    images = valid_ref.shape[0]
    quarter = rows // (4 * images)
    mean = moments_ref[0:1, :]
    inv = lax.rsqrt(moments_ref[1:2, :] / scalar_ref[0] + EPS)
    sums = sums_ref[...] / scalar_ref[0]
    for span in spans(rows, size):
        values = norm_back_values(grad_ref[span, :], reduced_ref[span, :], mean, inv, affine_ref[0:1, :], sums)
        d_ref[span, :] = (values * valid_ref[span.start // quarter % images]).astype(LOW)
    half = low_ref.shape[0]
    for at, ref in ((0, low_ref), (half, high_ref)):
        total = None
        for plane, planes_ref in enumerate(planes_refs):
            deep = planes_ref.shape[2]
            left = planes_ref[at : at + half].reshape(half * planes_ref.shape[1], deep)
            term = dot(left, d_ref[plane * deep : (plane + 1) * deep, :])
            total = term if total is None else total + term
        ref[...] = total.astype(LOW).reshape(ref.shape)


def images_back_kernel(dims, d_ref, w_ref, side_ref, out_ref, order_ref):
    image_rows, cols = dims
    pixels = image_rows * cols
    quarter = pixels // 4

    @pl.when(pl.program_id(0) == 0)
    def _():
        order_ref[...] = parity_order(image_rows, cols, 1)

    values = dot_nt(d_ref[...].reshape(pixels, d_ref.shape[-1]), w_ref[...])
    first = values[:quarter] + side_ref[...]
    planes = jnp.concatenate([first, values[quarter:]], axis=0).astype(LOW)
    out_ref[...] = dot(order_ref[...], planes).astype(LOW)


def whole(shape):
    return pl.BlockSpec(shape, lambda i: (0,) * len(shape))


def wide_cols(rows, width):
    return pl.BlockSpec((rows, width), lambda i: (0, i))


SCALARS = pl.BlockSpec(memory_space=pltpu.SMEM)


def place(shape, kind):
    if math.prod(shape) * jnp.dtype(kind).itemsize >= 4 << 20:
        return pltpu.HBM(shape, kind)
    return jax.ShapeDtypeStruct(shape, kind)


def call(kernel, grid, in_specs, out_specs, out_shapes, cost, scratch=()):
    flops, moved = cost
    return pl.pallas_call(
        kernel,
        grid=(grid,),
        in_specs=in_specs,
        out_specs=out_specs,
        out_shape=[place(shape, kind) for shape, kind in out_shapes],
        scratch_shapes=list(scratch),
        compiler_params=pltpu.CompilerParams(vmem_limit_bytes=VMEM_LIMIT),
        cost_estimate=pl.CostEstimate(flops=flops, bytes_accessed=moved, transcendentals=0),
    )


def per_device(
    images_in,
    reduce_w,
    gain_one,
    shift_one,
    group_w,
    gain_two,
    shift_two,
    expand_w,
    gain_three,
    shift_three,
    proj_w,
    gain_proj,
    shift_proj,
    valid_mask,
    cotangent,
):
    images, image_rows, cols, chans = images_in.shape
    mid = reduce_w.shape[1]
    wide = expand_w.shape[1]
    tall, half_cols = image_rows // 2, cols // 2
    quarter = tall * half_cols
    rows = images * quarter
    pixels = images * image_rows * cols
    block = 256
    steps = mid // block
    strip = 512
    strips = wide // strip

    valid = valid_mask.astype(WIDE)
    row_index = lax.axis_index("ha")
    has_upper = (row_index > 0).astype(WIDE)
    has_lower = (row_index < lax.axis_size("ha") - 1).astype(WIDE)
    swapped = (CUTS[0], CUTS[2], CUTS[1], CUTS[3], CUTS[4])
    own_plain, own_swapped = own_part(CUTS), own_part(swapped)
    own_one, own_two = own_plain.reshape(1), own_swapped.reshape(1)
    affine_one = jnp.stack([gain_one, shift_one])
    affine_two = jnp.stack([gain_two, shift_two])
    affine_out = jnp.stack([gain_three, shift_three, gain_proj, shift_proj])
    taps = TAPS * TAPS * GW
    group_flat = group_w.reshape(taps, mid)
    rounds = sum_plan(("ba", "ha"))
    back_rounds = sum_plan(("ha", "ba"))

    halo_images = shifted(images_in[:, -1], "ha", 1).reshape(images * cols, chans)
    planes, reduced, stats, sampled = call(
        functools.partial(reduce_kernel, (images, image_rows, cols)),
        steps,
        [SCALARS, whole((pixels, chans)), wide_cols(chans, block)],
        [whole((pixels, chans)), wide_cols(pixels, block), wide_cols(3, block), whole((1, chans))],
        [((pixels, chans), LOW), ((pixels, mid), WIDE), ((3, mid), WIDE), ((1, chans), WIDE)],
        (2 * pixels * chans * (mid + 256), 20 << 20),
    )(valid, images_in.reshape(pixels, chans), reduce_w)
    stats, halo_images = tie(jnp.concatenate([stats, sampled]), halo_images)
    stats = mesh_moments(stats, rounds)

    def turn(value, at, own):
        width = value.shape[1]
        return call(
            turn_kernel,
            1,
            [SCALARS, pl.BlockSpec((rows, width), lambda i: (at, 0))],
            [whole((PARTS, width // PARTS, rows))],
            [((PARTS, width // PARTS, rows), LOW)],
            (0, 2 << 20),
        )(own, value)[0]

    planes_turned = [turn(planes, plane, own_two) for plane in range(4)]
    stats, *planes_turned = tie(stats, *planes_turned)
    count_in, moments_one, sampled_mean = stats[0, 0], stats[1:3], stats[3:4]
    scalars = jnp.stack([count_in, count_in / 4.0, has_upper, has_lower])

    grouped, sums, base_two, first_row, edge = call(
        functools.partial(conv_kernel, (images, tall, half_cols)),
        steps,
        [
            SCALARS,
            SCALARS,
            wide_cols(pixels, block),
            wide_cols(2, block),
            wide_cols(2, block),
            whole((images * cols, chans)),
            wide_cols(chans, block),
            wide_cols(taps, block),
        ],
        [
            wide_cols(rows, block),
            wide_cols(2, block),
            wide_cols(1, block),
            wide_cols(images * half_cols, block),
            wide_cols(images * cols, block),
        ],
        [
            ((rows, mid), WIDE),
            ((2, mid), WIDE),
            ((1, mid), WIDE),
            ((images * half_cols, mid), LOW),
            ((images * cols, mid), LOW),
        ],
        (2 * rows * mid * 9 * 256, 14 << 20),
        [pltpu.VMEM((images * cols, chans), LOW)] + window_scratch(images, tall, half_cols, block),
    )(scalars, valid, reduced, moments_one, affine_one, halo_images, reduce_w, group_flat)
    sums_two = mesh_sum(sums, rounds)
    below_grouped = shifted(first_row, "ha", -1)
    sums_two, below_grouped = tie(sums_two, below_grouped)
    projected, side = call(
        functools.partial(project_kernel, quarter),
        strips,
        [SCALARS, whole((rows, chans)), wide_cols(chans, strip), whole((1, chans))],
        [wide_cols(rows, strip), wide_cols(3, strip)],
        [((rows, wide), WIDE), ((3, wide), WIDE)],
        (2 * rows * chans * wide, 10 << 20),
    )(valid, planes, proj_w, sampled_mean)

    hidden_two, expanded, sums, base_out = call(
        functools.partial(expand_kernel, quarter),
        strips,
        [
            SCALARS,
            SCALARS,
            whole((rows, mid)),
            whole((2, mid)),
            whole((1, mid)),
            whole((2, mid)),
            wide_cols(mid, strip),
            wide_cols(3, strip),
        ],
        [whole((rows, mid)), wide_cols(rows, strip), wide_cols(4, strip), wide_cols(2, strip)],
        [((rows, mid), LOW), ((rows, wide), WIDE), ((4, wide), WIDE), ((2, wide), WIDE)],
        (2 * rows * mid * wide, 12 << 20),
    )(scalars, valid, grouped, sums_two, base_two, affine_two, expand_w, side)
    stats_out = mesh_sum(sums, rounds)
    stats_out, hidden_turned = tie(stats_out, turn(hidden_two, 0, own_one))

    cot = cotangent.reshape(rows, wide)
    output, sums = call(
        functools.partial(output_kernel, 16),
        strips,
        [
            SCALARS,
            SCALARS,
            wide_cols(rows, strip),
            wide_cols(rows, strip),
            wide_cols(4, strip),
            wide_cols(2, strip),
            wide_cols(4, strip),
            wide_cols(rows, strip),
        ],
        [wide_cols(rows, strip), wide_cols(3, strip)],
        [((rows, wide), LOW), ((3, wide), WIDE)],
        (20 * rows * wide, 12 << 20),
    )(scalars, valid, expanded, projected, stats_out, base_out, affine_out, cot)
    sums_out = mesh_sum(sums, rounds)

    def halves_specs(height, width):
        return [pl.BlockSpec((PARTS // 2, height // PARTS, width), lambda i: (0, 0, i))] * 2

    def halves_shapes(height, width):
        return [((PARTS // 2, height // PARTS, width), LOW)] * 2

    d_expanded, d_projected, *halves = call(
        functools.partial(weights_kernel, 16),
        strips,
        [
            SCALARS,
            SCALARS,
            wide_cols(rows, strip),
            wide_cols(rows, strip),
            wide_cols(4, strip),
            wide_cols(2, strip),
            wide_cols(4, strip),
            wide_cols(3, strip),
            wide_cols(rows, strip),
            whole((PARTS, mid // PARTS, rows)),
            whole((PARTS, chans // PARTS, rows)),
        ],
        [wide_cols(rows, strip), wide_cols(rows, strip)] + halves_specs(mid, strip) + halves_specs(chans, strip),
        [((rows, wide), LOW), ((rows, wide), LOW)] + halves_shapes(mid, wide) + halves_shapes(chans, wide),
        (4 * rows * mid * wide, 24 << 20),
    )(
        scalars,
        valid,
        expanded,
        projected,
        stats_out,
        base_out,
        affine_out,
        sums_out,
        cot,
        hidden_turned,
        planes_turned[0],
    )
    expand_sum = Gradient(*halves[:2], CUTS, own_plain)
    proj_sum = Gradient(*halves[2:], swapped, own_swapped)
    pair = [expand_sum, proj_sum]
    for grad in pair:
        grad.send()

    grad_two, sums, first_row = call(
        functools.partial(back_two_kernel, 16, (images, tall, half_cols)),
        steps,
        [
            SCALARS,
            whole((rows, wide)),
            pl.BlockSpec((block, wide), lambda i: (i, 0)),
            wide_cols(rows, block),
            wide_cols(2, block),
            wide_cols(1, block),
            wide_cols(2, block),
        ],
        [wide_cols(rows, block), wide_cols(2, block), wide_cols(images * half_cols, block)],
        [((rows, mid), WIDE), ((2, mid), WIDE), ((images * half_cols, mid), LOW)],
        (2 * rows * mid * wide, 10 << 20),
    )(scalars, d_expanded, expand_w, grouped, sums_two, base_two, affine_two)
    below_grad = shifted(first_row, "ha", -1)
    sums = mesh_sum(sums, back_rounds[:1])
    sums, below_grad = arrive(pair, sums, below_grad)
    for grad in pair:
        grad.step()
    grads_two = mesh_sum(sums, back_rounds[1:])
    (d_projected,) = tie(d_projected)
    side_grad = call(
        side_kernel,
        1,
        [whole((rows, wide)), whole((chans, wide))],
        [whole((rows, chans))],
        [((rows, chans), WIDE)],
        (2 * rows * chans * wide, 8 << 20),
    )(d_projected, proj_w)[0]

    deep = pltpu.VMEM((images, tall + 1, half_cols, block), LOW)
    grads_two, side_grad = tie(grads_two, side_grad)
    grad_one, sums, parts_group = call(
        functools.partial(conv_back_kernel, (images, tall, half_cols)),
        steps,
        [
            SCALARS,
            SCALARS,
            SCALARS,
            wide_cols(rows, block),
            wide_cols(rows, block),
            wide_cols(images * half_cols, block),
            wide_cols(images * half_cols, block),
            wide_cols(2, block),
            wide_cols(1, block),
            wide_cols(2, block),
            wide_cols(2, block),
            wide_cols(pixels, block),
            wide_cols(images * cols, block),
            wide_cols(2, block),
            wide_cols(2, block),
            wide_cols(taps, block),
        ],
        [wide_cols(pixels, block), wide_cols(2, block), pl.BlockSpec((TAPS * TAPS, GW, block), lambda i: (0, 0, i))],
        [((pixels, mid), WIDE), ((2, mid), WIDE), ((TAPS * TAPS, GW, mid), LOW)],
        (4 * rows * mid * 9 * 256, 24 << 20),
        window_scratch(images, tall, half_cols, block) + [deep, deep],
    )(
        scalars,
        own_two,
        valid,
        grad_two,
        grouped,
        below_grad,
        below_grouped,
        sums_two,
        base_two,
        affine_two,
        grads_two,
        reduced,
        edge,
        moments_one,
        affine_one,
        group_flat,
    )
    parts_group = jnp.pad(jnp.transpose(parts_group, (1, 0, 2)), ((0, 0), (0, 16 - TAPS * TAPS), (0, 0)))
    (sums,) = arrive(pair, sums)
    sums = mesh_sum(sums, back_rounds[:1])
    (sums,) = tie(sums)
    for grad in pair:
        grad.step()
    grads_one = mesh_sum(sums, back_rounds[1:])
    grads_one, parts_group = arrive(pair, grads_one, parts_group)
    for grad in pair:
        grad.step()

    d_reduced, *halves = call(
        functools.partial(reduced_back_kernel, 16),
        steps,
        [
            SCALARS,
            SCALARS,
            wide_cols(pixels, block),
            wide_cols(pixels, block),
            wide_cols(2, block),
            wide_cols(2, block),
            wide_cols(2, block),
        ]
        + [whole((PARTS, chans // PARTS, rows))] * 4,
        [wide_cols(pixels, block)] + halves_specs(chans, block),
        [((pixels, mid), LOW)] + halves_shapes(chans, mid),
        (2 * pixels * mid * chans, 26 << 20),
    )(scalars, valid, grad_one, reduced, moments_one, affine_one, grads_one, *planes_turned)
    (d_reduced,) = arrive(pair, d_reduced)
    parts_group = [parts_group[: PARTS // 2], parts_group[PARTS // 2 :]]
    halves = [jnp.concatenate(both, axis=1) for both in zip(halves, parts_group)]
    reduce_sum = Gradient(*halves, swapped, own_swapped)
    reduce_sum.send()
    for grad in pair:
        grad.step()
    everyone = pair + [reduce_sum]

    def images_back(d_part, side_part):
        part = d_part.shape[1]
        return call(
            functools.partial(images_back_kernel, (image_rows, cols)),
            part,
            [
                pl.BlockSpec((4, None, quarter, mid), lambda i: (0, i, 0, 0)),
                whole((chans, mid)),
                pl.BlockSpec((quarter, chans), lambda i: (i, 0)),
            ],
            [pl.BlockSpec((None, image_rows * cols, chans), lambda i: (i, 0, 0))],
            [((part, image_rows * cols, chans), LOW)],
            (2 * pixels * mid * chans, 16 << 20),
            [pltpu.VMEM((image_rows * cols, image_rows * cols), LOW)],
        )(d_part, reduce_w, side_part)[0]

    grad_images = images_back(d_reduced.reshape(4, images, quarter, mid), side_grad)
    (grad_images,) = arrive(everyone, grad_images)
    for grad in everyone:
        grad.step()
    for beside in (0, 0, 1, 2):
        arrive(everyone)
        for grad in everyone:
            grad.step()
        for _ in range(beside):
            reduce_sum.step()
    arrive(pair)
    for grad in pair:
        grad.take()
    (grad_expand,), (grad_proj,) = [grad.finish(width // PARTS) for grad, width in zip(pair, (mid, chans))]
    while reduce_sum.at < 2 * len(CUTS):
        reduce_sum.step()
    grad_reduce, grad_group = reduce_sum.finish(chans // PARTS, TAPS * TAPS)
    return (
        output.reshape(cotangent.shape),
        grad_images.reshape(images_in.shape),
        grad_reduce.reshape(reduce_w.shape),
        grads_one[1],
        grads_one[0],
        grad_group.reshape(group_w.shape),
        grads_two[1],
        grads_two[0],
        grad_expand.reshape(expand_w.shape),
        sums_out[1],
        sums_out[0],
        grad_proj.reshape(proj_w.shape),
        sums_out[2],
        sums_out[0],
    )


def solution(mesh):
    split = P("ba", "ha", None, None)
    rest = (P(),) * 12
    return jax.shard_map(
        per_device,
        mesh=mesh,
        in_specs=(split,) + rest + (P("ba"), split),
        out_specs=(split, split) + rest,
        check_vma=False,
    )
```

time: 485 us -> 349 us (0.72); the launches traced: 479 us -> 349 us
  Pallas kernels: 179 us -> 101 us
  other arithmetic: 27 us -> 7.88 us
  between operations: 17.4 us -> 2.46 us
  starting transfers between devices: 91.6 us -> 83.2 us
  local copies, waits for them, and re-layouts: 42.2 us -> 33.9 us
    pallas_call x8 -> x13, Pallas kernels: 109 us -> 39.7 us  [the longest x3 10.5 us: plain_order(): pl.pallas_call(spread_kernel, grid=(cols // width,), in_specs=[pl.BlockSp...]
    unnamed x68 -> x102, local copies, waits for them, and re-layouts: 14.5 us -> 29.3 us
    concatenate x9 -> x3, local copies, waits for them, and re-layouts: 11.9 us -> 0.25 us  [take(): self.blocks = jnp.concatenate([self.blocks, self.got], axis=0)]
    ppermute x82 -> x72, starting transfers between devices: 84.2 us -> 75.4 us  [exchange(): return lax.ppermute(value, axis, [(i, i ^ mask) for i in range(peers)])]
    slice x30 -> x18, local copies, waits for them, and re-layouts: 9.23 us -> 2.17 us  [the longest x1 0.6 us: per_device(): grads_two[0]]
    div x9 -> x5, other arithmetic: 6.94 us -> 0.19 us  [the longest x3 0.12 us: merge(): (one[0] * one[1] + two[0] * two[1]) / count]
    ppermute x82 -> x72, waiting for transfers between devices: 122 us -> 120 us  [exchange(): return lax.ppermute(value, axis, [(i, i ^ mask) for i in range(peers)])]
  transfers between devices with their start and end apart: 85 -> 75, of which waited for: 46 -> 45; matrix products, arithmetic and copies ran while one was open for 11% -> 2% of each run, Pallas kernels for 18% -> 19%
where the time goes in v3:
time: 349 us
  waiting for transfers between devices  120 us (34%)
  Pallas kernels  101 us (29%)
  starting transfers between devices  83.2 us (24%)
  local copies, waits for them, and re-layouts  33.9 us (10%)
  other arithmetic  7.88 us (2%)
    ppermute x72, waiting for transfers between devices, exchange(): return lax.ppermute(value, axis, [(i, i ^ mask) for i in range(peers)])  120 us
    ppermute x72, starting transfers between devices, exchange(): return lax.ppermute(value, axis, [(i, i ^ mask) for i in range(peers)])  75.4 us
    unnamed x102, local copies, waits for them, and re-layouts  29.3 us
    pallas_call x1, Pallas kernels, per_device(): call(functools.partial(conv_back_kernel, (images, tall, half_cols)), step...  17.5 us
    pallas_call x1, Pallas kernels, per_device(): call(functools.partial(weights_kernel, 16), strips, [SCALARS, SCALARS, wi...  11.9 us
    pallas_call x3, Pallas kernels, plain_order(): pl.pallas_call(spread_kernel, grid=(cols // width,), in_specs=[pl.BlockSp...  10.5 us
    pallas_call x1, Pallas kernels, per_device(): call(functools.partial(reduced_back_kernel, 16), steps, [SCALARS, SCALARS...  9.82 us
    pallas_call x1, Pallas kernels, per_device(): call(functools.partial(reduce_kernel, (images, image_rows, cols)), steps,...  9.48 us
  transfers between devices with their start and end apart: 75, of which 45 were waited for; matrix products, arithmetic and copies ran while one was open for 2% of the time, Pallas kernels for 19%

profile of v3, /device:TPU:0, one launch (start us, length us, event | category | flops | bytes accessed | tf_op | source)
XLA Modules:
  0.0 348.6 jit_solution(9335284142189410244)
XLA Ops:
  1.7 4.9 %collective-permute-start = (bf16[8,32,1024]{2,1,0:T(8,128)(2,1)S(1)}, bf16[8,32,1024]{2,1,0:T(8,128)(2,1)S(1)}, u32[]{:S(2)}, u32[]{:S(2)}) collective-permute-start(bf16[8,32,1024]{2,1,0:T(8,128)(2,1)S(1)} %slice_bitcast_fusion), channel_id=1, source_target_pairs={{0,8},{8,16},{16,24},{1,9},{9,17},{17,25},{2,10},{10,18},{18,26},{... | collective-permute-start | bytes 1572872 | tf_op jit(solution)/shard_map/ppermute | solution.py:19
  8.9 2.2 copy-done.28
  11.1 9.5 %shard_map.254 = (bf16[2048,1024]{1,0:T(8,128)(2,1)}, f32[2048,1024]{1,0:T(8,128)}, f32[3,1024]{1,0:T(4,128)S(1)}, f32[1,1024]{1,0:T(1,128)S(1)}) custom-call(f32[8]{0:T(128)S(1)} %convert_element_type.142.valid_ref, bf16[2048,1024]{1,0:T(8,128)(2,1)S(1)} %bitcast.42, bf16[1024,1024]{1,0:T(8,128)(2,1)S(1)} %copy-done.14), custom_call_target="tpu_custom_call" | custom-call | flops 5368709120 | bytes 20971520 | tf_op jit(solution)/shard_map/pallas_call | solution.py:826
  24.3 2.5 collective-permute-start.4
  26.9 2.9 collective-permute-done.4
  35.2 2.2 copy-done
  42.9 3.4 copy-done.2
  50.0 7.3 %shard_map.259 = (f32[512,1024]{1,0:T(8,128)S(1)}, f32[2,1024]{1,0:T(2,128)S(1)}, f32[1,1024]{1,0:T(1,128)S(1)}, bf16[128,1024]{1,0:T(8,128)(2,1)S(1)}, bf16[256,1024]{1,0:T(8,128)(2,1)S(1)}) custom-call(f32[4]{0:T(128)S(1)} %pad_maximum_fusion.17.scalar_ref, f32[8]{0:T(128)S(1)} %convert_element_type.142.valid_ref, f32[2048,1024]{1,0:T(8,128)S(1)} %copy-done.2, ...), custom_call_target="tpu_custom_call" | custom-call | flops 2415919104 | bytes 14680064 | tf_op jit(solution)/shard_map/pallas_call | solution.py:853
  59.4 2.9 collective-permute-start.11
  69.5 5.5 %shard_map.260 = (f32[512,2048]{1,0:T(8,128)}, f32[3,2048]{1,0:T(4,128)S(1)}) custom-call(f32[8]{0:T(128)S(1)} %convert_element_type.142.valid_ref, bf16[2048,1024]{1,0:T(8,128)(2,1)S(1)} %copy-done.1, bf16[1024,2048]{1,0:T(8,128)(2,1)S(1)} %copy-done.3, f32[1,1024]{1,0:T(1,128)S(1)} %slice.115.sampled_ref), custom_call_target="tpu_custom_call" | custom-call | flops 2147483648 | bytes 10485760 | tf_op jit(solution)/shard_map/pallas_call | solution.py:886
  75.1 6.1 %shard_map.261 = (bf16[512,1024]{1,0:T(8,128)(2,1)S(1)}, f32[512,2048]{1,0:T(8,128)}, f32[4,2048]{1,0:T(4,128)S(1)}, f32[2,2048]{1,0:T(2,128)S(1)}) custom-call(f32[4]{0:T(128)S(1)} %pad_maximum_fusion.17.scalar_ref, f32[8]{0:T(128)S(1)} %convert_element_type.142.valid_ref, f32[512,1024]{1,0:T(8,128)S(1)} %get-tuple-element.100.grouped_ref, ...), custom_call_target="tpu_custom_call" | custom-call | flops 2147483648 | bytes 12582912 | tf_op jit(solution)/shard_map/pallas_call | solution.py:895
  84.4 2.9 collective-permute-start.19
  98.2 2.2 copy-done.5
  100.4 2.2 copy-done.6
  102.6 5.9 %shard_map.263 = (bf16[512,2048]{1,0:T(8,128)(2,1)}, f32[3,2048]{1,0:T(4,128)S(1)}) custom-call(f32[4]{0:T(128)S(1)} %pad_maximum_fusion.17.scalar_ref, f32[8]{0:T(128)S(1)} %convert_element_type.142.valid_ref, f32[512,2048]{1,0:T(8,128)S(1)} %copy-done.6, f32[512,2048]{1,0:T(8,128)S(1)} %copy-done.5, f32[4,2048]{1,0:T(4,128)S(1)} %add_add_fusion.2.stats_ref, ...), custom_call_target="tpu_custom_call" | custom-call | flops 20971520 | bytes 12582912 | tf_op jit(solution)/shard_map/pallas_call | solution.py:916
  109.8 2.6 collective-permute-start.26
  113.3 2.4 collective-permute-done.25
  122.5 11.9 %shard_map.264 = (bf16[512,2048]{1,0:T(8,128)(2,1)S(1)}, bf16[512,2048]{1,0:T(8,128)(2,1)S(1)}, bf16[16,32,2048]{2,1,0:T(8,128)(2,1)S(1)}, bf16[16,32,2048]{2,1,...) custom-call(f32[4]{0:T(128)S(1)} %pad_maximum_fusion.17.scalar_ref, ...), custom_call_target="tpu_custom_call" | custom-call | flops 4294967296 | bytes 25165824 | tf_op jit(solution)/shard_map/pallas_call | solution.py:941
  137.9 4.3 %shard_map.265 = (f32[512,1024]{1,0:T(8,128)S(1)}, f32[2,1024]{1,0:T(2,128)S(1)}, bf16[128,1024]{1,0:T(8,128)(2,1)S(1)}) custom-call(f32[4]{0:T(128)S(1)} %pad_maximum_fusion.17.scalar_ref, bf16[512,2048]{1,0:T(8,128)(2,1)S(1)} %get-tuple-element.116.d_ref, bf16[1024,2048]{1,0:T(8,128)(2,1)S(1)} %copy-done.12, f32[512,1024]{1,0:T(8,128)S(1)} %copy-done.18, ...), custom_call_target="tpu_custom_call" | custom-call | flops 2147483648 | bytes 10485760 | tf_op jit(solution)/shard_map/pallas_call | solution.py:979
  143.7 3.5 %collective-permute-start.31 = (f32[2,1024]{1,0:T(2,128)S(1)}, f32[2,1024]{1,0:T(2,128)S(1)}, u32[]{:S(2)}, u32[]{:S(2)}) collective-permute-start(f32[2,1024]{1,0:T(2,128)S(1)} %get-tuple-element.118), channel_id=1, source_target_pairs={{0,16},{8,24},{16,0},{24,8},{1,17},{9,25},{17,1},{25,9},{2,18},{10... | collective-permute-start | bytes 24584 | tf_op jit(solution)/shard_map/ppermute | solution.py:24
  148.9 5.4 %collective-permute-start.30 = (f32[2,1024]{1,0:T(2,128)S(1)}, f32[2,1024]{1,0:T(2,128)S(1)}, u32[]{:S(2)}, u32[]{:S(2)}) collective-permute-start(f32[2,1024]{1,0:T(2,128)S(1)} %get-tuple-element.118), channel_id=1, source_target_pairs={{0,8},{8,0},{16,24},{24,16},{1,9},{9,1},{17,25},{25,17},{2,10},{10... | collective-permute-start | bytes 24584 | tf_op jit(solution)/shard_map/ppermute | solution.py:24
  156.8 2.2 collective-permute-start.40
  164.8 2.4 shard_map.266.side_ref
  168.2 17.5 %shard_map.267 = (f32[2048,1024]{1,0:T(8,128)}, f32[2,1024]{1,0:T(2,128)S(1)}, bf16[9,32,1024]{2,1,0:T(8,128)(2,1)S(1)}) custom-call(f32[4]{0:T(128)S(1)} %pad_maximum_fusion.17.scalar_ref, s32[1]{0:T(128)} %bitcast.3.own_ref, f32[8]{0:T(128)S(1)} %convert_element_type.142.valid_ref, f32[512,1024]{1,0:T(8,128)S(1)} %copy-done.31, ...), custom_call_target="tpu_custom_call" | custom-call | flops 4831838208 | bytes 25165824 | tf_op jit(solution)/shard_map/pallas_call | solution.py:1013
  190.1 3.3 collective-permute-start.44
  193.5 7.1 %collective-permute-done.43 = f32[2,1024]{1,0:T(2,128)S(1)} collective-permute-done((f32[2,1024]{1,0:T(2,128)S(1)}, f32[2,1024]{1,0:T(2,128)S(1)}, u32[]{:S(2)}, u32[]{:S(2)}) %collective-permute-start.43) | collective-permute-done | bytes 8224 | tf_op jit(solution)/shard_map/ppermute | solution.py:24
  208.5 2.5 collective-permute-done.48
  213.9 9.8 %shard_map.268 = (bf16[2048,1024]{1,0:T(8,128)(2,1)}, bf16[16,32,1024]{2,1,0:T(8,128)(2,1)S(1)}, bf16[16,32,1024]{2,1,0:T(8,128)(2,1)S(1)}) custom-call(f32[4]{0:T(128)S(1)} %pad_maximum_fusion.17.scalar_ref, f32[8]{0:T(128)S(1)} %convert_element_type.142.valid_ref, f32[2048,1024]{1,0:T(8,128)} %get-tuple-element.128.grad_ref, ...), custom_call_target="tpu_custom_call" | custom-call | flops 4294967296 | bytes 27262976 | tf_op jit(solution)/shard_map/pallas_call | solution.py:1067
  225.0 2.1 collective-permute-start.54
  227.1 2.2 copy-done.29
  229.3 8.9 %shard_map.269 = bf16[8,256,1024]{2,1,0:T(8,128)(2,1)} custom-call(bf16[4,8,64,1024]{3,2,1,0:T(8,128)(2,1)S(1)} %bitcast.43, bf16[1024,1024]{1,0:T(8,128)(2,1)S(1)} %copy-done.16, f32[512,1024]{1,0:T(8,128)S(1)} %shard_map.266.side_ref), custom_call_target="tpu_custom_call" | custom-call | flops 4294967296 | bytes 16777216 | tf_op jit(solution)/shard_map/pallas_call | solution.py:1095
  241.4 2.8 collective-permute-start.57
  244.2 7.9 %collective-permute-done.56 = bf16[1,32,2048]{2,1,0:T(8,128)(2,1)S(1)} collective-permute-done((bf16[1,32,2048]{2,1,0:T(8,128)(2,1)S(1)}, bf16[1,32,2048]{2,1,0:T(8,128)(2,1)S(1)}, u32[]{:S(2)}, u32[]{:S(2)}) %collective-permute-start.56) | collective-permute-done | bytes 131104 | tf_op jit(solution)/shard_map/ppermute | solution.py:24
  252.1 2.7 collective-permute-done.57
  254.8 4.3 %collective-permute-done.58 = bf16[8,48,1024]{2,1,0:T(8,128)(2,1)S(1)} collective-permute-done((bf16[8,48,1024]{2,1,0:T(8,128)(2,1)S(1)}, bf16[8,48,1024]{2,1,0:T(8,128)(2,1)S(1)}, u32[]{:S(2)}, u32[]{:S(2)}) %collective-permute-start.58) | collective-permute-done | bytes 786464 | tf_op jit(solution)/shard_map/ppermute | solution.py:24
  262.1 6.4 %collective-permute-done.59 = bf16[2,32,2048]{2,1,0:T(8,128)(2,1)S(1)} collective-permute-done((bf16[2,32,2048]{2,1,0:T(8,128)(2,1)S(1)}, bf16[2,32,2048]{2,1,0:T(8,128)(2,1)S(1)}, u32[]{:S(2)}, u32[]{:S(2)}) %collective-permute-start.59) | collective-permute-done | bytes 262176 | tf_op jit(solution)/shard_map/ppermute | solution.py:24
  268.5 3.8 %collective-permute-done.60 = bf16[2,32,2048]{2,1,0:T(8,128)(2,1)S(1)} collective-permute-done((bf16[2,32,2048]{2,1,0:T(8,128)(2,1)S(1)}, bf16[2,32,2048]{2,1,0:T(8,128)(2,1)S(1)}, u32[]{:S(2)}, u32[]{:S(2)}) %collective-permute-start.60) | collective-permute-done | bytes 262176 | tf_op jit(solution)/shard_map/ppermute | solution.py:24
  274.7 5.4 %collective-permute-done.64 = bf16[2,48,1024]{2,1,0:T(8,128)(2,1)S(1)} collective-permute-done((bf16[2,48,1024]{2,1,0:T(8,128)(2,1)S(1)}, bf16[2,48,1024]{2,1,0:T(8,128)(2,1)S(1)}, u32[]{:S(2)}, u32[]{:S(2)}) %collective-permute-start.64) | collective-permute-done | bytes 196640 | tf_op jit(solution)/shard_map/ppermute | solution.py:24
  280.1 4.4 %collective-permute-done.62 = bf16[4,32,2048]{2,1,0:T(8,128)(2,1)S(1)} collective-permute-done((bf16[4,32,2048]{2,1,0:T(8,128)(2,1)S(1)}, bf16[4,32,2048]{2,1,0:T(8,128)(2,1)S(1)}, u32[]{:S(2)}, u32[]{:S(2)}) %collective-permute-start.62) | collective-permute-done | bytes 524320 | tf_op jit(solution)/shard_map/ppermute | solution.py:24
  288.2 7.7 %collective-permute-done.65 = bf16[1,48,1024]{2,1,0:T(8,128)(2,1)S(1)} collective-permute-done((bf16[1,48,1024]{2,1,0:T(8,128)(2,1)S(1)}, bf16[1,48,1024]{2,1,0:T(8,128)(2,1)S(1)}, u32[]{:S(2)}, u32[]{:S(2)}) %collective-permute-start.65) | collective-permute-done | bytes 98336 | tf_op jit(solution)/shard_map/ppermute | solution.py:24
  296.0 5.5 %collective-permute-done.68 = bf16[1,48,1024]{2,1,0:T(8,128)(2,1)S(1)} collective-permute-done((bf16[1,48,1024]{2,1,0:T(8,128)(2,1)S(1)}, bf16[1,48,1024]{2,1,0:T(8,128)(2,1)S(1)}, u32[]{:S(2)}, u32[]{:S(2)}) %collective-permute-start.68) | collective-permute-done | bytes 98336 | tf_op jit(solution)/shard_map/ppermute | solution.py:24
  301.4 6.8 %collective-permute-done.66 = bf16[8,32,2048]{2,1,0:T(8,128)(2,1)S(1)} collective-permute-done((bf16[8,32,2048]{2,1,0:T(8,128)(2,1)S(1)}, bf16[8,32,2048]{2,1,0:T(8,128)(2,1)S(1)}, u32[]{:S(2)}, u32[]{:S(2)}) %collective-permute-start.66) | collective-permute-done | bytes 1048608 | tf_op jit(solution)/shard_map/ppermute | solution.py:24
  309.3 4.8 %collective-permute-done.69 = bf16[2,48,1024]{2,1,0:T(8,128)(2,1)S(1)} collective-permute-done((bf16[2,48,1024]{2,1,0:T(8,128)(2,1)S(1)}, bf16[2,48,1024]{2,1,0:T(8,128)(2,1)S(1)}, u32[]{:S(2)}, u32[]{:S(2)}) %collective-permute-start.69) | collective-permute-done | bytes 196640 | tf_op jit(solution)/shard_map/ppermute | solution.py:24
  316.0 6.0 %collective-permute-done.70 = bf16[4,48,1024]{2,1,0:T(8,128)(2,1)S(1)} collective-permute-done((bf16[4,48,1024]{2,1,0:T(8,128)(2,1)S(1)}, bf16[4,48,1024]{2,1,0:T(8,128)(2,1)S(1)}, u32[]{:S(2)}, u32[]{:S(2)}) %collective-permute-start.70) | collective-permute-done | bytes 393248 | tf_op jit(solution)/shard_map/ppermute | solution.py:24
  323.7 11.8 %collective-permute-done.71 = bf16[8,48,1024]{2,1,0:T(8,128)(2,1)S(1)} collective-permute-done((bf16[8,48,1024]{2,1,0:T(8,128)(2,1)S(1)}, bf16[8,48,1024]{2,1,0:T(8,128)(2,1)S(1)}, u32[]{:S(2)}, u32[]{:S(2)}) %collective-permute-start.71) | collective-permute-done | bytes 786464 | tf_op jit(solution)/shard_map/ppermute | solution.py:24
  337.4 3.8 %shard_map.271 = f32[32,32,2048]{2,1,0:T(8,128)} custom-call(s32[1]{0:T(128)} %bitcast.13.own_ref, bf16[16,32,2048]{2,1,0:T(8,128)(2,1)S(1)} %constant_dynamic-update-slice_fusion.5.low_ref, bf16[16,32,2048]{2,1,0:T(8,128)(2,1)S(1)} %collective-permute-done.73.high_ref), custom_call_target="tpu_custom_call" | custom-call | bytes 12582912 | tf_op jit(solution)/shard_map/pallas_call | solution.py:111
  341.3 3.8 %shard_map.272 = f32[32,32,2048]{2,1,0:T(8,128)} custom-call(s32[1]{0:T(128)} %bitcast.3.own_ref, bf16[16,32,2048]{2,1,0:T(8,128)(2,1)S(1)} %constant_dynamic-update-slice_fusion.10.low_ref, bf16[16,32,2048]{2,1,0:T(8,128)(2,1)S(1)} %collective-permute-done.74.high_ref), custom_call_target="tpu_custom_call" | custom-call | bytes 12582912 | tf_op jit(solution)/shard_map/pallas_call | solution.py:111
  345.1 2.9 shard_map.270
  (304 shorter events, 104.5 us)
Async XLA Ops:
  1.7 18.8 %collective-permute-start = (bf16[8,32,1024]{2,1,0:T(8,128)(2,1)S(1)}, bf16[8,32,1024]{2,1,0:T(8,128)(2,1)S(1)}, u32[]{:S(2)}, u32[]{:S(2)}) collective-permute-start(bf16[8,32,1024]{2,1,0:T(8,128)(2,1)S(1)} %slice_bitcast_fusion), channel_id=1, source_target_pairs={{0,8},{8,16},{16,24},{1,9},{9,17},{17,25},{2,10},{10,18},{18,26},{... | collective-permute-start | bytes 1572872 | tf_op jit(solution)/shard_map/ppermute | solution.py:19
  31.6 9.2 %collective-permute-start.5 = (f32[4,1024]{1,0:T(4,128)S(1)}, f32[4,1024]{1,0:T(4,128)S(1)}, u32[]{:S(2)}, u32[]{:S(2)}) collective-permute-start(f32[4,1024]{1,0:T(4,128)S(1)} %pad_maximum_fusion.13), channel_id=1, source_target_pairs={{0,8},{8,0},{16,24},{24,16},{1,9},{9,1},{17,25},{25,17},{2,10},{10... | collective-permute-start | bytes 49160 | tf_op jit(solution)/shard_map/ppermute | solution.py:24
  33.1 7.7 %collective-permute-start.7 = (f32[4,1024]{1,0:T(4,128)S(1)}, f32[4,1024]{1,0:T(4,128)S(1)}, u32[]{:S(2)}, u32[]{:S(2)}) collective-permute-start(f32[4,1024]{1,0:T(4,128)S(1)} %pad_maximum_fusion.13), channel_id=1, source_target_pairs={{0,24},{8,16},{16,8},{24,0},{1,25},{9,17},{17,9},{25,1},{2,26},{10... | collective-permute-start | bytes 49160 | tf_op jit(solution)/shard_map/ppermute | solution.py:24
  34.6 6.2 %collective-permute-start.6 = (f32[4,1024]{1,0:T(4,128)S(1)}, f32[4,1024]{1,0:T(4,128)S(1)}, u32[]{:S(2)}, u32[]{:S(2)}) collective-permute-start(f32[4,1024]{1,0:T(4,128)S(1)} %pad_maximum_fusion.13), channel_id=1, source_target_pairs={{0,16},{8,24},{16,0},{24,8},{1,17},{9,25},{17,1},{25,9},{2,18},{10... | collective-permute-start | bytes 49160 | tf_op jit(solution)/shard_map/ppermute | solution.py:24
  62.7 12.3 %collective-permute-start.15 = (bf16[128,1024]{1,0:T(8,128)(2,1)}, bf16[128,1024]{1,0:T(8,128)(2,1)S(1)}, u32[]{:S(2)}, u32[]{:S(2)}) collective-permute-start(bf16[128,1024]{1,0:T(8,128)(2,1)} %copy-done.36), channel_id=1, source_target_pairs={{8,0},{16,8},{24,16},{9,1},{17,9},{25,17},{10,2},{18,10},{26,18},{... | collective-permute-start | bytes 786440 | tf_op jit(solution)/shard_map/ppermute | solution.py:19
  66.0 9.0 %collective-permute-start.13 = (f32[2,1024]{1,0:T(2,128)S(1)}, f32[2,1024]{1,0:T(2,128)S(1)}, u32[]{:S(2)}, u32[]{:S(2)}) collective-permute-start(f32[2,1024]{1,0:T(2,128)S(1)} %add_add_fusion.9), channel_id=1, source_target_pairs={{0,16},{8,24},{16,0},{24,8},{1,17},{9,25},{17,1},{25,9},{2,18},{10... | collective-permute-start | bytes 24584 | tf_op jit(solution)/shard_map/ppermute | solution.py:24
  67.8 7.2 %collective-permute-start.14 = (f32[2,1024]{1,0:T(2,128)S(1)}, f32[2,1024]{1,0:T(2,128)S(1)}, u32[]{:S(2)}, u32[]{:S(2)}) collective-permute-start(f32[2,1024]{1,0:T(2,128)S(1)} %add_add_fusion.9), channel_id=1, source_target_pairs={{0,24},{8,16},{16,8},{24,0},{1,25},{9,17},{17,9},{25,1},{2,26},{10... | collective-permute-start | bytes 24584 | tf_op jit(solution)/shard_map/ppermute | solution.py:24
  69.0 6.1 %collective-permute-start.12 = (f32[2,1024]{1,0:T(2,128)S(1)}, f32[2,1024]{1,0:T(2,128)S(1)}, u32[]{:S(2)}, u32[]{:S(2)}) collective-permute-start(f32[2,1024]{1,0:T(2,128)S(1)} %add_add_fusion.9), channel_id=1, source_target_pairs={{0,8},{8,0},{16,24},{24,16},{1,9},{9,1},{17,25},{25,17},{2,10},{10... | collective-permute-start | bytes 24584 | tf_op jit(solution)/shard_map/ppermute | solution.py:24
  83.5 6.0 %collective-permute-start.18 = (f32[4,2048]{1,0:T(4,128)S(1)}, f32[4,2048]{1,0:T(4,128)S(1)}, u32[]{:S(2)}, u32[]{:S(2)}) collective-permute-start(f32[4,2048]{1,0:T(4,128)S(1)} %add.437), channel_id=1, source_target_pairs={{0,4},{1,5},{2,6},{3,7},{4,0},{5,1},{6,2},{7,3},{8,12},{9,13},{10,... | collective-permute-start | bytes 98312 | tf_op jit(solution)/shard_map/ppermute | solution.py:24
  84.4 5.8 %collective-permute-start.19 = (f32[4,2048]{1,0:T(4,128)S(1)}, f32[4,2048]{1,0:T(4,128)S(1)}, u32[]{:S(2)}, u32[]{:S(2)}) collective-permute-start(f32[4,2048]{1,0:T(4,128)S(1)} %add.437), channel_id=1, source_target_pairs={{0,6},{1,7},{2,4},{3,5},{4,2},{5,3},{6,0},{7,1},{8,14},{9,15},{10,... | collective-permute-start | bytes 98312 | tf_op jit(solution)/shard_map/ppermute | solution.py:24
  109.7 5.9 %collective-permute-start.25 = (f32[3,2048]{1,0:T(4,128)S(1)}, f32[3,2048]{1,0:T(4,128)S(1)}, u32[]{:S(2)}, u32[]{:S(2)}) collective-permute-start(f32[3,2048]{1,0:T(4,128)S(1)} %add.448), channel_id=1, source_target_pairs={{0,4},{1,5},{2,6},{3,7},{4,0},{5,1},{6,2},{7,3},{8,12},{9,13},{10,... | collective-permute-start | bytes 73736 | tf_op jit(solution)/shard_map/ppermute | solution.py:24
  109.8 6.1 %collective-permute-start.26 = (f32[3,2048]{1,0:T(4,128)S(1)}, f32[3,2048]{1,0:T(4,128)S(1)}, u32[]{:S(2)}, u32[]{:S(2)}) collective-permute-start(f32[3,2048]{1,0:T(4,128)S(1)} %add.448), channel_id=1, source_target_pairs={{0,6},{1,7},{2,4},{3,5},{4,2},{5,3},{6,0},{7,1},{8,14},{9,15},{10,... | collective-permute-start | bytes 73736 | tf_op jit(solution)/shard_map/ppermute | solution.py:24
  135.8 20.2 %collective-permute-start.34 = (bf16[16,32,2048]{2,1,0:T(8,128)(2,1)}, bf16[16,32,2048]{2,1,0:T(8,128)(2,1)S(1)}, u32[]{:S(2)}, u32[]{:S(2)}) collective-permute-start(bf16[16,32,2048]{2,1,0:T(8,128)(2,1)} %get-tuple-element.120), channel_id=1, source_target_pairs={{0,1},{1,0},{2,3},{3,2},{4,5},{5,4},{6,7},{7,6},{8,9},{9,8},{10,11... | collective-permute-start | bytes 6291464 | tf_op jit(solution)/shard_map/ppermute | solution.py:24
  135.8 20.2 %collective-permute-start.35 = (bf16[16,32,2048]{2,1,0:T(8,128)(2,1)}, bf16[16,32,2048]{2,1,0:T(8,128)(2,1)S(1)}, u32[]{:S(2)}, u32[]{:S(2)}) collective-permute-start(bf16[16,32,2048]{2,1,0:T(8,128)(2,1)} %get-tuple-element.121), channel_id=1, source_target_pairs={{0,1},{1,0},{2,3},{3,2},{4,5},{5,4},{6,7},{7,6},{8,9},{9,8},{10,11... | collective-permute-start | bytes 6291464 | tf_op jit(solution)/shard_map/ppermute | solution.py:24
  142.2 13.8 %collective-permute-start.33 = (bf16[128,1024]{1,0:T(8,128)(2,1)S(1)}, bf16[128,1024]{1,0:T(8,128)(2,1)S(1)}, u32[]{:S(2)}, u32[]{:S(2)}) collective-permute-start(bf16[128,1024]{1,0:T(8,128)(2,1)S(1)} %get-tuple-element.119), channel_id=1, source_target_pairs={{8,0},{16,8},{24,16},{9,1},{17,9},{25,17},{10,2},{18,10},{26,18},{... | collective-permute-start | bytes 786440 | tf_op jit(solution)/shard_map/ppermute | solution.py:19
  147.2 7.1 %collective-permute-start.32 = (f32[2,1024]{1,0:T(2,128)S(1)}, f32[2,1024]{1,0:T(2,128)S(1)}, u32[]{:S(2)}, u32[]{:S(2)}) collective-permute-start(f32[2,1024]{1,0:T(2,128)S(1)} %get-tuple-element.118), channel_id=1, source_target_pairs={{0,24},{8,16},{16,8},{24,0},{1,25},{9,17},{17,9},{25,1},{2,26},{10... | collective-permute-start | bytes 24584 | tf_op jit(solution)/shard_map/ppermute | solution.py:24
  148.9 7.1 %collective-permute-start.30 = (f32[2,1024]{1,0:T(2,128)S(1)}, f32[2,1024]{1,0:T(2,128)S(1)}, u32[]{:S(2)}, u32[]{:S(2)}) collective-permute-start(f32[2,1024]{1,0:T(2,128)S(1)} %get-tuple-element.118), channel_id=1, source_target_pairs={{0,8},{8,0},{16,24},{24,16},{1,9},{9,1},{17,25},{25,17},{2,10},{10... | collective-permute-start | bytes 24584 | tf_op jit(solution)/shard_map/ppermute | solution.py:24
  156.8 28.9 %collective-permute-start.40 = (bf16[8,32,2048]{2,1,0:T(8,128)(2,1)S(1)}, bf16[8,32,2048]{2,1,0:T(8,128)(2,1)}, u32[]{:S(2)}, u32[]{:S(2)}) collective-permute-start(bf16[8,32,2048]{2,1,0:T(8,128)(2,1)S(1)} %slice.149), channel_id=1, source_target_pairs={{0,8},{8,0},{16,24},{24,16},{1,9},{9,1},{17,25},{25,17},{2,10},{10... | collective-permute-start | bytes 3145736 | tf_op jit(solution)/shard_map/ppermute | solution.py:24
  159.9 25.9 %collective-permute-start.41 = (bf16[8,32,2048]{2,1,0:T(8,128)(2,1)S(1)}, bf16[8,32,2048]{2,1,0:T(8,128)(2,1)S(1)}, u32[]{:S(2)}, u32[]{:S(2)}) collective-permute-start(bf16[8,32,2048]{2,1,0:T(8,128)(2,1)S(1)} %slice.150), channel_id=1, source_target_pairs={{0,16},{8,24},{16,0},{24,8},{1,17},{9,25},{17,1},{25,9},{2,18},{10... | collective-permute-start | bytes 3145736 | tf_op jit(solution)/shard_map/ppermute | solution.py:24
  161.3 5.9 %collective-permute-start.38 = (f32[2,1024]{1,0:T(2,128)S(1)}, f32[2,1024]{1,0:T(2,128)S(1)}, u32[]{:S(2)}, u32[]{:S(2)}) collective-permute-start(f32[2,1024]{1,0:T(2,128)S(1)} %add.458), channel_id=1, source_target_pairs={{0,4},{1,5},{2,6},{3,7},{4,0},{5,1},{6,2},{7,3},{8,12},{9,13},{10,... | collective-permute-start | bytes 24584 | tf_op jit(solution)/shard_map/ppermute | solution.py:24
  187.4 23.8 %collective-permute-start.49 = (bf16[4,32,2048]{2,1,0:T(8,128)(2,1)S(1)}, bf16[4,32,2048]{2,1,0:T(8,128)(2,1)S(1)}, u32[]{:S(2)}, u32[]{:S(2)}) collective-permute-start(bf16[4,32,2048]{2,1,0:T(8,128)(2,1)S(1)} %slice.152), channel_id=1, source_target_pairs={{0,16},{8,24},{16,0},{24,8},{1,17},{9,25},{17,1},{25,9},{2,18},{10... | collective-permute-start | bytes 1572872 | tf_op jit(solution)/shard_map/ppermute | solution.py:24
  189.9 21.4 %collective-permute-start.50 = (bf16[4,32,2048]{2,1,0:T(8,128)(2,1)S(1)}, bf16[4,32,2048]{2,1,0:T(8,128)(2,1)S(1)}, u32[]{:S(2)}, u32[]{:S(2)}) collective-permute-start(bf16[4,32,2048]{2,1,0:T(8,128)(2,1)S(1)} %slice.154), channel_id=1, source_target_pairs={{0,8},{8,0},{16,24},{24,16},{1,9},{9,1},{17,25},{25,17},{2,10},{10... | collective-permute-start | bytes 1572872 | tf_op jit(solution)/shard_map/ppermute | solution.py:24
  190.0 10.7 %collective-permute-start.43 = (f32[2,1024]{1,0:T(2,128)S(1)}, f32[2,1024]{1,0:T(2,128)S(1)}, u32[]{:S(2)}, u32[]{:S(2)}) collective-permute-start(f32[2,1024]{1,0:T(2,128)S(1)} %get-tuple-element.134), channel_id=1, source_target_pairs={{0,16},{8,24},{16,0},{24,8},{1,17},{9,25},{17,1},{25,9},{2,18},{10... | collective-permute-start | bytes 24584 | tf_op jit(solution)/shard_map/ppermute | solution.py:24
  190.1 12.2 %collective-permute-start.44 = (f32[2,1024]{1,0:T(2,128)S(1)}, f32[2,1024]{1,0:T(2,128)S(1)}, u32[]{:S(2)}, u32[]{:S(2)}) collective-permute-start(f32[2,1024]{1,0:T(2,128)S(1)} %get-tuple-element.134), channel_id=1, source_target_pairs={{0,24},{8,16},{16,8},{24,0},{1,25},{9,17},{17,9},{25,1},{2,26},{10... | collective-permute-start | bytes 24584 | tf_op jit(solution)/shard_map/ppermute | solution.py:24
  193.4 9.3 %collective-permute-start.42 = (f32[2,1024]{1,0:T(2,128)S(1)}, f32[2,1024]{1,0:T(2,128)S(1)}, u32[]{:S(2)}, u32[]{:S(2)}) collective-permute-start(f32[2,1024]{1,0:T(2,128)S(1)} %get-tuple-element.134), channel_id=1, source_target_pairs={{0,8},{8,0},{16,24},{24,16},{1,9},{9,1},{17,25},{25,17},{2,10},{10... | collective-permute-start | bytes 24584 | tf_op jit(solution)/shard_map/ppermute | solution.py:24
  211.4 12.4 %collective-permute-start.51 = (bf16[2,32,2048]{2,1,0:T(8,128)(2,1)S(1)}, bf16[2,32,2048]{2,1,0:T(8,128)(2,1)S(1)}, u32[]{:S(2)}, u32[]{:S(2)}) collective-permute-start(bf16[2,32,2048]{2,1,0:T(8,128)(2,1)S(1)} %slice.156), channel_id=1, source_target_pairs={{0,2},{1,3},{2,0},{3,1},{4,6},{5,7},{6,4},{7,5},{8,10},{9,11},{10,... | collective-permute-start | bytes 786440 | tf_op jit(solution)/shard_map/ppermute | solution.py:24
  211.7 12.1 %collective-permute-start.52 = (bf16[2,32,2048]{2,1,0:T(8,128)(2,1)S(1)}, bf16[2,32,2048]{2,1,0:T(8,128)(2,1)S(1)}, u32[]{:S(2)}, u32[]{:S(2)}) collective-permute-start(bf16[2,32,2048]{2,1,0:T(8,128)(2,1)S(1)} %slice.158), channel_id=1, source_target_pairs={{0,2},{1,3},{2,0},{3,1},{4,6},{5,7},{6,4},{7,5},{8,10},{9,11},{10,... | collective-permute-start | bytes 786440 | tf_op jit(solution)/shard_map/ppermute | solution.py:24
  223.8 15.0 %collective-permute-start.55 = (bf16[16,48,1024]{2,1,0:T(8,128)(2,1)S(1)}, bf16[16,48,1024]{2,1,0:T(8,128)(2,1)S(1)}, u32[]{:S(2)}, u32[]{:S(2)}) collective-permute-start(bf16[16,48,1024]{2,1,0:T(8,128)(2,1)S(1)} %pad_maximum_fusion), channel_id=1, source_target_pairs={{0,1},{1,0},{2,3},{3,2},{4,5},{5,4},{6,7},{7,6},{8,9},{9,8},{10,11... | collective-permute-start | bytes 4718600 | tf_op jit(solution)/shard_map/ppermute | solution.py:24
  224.0 14.2 %collective-permute-start.53 = (bf16[1,32,2048]{2,1,0:T(8,128)(2,1)S(1)}, bf16[1,32,2048]{2,1,0:T(8,128)(2,1)S(1)}, u32[]{:S(2)}, u32[]{:S(2)}) collective-permute-start(bf16[1,32,2048]{2,1,0:T(8,128)(2,1)S(1)} %slice.160), channel_id=1, source_target_pairs={{0,4},{1,5},{2,6},{3,7},{4,0},{5,1},{6,2},{7,3},{8,12},{9,13},{10,... | collective-permute-start | bytes 393224 | tf_op jit(solution)/shard_map/ppermute | solution.py:24
  225.0 13.8 %collective-permute-start.54 = (bf16[1,32,2048]{2,1,0:T(8,128)(2,1)S(1)}, bf16[1,32,2048]{2,1,0:T(8,128)(2,1)S(1)}, u32[]{:S(2)}, u32[]{:S(2)}) collective-permute-start(bf16[1,32,2048]{2,1,0:T(8,128)(2,1)S(1)} %slice.162), channel_id=1, source_target_pairs={{0,4},{1,5},{2,6},{3,7},{4,0},{5,1},{6,2},{7,3},{8,12},{9,13},{10,... | collective-permute-start | bytes 393224 | tf_op jit(solution)/shard_map/ppermute | solution.py:24
  239.6 19.6 %collective-permute-start.58 = (bf16[8,48,1024]{2,1,0:T(8,128)(2,1)S(1)}, bf16[8,48,1024]{2,1,0:T(8,128)(2,1)S(1)}, u32[]{:S(2)}, u32[]{:S(2)}) collective-permute-start(bf16[8,48,1024]{2,1,0:T(8,128)(2,1)S(1)} %slice.166), channel_id=1, source_target_pairs={{0,16},{8,24},{16,0},{24,8},{1,17},{9,25},{17,1},{25,9},{2,18},{10... | collective-permute-start | bytes 2359304 | tf_op jit(solution)/shard_map/ppermute | solution.py:24
  241.1 11.0 %collective-permute-start.56 = (bf16[1,32,2048]{2,1,0:T(8,128)(2,1)S(1)}, bf16[1,32,2048]{2,1,0:T(8,128)(2,1)S(1)}, u32[]{:S(2)}, u32[]{:S(2)}) collective-permute-start(bf16[1,32,2048]{2,1,0:T(8,128)(2,1)S(1)} %get-tuple-element.175), channel_id=1, source_target_pairs={{0,4},{1,5},{2,6},{3,7},{4,0},{5,1},{6,2},{7,3},{8,12},{9,13},{10,... | collective-permute-start | bytes 393224 | tf_op jit(solution)/shard_map/ppermute | solution.py:24
  241.4 13.4 %collective-permute-start.57 = (bf16[1,32,2048]{2,1,0:T(8,128)(2,1)S(1)}, bf16[1,32,2048]{2,1,0:T(8,128)(2,1)S(1)}, u32[]{:S(2)}, u32[]{:S(2)}) collective-permute-start(bf16[1,32,2048]{2,1,0:T(8,128)(2,1)S(1)} %get-tuple-element.173), channel_id=1, source_target_pairs={{0,4},{1,5},{2,6},{3,7},{4,0},{5,1},{6,2},{7,3},{8,12},{9,13},{10,... | collective-permute-start | bytes 393224 | tf_op jit(solution)/shard_map/ppermute | solution.py:24
  259.2 9.3 %collective-permute-start.59 = (bf16[2,32,2048]{2,1,0:T(8,128)(2,1)S(1)}, bf16[2,32,2048]{2,1,0:T(8,128)(2,1)S(1)}, u32[]{:S(2)}, u32[]{:S(2)}) collective-permute-start(bf16[2,32,2048]{2,1,0:T(8,128)(2,1)S(1)} %pad_maximum_fusion.7), channel_id=1, source_target_pairs={{0,2},{1,3},{2,0},{3,1},{4,6},{5,7},{6,4},{7,5},{8,10},{9,11},{10,... | collective-permute-start | bytes 786440 | tf_op jit(solution)/shard_map/ppermute | solution.py:24
  259.6 12.7 %collective-permute-start.61 = (bf16[4,48,1024]{2,1,0:T(8,128)(2,1)S(1)}, bf16[4,48,1024]{2,1,0:T(8,128)(2,1)S(1)}, u32[]{:S(2)}, u32[]{:S(2)}) collective-permute-start(bf16[4,48,1024]{2,1,0:T(8,128)(2,1)S(1)} %slice.168), channel_id=1, source_target_pairs={{0,8},{8,0},{16,24},{24,16},{1,9},{9,1},{17,25},{25,17},{2,10},{10... | collective-permute-start | bytes 1179656 | tf_op jit(solution)/shard_map/ppermute | solution.py:24
  260.0 12.3 %collective-permute-start.60 = (bf16[2,32,2048]{2,1,0:T(8,128)(2,1)S(1)}, bf16[2,32,2048]{2,1,0:T(8,128)(2,1)S(1)}, u32[]{:S(2)}, u32[]{:S(2)}) collective-permute-start(bf16[2,32,2048]{2,1,0:T(8,128)(2,1)S(1)} %pad_maximum_fusion.8), channel_id=1, source_target_pairs={{0,2},{1,3},{2,0},{3,1},{4,6},{5,7},{6,4},{7,5},{8,10},{9,11},{10,... | collective-permute-start | bytes 786440 | tf_op jit(solution)/shard_map/ppermute | solution.py:24
  272.4 12.2 %collective-permute-start.62 = (bf16[4,32,2048]{2,1,0:T(8,128)(2,1)S(1)}, bf16[4,32,2048]{2,1,0:T(8,128)(2,1)S(1)}, u32[]{:S(2)}, u32[]{:S(2)}) collective-permute-start(bf16[4,32,2048]{2,1,0:T(8,128)(2,1)S(1)} %pad_maximum_fusion.4), channel_id=1, source_target_pairs={{0,16},{8,24},{16,0},{24,8},{1,17},{9,25},{17,1},{25,9},{2,18},{10... | collective-permute-start | bytes 1572872 | tf_op jit(solution)/shard_map/ppermute | solution.py:24
  273.9 12.0 %collective-permute-start.63 = (bf16[4,32,2048]{2,1,0:T(8,128)(2,1)S(1)}, bf16[4,32,2048]{2,1,0:T(8,128)(2,1)S(1)}, u32[]{:S(2)}, u32[]{:S(2)}) collective-permute-start(bf16[4,32,2048]{2,1,0:T(8,128)(2,1)S(1)} %pad_maximum_fusion.5), channel_id=1, source_target_pairs={{0,8},{8,0},{16,24},{24,16},{1,9},{9,1},{17,25},{25,17},{2,10},{10... | collective-permute-start | bytes 1572872 | tf_op jit(solution)/shard_map/ppermute | solution.py:24
  274.4 5.7 %collective-permute-start.64 = (bf16[2,48,1024]{2,1,0:T(8,128)(2,1)S(1)}, bf16[2,48,1024]{2,1,0:T(8,128)(2,1)S(1)}, u32[]{:S(2)}, u32[]{:S(2)}) collective-permute-start(bf16[2,48,1024]{2,1,0:T(8,128)(2,1)S(1)} %slice.170), channel_id=1, source_target_pairs={{0,2},{1,3},{2,0},{3,1},{4,6},{5,7},{6,4},{7,5},{8,10},{9,11},{10,... | collective-permute-start | bytes 589832 | tf_op jit(solution)/shard_map/ppermute | solution.py:24
  286.0 22.3 %collective-permute-start.66 = (bf16[8,32,2048]{2,1,0:T(8,128)(2,1)S(1)}, bf16[8,32,2048]{2,1,0:T(8,128)(2,1)S(1)}, u32[]{:S(2)}, u32[]{:S(2)}) collective-permute-start(bf16[8,32,2048]{2,1,0:T(8,128)(2,1)S(1)} %pad_maximum_fusion.1), channel_id=1, source_target_pairs={{0,8},{8,0},{16,24},{24,16},{1,9},{9,1},{17,25},{25,17},{2,10},{10... | collective-permute-start | bytes 3145736 | tf_op jit(solution)/shard_map/ppermute | solution.py:24
  286.4 21.9 %collective-permute-start.67 = (bf16[8,32,2048]{2,1,0:T(8,128)(2,1)S(1)}, bf16[8,32,2048]{2,1,0:T(8,128)(2,1)S(1)}, u32[]{:S(2)}, u32[]{:S(2)}) collective-permute-start(bf16[8,32,2048]{2,1,0:T(8,128)(2,1)S(1)} %pad_maximum_fusion.2), channel_id=1, source_target_pairs={{0,16},{8,24},{16,0},{24,8},{1,17},{9,25},{17,1},{25,9},{2,18},{10... | collective-permute-start | bytes 3145736 | tf_op jit(solution)/shard_map/ppermute | solution.py:24
  287.2 8.6 %collective-permute-start.65 = (bf16[1,48,1024]{2,1,0:T(8,128)(2,1)S(1)}, bf16[1,48,1024]{2,1,0:T(8,128)(2,1)S(1)}, u32[]{:S(2)}, u32[]{:S(2)}) collective-permute-start(bf16[1,48,1024]{2,1,0:T(8,128)(2,1)S(1)} %slice.172), channel_id=1, source_target_pairs={{0,4},{1,5},{2,6},{3,7},{4,0},{5,1},{6,2},{7,3},{8,12},{9,13},{10,... | collective-permute-start | bytes 294920 | tf_op jit(solution)/shard_map/ppermute | solution.py:24
  308.4 5.7 %collective-permute-start.69 = (bf16[2,48,1024]{2,1,0:T(8,128)(2,1)S(1)}, bf16[2,48,1024]{2,1,0:T(8,128)(2,1)S(1)}, u32[]{:S(2)}, u32[]{:S(2)}) collective-permute-start(bf16[2,48,1024]{2,1,0:T(8,128)(2,1)S(1)} %pad_maximum_fusion.9), channel_id=1, source_target_pairs={{0,2},{1,3},{2,0},{3,1},{4,6},{5,7},{6,4},{7,5},{8,10},{9,11},{10,... | collective-permute-start | bytes 589832 | tf_op jit(solution)/shard_map/ppermute | solution.py:24
  314.2 7.8 %collective-permute-start.70 = (bf16[4,48,1024]{2,1,0:T(8,128)(2,1)S(1)}, bf16[4,48,1024]{2,1,0:T(8,128)(2,1)S(1)}, u32[]{:S(2)}, u32[]{:S(2)}) collective-permute-start(bf16[4,48,1024]{2,1,0:T(8,128)(2,1)S(1)} %pad_maximum_fusion.6), channel_id=1, source_target_pairs={{0,8},{8,0},{16,24},{24,16},{1,9},{9,1},{17,25},{25,17},{2,10},{10... | collective-permute-start | bytes 1179656 | tf_op jit(solution)/shard_map/ppermute | solution.py:24
  322.1 13.4 %collective-permute-start.71 = (bf16[8,48,1024]{2,1,0:T(8,128)(2,1)S(1)}, bf16[8,48,1024]{2,1,0:T(8,128)(2,1)S(1)}, u32[]{:S(2)}, u32[]{:S(2)}) collective-permute-start(bf16[8,48,1024]{2,1,0:T(8,128)(2,1)S(1)} %pad_maximum_fusion.3), channel_id=1, source_target_pairs={{0,16},{8,24},{16,0},{24,8},{1,17},{9,25},{17,1},{25,9},{2,18},{10... | collective-permute-start | bytes 2359304 | tf_op jit(solution)/shard_map/ppermute | solution.py:24
  322.9 14.6 %collective-permute-start.73 = (bf16[16,32,2048]{2,1,0:T(8,128)(2,1)S(1)}, bf16[16,32,2048]{2,1,0:T(8,128)(2,1)S(1)}, u32[]{:S(2)}, u32[]{:S(2)}) collective-permute-start(bf16[16,32,2048]{2,1,0:T(8,128)(2,1)S(1)} %constant_dynamic-update-slice_fusion.5.low_ref), channel_id=1, source_target_pairs={{0,1},{1,0},{2,3},{3,2},{4,5},{5,4},{6,7},{7,6},{8,9},{9,8},{10,11... | collective-permute-start | bytes 6291464 | tf_op jit(solution)/shard_map/ppermute | solution.py:24
  323.1 14.4 %collective-permute-start.74 = (bf16[16,32,2048]{2,1,0:T(8,128)(2,1)S(1)}, bf16[16,32,2048]{2,1,0:T(8,128)(2,1)S(1)}, u32[]{:S(2)}, u32[]{:S(2)}) collective-permute-start(bf16[16,32,2048]{2,1,0:T(8,128)(2,1)S(1)} %constant_dynamic-update-slice_fusion.10.low_ref), channel_id=1, source_target_pairs={{0,1},{1,0},{2,3},{3,2},{4,5},{5,4},{6,7},{7,6},{8,9},{9,8},{10,11... | collective-permute-start | bytes 6291464 | tf_op jit(solution)/shard_map/ppermute | solution.py:24
  335.5 9.5 %collective-permute-start.72 = (bf16[16,48,1024]{2,1,0:T(8,128)(2,1)S(1)}, bf16[16,48,1024]{2,1,0:T(8,128)(2,1)S(1)}, u32[]{:S(2)}, u32[]{:S(2)}) collective-permute-start(bf16[16,48,1024]{2,1,0:T(8,128)(2,1)S(1)} %constant_dynamic-update-slice_fusion.low_ref), channel_id=1, source_target_pairs={{0,1},{1,0},{2,3},{3,2},{4,5},{5,4},{6,7},{7,6},{8,9},{9,8},{10,11... | collective-permute-start | bytes 4718600 | tf_op jit(solution)/shard_map/ppermute | solution.py:24
  (73 other events, 493.6 us)

commit v4 on v3

--- a/solution.py
+++ b/solution.py
@@ -77,16 +77,24 @@
     return packed
 
 
-CUTS = (("ba", 1), ("ha", 1), ("ha", 2), ("ba", 2), ("ba", 4))
 PARTS = 32
-
-
-def own_part(cuts):
+SPREAD = 8
+CORE, SIDE_ONE, SIDE_TWO, DEEP_ONE, DEEP_TWO = ("ba", 1), ("ha", 1), ("ha", 2), ("ba", 2), ("ba", 4)
+
+
+def own_part(rounds):
     index = jnp.int32(0)
-    for axis, mask in cuts:
+    for axis, mask in [bit for bits in rounds for bit in bits]:
         bit = jnp.bitwise_and(lax.axis_index(axis), mask) // mask
         index = index * 2 + bit.astype(jnp.int32)
     return index
+
+
+def partners(bits):
+    masks = [0]
+    for _, mask in bits:
+        masks = [old ^ new for old in masks for new in (0, mask)]
+    return [(bits[0][0], mask) for mask in masks[1:]]
 
 
 def spread_kernel(own_ref, low_ref, high_ref, *out_refs):
@@ -119,8 +127,11 @@
     )(own.reshape(1), low, high)
 
 
-def add_low(one, two):
-    return (one.astype(jnp.float32) + two.astype(jnp.float32)).astype(jnp.bfloat16)
+def add_low(parts):
+    total = parts[0].astype(jnp.float32)
+    for part in parts[1:]:
+        total = total + part.astype(jnp.float32)
+    return total.astype(jnp.bfloat16)
 
 
 def tie(*values):
@@ -128,53 +139,74 @@
 
 
 class Gradient:
-    def __init__(self, low, high, cuts, own):
-        self.low, self.high, self.cuts, self.own = low, high, cuts, own
-        self.blocks = None
+    def __init__(self, pieces, rounds, joins=None):
+        self.pieces, self.rounds, self.own = list(pieces), rounds, own_part(rounds)
+        self.joins = tuple(reversed(joins or rounds))
         self.at = 0
         self.got = None
 
+    def left(self):
+        return len(self.rounds) + len(self.joins) - self.at
+
     def send(self):
-        count = len(self.cuts)
+        count = len(self.rounds)
         if self.at < count:
-            self.got = exchange(self.high, *self.cuts[self.at])
+            pairs = zip(self.pieces[1:], partners(self.rounds[self.at]))
         else:
-            self.got = exchange(self.blocks, *self.cuts[2 * count - 1 - self.at])
+            pairs = [(self.pieces[0], peer) for peer in partners(self.joins[self.at - count])]
+        self.got = [exchange(piece, *peer) for piece, peer in pairs]
 
     def take(self):
-        count = len(self.cuts)
-        if self.at < count:
-            blocks = add_low(self.low, self.got)
-            half = blocks.shape[0] // 2
-            if half:
-                self.low, self.high = blocks[:half], blocks[half:]
-            else:
-                spare = 8
-                while spare < lax.axis_size("ba"):
-                    blocks = add_low(blocks, exchange(blocks, "ba", spare))
-                    spare *= 2
-                self.blocks = blocks
-        else:
-            if self.at == 2 * count - 1:
-                self.low, self.high = self.blocks, self.got
-            else:
-                self.blocks = jnp.concatenate([self.blocks, self.got], axis=0)
+        count = len(self.rounds)
+        parts = [self.pieces[0]] + self.got
         self.got = None
         self.at += 1
+        if self.at < count:
+            blocks = add_low(parts)
+            pieces = 1 << len(self.rounds[self.at])
+            size = blocks.shape[0] // pieces
+            self.pieces = [blocks[at * size : (at + 1) * size] for at in range(pieces)]
+        elif self.at == count:
+            part = add_low(parts)
+            mask = SPREAD
+            while mask < lax.axis_size("ba"):
+                part = add_low([part, exchange(part, "ba", mask)])
+                mask *= 2
+            self.pieces = [part]
+        elif self.left():
+            self.pieces = [jnp.concatenate(parts, axis=0)]
+        else:
+            self.pieces = parts
 
     def step(self):
         self.take()
-        if self.at < 2 * len(self.cuts):
+        if self.left():
             self.send()
 
     def finish(self, rows, more=0):
-        return plain_order(self.low, self.high, self.own, rows, more)
+        return plain_order(*self.pieces, self.own, rows, more)
+
+
+def join(grads):
+    both = Gradient.__new__(Gradient)
+    both.rounds, both.joins, both.at, both.got = grads[0].rounds, grads[0].joins, grads[0].at, None
+    both.pieces = [jnp.concatenate(pieces, axis=1) for pieces in zip(*[grad.pieces for grad in grads])]
+    return both
+
+
+def part_again(both, grads):
+    rows = both.pieces[0].shape[1] // len(grads)
+    for at, grad in enumerate(grads):
+        grad.at, grad.got = both.at, None
+        grad.pieces = [piece[:, at * rows : (at + 1) * rows] for piece in both.pieces]
 
 
 def arrive(grads, *values):
-    held = tie(*values, *[grad.got for grad in grads])
-    for grad, got in zip(grads, held[len(values) :]):
-        grad.got = got
+    flat = [got for grad in grads for got in grad.got]
+    held = list(tie(*values, *flat))
+    rest = held[len(values) :]
+    for grad in grads:
+        grad.got, rest = rest[: len(grad.got)], rest[len(grad.got) :]
     return held[: len(values)]
 
 
@@ -200,8 +232,14 @@
     return lax.broadcasted_iota(jnp.int32, shape, axis)
 
 
-def logistic(values):
-    return 0.5 * jnp.tanh(0.5 * values) + 0.5
+def silu(half):
+    return half * jnp.tanh(half) + half
+
+
+def silu_pair(half):
+    gate = jnp.tanh(half)
+    value = half * gate + half
+    return value, (1.0 + gate) + value * (1.0 - gate)
 
 
 def fold(values):
@@ -217,29 +255,28 @@
     return [slice(at, at + size) for at in range(0, rows, size)]
 
 
+def over(values, size):
+    assert size & (size - 1) == 0
+    return jnp.right_shift(values, size.bit_length() - 1), jnp.bitwise_and(values, size - 1)
+
+
 def parity_order(image_rows, cols, axis=0):
     pixels = image_rows * cols
-    quarter = pixels // 4
     half_cols = cols // 2
-    place = iota((pixels, pixels), axis)
-    source = iota((pixels, pixels), 1 - axis)
-    plane = place // quarter
-    inside = place % quarter
-    row = 2 * (inside // half_cols) + plane // 2
-    col = 2 * (inside % half_cols) + plane % 2
-    return (source == row * cols + col).astype(WIDE).astype(LOW)
+    line = (pixels, 1) if axis == 0 else (1, pixels)
+    plane, inside = over(iota(line, axis), pixels // 4)
+    row, col = over(inside, half_cols)
+    row_parity, col_parity = over(plane, 2)
+    pixel = (2 * row + row_parity) * cols + 2 * col + col_parity
+    return (iota((pixels, pixels), 1 - axis) == pixel).astype(WIDE).astype(LOW)
 
 
 def halo_order(images, cols):
     count = images * cols
     half_cols = cols // 2
-    place = iota((count, count), 0)
-    source = iota((count, count), 1)
-    parity = place // (count // 2)
-    inside = place % (count // 2)
-    image = inside // half_cols
-    col = 2 * (inside % half_cols) + parity
-    return (source == image * cols + col).astype(WIDE).astype(LOW)
+    parity, inside = over(iota((count, 1), 0), count // 2)
+    image, col = over(inside, half_cols)
+    return (iota((count, count), 1) == image * cols + 2 * col + parity).astype(WIDE).astype(LOW)
 
 
 def shifted_sums(ref, valid_ref, base, planes, images, quarter):
@@ -269,37 +306,49 @@
     return dot(jnp.broadcast_to(values, (16, values.shape[1])).astype(LOW), w)[0:1, :]
 
 
-def reduce_kernel(dims, valid_ref, x_ref, w_ref, planes_ref, reduced_ref, stats_ref, sampled_ref):
+def reduce_kernel(dims, lead, valid_ref, x_ref, w_ref, planes_ref, reduced_ref, stats_ref, sampled_ref, kept_ref, order_ref):
     images, image_rows, cols = dims
     pixels = image_rows * cols
     quarter = pixels // 4
     plane_rows = images * quarter
+    group = images // lead
     valid = valid_ref[0]
     for image in range(1, images):
         valid = valid + valid_ref[image]
-
-    @pl.when(pl.program_id(0) == 0)
+    step = pl.program_id(0)
+
+    @pl.when(step == 0)
     def _():
-        order = parity_order(image_rows, cols)
+        sampled_ref[...] = jnp.zeros(sampled_ref.shape, WIDE)
+        order_ref[...] = parity_order(image_rows, cols)
+
+    @pl.when(step < lead)
+    def _():
+        order = order_ref[...]
         total = jnp.zeros((8, x_ref.shape[1]), WIDE)
-        for image in range(images):
-            moved = dot(order, x_ref[image * pixels : (image + 1) * pixels, :])
+        for member in range(group):
+            image = step * group + member
+            moved = dot(order, x_ref[member * pixels : (member + 1) * pixels, :])
             total += fold(moved[:quarter, :]) * valid_ref[image]
             moved = moved.astype(LOW)
             for plane in range(4):
-                at = plane * plane_rows + image * quarter
-                planes_ref[at : at + quarter, :] = moved[plane * quarter : (plane + 1) * quarter, :]
-        sampled_ref[...] = close(total) / (valid * float(quarter))
-
-    for plane in range(4):
-        at = slice(plane * plane_rows, (plane + 1) * plane_rows)
-        reduced_ref[at, :] = dot(planes_ref[at, :], w_ref[...])
-    count = valid * float(pixels)
-    base = reduced_ref[0:1, :]
-    total, square = shifted_sums(reduced_ref, valid_ref, base, 4, images, quarter)
-    stats_ref[0:1, :] = jnp.full(base.shape, count, WIDE)
-    stats_ref[1:2, :] = base + total / count
-    stats_ref[2:3, :] = jnp.maximum(square - total * (total / count), 0.0)
+                part = moved[plane * quarter : (plane + 1) * quarter, :]
+                planes_ref[plane, member] = part
+                at = plane * plane_rows + pl.multiple_of(image * quarter, quarter)
+                kept_ref[pl.ds(at, quarter), :] = part
+        sampled_ref[...] += close(total) / (valid * float(quarter))
+
+    @pl.when(step >= lead)
+    def _():
+        for plane in range(4):
+            at = slice(plane * plane_rows, (plane + 1) * plane_rows)
+            reduced_ref[at, :] = dot(kept_ref[at, :], w_ref[...])
+        count = valid * float(pixels)
+        base = reduced_ref[0:1, :]
+        total, square = shifted_sums(reduced_ref, valid_ref, base, 4, images, quarter)
+        stats_ref[0:1, :] = jnp.full(base.shape, count, WIDE)
+        stats_ref[1:2, :] = base + total / count
+        stats_ref[2:3, :] = jnp.maximum(square - total * (total / count), 0.0)
 
 
 def turn_kernel(own_ref, value_ref, out_ref):
@@ -320,7 +369,9 @@
 
 
 def group_mask(width):
-    return (iota((width, width), 0) // GW == iota((width, width), 1) // GW).astype(WIDE).astype(LOW)
+    rows, _ = over(iota((width, 1), 0), GW)
+    cols, _ = over(iota((1, width), 1), GW)
+    return (rows == cols).astype(WIDE).astype(LOW)
 
 
 def block_weights(w_ref, mask, tap):
@@ -333,12 +384,12 @@
     rows, width = values.shape
     moved = pltpu.roll(values, by % rows, 0)
     edge = 0 if by > 0 else cols - 1
-    return jnp.where(iota((rows, width), 0) % cols == edge, 0.0, moved)
+    _, col = over(iota((rows, 1), 0), cols)
+    return jnp.where(col == edge, 0.0, moved)
 
 
 def activate(values, mean, scale, shift):
-    normal = (values - mean) * scale + shift
-    return normal * logistic(normal)
+    return silu((values - mean) * scale + shift)
 
 
 def windows(planes, odd, halves):
@@ -414,8 +465,8 @@
         moved_ref[...] = dot(halo_order(images, 2 * half_cols), halo_ref[...]).astype(LOW)
 
     mean = moments_ref[0:1, :]
-    scale = affine_ref[0:1, :] * lax.rsqrt(moments_ref[1:2, :] / scalar_ref[0] + EPS)
-    shift = affine_ref[1:2, :]
+    scale = 0.5 * affine_ref[0:1, :] * lax.rsqrt(moments_ref[1:2, :] / scalar_ref[0] + EPS)
+    shift = 0.5 * affine_ref[1:2, :]
     edge = activate(dot(moved_ref[...], reduce_ref[...]), mean, scale, shift) * scalar_ref[2]
     edge_ref[...] = edge.astype(LOW)
     half = edge.shape[0] // 2
@@ -436,7 +487,7 @@
     for tap in range(1, TAPS * TAPS):
         kernel = kernel + group_ref[tap * GW : (tap + 1) * GW, :].astype(WIDE)
     kernel = jnp.concatenate([kernel.astype(LOW)] * (width // GW), axis=0) * mask
-    base = row_of(shift * logistic(shift), kernel)
+    base = row_of(silu(shift), kernel)
     total, square = shifted_sums(grouped_ref, valid_ref, base, 1, images, quarter)
     sums_ref[0:1, :] = total
     sums_ref[1:2, :] = square
@@ -461,17 +512,17 @@
     sums_ref,
     base_ref,
 ):
-    shift = affine_ref[1:2, :]
+    shift = 0.5 * affine_ref[1:2, :]
 
     @pl.when(pl.program_id(0) == 0)
     def _():
         mean, inv = moments_of(sums_two_ref[...], base_two_ref[...], scalar_ref[1])
-        scale = affine_ref[0:1, :] * inv
+        scale = 0.5 * affine_ref[0:1, :] * inv
         for span in spans(grouped_ref.shape[0], 16):
             hidden_ref[span, :] = activate(grouped_ref[span, :], mean, scale, shift).astype(LOW)
 
     out_ref[...] = dot(hidden_ref[...], w_ref[...])
-    base = row_of(shift * logistic(shift), w_ref[...])
+    base = row_of(silu(shift), w_ref[...])
     images = out_ref.shape[0] // quarter
     total, square = shifted_sums(out_ref, valid_ref, base, 1, images, quarter)
     sums_ref[0:1, :] = total
@@ -481,10 +532,6 @@
     base_ref[1:2, :] = side_ref[2:3, :]
 
 
-def slope(values, gate):
-    return gate * (1.0 + values * (1.0 - gate))
-
-
 def tail_moments(sums_ref, base_ref, count):
     return (
         *moments_of(sums_ref[0:2, :], base_ref[0:1, :], count),
@@ -492,11 +539,12 @@
     )
 
 
-def tail_values(one, two, moments, affine):
-    first = (one - moments[0]) * moments[1]
-    second = (two - moments[2]) * moments[3]
-    summed = first * affine[0:1, :] + affine[1:2, :] + second * affine[2:3, :] + affine[3:4, :]
-    return first, second, summed
+def tail_halves(moments, affine):
+    return (
+        0.5 * affine[0:1, :] * moments[1],
+        0.5 * affine[2:3, :] * moments[3],
+        0.5 * (affine[1:2, :] + affine[3:4, :]),
+    )
 
 
 def output_kernel(
@@ -516,18 +564,20 @@
     quarter = rows // valid_ref.shape[0]
     totals = [jnp.zeros((8, width), WIDE) for _ in range(3)]
     moments = tail_moments(stats_ref, base_ref, scalar_ref[1])
-    affine = affine_ref[...]
+    one, two, both = tail_halves(moments, affine_ref[...])
     for span in spans(rows, size):
-        first, second, summed = tail_values(expanded_ref[span, :], projected_ref[span, :], moments, affine)
+        first = expanded_ref[span, :] - moments[0]
+        second = projected_ref[span, :] - moments[2]
         valid = valid_ref[span.start // quarter]
-        gate = logistic(summed)
-        out_ref[span, :] = (valid * (summed * gate)).astype(LOW)
-        upstream = (cot_ref[span, :].astype(WIDE) * valid) * slope(summed, gate)
+        value, slope = silu_pair(first * one + second * two + both)
+        out_ref[span, :] = (valid * value).astype(LOW)
+        upstream = (cot_ref[span, :].astype(WIDE) * (0.5 * valid)) * slope
         totals[0] += fold(upstream)
         totals[1] += fold(upstream * first)
         totals[2] += fold(upstream * second)
-    for at in range(3):
-        sums_ref[at : at + 1, :] = close(totals[at])
+    sums_ref[0:1, :] = close(totals[0])
+    sums_ref[1:2, :] = close(totals[1]) * moments[1]
+    sums_ref[2:3, :] = close(totals[2]) * moments[3]
 
 
 def weights_kernel(
@@ -555,15 +605,20 @@
     count = scalar_ref[1]
     moments = tail_moments(stats_ref, base_ref, count)
     affine = affine_ref[...]
+    one, two, both = tail_halves(moments, affine)
+    sums = sums_ref[...] / count
     gain_one = affine[0:1, :] * moments[1]
     gain_two = affine[2:3, :] * moments[3]
-    sums = sums_ref[...] / count
+    pull_one = gain_one * moments[1] * sums[1:2, :]
+    pull_two = gain_two * moments[3] * sums[2:3, :]
     for span in spans(rows, size):
-        first, second, summed = tail_values(expanded_ref[span, :], projected_ref[span, :], moments, affine)
+        first = expanded_ref[span, :] - moments[0]
+        second = projected_ref[span, :] - moments[2]
         valid = valid_ref[span.start // quarter]
-        upstream = cot_ref[span, :].astype(WIDE) * slope(summed, logistic(summed)) - sums[0:1, :]
-        d_expanded_ref[span, :] = ((valid * gain_one) * (upstream - first * sums[1:2, :])).astype(LOW)
-        d_projected_ref[span, :] = ((valid * gain_two) * (upstream - second * sums[2:3, :])).astype(LOW)
+        _, slope = silu_pair(first * one + second * two + both)
+        upstream = (cot_ref[span, :].astype(WIDE) * 0.5) * slope - sums[0:1, :]
+        d_expanded_ref[span, :] = (upstream * (gain_one * valid) - first * (pull_one * valid)).astype(LOW)
+        d_projected_ref[span, :] = (upstream * (gain_two * valid) - second * (pull_two * valid)).astype(LOW)
     store_halves(sampled_ref[...], d_projected_ref[...], proj_low_ref, proj_high_ref)
     store_halves(hidden_ref[...], d_expanded_ref[...], expand_low_ref, expand_high_ref)
 
@@ -583,15 +638,17 @@
     mean, inv = moments_of(sums_two_ref[...], base_two_ref[...], scalar_ref[1])
     out_ref[...] = dot_nt(d_ref[...], w_ref[...])
     totals = [jnp.zeros((8, width), WIDE) for _ in range(2)]
+    scale = 0.5 * affine_ref[0:1, :] * inv
+    shift = 0.5 * affine_ref[1:2, :]
     for span in spans(rows, size):
-        normed = (grouped_ref[span, :] - mean) * inv
-        before = normed * affine_ref[0:1, :] + affine_ref[1:2, :]
-        grad = out_ref[span, :] * slope(before, logistic(before))
+        gap = grouped_ref[span, :] - mean
+        _, slope = silu_pair(gap * scale + shift)
+        grad = (out_ref[span, :] * 0.5) * slope
         out_ref[span, :] = grad
         totals[0] += fold(grad)
-        totals[1] += fold(grad * normed)
-    for at in range(2):
-        sums_ref[at : at + 1, :] = close(totals[at])
+        totals[1] += fold(grad * gap)
+    sums_ref[0:1, :] = close(totals[0])
+    sums_ref[1:2, :] = close(totals[1]) * inv
     for image in range(images):
         at = image * tall * half_cols
         first_ref[image * half_cols : (image + 1) * half_cols, :] = out_ref[at : at + half_cols, :].astype(LOW)
@@ -601,8 +658,13 @@
     out_ref[...] = dot_nt(d_ref[...], w_ref[...])
 
 
-def norm_back_values(grad, values, mean, inv, gain, sums):
-    return gain * inv * (grad - (sums[0:1, :] + (values - mean) * inv * sums[1:2, :]))
+def norm_back_values(grad, values, mean, pull, valid):
+    gain, offset, along = pull
+    return (grad - offset) * (gain * valid) - (values - mean) * (along * valid)
+
+
+def norm_pull(gain, inv, sums, count):
+    return gain * inv, sums[0:1, :] / count, gain * inv * inv * (sums[1:2, :] / count)
 
 
 def conv_back_kernel(
@@ -636,21 +698,22 @@
     count_in, count_out = scalar_ref[0], scalar_ref[1]
 
     mean, inv = moments_of(sums_two_ref[...], base_two_ref[...], count_out)
-    gain = affine_two_ref[0:1, :]
-    sums = grads_two_ref[...] / count_out
+    pull = norm_pull(affine_two_ref[0:1, :], inv, grads_two_ref[...], count_out)
     for image in range(images):
         at = slice(image * quarter, (image + 1) * quarter)
-        values = norm_back_values(grad_ref[at, :], grouped_ref[at, :], mean, inv, gain, sums)
-        values = values * valid_ref[image]
+        values = norm_back_values(grad_ref[at, :], grouped_ref[at, :], mean, pull, valid_ref[image])
         below[0][image, :tall, :, :] = values.astype(LOW).reshape(tall, half_cols, width)
         below[1][image, :tall, :, :] = (
             shift_columns(values, half_cols, -1).astype(LOW).reshape(tall, half_cols, width)
         )
         at = slice(image * half_cols, (image + 1) * half_cols)
         values = norm_back_values(
-            below_grad_ref[at, :].astype(WIDE), below_grouped_ref[at, :].astype(WIDE), mean, inv, gain, sums
+            below_grad_ref[at, :].astype(WIDE),
+            below_grouped_ref[at, :].astype(WIDE),
+            mean,
+            pull,
+            valid_ref[image] * scalar_ref[3],
         )
-        values = values * (valid_ref[image] * scalar_ref[3])
         below[0][image, tall, :, :] = values.astype(LOW)
         below[1][image, tall, :, :] = shift_columns(values, half_cols, -1).astype(LOW)
 
@@ -658,7 +721,8 @@
         return ref[:, at : at + tall, :, :].reshape(plane_rows, width)
 
     mask = group_mask(width)
-    weights = [block_weights(group_ref, mask, tap) for tap in range(TAPS * TAPS)]
+    half_mask = mask * jnp.asarray(0.5, LOW)
+    weights = [block_weights(group_ref, half_mask, tap) for tap in range(TAPS * TAPS)]
     here, left = part(below[0], 0), part(below[1], 0)
     next_here, next_left = part(below[0], 1), part(below[1], 1)
     out_ref[0:plane_rows, :] = dot_nt(here, weights[4])
@@ -673,28 +737,33 @@
 
     mean_one = moments_one_ref[0:1, :]
     inv_one = lax.rsqrt(moments_one_ref[1:2, :] / count_in + EPS)
+    scale = 0.5 * affine_one_ref[0:1, :] * inv_one
+    shift = 0.5 * affine_one_ref[1:2, :]
     totals = [jnp.zeros((8, width), WIDE) for _ in range(2)]
 
     def get(plane, image):
         start = plane * plane_rows + image * quarter
-        at = slice(start, start + quarter)
-        normed = (reduced_ref[at, :] - mean_one) * inv_one
-        before = normed * affine_one_ref[0:1, :] + affine_one_ref[1:2, :]
-        gate = logistic(before)
-        grad = out_ref[at, :] * slope(before, gate)
-        out_ref[at, :] = grad
-        totals[0] += fold(grad)
-        totals[1] += fold(grad * normed)
-        return before * gate
+        parts = []
+        for span in spans(quarter, 32):
+            at = slice(start + span.start, start + span.stop)
+            gap = reduced_ref[at, :] - mean_one
+            value, slope = silu_pair(gap * scale + shift)
+            grad = out_ref[at, :] * slope
+            out_ref[at, :] = grad
+            totals[0] += fold(grad)
+            totals[1] += fold(grad * gap)
+            parts.append(value)
+        return jnp.concatenate(parts, axis=0)
 
     half = edge_ref.shape[0] // 2
     edge = edge_ref[...].astype(WIDE)
     store_hidden(dims, get, (edge[:half], edge[half:]), even, odd)
-    for at in range(2):
-        sums_ref[at : at + 1, :] = close(totals[at])
+    sums_ref[0:1, :] = close(totals[0])
+    sums_ref[1:2, :] = close(totals[1]) * inv_one
     turned = here.T
-    picked = jnp.bitwise_xor(iota((GW, width), 0), own_ref[0])
-    one_hot = (iota((GW, width), 1) % GW == picked).astype(WIDE).astype(LOW)
+    picked = jnp.bitwise_xor(iota((GW, 1), 0), own_ref[0])
+    _, channel = over(iota((1, width), 1), GW)
+    one_hot = (channel == picked).astype(WIDE).astype(LOW)
     for tap, window in enumerate(windows(even, odd, half_cols)):
         full = dot(turned, window).astype(LOW) * mask
         grad_group_ref[tap] = dot_nt(one_hot, full).astype(LOW)
@@ -717,10 +786,10 @@
     quarter = rows // (4 * images)
     mean = moments_ref[0:1, :]
     inv = lax.rsqrt(moments_ref[1:2, :] / scalar_ref[0] + EPS)
-    sums = sums_ref[...] / scalar_ref[0]
+    pull = norm_pull(affine_ref[0:1, :], inv, sums_ref[...], scalar_ref[0])
     for span in spans(rows, size):
-        values = norm_back_values(grad_ref[span, :], reduced_ref[span, :], mean, inv, affine_ref[0:1, :], sums)
-        d_ref[span, :] = (values * valid_ref[span.start // quarter % images]).astype(LOW)
+        valid = valid_ref[span.start // quarter % images]
+        d_ref[span, :] = norm_back_values(grad_ref[span, :], reduced_ref[span, :], mean, pull, valid).astype(LOW)
     half = low_ref.shape[0]
     for at, ref in ((0, low_ref), (half, high_ref)):
         total = None
@@ -732,7 +801,8 @@
         ref[...] = total.astype(LOW).reshape(ref.shape)
 
 
-def images_back_kernel(dims, d_ref, w_ref, side_ref, out_ref, order_ref):
+def images_back_kernel(dims, d_ref, w_ref, side_ref, *refs):
+    out_ref, order_ref = refs[-2:]
     image_rows, cols = dims
     pixels = image_rows * cols
     quarter = pixels // 4
@@ -776,6 +846,10 @@
         compiler_params=pltpu.CompilerParams(vmem_limit_bytes=VMEM_LIMIT),
         cost_estimate=pl.CostEstimate(flops=flops, bytes_accessed=moved, transcendentals=0),
     )
+
+
+def hbm(value):
+    return pltpu.with_memory_space_constraint(value, pltpu.HBM)
 
 
 def per_device(
@@ -811,9 +885,10 @@
     row_index = lax.axis_index("ha")
     has_upper = (row_index > 0).astype(WIDE)
     has_lower = (row_index < lax.axis_size("ha") - 1).astype(WIDE)
-    swapped = (CUTS[0], CUTS[2], CUTS[1], CUTS[3], CUTS[4])
-    own_plain, own_swapped = own_part(CUTS), own_part(swapped)
-    own_one, own_two = own_plain.reshape(1), own_swapped.reshape(1)
+    plain = ([CORE], [SIDE_ONE], [SIDE_TWO], [DEEP_ONE, DEEP_TWO])
+    swapped = ([CORE], [SIDE_TWO], [SIDE_ONE], [DEEP_ONE, DEEP_TWO])
+    short = ([CORE], [SIDE_TWO, SIDE_ONE], [DEEP_ONE, DEEP_TWO])
+    own_one, own_two = own_part(plain).reshape(1), own_part(swapped).reshape(1)
     affine_one = jnp.stack([gain_one, shift_one])
     affine_two = jnp.stack([gain_two, shift_two])
     affine_out = jnp.stack([gain_three, shift_three, gain_proj, shift_proj])
@@ -823,14 +898,26 @@
     back_rounds = sum_plan(("ha", "ba"))
 
     halo_images = shifted(images_in[:, -1], "ha", 1).reshape(images * cols, chans)
+    lead = images // 2
     planes, reduced, stats, sampled = call(
-        functools.partial(reduce_kernel, (images, image_rows, cols)),
-        steps,
-        [SCALARS, whole((pixels, chans)), wide_cols(chans, block)],
-        [whole((pixels, chans)), wide_cols(pixels, block), wide_cols(3, block), whole((1, chans))],
-        [((pixels, chans), LOW), ((pixels, mid), WIDE), ((3, mid), WIDE), ((1, chans), WIDE)],
+        functools.partial(reduce_kernel, (images, image_rows, cols), lead),
+        lead + steps,
+        [
+            SCALARS,
+            pl.BlockSpec((pixels // lead, chans), lambda i: (jnp.minimum(i, lead - 1), 0)),
+            pl.BlockSpec((chans, block), lambda i: (0, jnp.maximum(i - lead, 0))),
+        ],
+        [
+            pl.BlockSpec((4, images // lead, quarter, chans), lambda i: (0, jnp.minimum(i, lead - 1), 0, 0)),
+            pl.BlockSpec((pixels, block), lambda i: (0, jnp.maximum(i - lead, 0))),
+            pl.BlockSpec((3, block), lambda i: (0, jnp.maximum(i - lead, 0))),
+            whole((1, chans)),
+        ],
+        [((4, images, quarter, chans), LOW), ((pixels, mid), WIDE), ((3, mid), WIDE), ((1, chans), WIDE)],
         (2 * pixels * chans * (mid + 256), 20 << 20),
-    )(valid, images_in.reshape(pixels, chans), reduce_w)
+        [pltpu.VMEM((pixels, chans), LOW), pltpu.VMEM((image_rows * cols, image_rows * cols), LOW)],
+    )(valid, hbm(images_in.reshape(pixels, chans)), hbm(reduce_w))
+    planes = planes.reshape(pixels, chans)
     stats, halo_images = tie(jnp.concatenate([stats, sampled]), halo_images)
     stats = mesh_moments(stats, rounds)
 
@@ -839,11 +926,11 @@
         return call(
             turn_kernel,
             1,
-            [SCALARS, pl.BlockSpec((rows, width), lambda i: (at, 0))],
+            [SCALARS, pl.BlockSpec((rows, width), lambda i: (at or 0, 0))],
             [whole((PARTS, width // PARTS, rows))],
             [((PARTS, width // PARTS, rows), LOW)],
             (0, 2 << 20),
-        )(own, value)[0]
+        )(own, value if at is None else hbm(value))[0]
 
     planes_turned = [turn(planes, plane, own_two) for plane in range(4)]
     stats, *planes_turned = tie(stats, *planes_turned)
@@ -879,7 +966,7 @@
         ],
         (2 * rows * mid * 9 * 256, 14 << 20),
         [pltpu.VMEM((images * cols, chans), LOW)] + window_scratch(images, tall, half_cols, block),
-    )(scalars, valid, reduced, moments_one, affine_one, halo_images, reduce_w, group_flat)
+    )(scalars, valid, hbm(reduced), moments_one, affine_one, halo_images, hbm(reduce_w), group_flat)
     sums_two = mesh_sum(sums, rounds)
     below_grouped = shifted(first_row, "ha", -1)
     sums_two, below_grouped = tie(sums_two, below_grouped)
@@ -890,7 +977,7 @@
         [wide_cols(rows, strip), wide_cols(3, strip)],
         [((rows, wide), WIDE), ((3, wide), WIDE)],
         (2 * rows * chans * wide, 10 << 20),
-    )(valid, planes, proj_w, sampled_mean)
+    )(valid, hbm(planes), proj_w, sampled_mean)
 
     hidden_two, expanded, sums, base_out = call(
         functools.partial(expand_kernel, quarter),
@@ -910,7 +997,7 @@
         (2 * rows * mid * wide, 12 << 20),
     )(scalars, valid, grouped, sums_two, base_two, affine_two, expand_w, side)
     stats_out = mesh_sum(sums, rounds)
-    stats_out, hidden_turned = tie(stats_out, turn(hidden_two, 0, own_one))
+    stats_out, hidden_turned = tie(stats_out, turn(hidden_two, None, own_one))
 
     cot = cotangent.reshape(rows, wide)
     output, sums = call(
@@ -929,7 +1016,7 @@
         [wide_cols(rows, strip), wide_cols(3, strip)],
         [((rows, wide), LOW), ((3, wide), WIDE)],
         (20 * rows * wide, 12 << 20),
-    )(scalars, valid, expanded, projected, stats_out, base_out, affine_out, cot)
+    )(scalars, valid, hbm(expanded), hbm(projected), stats_out, base_out, affine_out, cot)
     sums_out = mesh_sum(sums, rounds)
 
     def halves_specs(height, width):
@@ -960,8 +1047,8 @@
     )(
         scalars,
         valid,
-        expanded,
-        projected,
+        hbm(expanded),
+        hbm(projected),
         stats_out,
         base_out,
         affine_out,
@@ -970,8 +1057,8 @@
         hidden_turned,
         planes_turned[0],
     )
-    expand_sum = Gradient(*halves[:2], CUTS, own_plain)
-    proj_sum = Gradient(*halves[2:], swapped, own_swapped)
+    expand_sum = Gradient(halves[:2], plain)
+    proj_sum = Gradient(halves[2:], swapped)
     pair = [expand_sum, proj_sum]
     for grad in pair:
         grad.send()
@@ -992,12 +1079,14 @@
         [((rows, mid), WIDE), ((2, mid), WIDE), ((images * half_cols, mid), LOW)],
         (2 * rows * mid * wide, 10 << 20),
     )(scalars, d_expanded, expand_w, grouped, sums_two, base_two, affine_two)
+    sums = mesh_sum(sums, back_rounds[:1])
+    sums, first_row = arrive(pair, sums, first_row)
     below_grad = shifted(first_row, "ha", -1)
-    sums = mesh_sum(sums, back_rounds[:1])
+    sums = mesh_sum(sums, back_rounds[1:2])
     sums, below_grad = arrive(pair, sums, below_grad)
     for grad in pair:
         grad.step()
-    grads_two = mesh_sum(sums, back_rounds[1:])
+    grads_two = mesh_sum(sums, back_rounds[2:])
     (d_projected,) = tie(d_projected)
     side_grad = call(
         side_kernel,
@@ -1047,7 +1136,7 @@
         base_two,
         affine_two,
         grads_two,
-        reduced,
+        hbm(reduced),
         edge,
         moments_one,
         affine_one,
@@ -1056,13 +1145,15 @@
     parts_group = jnp.pad(jnp.transpose(parts_group, (1, 0, 2)), ((0, 0), (0, 16 - TAPS * TAPS), (0, 0)))
     (sums,) = arrive(pair, sums)
     sums = mesh_sum(sums, back_rounds[:1])
-    (sums,) = tie(sums)
+    (sums,) = arrive(pair, sums)
     for grad in pair:
         grad.step()
     grads_one = mesh_sum(sums, back_rounds[1:])
     grads_one, parts_group = arrive(pair, grads_one, parts_group)
     for grad in pair:
-        grad.step()
+        grad.take()
+    both = join(pair)
+    both.send()
 
     d_reduced, *halves = call(
         functools.partial(reduced_back_kernel, 16),
@@ -1080,47 +1171,63 @@
         [wide_cols(pixels, block)] + halves_specs(chans, block),
         [((pixels, mid), LOW)] + halves_shapes(chans, mid),
         (2 * pixels * mid * chans, 26 << 20),
-    )(scalars, valid, grad_one, reduced, moments_one, affine_one, grads_one, *planes_turned)
-    (d_reduced,) = arrive(pair, d_reduced)
+    )(scalars, valid, hbm(grad_one), hbm(reduced), moments_one, affine_one, grads_one, *planes_turned)
+    d_reduced, *halves = arrive([both], d_reduced, *halves)
     parts_group = [parts_group[: PARTS // 2], parts_group[PARTS // 2 :]]
-    halves = [jnp.concatenate(both, axis=1) for both in zip(halves, parts_group)]
-    reduce_sum = Gradient(*halves, swapped, own_swapped)
+    halves = [jnp.concatenate(members, axis=1) for members in zip(halves, parts_group)]
+    reduce_sum = Gradient(halves, short)
     reduce_sum.send()
+
+    def images_back(d_part, side_part, half, before):
+        part = images // 2
+        kept = [] if before is None else [before]
+        return pl.pallas_call(
+            functools.partial(images_back_kernel, (image_rows, cols)),
+            grid=(part,),
+            in_specs=[
+                pl.BlockSpec((4, None, quarter, mid), lambda i: (0, i + half * part, 0, 0)),
+                whole((chans, mid)),
+                pl.BlockSpec((quarter, chans), lambda i: (i + half * part, 0)),
+            ]
+            + [pl.BlockSpec(memory_space=pl.ANY)] * len(kept),
+            out_specs=pl.BlockSpec((None, image_rows * cols, chans), lambda i: (i + half * part, 0, 0)),
+            out_shape=place((images, image_rows * cols, chans), LOW),
+            input_output_aliases={3: 0} if kept else {},
+            scratch_shapes=[pltpu.VMEM((image_rows * cols, image_rows * cols), LOW)],
+            compiler_params=pltpu.CompilerParams(vmem_limit_bytes=VMEM_LIMIT),
+            cost_estimate=pl.CostEstimate(
+                flops=pixels * mid * chans, bytes_accessed=8 << 20, transcendentals=0
+            ),
+        )(d_part, reduce_w, side_part, *kept)
+
+    d_reduced = d_reduced.reshape(4, images, quarter, mid)
+    both.step()
+    (d_reduced,) = arrive([reduce_sum], d_reduced)
+    reduce_sum.step()
+    grad_images = images_back(d_reduced, side_grad, 0, None)
+    grad_images, both.got[0] = tie(grad_images, both.got[0])
+    grad_images = images_back(d_reduced, side_grad, 1, grad_images)
+    (grad_images,) = arrive([both, reduce_sum], grad_images)
+    both.take()
+    part_again(both, pair)
     for grad in pair:
-        grad.step()
+        grad.send()
     everyone = pair + [reduce_sum]
-
-    def images_back(d_part, side_part):
-        part = d_part.shape[1]
-        return call(
-            functools.partial(images_back_kernel, (image_rows, cols)),
-            part,
-            [
-                pl.BlockSpec((4, None, quarter, mid), lambda i: (0, i, 0, 0)),
-                whole((chans, mid)),
-                pl.BlockSpec((quarter, chans), lambda i: (i, 0)),
-            ],
-            [pl.BlockSpec((None, image_rows * cols, chans), lambda i: (i, 0, 0))],
-            [((part, image_rows * cols, chans), LOW)],
-            (2 * pixels * mid * chans, 16 << 20),
-            [pltpu.VMEM((image_rows * cols, image_rows * cols), LOW)],
-        )(d_part, reduce_w, side_part)[0]
-
-    grad_images = images_back(d_reduced.reshape(4, images, quarter, mid), side_grad)
-    (grad_images,) = arrive(everyone, grad_images)
-    for grad in everyone:
-        grad.step()
-    for beside in (0, 0, 1, 2):
+    reduce_sum.step()
+    while pair[0].left() > 1:
         arrive(everyone)
         for grad in everyone:
             grad.step()
-        for _ in range(beside):
-            reduce_sum.step()
-    arrive(pair)
-    for grad in pair:
+    done = []
+    for grad, width in zip(pair, (mid, chans)):
+        if done:
+            done[0] = arrive([grad], done[0])[0]
         grad.take()
-    (grad_expand,), (grad_proj,) = [grad.finish(width // PARTS) for grad, width in zip(pair, (mid, chans))]
-    while reduce_sum.at < 2 * len(CUTS):
+        done += grad.finish(width // PARTS)
+    grad_expand, grad_proj = done
+    (grad_proj,) = arrive([reduce_sum], grad_proj)
+    reduce_sum.step()
+    while reduce_sum.left():
         reduce_sum.step()
     grad_reduce, grad_group = reduce_sum.finish(chans // PARTS, TAPS * TAPS)
     return (

time: 349 us -> 317 us (0.908)
  waiting for transfers between devices: 120 us -> 89.5 us
  local copies, waits for them, and re-layouts: 33.9 us -> 15.5 us
  Pallas kernels: 101 us -> 110 us
  starting transfers between devices: 83.2 us -> 88.8 us
    ppermute x72 -> x74, waiting for transfers between devices: 120 us -> 83.4 us  [exchange(): return lax.ppermute(value, axis, [(i, i ^ mask) for i in range(peers)])]
    unnamed x102 -> x72, local copies, waits for them, and re-layouts: 29.3 us -> 9.93 us
    pallas_call x7 -> x8, Pallas kernels: 20 us -> 28.9 us  [the longest x1 12.6 us: per_device(): call(functools.partial(reduce_kernel, (images, image_rows, cols), lead),...]
    ppermute x3, waiting for transfers between devices: 0.01 us -> 6.14 us  [shifted(): return lax.ppermute(value, axis, pairs)]
    ppermute x72 -> x74, starting transfers between devices: 75.4 us -> 81.1 us  [exchange(): return lax.ppermute(value, axis, [(i, i ^ mask) for i in range(peers)])]
  transfers between devices with their start and end apart: 75 -> 77, of which waited for: 45 -> 44; matrix products, arithmetic and copies ran while one was open for 2% -> 2% of each run, Pallas kernels for 19% -> 24%
where the time goes in v4:
time: 317 us; the launch traced here: 316 us
  Pallas kernels  110 us (35%)
  waiting for transfers between devices  89.5 us (28%)
  starting transfers between devices  88.8 us (28%)
  local copies, waits for them, and re-layouts  15.5 us (5%)
  other arithmetic  10.3 us (3%)
    ppermute x74, waiting for transfers between devices, exchange(): return lax.ppermute(value, axis, [(i, i ^ mask) for i in range(peers)])  83.4 us
    ppermute x74, starting transfers between devices, exchange(): return lax.ppermute(value, axis, [(i, i ^ mask) for i in range(peers)])  81.1 us
    pallas_call x1, Pallas kernels, per_device(): call(functools.partial(conv_back_kernel, (images, tall, half_cols)), step...  15.8 us
    pallas_call x1, Pallas kernels, per_device(): call(functools.partial(reduce_kernel, (images, image_rows, cols), lead),...  12.6 us
    pallas_call x1, Pallas kernels, per_device(): call(functools.partial(weights_kernel, 16), strips, [SCALARS, SCALARS, wi...  11.4 us
    pallas_call x3, Pallas kernels, plain_order(): pl.pallas_call(spread_kernel, grid=(cols // width,), in_specs=[pl.BlockSp...  10.5 us
    unnamed x72, local copies, waits for them, and re-layouts  9.93 us
    pallas_call x2, Pallas kernels, images_back(): pl.pallas_call(functools.partial(images_back_kernel, (image_rows, cols)),...  9.68 us
  transfers between devices with their start and end apart: 77, of which 44 were waited for; matrix products, arithmetic and copies ran while one was open for 2% of the time, Pallas kernels for 24%

profile of v4, /device:TPU:0, one launch (start us, length us, event | category | flops | bytes accessed | tf_op | source)
XLA Modules:
  0.0 316.0 jit_solution(10941016424564028144)
XLA Ops:
  1.7 4.9 %collective-permute-start = (bf16[8,32,1024]{2,1,0:T(8,128)(2,1)S(1)}, bf16[8,32,1024]{2,1,0:T(8,128)(2,1)S(1)}, u32[]{:S(2)}, u32[]{:S(2)}) collective-permute-start(bf16[8,32,1024]{2,1,0:T(8,128)(2,1)S(1)} %slice_bitcast_fusion), channel_id=1, source_target_pairs={{0,8},{8,16},{16,24},{1,9},{9,17},{17,25},{2,10},{10,18},{18,26},{... | collective-permute-start | bytes 1572872 | tf_op jit(solution)/shard_map/ppermute | solution.py:19
  7.3 12.6 %shard_map.254 = (bf16[4,8,64,1024]{3,2,1,0:T(8,128)(2,1)}, f32[2048,1024]{1,0:T(8,128)}, f32[3,1024]{1,0:T(4,128)S(1)}, f32[1,1024]{1,0:T(1,128)S(1)}) custom-call(f32[8]{0:T(128)S(1)} %convert_element_type.123.valid_ref, bf16[2048,1024]{1,0:T(8,128)(2,1)} %bitcast.54, bf16[1024,1024]{1,0:T(8,128)(2,1)} %w_ref.13), custom_call_target="tpu_custom_call" | custom-call | flops 5368709120 | bytes 20971520 | tf_op jit(solution)/shard_map/pallas_call | solution.py:902
  23.7 2.5 collective-permute-start.4
  26.3 2.9 collective-permute-done.4
  46.1 7.8 %shard_map.259 = (f32[512,1024]{1,0:T(8,128)S(1)}, f32[2,1024]{1,0:T(2,128)S(1)}, f32[1,1024]{1,0:T(1,128)S(1)}, bf16[128,1024]{1,0:T(8,128)(2,1)S(1)}, bf16[256,1024]{1,0:T(8,128)(2,1)S(1)}) custom-call(f32[4]{0:T(128)S(1)} %pad_maximum_fusion.17.scalar_ref, f32[8]{0:T(128)S(1)} %convert_element_type.123.valid_ref, ...), custom_call_target="tpu_custom_call" | custom-call | flops 2415919104 | bytes 14680064 | tf_op jit(solution)/shard_map/pallas_call | solution.py:940
  55.3 2.9 collective-permute-start.11
  61.9 1.9 collective-permute-start.13
  65.5 6.1 %shard_map.260 = (f32[512,2048]{1,0:T(8,128)}, f32[3,2048]{1,0:T(4,128)S(1)}) custom-call(f32[8]{0:T(128)S(1)} %convert_element_type.123.valid_ref, bf16[2048,1024]{1,0:T(8,128)(2,1)} %bitcast.49, bf16[1024,2048]{1,0:T(8,128)(2,1)S(1)} %copy-done.2, f32[1,1024]{1,0:T(1,128)S(1)} %slice.121.sampled_ref), custom_call_target="tpu_custom_call" | custom-call | flops 2147483648 | bytes 10485760 | tf_op jit(solution)/shard_map/pallas_call | solution.py:973
  71.8 6.0 %shard_map.261 = (bf16[512,1024]{1,0:T(8,128)(2,1)S(1)}, f32[512,2048]{1,0:T(8,128)}, f32[4,2048]{1,0:T(4,128)S(1)}, f32[2,2048]{1,0:T(2,128)S(1)}) custom-call(f32[4]{0:T(128)S(1)} %pad_maximum_fusion.17.scalar_ref, f32[8]{0:T(128)S(1)} %convert_element_type.123.valid_ref, f32[512,1024]{1,0:T(8,128)S(1)} %get-tuple-element.119.grouped_ref, ...), custom_call_target="tpu_custom_call" | custom-call | flops 2147483648 | bytes 12582912 | tf_op jit(solution)/shard_map/pallas_call | solution.py:982
  80.9 2.9 collective-permute-start.19
  83.9 2.1 collective-permute-done.18
  87.8 2.0 collective-permute-start.21
  95.6 6.7 %shard_map.263 = (bf16[512,2048]{1,0:T(8,128)(2,1)}, f32[3,2048]{1,0:T(4,128)S(1)}) custom-call(f32[4]{0:T(128)S(1)} %pad_maximum_fusion.17.scalar_ref, f32[8]{0:T(128)S(1)} %convert_element_type.123.valid_ref, f32[512,2048]{1,0:T(8,128)} %get-tuple-element.125.expanded_ref, f32[512,2048]{1,0:T(8,128)} %get-tuple-element.126.projected_ref, ...), custom_call_target="tpu_custom_call" | custom-call | flops 20971520 | bytes 12582912 | tf_op jit(solution)/shard_map/pallas_call | solution.py:1003
  103.6 2.6 collective-permute-start.26
  107.1 2.4 collective-permute-done.25
  114.2 2.1 collective-permute-done.29
  116.3 11.4 %shard_map.264 = (bf16[512,2048]{1,0:T(8,128)(2,1)S(1)}, bf16[512,2048]{1,0:T(8,128)(2,1)S(1)}, bf16[16,32,2048]{2,1,0:T(8,128)(2,1)S(1)}, bf16[16,32,2048]{2,1,...) custom-call(f32[4]{0:T(128)S(1)} %pad_maximum_fusion.17.scalar_ref, ...), custom_call_target="tpu_custom_call" | custom-call | flops 4294967296 | bytes 25165824 | tf_op jit(solution)/shard_map/pallas_call | solution.py:1028
  131.2 4.2 %shard_map.265 = (f32[512,1024]{1,0:T(8,128)S(1)}, f32[2,1024]{1,0:T(2,128)S(1)}, bf16[128,1024]{1,0:T(8,128)(2,1)S(1)}) custom-call(f32[4]{0:T(128)S(1)} %pad_maximum_fusion.17.scalar_ref, bf16[512,2048]{1,0:T(8,128)(2,1)S(1)} %get-tuple-element.135.d_ref, bf16[1024,2048]{1,0:T(8,128)(2,1)S(1)} %copy-done.7, f32[512,1024]{1,0:T(8,128)S(1)} %copy-done.10, ...), custom_call_target="tpu_custom_call" | custom-call | flops 2147483648 | bytes 10485760 | tf_op jit(solution)/shard_map/pallas_call | solution.py:1066
  135.4 2.0 collective-permute-start.31
  139.2 2.8 collective-permute-done.32
  144.6 6.1 %collective-permute-done.36.below_grad_ref = bf16[128,1024]{1,0:T(8,128)(2,1)S(1)} collective-permute-done((bf16[128,1024]{1,0:T(8,128)(2,1)S(1)}, bf16[128,1024]{1,0:T(8,128)(2,1)S(1)}, u32[]{:S(2)}, u32[]{:S(2)}) %collective-permute-start.36) | collective-permute-done | bytes 262176 | tf_op jit(solution)/shard_map/ppermute | solution.py:19
  150.7 2.4 add_convert_fusion.1
  157.9 2.0 collective-permute-start.39
  160.3 2.4 shard_map.266.side_ref
  163.7 15.8 %shard_map.267 = (f32[2048,1024]{1,0:T(8,128)}, f32[2,1024]{1,0:T(2,128)S(1)}, bf16[9,32,1024]{2,1,0:T(8,128)(2,1)S(1)}) custom-call(f32[4]{0:T(128)S(1)} %pad_maximum_fusion.17.scalar_ref, s32[1]{0:T(128)} %bitcast.3.own_ref, f32[8]{0:T(128)S(1)} %convert_element_type.123.valid_ref, f32[512,1024]{1,0:T(8,128)S(1)} %copy-done.21, ...), custom_call_target="tpu_custom_call" | custom-call | flops 4831838208 | bytes 25165824 | tf_op jit(solution)/shard_map/pallas_call | solution.py:1102
  179.5 2.1 collective-permute-start.43
  183.2 3.0 collective-permute-done.44
  193.3 2.0 collective-permute-start.48
  196.8 1.9 collective-permute-done.48
  202.0 2.0 collective-permute-start.53
  204.0 9.6 %shard_map.268 = (bf16[2048,1024]{1,0:T(8,128)(2,1)}, bf16[16,32,1024]{2,1,0:T(8,128)(2,1)S(1)}, bf16[16,32,1024]{2,1,0:T(8,128)(2,1)S(1)}) custom-call(f32[4]{0:T(128)S(1)} %pad_maximum_fusion.17.scalar_ref, f32[8]{0:T(128)S(1)} %convert_element_type.123.valid_ref, f32[2048,1024]{1,0:T(8,128)} %get-tuple-element.151.grad_ref, ...), custom_call_target="tpu_custom_call" | custom-call | flops 4294967296 | bytes 27262976 | tf_op jit(solution)/shard_map/pallas_call | solution.py:1158
  215.1 3.4 %collective-permute-done.53 = bf16[1,64,2048]{2,1,0:T(8,128)(2,1)S(1)} collective-permute-done((bf16[1,64,2048]{2,1,0:T(8,128)(2,1)S(1)}, bf16[1,64,2048]{2,1,0:T(8,128)(2,1)S(1)}, u32[]{:S(2)}, u32[]{:S(2)}) %collective-permute-start.53) | collective-permute-done | bytes 262176 | tf_op jit(solution)/shard_map/ppermute | solution.py:24
  218.9 6.5 %collective-permute-start.55 = (bf16[1,64,2048]{2,1,0:T(8,128)(2,1)S(1)}, bf16[1,64,2048]{2,1,0:T(8,128)(2,1)S(1)}, u32[]{:S(2)}, u32[]{:S(2)}) collective-permute-start(bf16[1,64,2048]{2,1,0:T(8,128)(2,1)S(1)} %add_convert_fusion.8), channel_id=1, source_target_pairs={{0,4},{1,5},{2,6},{3,7},{4,0},{5,1},{6,2},{7,3},{8,12},{9,13},{10,... | collective-permute-start | bytes 786440 | tf_op jit(solution)/shard_map/ppermute | solution.py:24
  225.4 1.9 collective-permute-start.57
  229.9 8.3 %collective-permute-done.55 = bf16[1,64,2048]{2,1,0:T(8,128)(2,1)S(1)} collective-permute-done((bf16[1,64,2048]{2,1,0:T(8,128)(2,1)S(1)}, bf16[1,64,2048]{2,1,0:T(8,128)(2,1)S(1)}, u32[]{:S(2)}, u32[]{:S(2)}) %collective-permute-start.55) | collective-permute-done | bytes 262176 | tf_op jit(solution)/shard_map/ppermute | solution.py:24
  239.3 4.8 %shard_map.269.refs_0_ = bf16[8,256,1024]{2,1,0:T(8,128)(2,1)} custom-call(bf16[4,8,64,1024]{3,2,1,0:T(8,128)(2,1)S(1)} %bitcast.38, bf16[1024,1024]{1,0:T(8,128)(2,1)S(1)} %copy-done, f32[512,1024]{1,0:T(8,128)S(1)} %shard_map.266.side_ref), custom_call_target="tpu_custom_call" | custom-call | flops 2147483648 | bytes 8388608 | tf_op jit(solution)/shard_map/pallas_call | solution.py:1184
  244.1 4.8 %shard_map.270 = bf16[8,256,1024]{2,1,0:T(8,128)(2,1)} custom-call(bf16[4,8,64,1024]{3,2,1,0:T(8,128)(2,1)S(1)} %bitcast.39, bf16[1024,1024]{1,0:T(8,128)(2,1)S(1)} %copy-done, f32[512,1024]{1,0:T(8,128)S(1)} %shard_map.266.side_ref, bf16[8,256,1024]{2,1,0:T(8,128)(2,1)} %shard_map.269.refs_0_), custom_call_target="tpu_custom_call", output_to_operand_aliasing={{}: (3, {})} | custom-call | flops 2147483648 | bytes 8388608 | tf_op jit(solution)/shard_map/pallas_call | solution.py:1184
  252.6 2.0 collective-permute-start.64
  254.7 1.8 collective-permute-start.65
  256.5 5.1 %collective-permute-done.63 = bf16[1,48,1024]{2,1,0:T(8,128)(2,1)S(1)} collective-permute-done((bf16[1,48,1024]{2,1,0:T(8,128)(2,1)S(1)}, bf16[1,48,1024]{2,1,0:T(8,128)(2,1)S(1)}, u32[]{:S(2)}, u32[]{:S(2)}) %collective-permute-start.63) | collective-permute-done | bytes 98336 | tf_op jit(solution)/shard_map/ppermute | solution.py:24
  268.0 1.9 collective-permute-start.70
  269.9 3.3 %collective-permute-done.68 = bf16[1,48,1024]{2,1,0:T(8,128)(2,1)S(1)} collective-permute-done((bf16[1,48,1024]{2,1,0:T(8,128)(2,1)S(1)}, bf16[1,48,1024]{2,1,0:T(8,128)(2,1)S(1)}, u32[]{:S(2)}, u32[]{:S(2)}) %collective-permute-start.68) | collective-permute-done | bytes 98336 | tf_op jit(solution)/shard_map/ppermute | solution.py:24
  274.5 12.1 %collective-permute-done.66 = bf16[8,32,2048]{2,1,0:T(8,128)(2,1)S(1)} collective-permute-done((bf16[8,32,2048]{2,1,0:T(8,128)(2,1)S(1)}, bf16[8,32,2048]{2,1,0:T(8,128)(2,1)S(1)}, u32[]{:S(2)}, u32[]{:S(2)}) %collective-permute-start.66) | collective-permute-done | bytes 1048608 | tf_op jit(solution)/shard_map/ppermute | solution.py:24
  290.5 2.2 collective-permute-start.75
  292.8 3.8 %shard_map.271 = f32[32,32,2048]{2,1,0:T(8,128)} custom-call(s32[1]{0:T(128)} %bitcast.14.own_ref, bf16[16,32,2048]{2,1,0:T(8,128)(2,1)S(1)} %pad_maximum_fusion.1.low_ref, bf16[16,32,2048]{2,1,0:T(8,128)(2,1)S(1)} %collective-permute-done.71.high_ref), custom_call_target="tpu_custom_call" | custom-call | bytes 12582912 | tf_op jit(solution)/shard_map/pallas_call | solution.py:119
  296.6 3.8 %shard_map.272 = f32[32,32,2048]{2,1,0:T(8,128)} custom-call(s32[1]{0:T(128)} %bitcast.3.own_ref, bf16[16,32,2048]{2,1,0:T(8,128)(2,1)S(1)} %pad_maximum_fusion.low_ref, bf16[16,32,2048]{2,1,0:T(8,128)(2,1)S(1)} %collective-permute-done.72.high_ref), custom_call_target="tpu_custom_call" | custom-call | bytes 12582912 | tf_op jit(solution)/shard_map/pallas_call | solution.py:119
  301.2 7.8 %collective-permute-done.74 = bf16[4,48,1024]{2,1,0:T(8,128)(2,1)S(1)} collective-permute-done((bf16[4,48,1024]{2,1,0:T(8,128)(2,1)S(1)}, bf16[4,48,1024]{2,1,0:T(8,128)(2,1)S(1)}, u32[]{:S(2)}, u32[]{:S(2)}) %collective-permute-start.74) | collective-permute-done | bytes 393248 | tf_op jit(solution)/shard_map/ppermute | solution.py:24
  312.5 2.9 shard_map.273
  (269 shorter events, 98.7 us)
Async XLA Ops:
  1.7 18.2 %collective-permute-start = (bf16[8,32,1024]{2,1,0:T(8,128)(2,1)S(1)}, bf16[8,32,1024]{2,1,0:T(8,128)(2,1)S(1)}, u32[]{:S(2)}, u32[]{:S(2)}) collective-permute-start(bf16[8,32,1024]{2,1,0:T(8,128)(2,1)S(1)} %slice_bitcast_fusion), channel_id=1, source_target_pairs={{0,8},{8,16},{16,24},{1,9},{9,17},{17,25},{2,10},{10,18},{18,26},{... | collective-permute-start | bytes 1572872 | tf_op jit(solution)/shard_map/ppermute | solution.py:19
  23.7 5.5 %collective-permute-start.4 = (f32[4,1024]{1,0:T(4,128)S(1)}, f32[4,1024]{1,0:T(4,128)S(1)}, u32[]{:S(2)}, u32[]{:S(2)}) collective-permute-start(f32[4,1024]{1,0:T(4,128)S(1)} %pad_maximum_fusion.12), channel_id=1, source_target_pairs={{0,6},{1,7},{2,4},{3,5},{4,2},{5,3},{6,0},{7,1},{8,14},{9,15},{10,... | collective-permute-start | bytes 49160 | tf_op jit(solution)/shard_map/ppermute | solution.py:24
  31.0 10.9 %collective-permute-start.5 = (f32[4,1024]{1,0:T(4,128)S(1)}, f32[4,1024]{1,0:T(4,128)S(1)}, u32[]{:S(2)}, u32[]{:S(2)}) collective-permute-start(f32[4,1024]{1,0:T(4,128)S(1)} %pad_maximum_fusion.13), channel_id=1, source_target_pairs={{0,8},{8,0},{16,24},{24,16},{1,9},{9,1},{17,25},{25,17},{2,10},{10... | collective-permute-start | bytes 49160 | tf_op jit(solution)/shard_map/ppermute | solution.py:24
  32.5 9.4 %collective-permute-start.7 = (f32[4,1024]{1,0:T(4,128)S(1)}, f32[4,1024]{1,0:T(4,128)S(1)}, u32[]{:S(2)}, u32[]{:S(2)}) collective-permute-start(f32[4,1024]{1,0:T(4,128)S(1)} %pad_maximum_fusion.13), channel_id=1, source_target_pairs={{0,24},{8,16},{16,8},{24,0},{1,25},{9,17},{17,9},{25,1},{2,26},{10... | collective-permute-start | bytes 49160 | tf_op jit(solution)/shard_map/ppermute | solution.py:24
  34.0 7.9 %collective-permute-start.6 = (f32[4,1024]{1,0:T(4,128)S(1)}, f32[4,1024]{1,0:T(4,128)S(1)}, u32[]{:S(2)}, u32[]{:S(2)}) collective-permute-start(f32[4,1024]{1,0:T(4,128)S(1)} %pad_maximum_fusion.13), channel_id=1, source_target_pairs={{0,16},{8,24},{16,0},{24,8},{1,17},{9,25},{17,1},{25,9},{2,18},{10... | collective-permute-start | bytes 49160 | tf_op jit(solution)/shard_map/ppermute | solution.py:24
  55.3 5.4 %collective-permute-start.11 = (f32[2,1024]{1,0:T(2,128)S(1)}, f32[2,1024]{1,0:T(2,128)S(1)}, u32[]{:S(2)}, u32[]{:S(2)}) collective-permute-start(f32[2,1024]{1,0:T(2,128)S(1)} %add.445), channel_id=1, source_target_pairs={{0,6},{1,7},{2,4},{3,5},{4,2},{5,3},{6,0},{7,1},{8,14},{9,15},{10,... | collective-permute-start | bytes 24584 | tf_op jit(solution)/shard_map/ppermute | solution.py:24
  58.7 13.0 %collective-permute-start.15 = (bf16[128,1024]{1,0:T(8,128)(2,1)S(1)}, bf16[128,1024]{1,0:T(8,128)(2,1)S(1)}, u32[]{:S(2)}, u32[]{:S(2)}) collective-permute-start(bf16[128,1024]{1,0:T(8,128)(2,1)S(1)} %get-tuple-element.121), channel_id=1, source_target_pairs={{8,0},{16,8},{24,16},{9,1},{17,9},{25,17},{10,2},{18,10},{26,18},{... | collective-permute-start | bytes 786440 | tf_op jit(solution)/shard_map/ppermute | solution.py:19
  61.9 9.7 %collective-permute-start.13 = (f32[2,1024]{1,0:T(2,128)S(1)}, f32[2,1024]{1,0:T(2,128)S(1)}, u32[]{:S(2)}, u32[]{:S(2)}) collective-permute-start(f32[2,1024]{1,0:T(2,128)S(1)} %add_add_fusion.9), channel_id=1, source_target_pairs={{0,16},{8,24},{16,0},{24,8},{1,17},{9,25},{17,1},{25,9},{2,18},{10... | collective-permute-start | bytes 24584 | tf_op jit(solution)/shard_map/ppermute | solution.py:24
  63.8 7.8 %collective-permute-start.14 = (f32[2,1024]{1,0:T(2,128)S(1)}, f32[2,1024]{1,0:T(2,128)S(1)}, u32[]{:S(2)}, u32[]{:S(2)}) collective-permute-start(f32[2,1024]{1,0:T(2,128)S(1)} %add_add_fusion.9), channel_id=1, source_target_pairs={{0,24},{8,16},{16,8},{24,0},{1,25},{9,17},{17,9},{25,1},{2,26},{10... | collective-permute-start | bytes 24584 | tf_op jit(solution)/shard_map/ppermute | solution.py:24
  64.9 6.7 %collective-permute-start.12 = (f32[2,1024]{1,0:T(2,128)S(1)}, f32[2,1024]{1,0:T(2,128)S(1)}, u32[]{:S(2)}, u32[]{:S(2)}) collective-permute-start(f32[2,1024]{1,0:T(2,128)S(1)} %add_add_fusion.9), channel_id=1, source_target_pairs={{0,8},{8,0},{16,24},{24,16},{1,9},{9,1},{17,25},{25,17},{2,10},{10... | collective-permute-start | bytes 24584 | tf_op jit(solution)/shard_map/ppermute | solution.py:24
  79.9 6.0 %collective-permute-start.18 = (f32[4,2048]{1,0:T(4,128)S(1)}, f32[4,2048]{1,0:T(4,128)S(1)}, u32[]{:S(2)}, u32[]{:S(2)}) collective-permute-start(f32[4,2048]{1,0:T(4,128)S(1)} %add.452), channel_id=1, source_target_pairs={{0,4},{1,5},{2,6},{3,7},{4,0},{5,1},{6,2},{7,3},{8,12},{9,13},{10,... | collective-permute-start | bytes 98312 | tf_op jit(solution)/shard_map/ppermute | solution.py:24
  80.9 5.8 %collective-permute-start.19 = (f32[4,2048]{1,0:T(4,128)S(1)}, f32[4,2048]{1,0:T(4,128)S(1)}, u32[]{:S(2)}, u32[]{:S(2)}) collective-permute-start(f32[4,2048]{1,0:T(4,128)S(1)} %add.452), channel_id=1, source_target_pairs={{0,6},{1,7},{2,4},{3,5},{4,2},{5,3},{6,0},{7,1},{8,14},{9,15},{10,... | collective-permute-start | bytes 98312 | tf_op jit(solution)/shard_map/ppermute | solution.py:24
  103.5 5.9 %collective-permute-start.25 = (f32[3,2048]{1,0:T(4,128)S(1)}, f32[3,2048]{1,0:T(4,128)S(1)}, u32[]{:S(2)}, u32[]{:S(2)}) collective-permute-start(f32[3,2048]{1,0:T(4,128)S(1)} %add.463), channel_id=1, source_target_pairs={{0,4},{1,5},{2,6},{3,7},{4,0},{5,1},{6,2},{7,3},{8,12},{9,13},{10,... | collective-permute-start | bytes 73736 | tf_op jit(solution)/shard_map/ppermute | solution.py:24
  103.6 6.1 %collective-permute-start.26 = (f32[3,2048]{1,0:T(4,128)S(1)}, f32[3,2048]{1,0:T(4,128)S(1)}, u32[]{:S(2)}, u32[]{:S(2)}) collective-permute-start(f32[3,2048]{1,0:T(4,128)S(1)} %add.463), channel_id=1, source_target_pairs={{0,6},{1,7},{2,4},{3,5},{4,2},{5,3},{6,0},{7,1},{8,14},{9,15},{10,... | collective-permute-start | bytes 73736 | tf_op jit(solution)/shard_map/ppermute | solution.py:24
  129.1 12.9 %collective-permute-start.33 = (bf16[16,32,2048]{2,1,0:T(8,128)(2,1)S(1)}, bf16[16,32,2048]{2,1,0:T(8,128)(2,1)}, u32[]{:S(2)}, u32[]{:S(2)}) collective-permute-start(bf16[16,32,2048]{2,1,0:T(8,128)(2,1)S(1)} %get-tuple-element.139), channel_id=1, source_target_pairs={{0,1},{1,0},{2,3},{3,2},{4,5},{5,4},{6,7},{7,6},{8,9},{9,8},{10,11... | collective-permute-start | bytes 6291464 | tf_op jit(solution)/shard_map/ppermute | solution.py:24
  129.1 12.9 %collective-permute-start.34 = (bf16[16,32,2048]{2,1,0:T(8,128)(2,1)}, bf16[16,32,2048]{2,1,0:T(8,128)(2,1)S(1)}, u32[]{:S(2)}, u32[]{:S(2)}) collective-permute-start(bf16[16,32,2048]{2,1,0:T(8,128)(2,1)} %get-tuple-element.140), channel_id=1, source_target_pairs={{0,1},{1,0},{2,3},{3,2},{4,5},{5,4},{6,7},{7,6},{8,9},{9,8},{10,11... | collective-permute-start | bytes 6291464 | tf_op jit(solution)/shard_map/ppermute | solution.py:24
  142.0 8.7 %collective-permute-start.36 = (bf16[128,1024]{1,0:T(8,128)(2,1)S(1)}, bf16[128,1024]{1,0:T(8,128)(2,1)S(1)}, u32[]{:S(2)}, u32[]{:S(2)}) collective-permute-start(bf16[128,1024]{1,0:T(8,128)(2,1)S(1)} %get-tuple-element.142), channel_id=1, source_target_pairs={{8,0},{16,8},{24,16},{9,1},{17,9},{25,17},{10,2},{18,10},{26,18},{... | collective-permute-start | bytes 786440 | tf_op jit(solution)/shard_map/ppermute | solution.py:19
  154.2 25.3 %collective-permute-start.40 = (bf16[8,32,2048]{2,1,0:T(8,128)(2,1)}, bf16[8,32,2048]{2,1,0:T(8,128)(2,1)}, u32[]{:S(2)}, u32[]{:S(2)}) collective-permute-start(bf16[8,32,2048]{2,1,0:T(8,128)(2,1)} %slice.157), channel_id=1, source_target_pairs={{0,8},{8,0},{16,24},{24,16},{1,9},{9,1},{17,25},{25,17},{2,10},{10... | collective-permute-start | bytes 3145736 | tf_op jit(solution)/shard_map/ppermute | solution.py:24
  156.6 22.9 %collective-permute-start.41 = (bf16[8,32,2048]{2,1,0:T(8,128)(2,1)S(1)}, bf16[8,32,2048]{2,1,0:T(8,128)(2,1)S(1)}, u32[]{:S(2)}, u32[]{:S(2)}) collective-permute-start(bf16[8,32,2048]{2,1,0:T(8,128)(2,1)S(1)} %slice.158), channel_id=1, source_target_pairs={{0,16},{8,24},{16,0},{24,8},{1,17},{9,25},{17,1},{25,9},{2,18},{10... | collective-permute-start | bytes 3145736 | tf_op jit(solution)/shard_map/ppermute | solution.py:24
  156.8 5.9 %collective-permute-start.38 = (f32[2,1024]{1,0:T(2,128)S(1)}, f32[2,1024]{1,0:T(2,128)S(1)}, u32[]{:S(2)}, u32[]{:S(2)}) collective-permute-start(f32[2,1024]{1,0:T(2,128)S(1)} %add.473), channel_id=1, source_target_pairs={{0,4},{1,5},{2,6},{3,7},{4,0},{5,1},{6,2},{7,3},{8,12},{9,13},{10,... | collective-permute-start | bytes 24584 | tf_op jit(solution)/shard_map/ppermute | solution.py:24
  157.9 5.4 %collective-permute-start.39 = (f32[2,1024]{1,0:T(2,128)S(1)}, f32[2,1024]{1,0:T(2,128)S(1)}, u32[]{:S(2)}, u32[]{:S(2)}) collective-permute-start(f32[2,1024]{1,0:T(2,128)S(1)} %add.473), channel_id=1, source_target_pairs={{0,6},{1,7},{2,4},{3,5},{4,2},{5,3},{6,0},{7,1},{8,14},{9,15},{10,... | collective-permute-start | bytes 24584 | tf_op jit(solution)/shard_map/ppermute | solution.py:24
  188.0 11.0 %collective-permute-start.49 = (bf16[4,32,2048]{2,1,0:T(8,128)(2,1)S(1)}, bf16[4,32,2048]{2,1,0:T(8,128)(2,1)S(1)}, u32[]{:S(2)}, u32[]{:S(2)}) collective-permute-start(bf16[4,32,2048]{2,1,0:T(8,128)(2,1)S(1)} %slice.160), channel_id=1, source_target_pairs={{0,16},{8,24},{16,0},{24,8},{1,17},{9,25},{17,1},{25,9},{2,18},{10... | collective-permute-start | bytes 1572872 | tf_op jit(solution)/shard_map/ppermute | solution.py:24
  189.4 9.5 %collective-permute-start.50 = (bf16[4,32,2048]{2,1,0:T(8,128)(2,1)S(1)}, bf16[4,32,2048]{2,1,0:T(8,128)(2,1)S(1)}, u32[]{:S(2)}, u32[]{:S(2)}) collective-permute-start(bf16[4,32,2048]{2,1,0:T(8,128)(2,1)S(1)} %slice.162), channel_id=1, source_target_pairs={{0,8},{8,0},{16,24},{24,16},{1,9},{9,1},{17,25},{25,17},{2,10},{10... | collective-permute-start | bytes 1572872 | tf_op jit(solution)/shard_map/ppermute | solution.py:24
  193.3 5.4 %collective-permute-start.48 = (f32[2,1024]{1,0:T(2,128)S(1)}, f32[2,1024]{1,0:T(2,128)S(1)}, u32[]{:S(2)}, u32[]{:S(2)}) collective-permute-start(f32[2,1024]{1,0:T(2,128)S(1)} %add.482), channel_id=1, source_target_pairs={{0,6},{1,7},{2,4},{3,5},{4,2},{5,3},{6,0},{7,1},{8,14},{9,15},{10,... | collective-permute-start | bytes 24584 | tf_op jit(solution)/shard_map/ppermute | solution.py:24
  199.4 15.7 %collective-permute-start.51 = (bf16[1,64,2048]{2,1,0:T(8,128)(2,1)S(1)}, bf16[1,64,2048]{2,1,0:T(8,128)(2,1)S(1)}, u32[]{:S(2)}, u32[]{:S(2)}) collective-permute-start(bf16[1,64,2048]{2,1,0:T(8,128)(2,1)S(1)} %pad_maximum_fusion.7), channel_id=1, source_target_pairs={{0,4},{1,5},{2,6},{3,7},{4,0},{5,1},{6,2},{7,3},{8,12},{9,13},{10,... | collective-permute-start | bytes 786440 | tf_op jit(solution)/shard_map/ppermute | solution.py:24
  200.3 14.8 %collective-permute-start.52 = (bf16[1,64,2048]{2,1,0:T(8,128)(2,1)S(1)}, bf16[1,64,2048]{2,1,0:T(8,128)(2,1)S(1)}, u32[]{:S(2)}, u32[]{:S(2)}) collective-permute-start(bf16[1,64,2048]{2,1,0:T(8,128)(2,1)S(1)} %pad_maximum_fusion.8), channel_id=1, source_target_pairs={{0,2},{1,3},{2,0},{3,1},{4,6},{5,7},{6,4},{7,5},{8,10},{9,11},{10,... | collective-permute-start | bytes 786440 | tf_op jit(solution)/shard_map/ppermute | solution.py:24
  202.0 16.5 %collective-permute-start.53 = (bf16[1,64,2048]{2,1,0:T(8,128)(2,1)S(1)}, bf16[1,64,2048]{2,1,0:T(8,128)(2,1)S(1)}, u32[]{:S(2)}, u32[]{:S(2)}) collective-permute-start(bf16[1,64,2048]{2,1,0:T(8,128)(2,1)S(1)} %pad_maximum_fusion.9), channel_id=1, source_target_pairs={{0,6},{1,7},{2,4},{3,5},{4,2},{5,3},{6,0},{7,1},{8,14},{9,15},{10,... | collective-permute-start | bytes 786440 | tf_op jit(solution)/shard_map/ppermute | solution.py:24
  218.7 8.7 %collective-permute-start.54 = (bf16[16,48,1024]{2,1,0:T(8,128)(2,1)S(1)}, bf16[16,48,1024]{2,1,0:T(8,128)(2,1)S(1)}, u32[]{:S(2)}, u32[]{:S(2)}) collective-permute-start(bf16[16,48,1024]{2,1,0:T(8,128)(2,1)S(1)} %pad_maximum_fusion.2), channel_id=1, source_target_pairs={{0,1},{1,0},{2,3},{3,2},{4,5},{5,4},{6,7},{7,6},{8,9},{9,8},{10,11... | collective-permute-start | bytes 4718600 | tf_op jit(solution)/shard_map/ppermute | solution.py:24
  218.9 19.3 %collective-permute-start.55 = (bf16[1,64,2048]{2,1,0:T(8,128)(2,1)S(1)}, bf16[1,64,2048]{2,1,0:T(8,128)(2,1)S(1)}, u32[]{:S(2)}, u32[]{:S(2)}) collective-permute-start(bf16[1,64,2048]{2,1,0:T(8,128)(2,1)S(1)} %add_convert_fusion.8), channel_id=1, source_target_pairs={{0,4},{1,5},{2,6},{3,7},{4,0},{5,1},{6,2},{7,3},{8,12},{9,13},{10,... | collective-permute-start | bytes 786440 | tf_op jit(solution)/shard_map/ppermute | solution.py:24
  225.4 23.5 %collective-permute-start.56 = (bf16[1,64,2048]{2,1,0:T(8,128)(2,1)S(1)}, bf16[1,64,2048]{2,1,0:T(8,128)(2,1)S(1)}, u32[]{:S(2)}, u32[]{:S(2)}) collective-permute-start(bf16[1,64,2048]{2,1,0:T(8,128)(2,1)S(1)} %add_convert_fusion.8), channel_id=1, source_target_pairs={{0,2},{1,3},{2,0},{3,1},{4,6},{5,7},{6,4},{7,5},{8,10},{9,11},{10,... | collective-permute-start | bytes 786440 | tf_op jit(solution)/shard_map/ppermute | solution.py:24
  225.4 23.5 %collective-permute-start.57 = (bf16[1,64,2048]{2,1,0:T(8,128)(2,1)S(1)}, bf16[1,64,2048]{2,1,0:T(8,128)(2,1)S(1)}, u32[]{:S(2)}, u32[]{:S(2)}) collective-permute-start(bf16[1,64,2048]{2,1,0:T(8,128)(2,1)S(1)} %add_convert_fusion.8), channel_id=1, source_target_pairs={{0,6},{1,7},{2,4},{3,5},{4,2},{5,3},{6,0},{7,1},{8,14},{9,15},{10,... | collective-permute-start | bytes 786440 | tf_op jit(solution)/shard_map/ppermute | solution.py:24
  228.2 20.8 %collective-permute-start.58 = (bf16[4,48,1024]{2,1,0:T(8,128)(2,1)S(1)}, bf16[4,48,1024]{2,1,0:T(8,128)(2,1)S(1)}, u32[]{:S(2)}, u32[]{:S(2)}) collective-permute-start(bf16[4,48,1024]{2,1,0:T(8,128)(2,1)S(1)} %get-tuple-element.221), channel_id=1, source_target_pairs={{0,8},{8,0},{16,24},{24,16},{1,9},{9,1},{17,25},{25,17},{2,10},{10... | collective-permute-start | bytes 1179656 | tf_op jit(solution)/shard_map/ppermute | solution.py:24
  228.7 20.2 %collective-permute-start.59 = (bf16[4,48,1024]{2,1,0:T(8,128)(2,1)S(1)}, bf16[4,48,1024]{2,1,0:T(8,128)(2,1)S(1)}, u32[]{:S(2)}, u32[]{:S(2)}) collective-permute-start(bf16[4,48,1024]{2,1,0:T(8,128)(2,1)S(1)} %get-tuple-element.220), channel_id=1, source_target_pairs={{0,16},{8,24},{16,0},{24,8},{1,17},{9,25},{17,1},{25,9},{2,18},{10... | collective-permute-start | bytes 1179656 | tf_op jit(solution)/shard_map/ppermute | solution.py:24
  238.2 11.6 %collective-permute-start.60 = (bf16[4,48,1024]{2,1,0:T(8,128)(2,1)S(1)}, bf16[4,48,1024]{2,1,0:T(8,128)(2,1)S(1)}, u32[]{:S(2)}, u32[]{:S(2)}) collective-permute-start(bf16[4,48,1024]{2,1,0:T(8,128)(2,1)S(1)} %get-tuple-element.219), channel_id=1, source_target_pairs={{0,24},{8,16},{16,8},{24,0},{1,25},{9,17},{17,9},{25,1},{2,26},{10... | collective-permute-start | bytes 1179656 | tf_op jit(solution)/shard_map/ppermute | solution.py:24
  250.1 12.7 %collective-permute-start.61 = (bf16[4,32,2048]{2,1,0:T(8,128)(2,1)S(1)}, bf16[4,32,2048]{2,1,0:T(8,128)(2,1)S(1)}, u32[]{:S(2)}, u32[]{:S(2)}) collective-permute-start(bf16[4,32,2048]{2,1,0:T(8,128)(2,1)S(1)} %get-tuple-element.223), channel_id=1, source_target_pairs={{0,16},{8,24},{16,0},{24,8},{1,17},{9,25},{17,1},{25,9},{2,18},{10... | collective-permute-start | bytes 1572872 | tf_op jit(solution)/shard_map/ppermute | solution.py:24
  250.3 13.0 %collective-permute-start.62 = (bf16[4,32,2048]{2,1,0:T(8,128)(2,1)S(1)}, bf16[4,32,2048]{2,1,0:T(8,128)(2,1)S(1)}, u32[]{:S(2)}, u32[]{:S(2)}) collective-permute-start(bf16[4,32,2048]{2,1,0:T(8,128)(2,1)S(1)} %get-tuple-element.222), channel_id=1, source_target_pairs={{0,8},{8,0},{16,24},{24,16},{1,9},{9,1},{17,25},{25,17},{2,10},{10... | collective-permute-start | bytes 1572872 | tf_op jit(solution)/shard_map/ppermute | solution.py:24
  252.0 9.5 %collective-permute-start.63 = (bf16[1,48,1024]{2,1,0:T(8,128)(2,1)S(1)}, bf16[1,48,1024]{2,1,0:T(8,128)(2,1)S(1)}, u32[]{:S(2)}, u32[]{:S(2)}) collective-permute-start(bf16[1,48,1024]{2,1,0:T(8,128)(2,1)S(1)} %get-tuple-element.236), channel_id=1, source_target_pairs={{0,4},{1,5},{2,6},{3,7},{4,0},{5,1},{6,2},{7,3},{8,12},{9,13},{10,... | collective-permute-start | bytes 294920 | tf_op jit(solution)/shard_map/ppermute | solution.py:24
  252.6 8.9 %collective-permute-start.64 = (bf16[1,48,1024]{2,1,0:T(8,128)(2,1)S(1)}, bf16[1,48,1024]{2,1,0:T(8,128)(2,1)S(1)}, u32[]{:S(2)}, u32[]{:S(2)}) collective-permute-start(bf16[1,48,1024]{2,1,0:T(8,128)(2,1)S(1)} %get-tuple-element.235), channel_id=1, source_target_pairs={{0,2},{1,3},{2,0},{3,1},{4,6},{5,7},{6,4},{7,5},{8,10},{9,11},{10,... | collective-permute-start | bytes 294920 | tf_op jit(solution)/shard_map/ppermute | solution.py:24
  254.7 6.9 %collective-permute-start.65 = (bf16[1,48,1024]{2,1,0:T(8,128)(2,1)S(1)}, bf16[1,48,1024]{2,1,0:T(8,128)(2,1)S(1)}, u32[]{:S(2)}, u32[]{:S(2)}) collective-permute-start(bf16[1,48,1024]{2,1,0:T(8,128)(2,1)S(1)} %get-tuple-element.234), channel_id=1, source_target_pairs={{0,6},{1,7},{2,4},{3,5},{4,2},{5,3},{6,0},{7,1},{8,14},{9,15},{10,... | collective-permute-start | bytes 294920 | tf_op jit(solution)/shard_map/ppermute | solution.py:24
  263.3 23.4 %collective-permute-start.66 = (bf16[8,32,2048]{2,1,0:T(8,128)(2,1)S(1)}, bf16[8,32,2048]{2,1,0:T(8,128)(2,1)S(1)}, u32[]{:S(2)}, u32[]{:S(2)}) collective-permute-start(bf16[8,32,2048]{2,1,0:T(8,128)(2,1)S(1)} %pad_maximum_fusion.4), channel_id=1, source_target_pairs={{0,8},{8,0},{16,24},{24,16},{1,9},{9,1},{17,25},{25,17},{2,10},{10... | collective-permute-start | bytes 3145736 | tf_op jit(solution)/shard_map/ppermute | solution.py:24
  265.0 23.1 %collective-permute-start.67 = (bf16[8,32,2048]{2,1,0:T(8,128)(2,1)S(1)}, bf16[8,32,2048]{2,1,0:T(8,128)(2,1)S(1)}, u32[]{:S(2)}, u32[]{:S(2)}) collective-permute-start(bf16[8,32,2048]{2,1,0:T(8,128)(2,1)S(1)} %pad_maximum_fusion.5), channel_id=1, source_target_pairs={{0,16},{8,24},{16,0},{24,8},{1,17},{9,25},{17,1},{25,9},{2,18},{10... | collective-permute-start | bytes 3145736 | tf_op jit(solution)/shard_map/ppermute | solution.py:24
  265.5 7.7 %collective-permute-start.68 = (bf16[1,48,1024]{2,1,0:T(8,128)(2,1)S(1)}, bf16[1,48,1024]{2,1,0:T(8,128)(2,1)S(1)}, u32[]{:S(2)}, u32[]{:S(2)}) collective-permute-start(bf16[1,48,1024]{2,1,0:T(8,128)(2,1)S(1)} %get-tuple-element.211), channel_id=1, source_target_pairs={{0,4},{1,5},{2,6},{3,7},{4,0},{5,1},{6,2},{7,3},{8,12},{9,13},{10,... | collective-permute-start | bytes 294920 | tf_op jit(solution)/shard_map/ppermute | solution.py:24
  267.0 6.2 %collective-permute-start.69 = (bf16[1,48,1024]{2,1,0:T(8,128)(2,1)S(1)}, bf16[1,48,1024]{2,1,0:T(8,128)(2,1)S(1)}, u32[]{:S(2)}, u32[]{:S(2)}) collective-permute-start(bf16[1,48,1024]{2,1,0:T(8,128)(2,1)S(1)} %get-tuple-element.211), channel_id=1, source_target_pairs={{0,2},{1,3},{2,0},{3,1},{4,6},{5,7},{6,4},{7,5},{8,10},{9,11},{10,... | collective-permute-start | bytes 294920 | tf_op jit(solution)/shard_map/ppermute | solution.py:24
  268.0 6.5 %collective-permute-start.70 = (bf16[1,48,1024]{2,1,0:T(8,128)(2,1)S(1)}, bf16[1,48,1024]{2,1,0:T(8,128)(2,1)S(1)}, u32[]{:S(2)}, u32[]{:S(2)}) collective-permute-start(bf16[1,48,1024]{2,1,0:T(8,128)(2,1)S(1)} %get-tuple-element.211), channel_id=1, source_target_pairs={{0,6},{1,7},{2,4},{3,5},{4,2},{5,3},{6,0},{7,1},{8,14},{9,15},{10,... | collective-permute-start | bytes 294920 | tf_op jit(solution)/shard_map/ppermute | solution.py:24
  288.6 8.0 %collective-permute-start.72 = (bf16[16,32,2048]{2,1,0:T(8,128)(2,1)S(1)}, bf16[16,32,2048]{2,1,0:T(8,128)(2,1)S(1)}, u32[]{:S(2)}, u32[]{:S(2)}) collective-permute-start(bf16[16,32,2048]{2,1,0:T(8,128)(2,1)S(1)} %pad_maximum_fusion.low_ref), channel_id=1, source_target_pairs={{0,1},{1,0},{2,3},{3,2},{4,5},{5,4},{6,7},{7,6},{8,9},{9,8},{10,11... | collective-permute-start | bytes 6291464 | tf_op jit(solution)/shard_map/ppermute | solution.py:24
  289.2 12.0 %collective-permute-start.73 = (bf16[4,48,1024]{2,1,0:T(8,128)(2,1)S(1)}, bf16[4,48,1024]{2,1,0:T(8,128)(2,1)S(1)}, u32[]{:S(2)}, u32[]{:S(2)}) collective-permute-start(bf16[4,48,1024]{2,1,0:T(8,128)(2,1)S(1)} %pad_maximum_fusion.6), channel_id=1, source_target_pairs={{0,8},{8,0},{16,24},{24,16},{1,9},{9,1},{17,25},{25,17},{2,10},{10... | collective-permute-start | bytes 1179656 | tf_op jit(solution)/shard_map/ppermute | solution.py:24
  289.8 19.2 %collective-permute-start.74 = (bf16[4,48,1024]{2,1,0:T(8,128)(2,1)S(1)}, bf16[4,48,1024]{2,1,0:T(8,128)(2,1)S(1)}, u32[]{:S(2)}, u32[]{:S(2)}) collective-permute-start(bf16[4,48,1024]{2,1,0:T(8,128)(2,1)S(1)} %pad_maximum_fusion.6), channel_id=1, source_target_pairs={{0,16},{8,24},{16,0},{24,8},{1,17},{9,25},{17,1},{25,9},{2,18},{10... | collective-permute-start | bytes 1179656 | tf_op jit(solution)/shard_map/ppermute | solution.py:24
  290.5 18.5 %collective-permute-start.75 = (bf16[4,48,1024]{2,1,0:T(8,128)(2,1)S(1)}, bf16[4,48,1024]{2,1,0:T(8,128)(2,1)S(1)}, u32[]{:S(2)}, u32[]{:S(2)}) collective-permute-start(bf16[4,48,1024]{2,1,0:T(8,128)(2,1)S(1)} %pad_maximum_fusion.6), channel_id=1, source_target_pairs={{0,24},{8,16},{16,8},{24,0},{1,25},{9,17},{17,9},{25,1},{2,26},{10... | collective-permute-start | bytes 1179656 | tf_op jit(solution)/shard_map/ppermute | solution.py:24
  (62 other events, 470.3 us)

commit v5 on v4

--- a/solution.py
+++ b/solution.py
@@ -97,11 +97,11 @@
     return [(bits[0][0], mask) for mask in masks[1:]]
 
 
-def spread_kernel(own_ref, low_ref, high_ref, *out_refs):
+def spread_kernel(order, own_ref, low_ref, high_ref, *out_refs):
     half = low_ref.shape[0]
     rows = out_refs[0].shape[1]
     for part in range(2 * half):
-        at = jnp.bitwise_xor(own_ref[0], part)
+        at = jnp.bitwise_xor(own_ref[0], order[part])
         ref = low_ref if part < half else high_ref
         out_refs[0][at] = ref[part % half, :rows, :].astype(jnp.float32)
         if len(out_refs) > 1:
@@ -111,13 +111,13 @@
                 out_refs[1][row, pl.ds(at, 1), :] = extra[row : row + 1, :]
 
 
-def plain_order(low, high, own, rows, more):
+def plain_order(low, high, own, order, rows, more):
     half, deep, cols = low.shape
     width = 512
     shapes = [(2 * half, rows)] + ([(more, 2 * half)] if more else [])
     block = pl.BlockSpec((half, deep, width), lambda i: (0, 0, i))
     return pl.pallas_call(
-        spread_kernel,
+        functools.partial(spread_kernel, order),
         grid=(cols // width,),
         in_specs=[pl.BlockSpec(memory_space=pltpu.SMEM), block, block],
         out_specs=[pl.BlockSpec(shape + (width,), lambda i: (0, 0, i)) for shape in shapes],
@@ -184,7 +184,11 @@
             self.send()
 
     def finish(self, rows, more=0):
-        return plain_order(*self.pieces, self.own, rows, more)
+        cut = [bit for bits in self.rounds for bit in bits]
+        joined = [bit for bits in reversed(self.joins) for bit in bits]
+        places = [1 << (len(cut) - 1 - cut.index(bit)) for bit in reversed(joined)]
+        order = [sum(place for at, place in enumerate(places) if part >> at & 1) for part in range(PARTS)]
+        return plain_order(*self.pieces, self.own, order, rows, more)
 
 
 def join(grads):
@@ -279,21 +283,26 @@
     return (iota((count, count), 1) == image * cols + 2 * col + parity).astype(WIDE).astype(LOW)
 
 
-def shifted_sums(ref, valid_ref, base, planes, images, quarter):
-    width = ref.shape[1]
-    total = jnp.zeros((8, width), WIDE)
-    square = jnp.zeros((8, width), WIDE)
-    for image in range(images):
-        first = jnp.zeros((8, width), WIDE)
-        second = jnp.zeros((8, width), WIDE)
-        for plane in range(planes):
-            at = (plane * images + image) * quarter
-            gap = ref[at : at + quarter, :] - base
-            first += fold(gap)
-            second += fold(gap * gap)
-        total += first * valid_ref[image]
-        square += second * valid_ref[image]
-    return close(total), close(square)
+class Sums:
+    def __init__(self, valid_ref, base, quarter):
+        self.valid_ref, self.base, self.quarter = valid_ref, base, quarter
+        self.total = jnp.zeros((8, base.shape[1]), WIDE)
+        self.square = jnp.zeros((8, base.shape[1]), WIDE)
+
+    def add(self, ref, start, cols):
+        for image in range(self.valid_ref.shape[0]):
+            at = start + image * self.quarter
+            first = jnp.zeros(self.total.shape, WIDE)
+            second = jnp.zeros(self.total.shape, WIDE)
+            for span in spans(self.quarter, 32):
+                gap = ref[at + span.start : at + span.stop, cols] - self.base
+                first += fold(gap)
+                second += fold(gap * gap)
+            self.total += first * self.valid_ref[image]
+            self.square += second * self.valid_ref[image]
+
+    def close(self):
+        return close(self.total), close(self.square)
 
 
 def moments_of(sums, base, count):
@@ -340,12 +349,14 @@
 
     @pl.when(step >= lead)
     def _():
+        count = valid * float(pixels)
+        base = dot(kept_ref[0:16, :], w_ref[...])[0:1, :]
+        sums = Sums(valid_ref, base, quarter)
         for plane in range(4):
-            at = slice(plane * plane_rows, (plane + 1) * plane_rows)
-            reduced_ref[at, :] = dot(kept_ref[at, :], w_ref[...])
-        count = valid * float(pixels)
-        base = reduced_ref[0:1, :]
-        total, square = shifted_sums(reduced_ref, valid_ref, base, 4, images, quarter)
+            start = plane * plane_rows
+            reduced_ref[start : start + plane_rows, :] = dot(kept_ref[start : start + plane_rows, :], w_ref[...])
+            sums.add(reduced_ref, start, slice(None))
+        total, square = sums.close()
         stats_ref[0:1, :] = jnp.full(base.shape, count, WIDE)
         stats_ref[1:2, :] = base + total / count
         stats_ref[2:3, :] = jnp.maximum(square - total * (total / count), 0.0)
@@ -358,14 +369,18 @@
         out_ref[jnp.bitwise_xor(own_ref[0], part)] = turned[part * rows : (part + 1) * rows, :]
 
 
+def product_sums(quarter, valid_ref, x_ref, w_ref, base, out_ref, sums_ref):
+    for cols in spans(out_ref.shape[1], 256):
+        out_ref[:, cols] = dot(x_ref[...], w_ref[:, cols])
+        sums = Sums(valid_ref, base[:, cols], quarter)
+        sums.add(out_ref, 0, cols)
+        sums_ref[0:1, cols], sums_ref[1:2, cols] = sums.close()
+
+
 def project_kernel(quarter, valid_ref, x_ref, w_ref, sampled_ref, out_ref, sums_ref):
-    out_ref[...] = dot(x_ref[...], w_ref[...])
     base = row_of(sampled_ref[...], w_ref[...])
-    images = out_ref.shape[0] // quarter
-    total, square = shifted_sums(out_ref, valid_ref, base, 1, images, quarter)
-    sums_ref[0:1, :] = total
-    sums_ref[1:2, :] = square
     sums_ref[2:3, :] = base
+    product_sums(quarter, valid_ref, x_ref, w_ref, base, out_ref, sums_ref)
 
 
 def group_mask(width):
@@ -392,43 +407,44 @@
     return silu((values - mean) * scale + shift)
 
 
-def windows(planes, odd, halves):
-    even_even, even_odd, even_moved = planes
+def plane_windows(plane, even, odd):
     images, deep, half_cols, width = odd[0].shape
     tall = deep - 1
 
     def part(ref, at):
         return ref[:, at : at + tall, :, :].reshape(images * tall * half_cols, width)
 
-    result = []
-    for row_tap in range(TAPS):
-        if row_tap == 1:
-            result += [even_moved[...], even_even[...], even_odd[...]]
-        else:
-            at = 0 if row_tap == 0 else 1
-            result += [part(odd[2], at), part(odd[0], at), part(odd[1], at)]
-    return result
-
-
-def store_hidden(dims, get, halo, even, odd):
+    if plane == 0:
+        return [(4, even[0][...])]
+    if plane == 1:
+        return [(3, even[2][...]), (5, even[1][...])]
+    if plane == 2:
+        return [(1, part(odd[0], 0)), (7, part(odd[0], 1))]
+    return [(0, part(odd[2], 0)), (2, part(odd[1], 0)), (6, part(odd[2], 1)), (8, part(odd[1], 1))]
+
+
+def store_plane(dims, plane, get, halo, even, odd):
     images, tall, half_cols = dims
     quarter = tall * half_cols
+
+    def deep(values):
+        return values.astype(LOW).reshape(values.shape[0] // half_cols, half_cols, values.shape[1])
+
     for image in range(images):
         at = slice(image * quarter, (image + 1) * quarter)
-        even[0][at, :] = get(0, image).astype(LOW)
-        values = get(1, image)
-        even[1][at, :] = values.astype(LOW)
-        even[2][at, :] = shift_columns(values, half_cols, 1).astype(LOW)
-        values = get(2, image)
-        width = values.shape[1]
-        odd[0][image, 1:, :, :] = values.astype(LOW).reshape(tall, half_cols, width)
-        values = get(3, image)
-        odd[1][image, 1:, :, :] = values.astype(LOW).reshape(tall, half_cols, width)
-        odd[2][image, 1:, :, :] = shift_columns(values, half_cols, 1).astype(LOW).reshape(tall, half_cols, width)
-    width = halo[0].shape[1]
-    odd[0][:, 0, :, :] = halo[0].astype(LOW).reshape(images, half_cols, width)
-    odd[1][:, 0, :, :] = halo[1].astype(LOW).reshape(images, half_cols, width)
-    odd[2][:, 0, :, :] = shift_columns(halo[1], half_cols, 1).astype(LOW).reshape(images, half_cols, width)
+        values = get(image)
+        if plane < 2:
+            even[plane][at, :] = values.astype(LOW)
+        else:
+            odd[plane - 2][image, 1:, :, :] = deep(values)
+        if plane == 1:
+            even[2][at, :] = shift_columns(values, half_cols, 1).astype(LOW)
+        if plane == 3:
+            odd[2][image, 1:, :, :] = deep(shift_columns(values, half_cols, 1))
+    if plane >= 2:
+        odd[plane - 2][:, 0, :, :] = deep(halo)
+    if plane == 3:
+        odd[2][:, 0, :, :] = deep(shift_columns(halo, half_cols, 1))
 
 
 def window_scratch(images, tall, half_cols, width):
@@ -471,26 +487,36 @@
     edge_ref[...] = edge.astype(LOW)
     half = edge.shape[0] // 2
 
-    def get(plane, image):
-        at = plane * plane_rows + image * quarter
-        return activate(reduced_ref[at : at + quarter, :], mean, scale, shift)
-
     even, odd = buffers[:3], buffers[3:]
-    store_hidden(dims, get, (edge[:half], edge[half:]), even, odd)
     mask = group_mask(width)
-    total = None
-    for tap, window in enumerate(windows(even, odd, half_cols)):
-        term = dot(window, block_weights(group_ref, mask, tap))
-        total = term if total is None else total + term
-    grouped_ref[...] = total
+    for plane in range(4):
+
+        def get(image):
+            start = plane * plane_rows + image * quarter
+            parts = []
+            for span in spans(quarter, 32):
+                part = reduced_ref[start + span.start : start + span.stop, :]
+                parts.append(activate(part, mean, scale, shift))
+            return jnp.concatenate(parts, axis=0)
+
+        halo = (None, None, edge[:half], edge[half:])[plane]
+        store_plane(dims, plane, get, halo, even, odd)
+        total = None
+        for tap, window in plane_windows(plane, even, odd):
+            term = dot(window, block_weights(group_ref, mask, tap))
+            total = term if total is None else total + term
+        if plane == 0:
+            grouped_ref[...] = total
+        else:
+            grouped_ref[...] += total
     kernel = group_ref[0:GW, :].astype(WIDE)
     for tap in range(1, TAPS * TAPS):
         kernel = kernel + group_ref[tap * GW : (tap + 1) * GW, :].astype(WIDE)
     kernel = jnp.concatenate([kernel.astype(LOW)] * (width // GW), axis=0) * mask
     base = row_of(silu(shift), kernel)
-    total, square = shifted_sums(grouped_ref, valid_ref, base, 1, images, quarter)
-    sums_ref[0:1, :] = total
-    sums_ref[1:2, :] = square
+    sums = Sums(valid_ref, base, quarter)
+    sums.add(grouped_ref, 0, slice(None))
+    sums_ref[0:1, :], sums_ref[1:2, :] = sums.close()
     base_ref[...] = base
     for image in range(images):
         at = image * quarter
@@ -521,12 +547,8 @@
         for span in spans(grouped_ref.shape[0], 16):
             hidden_ref[span, :] = activate(grouped_ref[span, :], mean, scale, shift).astype(LOW)
 
-    out_ref[...] = dot(hidden_ref[...], w_ref[...])
     base = row_of(silu(shift), w_ref[...])
-    images = out_ref.shape[0] // quarter
-    total, square = shifted_sums(out_ref, valid_ref, base, 1, images, quarter)
-    sums_ref[0:1, :] = total
-    sums_ref[1:2, :] = square
+    product_sums(quarter, valid_ref, hidden_ref, w_ref, base, out_ref, sums_ref)
     sums_ref[2:4, :] = side_ref[0:2, :]
     base_ref[0:1, :] = base
     base_ref[1:2, :] = side_ref[2:3, :]
@@ -611,23 +633,26 @@
     gain_two = affine[2:3, :] * moments[3]
     pull_one = gain_one * moments[1] * sums[1:2, :]
     pull_two = gain_two * moments[3] * sums[2:3, :]
-    for span in spans(rows, size):
-        first = expanded_ref[span, :] - moments[0]
-        second = projected_ref[span, :] - moments[2]
-        valid = valid_ref[span.start // quarter]
-        _, slope = silu_pair(first * one + second * two + both)
-        upstream = (cot_ref[span, :].astype(WIDE) * 0.5) * slope - sums[0:1, :]
-        d_expanded_ref[span, :] = (upstream * (gain_one * valid) - first * (pull_one * valid)).astype(LOW)
-        d_projected_ref[span, :] = (upstream * (gain_two * valid) - second * (pull_two * valid)).astype(LOW)
-    store_halves(sampled_ref[...], d_projected_ref[...], proj_low_ref, proj_high_ref)
-    store_halves(hidden_ref[...], d_expanded_ref[...], expand_low_ref, expand_high_ref)
-
-
-def store_halves(turned, grads, low_ref, high_ref):
-    half = low_ref.shape[0]
+    for cols in spans(width, 256):
+        for span in spans(rows, size):
+            first = expanded_ref[span, cols] - moments[0][:, cols]
+            second = projected_ref[span, cols] - moments[2][:, cols]
+            valid = valid_ref[span.start // quarter]
+            _, slope = silu_pair(first * one[:, cols] + second * two[:, cols] + both[:, cols])
+            upstream = (cot_ref[span, cols].astype(WIDE) * 0.5) * slope - sums[0:1, cols]
+            along = first * (pull_one[:, cols] * valid)
+            d_expanded_ref[span, cols] = (upstream * (gain_one[:, cols] * valid) - along).astype(LOW)
+            along = second * (pull_two[:, cols] * valid)
+            d_projected_ref[span, cols] = (upstream * (gain_two[:, cols] * valid) - along).astype(LOW)
+        store_halves(sampled_ref, d_projected_ref[:, cols], proj_low_ref, proj_high_ref, cols)
+        store_halves(hidden_ref, d_expanded_ref[:, cols], expand_low_ref, expand_high_ref, cols)
+
+
+def store_halves(turned_ref, grads, low_ref, high_ref, cols):
+    half, rows, _ = low_ref.shape
     for at, ref in ((0, low_ref), (half, high_ref)):
-        left = turned[at : at + half].reshape(half * turned.shape[1], turned.shape[2])
-        ref[...] = dot(left, grads).astype(LOW).reshape(ref.shape)
+        left = turned_ref[at : at + half].reshape(half * rows, turned_ref.shape[2])
+        ref[:, :, cols] = dot(left, grads).astype(LOW).reshape(half, rows, grads.shape[1])
 
 
 def back_two_kernel(
@@ -725,48 +750,53 @@
     weights = [block_weights(group_ref, half_mask, tap) for tap in range(TAPS * TAPS)]
     here, left = part(below[0], 0), part(below[1], 0)
     next_here, next_left = part(below[0], 1), part(below[1], 1)
-    out_ref[0:plane_rows, :] = dot_nt(here, weights[4])
-    out_ref[plane_rows : 2 * plane_rows, :] = dot_nt(here, weights[5]) + dot_nt(left, weights[3])
-    out_ref[2 * plane_rows : 3 * plane_rows, :] = dot_nt(here, weights[7]) + dot_nt(next_here, weights[1])
-    out_ref[3 * plane_rows : 4 * plane_rows, :] = (
-        dot_nt(here, weights[8])
-        + dot_nt(left, weights[6])
-        + dot_nt(next_here, weights[2])
-        + dot_nt(next_left, weights[0])
+    terms = (
+        [(here, 4)],
+        [(here, 5), (left, 3)],
+        [(here, 7), (next_here, 1)],
+        [(here, 8), (left, 6), (next_here, 2), (next_left, 0)],
     )
 
+    turned = here.T
+    picked = jnp.bitwise_xor(iota((GW, 1), 0), own_ref[0])
+    _, channel = over(iota((1, width), 1), GW)
+    one_hot = (channel == picked).astype(WIDE).astype(LOW)
     mean_one = moments_one_ref[0:1, :]
     inv_one = lax.rsqrt(moments_one_ref[1:2, :] / count_in + EPS)
     scale = 0.5 * affine_one_ref[0:1, :] * inv_one
     shift = 0.5 * affine_one_ref[1:2, :]
     totals = [jnp.zeros((8, width), WIDE) for _ in range(2)]
-
-    def get(plane, image):
-        start = plane * plane_rows + image * quarter
-        parts = []
-        for span in spans(quarter, 32):
-            at = slice(start + span.start, start + span.stop)
-            gap = reduced_ref[at, :] - mean_one
-            value, slope = silu_pair(gap * scale + shift)
-            grad = out_ref[at, :] * slope
-            out_ref[at, :] = grad
-            totals[0] += fold(grad)
-            totals[1] += fold(grad * gap)
-            parts.append(value)
-        return jnp.concatenate(parts, axis=0)
-
     half = edge_ref.shape[0] // 2
     edge = edge_ref[...].astype(WIDE)
-    store_hidden(dims, get, (edge[:half], edge[half:]), even, odd)
+    for plane in range(4):
+        base = plane * plane_rows
+        total = None
+        for grads, tap in terms[plane]:
+            term = dot_nt(grads, weights[tap])
+            total = term if total is None else total + term
+        out_ref[base : base + plane_rows, :] = total
+
+        def get(image):
+            start = base + image * quarter
+            parts = []
+            for span in spans(quarter, 32):
+                at = slice(start + span.start, start + span.stop)
+                gap = reduced_ref[at, :] - mean_one
+                value, slope = silu_pair(gap * scale + shift)
+                grad = out_ref[at, :] * slope
+                out_ref[at, :] = grad
+                totals[0] += fold(grad)
+                totals[1] += fold(grad * gap)
+                parts.append(value)
+            return jnp.concatenate(parts, axis=0)
+
+        halo = (None, None, edge[:half], edge[half:])[plane]
+        store_plane(dims, plane, get, halo, even, odd)
+        for tap, window in plane_windows(plane, even, odd):
+            full = dot(turned, window).astype(LOW) * mask
+            grad_group_ref[tap] = dot_nt(one_hot, full).astype(LOW)
     sums_ref[0:1, :] = close(totals[0])
     sums_ref[1:2, :] = close(totals[1]) * inv_one
-    turned = here.T
-    picked = jnp.bitwise_xor(iota((GW, 1), 0), own_ref[0])
-    _, channel = over(iota((1, width), 1), GW)
-    one_hot = (channel == picked).astype(WIDE).astype(LOW)
-    for tap, window in enumerate(windows(even, odd, half_cols)):
-        full = dot(turned, window).astype(LOW) * mask
-        grad_group_ref[tap] = dot_nt(one_hot, full).astype(LOW)
 
 
 def reduced_back_kernel(
@@ -898,7 +928,7 @@
     back_rounds = sum_plan(("ha", "ba"))
 
     halo_images = shifted(images_in[:, -1], "ha", 1).reshape(images * cols, chans)
-    lead = images // 2
+    lead = images // 4
     planes, reduced, stats, sampled = call(
         functools.partial(reduce_kernel, (images, image_rows, cols), lead),
         lead + steps,
@@ -932,8 +962,8 @@
             (0, 2 << 20),
         )(own, value if at is None else hbm(value))[0]
 
-    planes_turned = [turn(planes, plane, own_two) for plane in range(4)]
-    stats, *planes_turned = tie(stats, *planes_turned)
+    sampled_turned = turn(planes, 0, own_two)
+    stats, sampled_turned = tie(stats, sampled_turned)
     count_in, moments_one, sampled_mean = stats[0, 0], stats[1:3], stats[3:4]
     scalars = jnp.stack([count_in, count_in / 4.0, has_upper, has_lower])
 
@@ -1055,10 +1085,10 @@
         sums_out,
         cot,
         hidden_turned,
-        planes_turned[0],
+        sampled_turned,
     )
-    expand_sum = Gradient(halves[:2], plain)
-    proj_sum = Gradient(halves[2:], swapped)
+    expand_sum = Gradient(halves[:2], plain, plain[:3] + ([DEEP_ONE], [DEEP_TWO]))
+    proj_sum = Gradient(halves[2:], swapped, swapped[:3] + ([DEEP_ONE], [DEEP_TWO]))
     pair = [expand_sum, proj_sum]
     for grad in pair:
         grad.send()
@@ -1083,11 +1113,6 @@
     sums, first_row = arrive(pair, sums, first_row)
     below_grad = shifted(first_row, "ha", -1)
     sums = mesh_sum(sums, back_rounds[1:2])
-    sums, below_grad = arrive(pair, sums, below_grad)
-    for grad in pair:
-        grad.step()
-    grads_two = mesh_sum(sums, back_rounds[2:])
-    (d_projected,) = tie(d_projected)
     side_grad = call(
         side_kernel,
         1,
@@ -1096,7 +1121,11 @@
         [((rows, chans), WIDE)],
         (2 * rows * chans * wide, 8 << 20),
     )(d_projected, proj_w)[0]
-
+    planes_turned = [sampled_turned] + [turn(planes, plane, own_two) for plane in range(1, 4)]
+    sums, below_grad, side_grad, *planes_turned = arrive(pair, sums, below_grad, side_grad, *planes_turned)
+    for grad in pair:
+        grad.step()
+    grads_two = mesh_sum(sums, back_rounds[2:])
     deep = pltpu.VMEM((images, tall + 1, half_cols, block), LOW)
     grads_two, side_grad = tie(grads_two, side_grad)
     grad_one, sums, parts_group = call(
@@ -1178,46 +1207,41 @@
     reduce_sum = Gradient(halves, short)
     reduce_sum.send()
 
-    def images_back(d_part, side_part, half, before):
-        part = images // 2
-        kept = [] if before is None else [before]
-        return pl.pallas_call(
+    def images_back(d_part, side_part):
+        return call(
             functools.partial(images_back_kernel, (image_rows, cols)),
-            grid=(part,),
-            in_specs=[
-                pl.BlockSpec((4, None, quarter, mid), lambda i: (0, i + half * part, 0, 0)),
+            images,
+            [
+                pl.BlockSpec((4, None, quarter, mid), lambda i: (0, i, 0, 0)),
                 whole((chans, mid)),
-                pl.BlockSpec((quarter, chans), lambda i: (i + half * part, 0)),
-            ]
-            + [pl.BlockSpec(memory_space=pl.ANY)] * len(kept),
-            out_specs=pl.BlockSpec((None, image_rows * cols, chans), lambda i: (i + half * part, 0, 0)),
-            out_shape=place((images, image_rows * cols, chans), LOW),
-            input_output_aliases={3: 0} if kept else {},
-            scratch_shapes=[pltpu.VMEM((image_rows * cols, image_rows * cols), LOW)],
-            compiler_params=pltpu.CompilerParams(vmem_limit_bytes=VMEM_LIMIT),
-            cost_estimate=pl.CostEstimate(
-                flops=pixels * mid * chans, bytes_accessed=8 << 20, transcendentals=0
-            ),
-        )(d_part, reduce_w, side_part, *kept)
-
-    d_reduced = d_reduced.reshape(4, images, quarter, mid)
+                pl.BlockSpec((quarter, chans), lambda i: (i, 0)),
+            ],
+            [pl.BlockSpec((None, image_rows * cols, chans), lambda i: (i, 0, 0))],
+            [((images, image_rows * cols, chans), LOW)],
+            (2 * pixels * mid * chans, 16 << 20),
+            [pltpu.VMEM((image_rows * cols, image_rows * cols), LOW)],
+        )(d_part, reduce_w, side_part)[0]
+
+    everyone = pair + [reduce_sum]
     both.step()
-    (d_reduced,) = arrive([reduce_sum], d_reduced)
+    arrive([reduce_sum])
     reduce_sum.step()
-    grad_images = images_back(d_reduced, side_grad, 0, None)
-    grad_images, both.got[0] = tie(grad_images, both.got[0])
-    grad_images = images_back(d_reduced, side_grad, 1, grad_images)
-    (grad_images,) = arrive([both, reduce_sum], grad_images)
+    both.got[0], *reduce_sum.got[:2] = tie(both.got[0], *reduce_sum.got[:2])
+    both.step()
+    arrive([both, reduce_sum])
     both.take()
     part_again(both, pair)
     for grad in pair:
         grad.send()
-    everyone = pair + [reduce_sum]
     reduce_sum.step()
-    while pair[0].left() > 1:
-        arrive(everyone)
-        for grad in everyone:
-            grad.step()
+    (d_reduced,) = arrive(everyone, d_reduced)
+    for grad in everyone:
+        grad.step()
+    d_reduced = d_reduced.reshape(4, images, quarter, mid)
+    grad_images = images_back(d_reduced, side_grad)
+    (grad_images,) = arrive(everyone, grad_images)
+    for grad in everyone:
+        grad.step()
     done = []
     for grad, width in zip(pair, (mid, chans)):
         if done:
@@ -1227,8 +1251,7 @@
     grad_expand, grad_proj = done
     (grad_proj,) = arrive([reduce_sum], grad_proj)
     reduce_sum.step()
-    while reduce_sum.left():
-        reduce_sum.step()
+    reduce_sum.take()
     grad_reduce, grad_group = reduce_sum.finish(chans // PARTS, TAPS * TAPS)
     return (
         output.reshape(cotangent.shape),

time: 317 us -> 314 us (level)
  Pallas kernels: 110 us -> 106 us
  starting transfers between devices: 88.8 us -> 92.4 us
    ppermute x74 -> x73, waiting for transfers between devices: 83.4 us -> 90.3 us  [exchange(): return lax.ppermute(value, axis, [(i, i ^ mask) for i in range(peers)])]
    ppermute x3, waiting for transfers between devices: 6.14 us -> 0.01 us  [shifted(): return lax.ppermute(value, axis, pairs)]
    ppermute x74 -> x73, starting transfers between devices: 81.1 us -> 84.6 us  [exchange(): return lax.ppermute(value, axis, [(i, i ^ mask) for i in range(peers)])]
    unnamed x72 -> x64, local copies, waits for them, and re-layouts: 9.93 us -> 7.82 us
    pallas_call x5 -> x4, Pallas kernels: 20.2 us -> 19.4 us  [the longest x3 10.5 us: plain_order(): pl.pallas_call(functools.partial(spread_kernel, order), grid=(cols // wid...]
  transfers between devices with their start and end apart: 77 -> 76, of which waited for: 44 -> 49; matrix products, arithmetic and copies ran while one was open for 2% -> 1% of each run, Pallas kernels for 24% -> 23%
where the time goes in v5:
time: 314 us; the launch traced here: 313 us
  Pallas kernels  106 us (34%)
  starting transfers between devices  92.4 us (29%)
  waiting for transfers between devices  90.3 us (29%)
  local copies, waits for them, and re-layouts  12.4 us (4%)
  other arithmetic  9.28 us (3%)
    ppermute x73, waiting for transfers between devices, exchange(): return lax.ppermute(value, axis, [(i, i ^ mask) for i in range(peers)])  90.3 us
    ppermute x73, starting transfers between devices, exchange(): return lax.ppermute(value, axis, [(i, i ^ mask) for i in range(peers)])  84.6 us
    pallas_call x1, Pallas kernels, per_device(): call(functools.partial(conv_back_kernel, (images, tall, half_cols)), step...  15 us
    pallas_call x1, Pallas kernels, per_device(): call(functools.partial(reduce_kernel, (images, image_rows, cols), lead),...  11.6 us
    pallas_call x3, Pallas kernels, plain_order(): pl.pallas_call(functools.partial(spread_kernel, order), grid=(cols // wid...  10.5 us
    pallas_call x1, Pallas kernels, per_device(): call(functools.partial(weights_kernel, 16), strips, [SCALARS, SCALARS, wi...  10.2 us
    pallas_call x1, Pallas kernels, per_device(): call(functools.partial(reduced_back_kernel, 16), steps, [SCALARS, SCALARS...  9.62 us
    pallas_call x1, Pallas kernels, images_back(): call(functools.partial(images_back_kernel, (image_rows, cols)), images, [...  8.85 us
  transfers between devices with their start and end apart: 76, of which 49 were waited for; matrix products, arithmetic and copies ran while one was open for 1% of the time, Pallas kernels for 23%

profile of v5, /device:TPU:0, one launch (start us, length us, event | category | flops | bytes accessed | tf_op | source)
XLA Modules:
  0.0 313.0 jit_solution(11283708443400959315)
XLA Ops:
  1.7 4.9 %collective-permute-start = (bf16[8,32,1024]{2,1,0:T(8,128)(2,1)S(1)}, bf16[8,32,1024]{2,1,0:T(8,128)(2,1)S(1)}, u32[]{:S(2)}, u32[]{:S(2)}) collective-permute-start(bf16[8,32,1024]{2,1,0:T(8,128)(2,1)S(1)} %slice_bitcast_fusion), channel_id=1, source_target_pairs={{0,8},{8,16},{16,24},{1,9},{9,17},{17,25},{2,10},{10,18},{18,26},{... | collective-permute-start | bytes 1572872 | tf_op jit(solution)/shard_map/ppermute | solution.py:19
  7.3 11.6 %shard_map.254 = (bf16[4,8,64,1024]{3,2,1,0:T(8,128)(2,1)}, f32[2048,1024]{1,0:T(8,128)}, f32[3,1024]{1,0:T(4,128)S(1)}, f32[1,1024]{1,0:T(1,128)S(1)}) custom-call(f32[8]{0:T(128)S(1)} %convert_element_type.123.valid_ref, bf16[2048,1024]{1,0:T(8,128)(2,1)} %bitcast.52, bf16[1024,1024]{1,0:T(8,128)(2,1)} %w_ref.11), custom_call_target="tpu_custom_call" | custom-call | flops 5368709120 | bytes 20971520 | tf_op jit(solution)/shard_map/pallas_call | solution.py:932
  20.3 3.7 %collective-permute-start.4 = (f32[4,1024]{1,0:T(4,128)S(1)}, f32[4,1024]{1,0:T(4,128)S(1)}, u32[]{:S(2)}, u32[]{:S(2)}) collective-permute-start(f32[4,1024]{1,0:T(4,128)S(1)} %pad_maximum_fusion.13), channel_id=1, source_target_pairs={{0,6},{1,7},{2,4},{3,5},{4,2},{5,3},{6,0},{7,1},{8,14},{9,15},{10,... | collective-permute-start | bytes 49160 | tf_op jit(solution)/shard_map/ppermute | solution.py:24
  25.9 2.7 collective-permute-done.3
  28.8 2.2 collective-permute-start.7
  37.6 8.4 %shard_map.256 = (f32[512,1024]{1,0:T(8,128)S(1)}, f32[2,1024]{1,0:T(2,128)S(1)}, f32[1,1024]{1,0:T(1,128)S(1)}, bf16[128,1024]{1,0:T(8,128)(2,1)S(1)}, bf16[256,1024]{1,0:T(8,128)(2,1)S(1)}) custom-call(f32[4]{0:T(128)S(1)} %pad_maximum_fusion.18.scalar_ref, f32[8]{0:T(128)S(1)} %convert_element_type.123.valid_ref, ...), custom_call_target="tpu_custom_call" | custom-call | flops 2415919104 | bytes 14680064 | tf_op jit(solution)/shard_map/pallas_call | solution.py:970
  49.3 2.3 collective-permute-start.9
  53.4 3.2 %collective-permute-start.14 = (f32[2,1024]{1,0:T(2,128)S(1)}, f32[2,1024]{1,0:T(2,128)S(1)}, u32[]{:S(2)}, u32[]{:S(2)}) collective-permute-start(f32[2,1024]{1,0:T(2,128)S(1)} %add_add_fusion.9), channel_id=1, source_target_pairs={{0,24},{8,16},{16,8},{24,0},{1,25},{9,17},{17,9},{25,1},{2,26},{10... | collective-permute-start | bytes 24584 | tf_op jit(solution)/shard_map/ppermute | solution.py:24
  57.4 6.0 %shard_map.257 = (f32[512,2048]{1,0:T(8,128)}, f32[3,2048]{1,0:T(4,128)S(1)}) custom-call(f32[8]{0:T(128)S(1)} %convert_element_type.123.valid_ref, bf16[2048,1024]{1,0:T(8,128)(2,1)} %bitcast.45, bf16[1024,2048]{1,0:T(8,128)(2,1)S(1)} %copy-done, f32[1,1024]{1,0:T(1,128)S(1)} %slice.121.sampled_ref), custom_call_target="tpu_custom_call" | custom-call | flops 2147483648 | bytes 10485760 | tf_op jit(solution)/shard_map/pallas_call | solution.py:1003
  63.5 5.8 %shard_map.258 = (bf16[512,1024]{1,0:T(8,128)(2,1)S(1)}, f32[512,2048]{1,0:T(8,128)}, f32[4,2048]{1,0:T(4,128)S(1)}, f32[2,2048]{1,0:T(2,128)S(1)}) custom-call(f32[4]{0:T(128)S(1)} %pad_maximum_fusion.18.scalar_ref, f32[8]{0:T(128)S(1)} %convert_element_type.123.valid_ref, f32[512,1024]{1,0:T(8,128)S(1)} %get-tuple-element.119.grouped_ref, ...), custom_call_target="tpu_custom_call" | custom-call | flops 2147483648 | bytes 12582912 | tf_op jit(solution)/shard_map/pallas_call | solution.py:1012
  71.6 2.0 collective-permute-start.19
  78.9 2.4 collective-permute-start.22
  86.8 6.7 %shard_map.260 = (bf16[512,2048]{1,0:T(8,128)(2,1)}, f32[3,2048]{1,0:T(4,128)S(1)}) custom-call(f32[4]{0:T(128)S(1)} %pad_maximum_fusion.18.scalar_ref, f32[8]{0:T(128)S(1)} %convert_element_type.123.valid_ref, f32[512,2048]{1,0:T(8,128)} %get-tuple-element.125.expanded_ref, f32[512,2048]{1,0:T(8,128)} %get-tuple-element.126.projected_ref, ...), custom_call_target="tpu_custom_call" | custom-call | flops 20971520 | bytes 12582912 | tf_op jit(solution)/shard_map/pallas_call | solution.py:1033
  94.8 1.8 collective-permute-start.26
  103.7 1.9 collective-permute-start.27
  107.7 10.2 %shard_map.261 = (bf16[512,2048]{1,0:T(8,128)(2,1)S(1)}, bf16[512,2048]{1,0:T(8,128)(2,1)S(1)}, bf16[16,32,2048]{2,1,0:T(8,128)(2,1)S(1)}, bf16[16,32,2048]{2,1,...) custom-call(f32[4]{0:T(128)S(1)} %pad_maximum_fusion.18.scalar_ref, ...), custom_call_target="tpu_custom_call" | custom-call | flops 4294967296 | bytes 25165824 | tf_op jit(solution)/shard_map/pallas_call | solution.py:1058
  119.8 4.2 %shard_map.262 = (f32[512,1024]{1,0:T(8,128)S(1)}, f32[2,1024]{1,0:T(2,128)S(1)}, bf16[128,1024]{1,0:T(8,128)(2,1)S(1)}) custom-call(f32[4]{0:T(128)S(1)} %pad_maximum_fusion.18.scalar_ref, bf16[512,2048]{1,0:T(8,128)(2,1)S(1)} %get-tuple-element.135.d_ref, bf16[1024,2048]{1,0:T(8,128)(2,1)S(1)} %copy-done.3, f32[512,1024]{1,0:T(8,128)S(1)} %copy-done.7, ...), custom_call_target="tpu_custom_call" | custom-call | flops 2147483648 | bytes 10485760 | tf_op jit(solution)/shard_map/pallas_call | solution.py:1096
  124.0 2.7 collective-permute-start.32
  139.8 2.4 shard_map.263.side_ref
  142.3 2.4 add_convert_fusion.1
  147.2 2.2 collective-permute-start.41
  153.8 1.9 collective-permute-start.37
  157.6 15.0 %shard_map.267 = (f32[2048,1024]{1,0:T(8,128)}, f32[2,1024]{1,0:T(2,128)S(1)}, bf16[9,32,1024]{2,1,0:T(8,128)(2,1)S(1)}) custom-call(f32[4]{0:T(128)S(1)} %pad_maximum_fusion.18.scalar_ref, s32[1]{0:T(128)} %bitcast.3.own_ref, f32[8]{0:T(128)S(1)} %convert_element_type.123.valid_ref, f32[512,1024]{1,0:T(8,128)S(1)} %get-tuple-element.136.grad_ref, ...), custom_call_target="tpu_custom_call" | custom-call | flops 4831838208 | bytes 25165824 | tf_op jit(solution)/shard_map/pallas_call | solution.py:1131
  174.1 1.9 collective-permute-start.44
  186.6 1.9 collective-permute-start.46
  190.4 2.2 collective-permute-done.50
  195.6 2.1 collective-permute-start.53
  197.7 9.6 %shard_map.268 = (bf16[2048,1024]{1,0:T(8,128)(2,1)}, bf16[16,32,1024]{2,1,0:T(8,128)(2,1)S(1)}, bf16[16,32,1024]{2,1,0:T(8,128)(2,1)S(1)}) custom-call(f32[4]{0:T(128)S(1)} %pad_maximum_fusion.18.scalar_ref, f32[8]{0:T(128)S(1)} %convert_element_type.123.valid_ref, f32[2048,1024]{1,0:T(8,128)} %get-tuple-element.152.grad_ref, ...), custom_call_target="tpu_custom_call" | custom-call | flops 4294967296 | bytes 27262976 | tf_op jit(solution)/shard_map/pallas_call | solution.py:1187
  207.3 4.3 %collective-permute-done.51 = bf16[1,64,2048]{2,1,0:T(8,128)(2,1)S(1)} collective-permute-done((bf16[1,64,2048]{2,1,0:T(8,128)(2,1)S(1)}, bf16[1,64,2048]{2,1,0:T(8,128)(2,1)S(1)}, u32[]{:S(2)}, u32[]{:S(2)}) %collective-permute-start.51) | collective-permute-done | bytes 262176 | tf_op jit(solution)/shard_map/ppermute | solution.py:24
  211.9 3.4 %collective-permute-done.55 = bf16[16,48,1024]{2,1,0:T(8,128)(2,1)S(1)} collective-permute-done((bf16[16,48,1024]{2,1,0:T(8,128)(2,1)S(1)}, bf16[16,48,1024]{2,1,0:T(8,128)(2,1)S(1)}, u32[]{:S(2)}, u32[]{:S(2)}) %collective-permute-start.55) | collective-permute-done | bytes 1572896 | tf_op jit(solution)/shard_map/ppermute | solution.py:24
  219.0 5.7 %collective-permute-start.54 = (bf16[1,64,2048]{2,1,0:T(8,128)(2,1)S(1)}, bf16[1,64,2048]{2,1,0:T(8,128)(2,1)S(1)}, u32[]{:S(2)}, u32[]{:S(2)}) collective-permute-start(bf16[1,64,2048]{2,1,0:T(8,128)(2,1)S(1)} %add_convert_fusion.8), channel_id=1, source_target_pairs={{0,4},{1,5},{2,6},{3,7},{4,0},{5,1},{6,2},{7,3},{8,12},{9,13},{10,... | collective-permute-start | bytes 786440 | tf_op jit(solution)/shard_map/ppermute | solution.py:24
  224.7 11.7 %collective-permute-done.54 = bf16[1,64,2048]{2,1,0:T(8,128)(2,1)S(1)} collective-permute-done((bf16[1,64,2048]{2,1,0:T(8,128)(2,1)S(1)}, bf16[1,64,2048]{2,1,0:T(8,128)(2,1)S(1)}, u32[]{:S(2)}, u32[]{:S(2)}) %collective-permute-start.54) | collective-permute-done | bytes 262176 | tf_op jit(solution)/shard_map/ppermute | solution.py:24
  237.0 10.4 %collective-permute-done.59 = bf16[4,48,1024]{2,1,0:T(8,128)(2,1)S(1)} collective-permute-done((bf16[4,48,1024]{2,1,0:T(8,128)(2,1)S(1)}, bf16[4,48,1024]{2,1,0:T(8,128)(2,1)S(1)}, u32[]{:S(2)}, u32[]{:S(2)}) %collective-permute-start.59) | collective-permute-done | bytes 393248 | tf_op jit(solution)/shard_map/ppermute | solution.py:24
  247.4 1.8 collective-permute-done.58
  250.9 1.9 collective-permute-start.64
  252.8 2.5 collective-permute-start.62
  255.3 2.1 collective-permute-done.64
  257.4 1.9 collective-permute-done.63
  262.5 1.9 collective-permute-start.65
  264.4 1.9 collective-permute-start.69
  266.4 2.5 collective-permute-start.67
  268.9 8.9 %shard_map.269 = bf16[8,256,1024]{2,1,0:T(8,128)(2,1)} custom-call(bf16[4,8,64,1024]{3,2,1,0:T(8,128)(2,1)S(1)} %bitcast.43, bf16[1024,1024]{1,0:T(8,128)(2,1)S(1)} %copy-done.5, f32[512,1024]{1,0:T(8,128)S(1)} %shard_map.263.side_ref), custom_call_target="tpu_custom_call" | custom-call | flops 4294967296 | bytes 16777216 | tf_op jit(solution)/shard_map/pallas_call | solution.py:1211
  277.8 6.3 %collective-permute-done.66 = bf16[8,32,2048]{2,1,0:T(8,128)(2,1)S(1)} collective-permute-done((bf16[8,32,2048]{2,1,0:T(8,128)(2,1)S(1)}, bf16[8,32,2048]{2,1,0:T(8,128)(2,1)S(1)}, u32[]{:S(2)}, u32[]{:S(2)}) %collective-permute-start.66) | collective-permute-done | bytes 1048608 | tf_op jit(solution)/shard_map/ppermute | solution.py:24
  285.5 2.2 collective-permute-start.74
  289.1 3.8 %shard_map.270 = f32[32,32,2048]{2,1,0:T(8,128)} custom-call(s32[1]{0:T(128)} %bitcast.14.own_ref, bf16[16,32,2048]{2,1,0:T(8,128)(2,1)S(1)} %pad_maximum_fusion.1.low_ref, bf16[16,32,2048]{2,1,0:T(8,128)(2,1)S(1)} %collective-permute-done.70.high_ref), custom_call_target="tpu_custom_call" | custom-call | bytes 12582912 | tf_op jit(solution)/shard_map/pallas_call | solution.py:119
  292.9 3.8 %shard_map.271 = f32[32,32,2048]{2,1,0:T(8,128)} custom-call(s32[1]{0:T(128)} %bitcast.3.own_ref, bf16[16,32,2048]{2,1,0:T(8,128)(2,1)S(1)} %pad_maximum_fusion.low_ref, bf16[16,32,2048]{2,1,0:T(8,128)(2,1)S(1)} %collective-permute-done.71.high_ref), custom_call_target="tpu_custom_call" | custom-call | bytes 12582912 | tf_op jit(solution)/shard_map/pallas_call | solution.py:119
  298.5 7.4 %collective-permute-done.73 = bf16[4,48,1024]{2,1,0:T(8,128)(2,1)S(1)} collective-permute-done((bf16[4,48,1024]{2,1,0:T(8,128)(2,1)S(1)}, bf16[4,48,1024]{2,1,0:T(8,128)(2,1)S(1)}, u32[]{:S(2)}, u32[]{:S(2)}) %collective-permute-start.73) | collective-permute-done | bytes 393248 | tf_op jit(solution)/shard_map/ppermute | solution.py:24
  309.5 2.9 shard_map.272
  (259 shorter events, 98.9 us)
Async XLA Ops:
  1.7 17.2 %collective-permute-start = (bf16[8,32,1024]{2,1,0:T(8,128)(2,1)S(1)}, bf16[8,32,1024]{2,1,0:T(8,128)(2,1)S(1)}, u32[]{:S(2)}, u32[]{:S(2)}) collective-permute-start(bf16[8,32,1024]{2,1,0:T(8,128)(2,1)S(1)} %slice_bitcast_fusion), channel_id=1, source_target_pairs={{0,8},{8,16},{16,24},{1,9},{9,17},{17,25},{2,10},{10,18},{18,26},{... | collective-permute-start | bytes 1572872 | tf_op jit(solution)/shard_map/ppermute | solution.py:19
  20.3 5.6 %collective-permute-start.4 = (f32[4,1024]{1,0:T(4,128)S(1)}, f32[4,1024]{1,0:T(4,128)S(1)}, u32[]{:S(2)}, u32[]{:S(2)}) collective-permute-start(f32[4,1024]{1,0:T(4,128)S(1)} %pad_maximum_fusion.13), channel_id=1, source_target_pairs={{0,6},{1,7},{2,4},{3,5},{4,2},{5,3},{6,0},{7,1},{8,14},{9,15},{10,... | collective-permute-start | bytes 49160 | tf_op jit(solution)/shard_map/ppermute | solution.py:24
  24.0 4.6 %collective-permute-start.3 = (f32[4,1024]{1,0:T(4,128)S(1)}, f32[4,1024]{1,0:T(4,128)S(1)}, u32[]{:S(2)}, u32[]{:S(2)}) collective-permute-start(f32[4,1024]{1,0:T(4,128)S(1)} %pad_maximum_fusion.13), channel_id=1, source_target_pairs={{0,4},{1,5},{2,6},{3,7},{4,0},{5,1},{6,2},{7,3},{8,12},{9,13},{10,... | collective-permute-start | bytes 49160 | tf_op jit(solution)/shard_map/ppermute | solution.py:24
  24.0 4.6 %collective-permute-start.2 = (f32[4,1024]{1,0:T(4,128)S(1)}, f32[4,1024]{1,0:T(4,128)S(1)}, u32[]{:S(2)}, u32[]{:S(2)}) collective-permute-start(f32[4,1024]{1,0:T(4,128)S(1)} %pad_maximum_fusion.13), channel_id=1, source_target_pairs={{0,2},{1,3},{2,0},{3,1},{4,6},{5,7},{6,4},{7,5},{8,10},{9,11},{10,... | collective-permute-start | bytes 49160 | tf_op jit(solution)/shard_map/ppermute | solution.py:24
  28.8 5.4 %collective-permute-start.7 = (f32[4,1024]{1,0:T(4,128)S(1)}, f32[4,1024]{1,0:T(4,128)S(1)}, u32[]{:S(2)}, u32[]{:S(2)}) collective-permute-start(f32[4,1024]{1,0:T(4,128)S(1)} %pad_maximum_fusion.14), channel_id=1, source_target_pairs={{0,24},{8,16},{16,8},{24,0},{1,25},{9,17},{17,9},{25,1},{2,26},{10... | collective-permute-start | bytes 49160 | tf_op jit(solution)/shard_map/ppermute | solution.py:24
  47.2 5.9 %collective-permute-start.11 = (f32[2,1024]{1,0:T(2,128)S(1)}, f32[2,1024]{1,0:T(2,128)S(1)}, u32[]{:S(2)}, u32[]{:S(2)}) collective-permute-start(f32[2,1024]{1,0:T(2,128)S(1)} %add.445), channel_id=1, source_target_pairs={{0,6},{1,7},{2,4},{3,5},{4,2},{5,3},{6,0},{7,1},{8,14},{9,15},{10,... | collective-permute-start | bytes 24584 | tf_op jit(solution)/shard_map/ppermute | solution.py:24
  51.6 11.8 %collective-permute-start.15 = (bf16[128,1024]{1,0:T(8,128)(2,1)S(1)}, bf16[128,1024]{1,0:T(8,128)(2,1)S(1)}, u32[]{:S(2)}, u32[]{:S(2)}) collective-permute-start(bf16[128,1024]{1,0:T(8,128)(2,1)S(1)} %get-tuple-element.121), channel_id=1, source_target_pairs={{8,0},{16,8},{24,16},{9,1},{17,9},{25,17},{10,2},{18,10},{26,18},{... | collective-permute-start | bytes 786440 | tf_op jit(solution)/shard_map/ppermute | solution.py:19
  53.4 10.1 %collective-permute-start.14 = (f32[2,1024]{1,0:T(2,128)S(1)}, f32[2,1024]{1,0:T(2,128)S(1)}, u32[]{:S(2)}, u32[]{:S(2)}) collective-permute-start(f32[2,1024]{1,0:T(2,128)S(1)} %add_add_fusion.9), channel_id=1, source_target_pairs={{0,24},{8,16},{16,8},{24,0},{1,25},{9,17},{17,9},{25,1},{2,26},{10... | collective-permute-start | bytes 24584 | tf_op jit(solution)/shard_map/ppermute | solution.py:24
  56.6 6.9 %collective-permute-start.13 = (f32[2,1024]{1,0:T(2,128)S(1)}, f32[2,1024]{1,0:T(2,128)S(1)}, u32[]{:S(2)}, u32[]{:S(2)}) collective-permute-start(f32[2,1024]{1,0:T(2,128)S(1)} %add_add_fusion.9), channel_id=1, source_target_pairs={{0,16},{8,24},{16,0},{24,8},{1,17},{9,25},{17,1},{25,9},{2,18},{10... | collective-permute-start | bytes 24584 | tf_op jit(solution)/shard_map/ppermute | solution.py:24
  57.3 6.1 %collective-permute-start.12 = (f32[2,1024]{1,0:T(2,128)S(1)}, f32[2,1024]{1,0:T(2,128)S(1)}, u32[]{:S(2)}, u32[]{:S(2)}) collective-permute-start(f32[2,1024]{1,0:T(2,128)S(1)} %add_add_fusion.9), channel_id=1, source_target_pairs={{0,8},{8,0},{16,24},{24,16},{1,9},{9,1},{17,25},{25,17},{2,10},{10... | collective-permute-start | bytes 24584 | tf_op jit(solution)/shard_map/ppermute | solution.py:24
  71.6 5.8 %collective-permute-start.19 = (f32[4,2048]{1,0:T(4,128)S(1)}, f32[4,2048]{1,0:T(4,128)S(1)}, u32[]{:S(2)}, u32[]{:S(2)}) collective-permute-start(f32[4,2048]{1,0:T(4,128)S(1)} %add.452), channel_id=1, source_target_pairs={{0,6},{1,7},{2,4},{3,5},{4,2},{5,3},{6,0},{7,1},{8,14},{9,15},{10,... | collective-permute-start | bytes 98312 | tf_op jit(solution)/shard_map/ppermute | solution.py:24
  73.6 4.9 %collective-permute-start.18 = (f32[4,2048]{1,0:T(4,128)S(1)}, f32[4,2048]{1,0:T(4,128)S(1)}, u32[]{:S(2)}, u32[]{:S(2)}) collective-permute-start(f32[4,2048]{1,0:T(4,128)S(1)} %add.452), channel_id=1, source_target_pairs={{0,4},{1,5},{2,6},{3,7},{4,0},{5,1},{6,2},{7,3},{8,12},{9,13},{10,... | collective-permute-start | bytes 98312 | tf_op jit(solution)/shard_map/ppermute | solution.py:24
  78.9 5.2 %collective-permute-start.22 = (f32[4,2048]{1,0:T(4,128)S(1)}, f32[4,2048]{1,0:T(4,128)}, u32[]{:S(2)}, u32[]{:S(2)}) collective-permute-start(f32[4,2048]{1,0:T(4,128)S(1)} %add_add_fusion.3), channel_id=1, source_target_pairs={{0,24},{8,16},{16,8},{24,0},{1,25},{9,17},{17,9},{25,1},{2,26},{10... | collective-permute-start | bytes 98312 | tf_op jit(solution)/shard_map/ppermute | solution.py:24
  94.8 5.9 %collective-permute-start.26 = (f32[3,2048]{1,0:T(4,128)S(1)}, f32[3,2048]{1,0:T(4,128)S(1)}, u32[]{:S(2)}, u32[]{:S(2)}) collective-permute-start(f32[3,2048]{1,0:T(4,128)S(1)} %add.463), channel_id=1, source_target_pairs={{0,6},{1,7},{2,4},{3,5},{4,2},{5,3},{6,0},{7,1},{8,14},{9,15},{10,... | collective-permute-start | bytes 73736 | tf_op jit(solution)/shard_map/ppermute | solution.py:24
  96.6 5.2 %collective-permute-start.25 = (f32[3,2048]{1,0:T(4,128)S(1)}, f32[3,2048]{1,0:T(4,128)S(1)}, u32[]{:S(2)}, u32[]{:S(2)}) collective-permute-start(f32[3,2048]{1,0:T(4,128)S(1)} %add.463), channel_id=1, source_target_pairs={{0,4},{1,5},{2,6},{3,7},{4,0},{5,1},{6,2},{7,3},{8,12},{9,13},{10,... | collective-permute-start | bytes 73736 | tf_op jit(solution)/shard_map/ppermute | solution.py:24
  102.1 5.0 %collective-permute-start.29 = (f32[3,2048]{1,0:T(4,128)S(1)}, f32[3,2048]{1,0:T(4,128)S(1)}, u32[]{:S(2)}, u32[]{:S(2)}) collective-permute-start(f32[3,2048]{1,0:T(4,128)S(1)} %add_add_fusion.1), channel_id=1, source_target_pairs={{0,24},{8,16},{16,8},{24,0},{1,25},{9,17},{17,9},{25,1},{2,26},{10... | collective-permute-start | bytes 73736 | tf_op jit(solution)/shard_map/ppermute | solution.py:24
  119.3 11.9 %collective-permute-start.33 = (bf16[16,32,2048]{2,1,0:T(8,128)(2,1)S(1)}, bf16[16,32,2048]{2,1,0:T(8,128)(2,1)}, u32[]{:S(2)}, u32[]{:S(2)}) collective-permute-start(bf16[16,32,2048]{2,1,0:T(8,128)(2,1)S(1)} %get-tuple-element.139), channel_id=1, source_target_pairs={{0,1},{1,0},{2,3},{3,2},{4,5},{5,4},{6,7},{7,6},{8,9},{9,8},{10,11... | collective-permute-start | bytes 6291464 | tf_op jit(solution)/shard_map/ppermute | solution.py:24
  119.3 11.9 %collective-permute-start.34 = (bf16[16,32,2048]{2,1,0:T(8,128)(2,1)}, bf16[16,32,2048]{2,1,0:T(8,128)(2,1)S(1)}, u32[]{:S(2)}, u32[]{:S(2)}) collective-permute-start(bf16[16,32,2048]{2,1,0:T(8,128)(2,1)} %get-tuple-element.140), channel_id=1, source_target_pairs={{0,1},{1,0},{2,3},{3,2},{4,5},{5,4},{6,7},{7,6},{8,9},{9,8},{10,11... | collective-permute-start | bytes 6291464 | tf_op jit(solution)/shard_map/ppermute | solution.py:24
  124.0 4.6 %collective-permute-start.32 = (f32[2,1024]{1,0:T(2,128)S(1)}, f32[2,1024]{1,0:T(2,128)S(1)}, u32[]{:S(2)}, u32[]{:S(2)}) collective-permute-start(f32[2,1024]{1,0:T(2,128)S(1)} %get-tuple-element.137), channel_id=1, source_target_pairs={{0,24},{8,16},{16,8},{24,0},{1,25},{9,17},{17,9},{25,1},{2,26},{10... | collective-permute-start | bytes 24584 | tf_op jit(solution)/shard_map/ppermute | solution.py:24
  132.5 9.8 %collective-permute-start.36 = (bf16[128,1024]{1,0:T(8,128)(2,1)S(1)}, bf16[128,1024]{1,0:T(8,128)(2,1)S(1)}, u32[]{:S(2)}, u32[]{:S(2)}) collective-permute-start(bf16[128,1024]{1,0:T(8,128)(2,1)S(1)} %get-tuple-element.142), channel_id=1, source_target_pairs={{8,0},{16,8},{24,16},{9,1},{17,9},{25,17},{10,2},{18,10},{26,18},{... | collective-permute-start | bytes 786440 | tf_op jit(solution)/shard_map/ppermute | solution.py:19
  147.2 25.3 %collective-permute-start.41 = (bf16[8,32,2048]{2,1,0:T(8,128)(2,1)S(1)}, bf16[8,32,2048]{2,1,0:T(8,128)(2,1)S(1)}, u32[]{:S(2)}, u32[]{:S(2)}) collective-permute-start(bf16[8,32,2048]{2,1,0:T(8,128)(2,1)S(1)} %slice.158), channel_id=1, source_target_pairs={{0,16},{8,24},{16,0},{24,8},{1,17},{9,25},{17,1},{25,9},{2,18},{10... | collective-permute-start | bytes 3145736 | tf_op jit(solution)/shard_map/ppermute | solution.py:24
  149.5 24.6 %collective-permute-start.40 = (bf16[8,32,2048]{2,1,0:T(8,128)(2,1)S(1)}, bf16[8,32,2048]{2,1,0:T(8,128)(2,1)S(1)}, u32[]{:S(2)}, u32[]{:S(2)}) collective-permute-start(bf16[8,32,2048]{2,1,0:T(8,128)(2,1)S(1)} %slice.157), channel_id=1, source_target_pairs={{0,8},{8,0},{16,24},{24,16},{1,9},{9,1},{17,25},{25,17},{2,10},{10... | collective-permute-start | bytes 3145736 | tf_op jit(solution)/shard_map/ppermute | solution.py:24
  151.3 5.5 %collective-permute-start.39 = (f32[2,1024]{1,0:T(2,128)S(1)}, f32[2,1024]{1,0:T(2,128)S(1)}, u32[]{:S(2)}, u32[]{:S(2)}) collective-permute-start(f32[2,1024]{1,0:T(2,128)S(1)} %add.473), channel_id=1, source_target_pairs={{0,6},{1,7},{2,4},{3,5},{4,2},{5,3},{6,0},{7,1},{8,14},{9,15},{10,... | collective-permute-start | bytes 24584 | tf_op jit(solution)/shard_map/ppermute | solution.py:24
  181.8 10.8 %collective-permute-start.50 = (bf16[4,32,2048]{2,1,0:T(8,128)(2,1)S(1)}, bf16[4,32,2048]{2,1,0:T(8,128)(2,1)S(1)}, u32[]{:S(2)}, u32[]{:S(2)}) collective-permute-start(bf16[4,32,2048]{2,1,0:T(8,128)(2,1)S(1)} %slice.162), channel_id=1, source_target_pairs={{0,8},{8,0},{16,24},{24,16},{1,9},{9,1},{17,25},{25,17},{2,10},{10... | collective-permute-start | bytes 1572872 | tf_op jit(solution)/shard_map/ppermute | solution.py:24
  182.1 10.5 %collective-permute-start.49 = (bf16[4,32,2048]{2,1,0:T(8,128)(2,1)S(1)}, bf16[4,32,2048]{2,1,0:T(8,128)(2,1)S(1)}, u32[]{:S(2)}, u32[]{:S(2)}) collective-permute-start(bf16[4,32,2048]{2,1,0:T(8,128)(2,1)S(1)} %slice.160), channel_id=1, source_target_pairs={{0,16},{8,24},{16,0},{24,8},{1,17},{9,25},{17,1},{25,9},{2,18},{10... | collective-permute-start | bytes 1572872 | tf_op jit(solution)/shard_map/ppermute | solution.py:24
  184.1 5.4 %collective-permute-start.48 = (f32[2,1024]{1,0:T(2,128)S(1)}, f32[2,1024]{1,0:T(2,128)S(1)}, u32[]{:S(2)}, u32[]{:S(2)}) collective-permute-start(f32[2,1024]{1,0:T(2,128)S(1)} %add.482), channel_id=1, source_target_pairs={{0,6},{1,7},{2,4},{3,5},{4,2},{5,3},{6,0},{7,1},{8,14},{9,15},{10,... | collective-permute-start | bytes 24584 | tf_op jit(solution)/shard_map/ppermute | solution.py:24
  193.0 18.6 %collective-permute-start.51 = (bf16[1,64,2048]{2,1,0:T(8,128)(2,1)S(1)}, bf16[1,64,2048]{2,1,0:T(8,128)(2,1)S(1)}, u32[]{:S(2)}, u32[]{:S(2)}) collective-permute-start(bf16[1,64,2048]{2,1,0:T(8,128)(2,1)S(1)} %pad_maximum_fusion.8), channel_id=1, source_target_pairs={{0,4},{1,5},{2,6},{3,7},{4,0},{5,1},{6,2},{7,3},{8,12},{9,13},{10,... | collective-permute-start | bytes 786440 | tf_op jit(solution)/shard_map/ppermute | solution.py:24
  194.7 17.0 %collective-permute-start.52 = (bf16[1,64,2048]{2,1,0:T(8,128)(2,1)S(1)}, bf16[1,64,2048]{2,1,0:T(8,128)(2,1)S(1)}, u32[]{:S(2)}, u32[]{:S(2)}) collective-permute-start(bf16[1,64,2048]{2,1,0:T(8,128)(2,1)S(1)} %pad_maximum_fusion.9), channel_id=1, source_target_pairs={{0,2},{1,3},{2,0},{3,1},{4,6},{5,7},{6,4},{7,5},{8,10},{9,11},{10,... | collective-permute-start | bytes 786440 | tf_op jit(solution)/shard_map/ppermute | solution.py:24
  195.6 16.1 %collective-permute-start.53 = (bf16[1,64,2048]{2,1,0:T(8,128)(2,1)S(1)}, bf16[1,64,2048]{2,1,0:T(8,128)(2,1)S(1)}, u32[]{:S(2)}, u32[]{:S(2)}) collective-permute-start(bf16[1,64,2048]{2,1,0:T(8,128)(2,1)S(1)} %pad_maximum_fusion.10), channel_id=1, source_target_pairs={{0,6},{1,7},{2,4},{3,5},{4,2},{5,3},{6,0},{7,1},{8,14},{9,15},{10,... | collective-permute-start | bytes 786440 | tf_op jit(solution)/shard_map/ppermute | solution.py:24
  216.1 20.2 %collective-permute-start.57 = (bf16[4,48,1024]{2,1,0:T(8,128)(2,1)S(1)}, bf16[4,48,1024]{2,1,0:T(8,128)(2,1)S(1)}, u32[]{:S(2)}, u32[]{:S(2)}) collective-permute-start(bf16[4,48,1024]{2,1,0:T(8,128)(2,1)S(1)} %get-tuple-element.220), channel_id=1, source_target_pairs={{0,16},{8,24},{16,0},{24,8},{1,17},{9,25},{17,1},{25,9},{2,18},{10... | collective-permute-start | bytes 1179656 | tf_op jit(solution)/shard_map/ppermute | solution.py:24
  217.2 19.2 %collective-permute-start.56 = (bf16[4,48,1024]{2,1,0:T(8,128)(2,1)S(1)}, bf16[4,48,1024]{2,1,0:T(8,128)(2,1)S(1)}, u32[]{:S(2)}, u32[]{:S(2)}) collective-permute-start(bf16[4,48,1024]{2,1,0:T(8,128)(2,1)S(1)} %get-tuple-element.221), channel_id=1, source_target_pairs={{0,8},{8,0},{16,24},{24,16},{1,9},{9,1},{17,25},{25,17},{2,10},{10... | collective-permute-start | bytes 1179656 | tf_op jit(solution)/shard_map/ppermute | solution.py:24
  219.0 17.3 %collective-permute-start.54 = (bf16[1,64,2048]{2,1,0:T(8,128)(2,1)S(1)}, bf16[1,64,2048]{2,1,0:T(8,128)(2,1)S(1)}, u32[]{:S(2)}, u32[]{:S(2)}) collective-permute-start(bf16[1,64,2048]{2,1,0:T(8,128)(2,1)S(1)} %add_convert_fusion.8), channel_id=1, source_target_pairs={{0,4},{1,5},{2,6},{3,7},{4,0},{5,1},{6,2},{7,3},{8,12},{9,13},{10,... | collective-permute-start | bytes 786440 | tf_op jit(solution)/shard_map/ppermute | solution.py:24
  236.4 12.9 %collective-permute-start.58 = (bf16[2,64,2048]{2,1,0:T(8,128)(2,1)S(1)}, bf16[2,64,2048]{2,1,0:T(8,128)(2,1)S(1)}, u32[]{:S(2)}, u32[]{:S(2)}) collective-permute-start(bf16[2,64,2048]{2,1,0:T(8,128)(2,1)S(1)} %pad_maximum_fusion.6), channel_id=1, source_target_pairs={{0,2},{1,3},{2,0},{3,1},{4,6},{5,7},{6,4},{7,5},{8,10},{9,11},{10,... | collective-permute-start | bytes 1572872 | tf_op jit(solution)/shard_map/ppermute | solution.py:24
  236.5 11.0 %collective-permute-start.59 = (bf16[4,48,1024]{2,1,0:T(8,128)(2,1)S(1)}, bf16[4,48,1024]{2,1,0:T(8,128)(2,1)S(1)}, u32[]{:S(2)}, u32[]{:S(2)}) collective-permute-start(bf16[4,48,1024]{2,1,0:T(8,128)(2,1)S(1)} %get-tuple-element.219), channel_id=1, source_target_pairs={{0,24},{8,16},{16,8},{24,0},{1,25},{9,17},{17,9},{25,1},{2,26},{10... | collective-permute-start | bytes 1179656 | tf_op jit(solution)/shard_map/ppermute | solution.py:24
  249.5 12.0 %collective-permute-start.61 = (bf16[4,32,2048]{2,1,0:T(8,128)(2,1)S(1)}, bf16[4,32,2048]{2,1,0:T(8,128)(2,1)S(1)}, u32[]{:S(2)}, u32[]{:S(2)}) collective-permute-start(bf16[4,32,2048]{2,1,0:T(8,128)(2,1)S(1)} %get-tuple-element.222), channel_id=1, source_target_pairs={{0,8},{8,0},{16,24},{24,16},{1,9},{9,1},{17,25},{25,17},{2,10},{10... | collective-permute-start | bytes 1572872 | tf_op jit(solution)/shard_map/ppermute | solution.py:24
  250.0 11.7 %collective-permute-start.60 = (bf16[4,32,2048]{2,1,0:T(8,128)(2,1)S(1)}, bf16[4,32,2048]{2,1,0:T(8,128)(2,1)S(1)}, u32[]{:S(2)}, u32[]{:S(2)}) collective-permute-start(bf16[4,32,2048]{2,1,0:T(8,128)(2,1)S(1)} %get-tuple-element.223), channel_id=1, source_target_pairs={{0,16},{8,24},{16,0},{24,8},{1,17},{9,25},{17,1},{25,9},{2,18},{10... | collective-permute-start | bytes 1572872 | tf_op jit(solution)/shard_map/ppermute | solution.py:24
  250.9 6.6 %collective-permute-start.64 = (bf16[1,48,1024]{2,1,0:T(8,128)(2,1)S(1)}, bf16[1,48,1024]{2,1,0:T(8,128)(2,1)S(1)}, u32[]{:S(2)}, u32[]{:S(2)}) collective-permute-start(bf16[1,48,1024]{2,1,0:T(8,128)(2,1)S(1)} %get-tuple-element.234), channel_id=1, source_target_pairs={{0,6},{1,7},{2,4},{3,5},{4,2},{5,3},{6,0},{7,1},{8,14},{9,15},{10,... | collective-permute-start | bytes 294920 | tf_op jit(solution)/shard_map/ppermute | solution.py:24
  252.8 6.5 %collective-permute-start.63 = (bf16[1,48,1024]{2,1,0:T(8,128)(2,1)S(1)}, bf16[1,48,1024]{2,1,0:T(8,128)(2,1)S(1)}, u32[]{:S(2)}, u32[]{:S(2)}) collective-permute-start(bf16[1,48,1024]{2,1,0:T(8,128)(2,1)S(1)} %get-tuple-element.235), channel_id=1, source_target_pairs={{0,2},{1,3},{2,0},{3,1},{4,6},{5,7},{6,4},{7,5},{8,10},{9,11},{10,... | collective-permute-start | bytes 294920 | tf_op jit(solution)/shard_map/ppermute | solution.py:24
  252.8 7.5 %collective-permute-start.62 = (bf16[1,48,1024]{2,1,0:T(8,128)(2,1)S(1)}, bf16[1,48,1024]{2,1,0:T(8,128)(2,1)S(1)}, u32[]{:S(2)}, u32[]{:S(2)}) collective-permute-start(bf16[1,48,1024]{2,1,0:T(8,128)(2,1)S(1)} %get-tuple-element.236), channel_id=1, source_target_pairs={{0,4},{1,5},{2,6},{3,7},{4,0},{5,1},{6,2},{7,3},{8,12},{9,13},{10,... | collective-permute-start | bytes 294920 | tf_op jit(solution)/shard_map/ppermute | solution.py:24
  261.9 22.1 %collective-permute-start.66 = (bf16[8,32,2048]{2,1,0:T(8,128)(2,1)S(1)}, bf16[8,32,2048]{2,1,0:T(8,128)(2,1)S(1)}, u32[]{:S(2)}, u32[]{:S(2)}) collective-permute-start(bf16[8,32,2048]{2,1,0:T(8,128)(2,1)S(1)} %pad_maximum_fusion.5), channel_id=1, source_target_pairs={{0,16},{8,24},{16,0},{24,8},{1,17},{9,25},{17,1},{25,9},{2,18},{10... | collective-permute-start | bytes 3145736 | tf_op jit(solution)/shard_map/ppermute | solution.py:24
  262.5 21.8 %collective-permute-start.65 = (bf16[8,32,2048]{2,1,0:T(8,128)(2,1)S(1)}, bf16[8,32,2048]{2,1,0:T(8,128)(2,1)S(1)}, u32[]{:S(2)}, u32[]{:S(2)}) collective-permute-start(bf16[8,32,2048]{2,1,0:T(8,128)(2,1)S(1)} %pad_maximum_fusion.4), channel_id=1, source_target_pairs={{0,8},{8,0},{16,24},{24,16},{1,9},{9,1},{17,25},{25,17},{2,10},{10... | collective-permute-start | bytes 3145736 | tf_op jit(solution)/shard_map/ppermute | solution.py:24
  264.4 13.3 %collective-permute-start.69 = (bf16[1,48,1024]{2,1,0:T(8,128)(2,1)S(1)}, bf16[1,48,1024]{2,1,0:T(8,128)(2,1)S(1)}, u32[]{:S(2)}, u32[]{:S(2)}) collective-permute-start(bf16[1,48,1024]{2,1,0:T(8,128)(2,1)S(1)} %get-tuple-element.211), channel_id=1, source_target_pairs={{0,6},{1,7},{2,4},{3,5},{4,2},{5,3},{6,0},{7,1},{8,14},{9,15},{10,... | collective-permute-start | bytes 294920 | tf_op jit(solution)/shard_map/ppermute | solution.py:24
  266.4 11.4 %collective-permute-start.68 = (bf16[1,48,1024]{2,1,0:T(8,128)(2,1)S(1)}, bf16[1,48,1024]{2,1,0:T(8,128)(2,1)S(1)}, u32[]{:S(2)}, u32[]{:S(2)}) collective-permute-start(bf16[1,48,1024]{2,1,0:T(8,128)(2,1)S(1)} %get-tuple-element.211), channel_id=1, source_target_pairs={{0,2},{1,3},{2,0},{3,1},{4,6},{5,7},{6,4},{7,5},{8,10},{9,11},{10,... | collective-permute-start | bytes 294920 | tf_op jit(solution)/shard_map/ppermute | solution.py:24
  266.4 11.4 %collective-permute-start.67 = (bf16[1,48,1024]{2,1,0:T(8,128)(2,1)S(1)}, bf16[1,48,1024]{2,1,0:T(8,128)(2,1)S(1)}, u32[]{:S(2)}, u32[]{:S(2)}) collective-permute-start(bf16[1,48,1024]{2,1,0:T(8,128)(2,1)S(1)} %get-tuple-element.211), channel_id=1, source_target_pairs={{0,4},{1,5},{2,6},{3,7},{4,0},{5,1},{6,2},{7,3},{8,12},{9,13},{10,... | collective-permute-start | bytes 294920 | tf_op jit(solution)/shard_map/ppermute | solution.py:24
  284.9 8.0 %collective-permute-start.71 = (bf16[16,32,2048]{2,1,0:T(8,128)(2,1)S(1)}, bf16[16,32,2048]{2,1,0:T(8,128)(2,1)S(1)}, u32[]{:S(2)}, u32[]{:S(2)}) collective-permute-start(bf16[16,32,2048]{2,1,0:T(8,128)(2,1)S(1)} %pad_maximum_fusion.low_ref), channel_id=1, source_target_pairs={{0,1},{1,0},{2,3},{3,2},{4,5},{5,4},{6,7},{7,6},{8,9},{9,8},{10,11... | collective-permute-start | bytes 6291464 | tf_op jit(solution)/shard_map/ppermute | solution.py:24
  285.5 13.0 %collective-permute-start.74 = (bf16[4,48,1024]{2,1,0:T(8,128)(2,1)S(1)}, bf16[4,48,1024]{2,1,0:T(8,128)(2,1)S(1)}, u32[]{:S(2)}, u32[]{:S(2)}) collective-permute-start(bf16[4,48,1024]{2,1,0:T(8,128)(2,1)S(1)} %pad_maximum_fusion.7), channel_id=1, source_target_pairs={{0,24},{8,16},{16,8},{24,0},{1,25},{9,17},{17,9},{25,1},{2,26},{10... | collective-permute-start | bytes 1179656 | tf_op jit(solution)/shard_map/ppermute | solution.py:24
  287.7 18.2 %collective-permute-start.73 = (bf16[4,48,1024]{2,1,0:T(8,128)(2,1)S(1)}, bf16[4,48,1024]{2,1,0:T(8,128)(2,1)S(1)}, u32[]{:S(2)}, u32[]{:S(2)}) collective-permute-start(bf16[4,48,1024]{2,1,0:T(8,128)(2,1)S(1)} %pad_maximum_fusion.7), channel_id=1, source_target_pairs={{0,16},{8,24},{16,0},{24,8},{1,17},{9,25},{17,1},{25,9},{2,18},{10... | collective-permute-start | bytes 1179656 | tf_op jit(solution)/shard_map/ppermute | solution.py:24
  288.5 17.4 %collective-permute-start.72 = (bf16[4,48,1024]{2,1,0:T(8,128)(2,1)S(1)}, bf16[4,48,1024]{2,1,0:T(8,128)(2,1)S(1)}, u32[]{:S(2)}, u32[]{:S(2)}) collective-permute-start(bf16[4,48,1024]{2,1,0:T(8,128)(2,1)S(1)} %pad_maximum_fusion.7), channel_id=1, source_target_pairs={{0,8},{8,0},{16,24},{24,16},{1,9},{9,1},{17,25},{25,17},{2,10},{10... | collective-permute-start | bytes 1179656 | tf_op jit(solution)/shard_map/ppermute | solution.py:24
  (57 other events, 470.4 us)

commit v6 on v5

--- a/solution.py
+++ b/solution.py
@@ -10,7 +10,7 @@
 
 GW = 32
 EPS = 1e-05
-VMEM_LIMIT = 40 * 1024 * 1024
+VMEM_LIMIT = 36 * 1024 * 1024
 
 
 def shifted(value, axis, by):
@@ -1121,7 +1121,7 @@
         [((rows, chans), WIDE)],
         (2 * rows * chans * wide, 8 << 20),
     )(d_projected, proj_w)[0]
-    planes_turned = [sampled_turned] + [turn(planes, plane, own_two) for plane in range(1, 4)]
+    planes_turned = [sampled_turned, turn(planes, 1, own_two)]
     sums, below_grad, side_grad, *planes_turned = arrive(pair, sums, below_grad, side_grad, *planes_turned)
     for grad in pair:
         grad.step()
@@ -1178,7 +1178,8 @@
     for grad in pair:
         grad.step()
     grads_one = mesh_sum(sums, back_rounds[1:])
-    grads_one, parts_group = arrive(pair, grads_one, parts_group)
+    planes_turned += [turn(planes, plane, own_two) for plane in (2, 3)]
+    grads_one, parts_group, *planes_turned = arrive(pair, grads_one, parts_group, *planes_turned)
     for grad in pair:
         grad.take()
     both = join(pair)

time: 314 us -> 311 us (level)
  transfers between devices with their start and end apart: 76 -> 76, of which waited for: 49 -> 48; matrix products, arithmetic and copies ran while one was open for 1% -> 1% of each run, Pallas kernels for 23% -> 23%
where the time goes in v6:
time: 311 us; the launch traced here: 310 us
  Pallas kernels  105 us (34%)
  starting transfers between devices  91.2 us (29%)
  waiting for transfers between devices  90.6 us (29%)
  local copies, waits for them, and re-layouts  11.7 us (4%)
  other arithmetic  9.24 us (3%)
    ppermute x73, waiting for transfers between devices, exchange(): return lax.ppermute(value, axis, [(i, i ^ mask) for i in range(peers)])  87.5 us
    ppermute x73, starting transfers between devices, exchange(): return lax.ppermute(value, axis, [(i, i ^ mask) for i in range(peers)])  83.3 us
    pallas_call x1, Pallas kernels, per_device(): call(functools.partial(conv_back_kernel, (images, tall, half_cols)), step...  15.2 us
    pallas_call x1, Pallas kernels, per_device(): call(functools.partial(reduce_kernel, (images, image_rows, cols), lead),...  11.6 us
    pallas_call x3, Pallas kernels, plain_order(): pl.pallas_call(functools.partial(spread_kernel, order), grid=(cols // wid...  10.5 us
    pallas_call x1, Pallas kernels, per_device(): call(functools.partial(reduced_back_kernel, 16), steps, [SCALARS, SCALARS...  9.61 us
    pallas_call x1, Pallas kernels, per_device(): call(functools.partial(weights_kernel, 16), strips, [SCALARS, SCALARS, wi...  9.42 us
    pallas_call x1, Pallas kernels, images_back(): call(functools.partial(images_back_kernel, (image_rows, cols)), images, [...  8.84 us
  transfers between devices with their start and end apart: 76, of which 48 were waited for; matrix products, arithmetic and copies ran while one was open for 1% of the time, Pallas kernels for 23%

profile of v6, /device:TPU:0, one launch (start us, length us, event | category | flops | bytes accessed | tf_op | source)
XLA Modules:
  0.0 310.4 jit_solution(4187025223816198515)
XLA Ops:
  1.7 4.9 %collective-permute-start = (bf16[8,32,1024]{2,1,0:T(8,128)(2,1)S(1)}, bf16[8,32,1024]{2,1,0:T(8,128)(2,1)S(1)}, u32[]{:S(2)}, u32[]{:S(2)}) collective-permute-start(bf16[8,32,1024]{2,1,0:T(8,128)(2,1)S(1)} %slice_bitcast_fusion), channel_id=1, source_target_pairs={{0,8},{8,16},{16,24},{1,9},{9,17},{17,25},{2,10},{10,18},{18,26},{... | collective-permute-start | bytes 1572872 | tf_op jit(solution)/shard_map/ppermute | solution.py:19
  7.3 11.6 %shard_map.254 = (bf16[4,8,64,1024]{3,2,1,0:T(8,128)(2,1)}, f32[2048,1024]{1,0:T(8,128)}, f32[3,1024]{1,0:T(4,128)S(1)}, f32[1,1024]{1,0:T(1,128)S(1)}) custom-call(f32[8]{0:T(128)S(1)} %convert_element_type.123.valid_ref, bf16[2048,1024]{1,0:T(8,128)(2,1)} %bitcast.52, bf16[1024,1024]{1,0:T(8,128)(2,1)} %w_ref.11), custom_call_target="tpu_custom_call" | custom-call | flops 5368709120 | bytes 20971520 | tf_op jit(solution)/shard_map/pallas_call | solution.py:932
  20.3 3.7 %collective-permute-start.4 = (f32[4,1024]{1,0:T(4,128)S(1)}, f32[4,1024]{1,0:T(4,128)S(1)}, u32[]{:S(2)}, u32[]{:S(2)}) collective-permute-start(f32[4,1024]{1,0:T(4,128)S(1)} %pad_maximum_fusion.13), channel_id=1, source_target_pairs={{0,6},{1,7},{2,4},{3,5},{4,2},{5,3},{6,0},{7,1},{8,14},{9,15},{10,... | collective-permute-start | bytes 49160 | tf_op jit(solution)/shard_map/ppermute | solution.py:24
  25.9 2.7 collective-permute-done.3
  28.8 2.2 collective-permute-start.7
  37.6 8.4 %shard_map.256 = (f32[512,1024]{1,0:T(8,128)S(1)}, f32[2,1024]{1,0:T(2,128)S(1)}, f32[1,1024]{1,0:T(1,128)S(1)}, bf16[128,1024]{1,0:T(8,128)(2,1)S(1)}, bf16[256,1024]{1,0:T(8,128)(2,1)S(1)}) custom-call(f32[4]{0:T(128)S(1)} %pad_maximum_fusion.18.scalar_ref, f32[8]{0:T(128)S(1)} %convert_element_type.123.valid_ref, ...), custom_call_target="tpu_custom_call" | custom-call | flops 2415919104 | bytes 14680064 | tf_op jit(solution)/shard_map/pallas_call | solution.py:970
  49.3 2.3 collective-permute-start.9
  53.4 3.2 %collective-permute-start.14 = (f32[2,1024]{1,0:T(2,128)S(1)}, f32[2,1024]{1,0:T(2,128)S(1)}, u32[]{:S(2)}, u32[]{:S(2)}) collective-permute-start(f32[2,1024]{1,0:T(2,128)S(1)} %add_add_fusion.9), channel_id=1, source_target_pairs={{0,24},{8,16},{16,8},{24,0},{1,25},{9,17},{17,9},{25,1},{2,26},{10... | collective-permute-start | bytes 24584 | tf_op jit(solution)/shard_map/ppermute | solution.py:24
  57.4 6.0 %shard_map.257 = (f32[512,2048]{1,0:T(8,128)}, f32[3,2048]{1,0:T(4,128)S(1)}) custom-call(f32[8]{0:T(128)S(1)} %convert_element_type.123.valid_ref, bf16[2048,1024]{1,0:T(8,128)(2,1)} %bitcast.45, bf16[1024,2048]{1,0:T(8,128)(2,1)S(1)} %copy-done, f32[1,1024]{1,0:T(1,128)S(1)} %slice.121.sampled_ref), custom_call_target="tpu_custom_call" | custom-call | flops 2147483648 | bytes 10485760 | tf_op jit(solution)/shard_map/pallas_call | solution.py:1003
  63.5 5.8 %shard_map.258 = (bf16[512,1024]{1,0:T(8,128)(2,1)S(1)}, f32[512,2048]{1,0:T(8,128)}, f32[4,2048]{1,0:T(4,128)S(1)}, f32[2,2048]{1,0:T(2,128)S(1)}) custom-call(f32[4]{0:T(128)S(1)} %pad_maximum_fusion.18.scalar_ref, f32[8]{0:T(128)S(1)} %convert_element_type.123.valid_ref, f32[512,1024]{1,0:T(8,128)S(1)} %get-tuple-element.121.grouped_ref, ...), custom_call_target="tpu_custom_call" | custom-call | flops 2147483648 | bytes 12582912 | tf_op jit(solution)/shard_map/pallas_call | solution.py:1012
  71.6 2.0 collective-permute-start.19
  78.9 2.4 collective-permute-start.22
  86.8 6.7 %shard_map.260 = (bf16[512,2048]{1,0:T(8,128)(2,1)}, f32[3,2048]{1,0:T(4,128)S(1)}) custom-call(f32[4]{0:T(128)S(1)} %pad_maximum_fusion.18.scalar_ref, f32[8]{0:T(128)S(1)} %convert_element_type.123.valid_ref, f32[512,2048]{1,0:T(8,128)} %get-tuple-element.127.expanded_ref, f32[512,2048]{1,0:T(8,128)} %get-tuple-element.128.projected_ref, ...), custom_call_target="tpu_custom_call" | custom-call | flops 20971520 | bytes 12582912 | tf_op jit(solution)/shard_map/pallas_call | solution.py:1033
  94.8 1.8 collective-permute-start.26
  103.7 1.9 collective-permute-start.27
  107.7 9.4 %shard_map.261 = (bf16[512,2048]{1,0:T(8,128)(2,1)S(1)}, bf16[512,2048]{1,0:T(8,128)(2,1)S(1)}, bf16[16,32,2048]{2,1,0:T(8,128)(2,1)S(1)}, bf16[16,32,2048]{2,1,...) custom-call(f32[4]{0:T(128)S(1)} %pad_maximum_fusion.18.scalar_ref, ...), custom_call_target="tpu_custom_call" | custom-call | flops 4294967296 | bytes 25165824 | tf_op jit(solution)/shard_map/pallas_call | solution.py:1058
  119.0 4.2 %shard_map.262 = (f32[512,1024]{1,0:T(8,128)S(1)}, f32[2,1024]{1,0:T(2,128)S(1)}, bf16[128,1024]{1,0:T(8,128)(2,1)S(1)}) custom-call(f32[4]{0:T(128)S(1)} %pad_maximum_fusion.18.scalar_ref, bf16[512,2048]{1,0:T(8,128)(2,1)S(1)} %get-tuple-element.137.d_ref, bf16[1024,2048]{1,0:T(8,128)(2,1)S(1)} %copy-done.3, f32[512,1024]{1,0:T(8,128)S(1)} %copy-done.7, ...), custom_call_target="tpu_custom_call" | custom-call | flops 2147483648 | bytes 10485760 | tf_op jit(solution)/shard_map/pallas_call | solution.py:1096
  123.2 2.7 collective-permute-start.32
  134.8 2.4 shard_map.263.side_ref
  137.3 3.0 collective-permute-done.36.below_grad_ref
  140.3 2.4 add_convert_fusion.1
  146.7 1.7 collective-permute-start.39
  149.3 1.8 collective-permute-start.37
  153.1 15.2 %shard_map.265 = (f32[2048,1024]{1,0:T(8,128)}, f32[2,1024]{1,0:T(2,128)S(1)}, bf16[9,32,1024]{2,1,0:T(8,128)(2,1)S(1)}) custom-call(f32[4]{0:T(128)S(1)} %pad_maximum_fusion.18.scalar_ref, s32[1]{0:T(128)} %bitcast.3.own_ref, f32[8]{0:T(128)S(1)} %convert_element_type.123.valid_ref, f32[512,1024]{1,0:T(8,128)S(1)} %get-tuple-element.138.grad_ref, ...), custom_call_target="tpu_custom_call" | custom-call | flops 4831838208 | bytes 25165824 | tf_op jit(solution)/shard_map/pallas_call | solution.py:1131
  169.8 1.9 collective-permute-start.44
  179.8 1.9 collective-permute-start.48
  191.5 2.5 collective-permute-start.53
  194.0 9.6 %shard_map.268 = (bf16[2048,1024]{1,0:T(8,128)(2,1)}, bf16[16,32,1024]{2,1,0:T(8,128)(2,1)S(1)}, bf16[16,32,1024]{2,1,0:T(8,128)(2,1)S(1)}) custom-call(f32[4]{0:T(128)S(1)} %pad_maximum_fusion.18.scalar_ref, f32[8]{0:T(128)S(1)} %convert_element_type.123.valid_ref, f32[2048,1024]{1,0:T(8,128)} %get-tuple-element.154.grad_ref, ...), custom_call_target="tpu_custom_call" | custom-call | flops 4294967296 | bytes 27262976 | tf_op jit(solution)/shard_map/pallas_call | solution.py:1188
  203.7 4.6 %collective-permute-done.51 = bf16[1,64,2048]{2,1,0:T(8,128)(2,1)S(1)} collective-permute-done((bf16[1,64,2048]{2,1,0:T(8,128)(2,1)S(1)}, bf16[1,64,2048]{2,1,0:T(8,128)(2,1)S(1)}, u32[]{:S(2)}, u32[]{:S(2)}) %collective-permute-start.51) | collective-permute-done | bytes 262176 | tf_op jit(solution)/shard_map/ppermute | solution.py:24
  208.5 3.4 %collective-permute-done.55 = bf16[16,48,1024]{2,1,0:T(8,128)(2,1)S(1)} collective-permute-done((bf16[16,48,1024]{2,1,0:T(8,128)(2,1)S(1)}, bf16[16,48,1024]{2,1,0:T(8,128)(2,1)S(1)}, u32[]{:S(2)}, u32[]{:S(2)}) %collective-permute-start.55) | collective-permute-done | bytes 1572896 | tf_op jit(solution)/shard_map/ppermute | solution.py:24
  215.6 6.4 %collective-permute-start.54 = (bf16[1,64,2048]{2,1,0:T(8,128)(2,1)S(1)}, bf16[1,64,2048]{2,1,0:T(8,128)(2,1)S(1)}, u32[]{:S(2)}, u32[]{:S(2)}) collective-permute-start(bf16[1,64,2048]{2,1,0:T(8,128)(2,1)S(1)} %add_convert_fusion.8), channel_id=1, source_target_pairs={{0,4},{1,5},{2,6},{3,7},{4,0},{5,1},{6,2},{7,3},{8,12},{9,13},{10,... | collective-permute-start | bytes 786440 | tf_op jit(solution)/shard_map/ppermute | solution.py:24
  222.0 11.7 %collective-permute-done.54 = bf16[1,64,2048]{2,1,0:T(8,128)(2,1)S(1)} collective-permute-done((bf16[1,64,2048]{2,1,0:T(8,128)(2,1)S(1)}, bf16[1,64,2048]{2,1,0:T(8,128)(2,1)S(1)}, u32[]{:S(2)}, u32[]{:S(2)}) %collective-permute-start.54) | collective-permute-done | bytes 262176 | tf_op jit(solution)/shard_map/ppermute | solution.py:24
  234.6 10.2 %collective-permute-done.59 = bf16[4,48,1024]{2,1,0:T(8,128)(2,1)S(1)} collective-permute-done((bf16[4,48,1024]{2,1,0:T(8,128)(2,1)S(1)}, bf16[4,48,1024]{2,1,0:T(8,128)(2,1)S(1)}, u32[]{:S(2)}, u32[]{:S(2)}) %collective-permute-start.59) | collective-permute-done | bytes 393248 | tf_op jit(solution)/shard_map/ppermute | solution.py:24
  244.8 1.8 collective-permute-done.58
  248.5 2.1 collective-permute-start.64
  250.7 2.3 collective-permute-start.62
  253.0 2.1 collective-permute-done.64
  255.1 2.1 collective-permute-done.63
  261.8 2.2 collective-permute-start.69
  264.0 2.3 collective-permute-start.67
  266.2 8.8 %shard_map.269 = bf16[8,256,1024]{2,1,0:T(8,128)(2,1)} custom-call(bf16[4,8,64,1024]{3,2,1,0:T(8,128)(2,1)S(1)} %bitcast.43, bf16[1024,1024]{1,0:T(8,128)(2,1)S(1)} %copy-done.5, f32[512,1024]{1,0:T(8,128)S(1)} %shard_map.263.side_ref), custom_call_target="tpu_custom_call" | custom-call | flops 4294967296 | bytes 16777216 | tf_op jit(solution)/shard_map/pallas_call | solution.py:1212
  275.1 6.4 %collective-permute-done.66 = bf16[8,32,2048]{2,1,0:T(8,128)(2,1)S(1)} collective-permute-done((bf16[8,32,2048]{2,1,0:T(8,128)(2,1)S(1)}, bf16[8,32,2048]{2,1,0:T(8,128)(2,1)S(1)}, u32[]{:S(2)}, u32[]{:S(2)}) %collective-permute-start.66) | collective-permute-done | bytes 1048608 | tf_op jit(solution)/shard_map/ppermute | solution.py:24
  282.9 2.2 collective-permute-start.74
  286.5 3.8 %shard_map.270 = f32[32,32,2048]{2,1,0:T(8,128)} custom-call(s32[1]{0:T(128)} %bitcast.14.own_ref, bf16[16,32,2048]{2,1,0:T(8,128)(2,1)S(1)} %pad_maximum_fusion.1.low_ref, bf16[16,32,2048]{2,1,0:T(8,128)(2,1)S(1)} %collective-permute-done.70.high_ref), custom_call_target="tpu_custom_call" | custom-call | bytes 12582912 | tf_op jit(solution)/shard_map/pallas_call | solution.py:119
  290.3 3.8 %shard_map.271 = f32[32,32,2048]{2,1,0:T(8,128)} custom-call(s32[1]{0:T(128)} %bitcast.3.own_ref, bf16[16,32,2048]{2,1,0:T(8,128)(2,1)S(1)} %pad_maximum_fusion.low_ref, bf16[16,32,2048]{2,1,0:T(8,128)(2,1)S(1)} %collective-permute-done.71.high_ref), custom_call_target="tpu_custom_call" | custom-call | bytes 12582912 | tf_op jit(solution)/shard_map/pallas_call | solution.py:119
  294.1 1.8 collective-permute-done.74
  295.9 7.4 %collective-permute-done.73 = bf16[4,48,1024]{2,1,0:T(8,128)(2,1)S(1)} collective-permute-done((bf16[4,48,1024]{2,1,0:T(8,128)(2,1)S(1)}, bf16[4,48,1024]{2,1,0:T(8,128)(2,1)S(1)}, u32[]{:S(2)}, u32[]{:S(2)}) %collective-permute-start.73) | collective-permute-done | bytes 393248 | tf_op jit(solution)/shard_map/ppermute | solution.py:24
  306.9 2.9 shard_map.272
  (259 shorter events, 95.4 us)
Async XLA Ops:
  1.7 17.2 %collective-permute-start = (bf16[8,32,1024]{2,1,0:T(8,128)(2,1)S(1)}, bf16[8,32,1024]{2,1,0:T(8,128)(2,1)S(1)}, u32[]{:S(2)}, u32[]{:S(2)}) collective-permute-start(bf16[8,32,1024]{2,1,0:T(8,128)(2,1)S(1)} %slice_bitcast_fusion), channel_id=1, source_target_pairs={{0,8},{8,16},{16,24},{1,9},{9,17},{17,25},{2,10},{10,18},{18,26},{... | collective-permute-start | bytes 1572872 | tf_op jit(solution)/shard_map/ppermute | solution.py:19
  20.3 5.6 %collective-permute-start.4 = (f32[4,1024]{1,0:T(4,128)S(1)}, f32[4,1024]{1,0:T(4,128)S(1)}, u32[]{:S(2)}, u32[]{:S(2)}) collective-permute-start(f32[4,1024]{1,0:T(4,128)S(1)} %pad_maximum_fusion.13), channel_id=1, source_target_pairs={{0,6},{1,7},{2,4},{3,5},{4,2},{5,3},{6,0},{7,1},{8,14},{9,15},{10,... | collective-permute-start | bytes 49160 | tf_op jit(solution)/shard_map/ppermute | solution.py:24
  24.0 4.6 %collective-permute-start.3 = (f32[4,1024]{1,0:T(4,128)S(1)}, f32[4,1024]{1,0:T(4,128)S(1)}, u32[]{:S(2)}, u32[]{:S(2)}) collective-permute-start(f32[4,1024]{1,0:T(4,128)S(1)} %pad_maximum_fusion.13), channel_id=1, source_target_pairs={{0,4},{1,5},{2,6},{3,7},{4,0},{5,1},{6,2},{7,3},{8,12},{9,13},{10,... | collective-permute-start | bytes 49160 | tf_op jit(solution)/shard_map/ppermute | solution.py:24
  28.8 5.4 %collective-permute-start.7 = (f32[4,1024]{1,0:T(4,128)S(1)}, f32[4,1024]{1,0:T(4,128)S(1)}, u32[]{:S(2)}, u32[]{:S(2)}) collective-permute-start(f32[4,1024]{1,0:T(4,128)S(1)} %pad_maximum_fusion.14), channel_id=1, source_target_pairs={{0,24},{8,16},{16,8},{24,0},{1,25},{9,17},{17,9},{25,1},{2,26},{10... | collective-permute-start | bytes 49160 | tf_op jit(solution)/shard_map/ppermute | solution.py:24
  47.2 5.9 %collective-permute-start.11 = (f32[2,1024]{1,0:T(2,128)S(1)}, f32[2,1024]{1,0:T(2,128)S(1)}, u32[]{:S(2)}, u32[]{:S(2)}) collective-permute-start(f32[2,1024]{1,0:T(2,128)S(1)} %add.445), channel_id=1, source_target_pairs={{0,6},{1,7},{2,4},{3,5},{4,2},{5,3},{6,0},{7,1},{8,14},{9,15},{10,... | collective-permute-start | bytes 24584 | tf_op jit(solution)/shard_map/ppermute | solution.py:24
  51.6 11.8 %collective-permute-start.15 = (bf16[128,1024]{1,0:T(8,128)(2,1)S(1)}, bf16[128,1024]{1,0:T(8,128)(2,1)S(1)}, u32[]{:S(2)}, u32[]{:S(2)}) collective-permute-start(bf16[128,1024]{1,0:T(8,128)(2,1)S(1)} %get-tuple-element.123), channel_id=1, source_target_pairs={{8,0},{16,8},{24,16},{9,1},{17,9},{25,17},{10,2},{18,10},{26,18},{... | collective-permute-start | bytes 786440 | tf_op jit(solution)/shard_map/ppermute | solution.py:19
  53.4 10.1 %collective-permute-start.14 = (f32[2,1024]{1,0:T(2,128)S(1)}, f32[2,1024]{1,0:T(2,128)S(1)}, u32[]{:S(2)}, u32[]{:S(2)}) collective-permute-start(f32[2,1024]{1,0:T(2,128)S(1)} %add_add_fusion.9), channel_id=1, source_target_pairs={{0,24},{8,16},{16,8},{24,0},{1,25},{9,17},{17,9},{25,1},{2,26},{10... | collective-permute-start | bytes 24584 | tf_op jit(solution)/shard_map/ppermute | solution.py:24
  56.6 6.9 %collective-permute-start.13 = (f32[2,1024]{1,0:T(2,128)S(1)}, f32[2,1024]{1,0:T(2,128)S(1)}, u32[]{:S(2)}, u32[]{:S(2)}) collective-permute-start(f32[2,1024]{1,0:T(2,128)S(1)} %add_add_fusion.9), channel_id=1, source_target_pairs={{0,16},{8,24},{16,0},{24,8},{1,17},{9,25},{17,1},{25,9},{2,18},{10... | collective-permute-start | bytes 24584 | tf_op jit(solution)/shard_map/ppermute | solution.py:24
  57.3 6.1 %collective-permute-start.12 = (f32[2,1024]{1,0:T(2,128)S(1)}, f32[2,1024]{1,0:T(2,128)S(1)}, u32[]{:S(2)}, u32[]{:S(2)}) collective-permute-start(f32[2,1024]{1,0:T(2,128)S(1)} %add_add_fusion.9), channel_id=1, source_target_pairs={{0,8},{8,0},{16,24},{24,16},{1,9},{9,1},{17,25},{25,17},{2,10},{10... | collective-permute-start | bytes 24584 | tf_op jit(solution)/shard_map/ppermute | solution.py:24
  71.6 5.8 %collective-permute-start.19 = (f32[4,2048]{1,0:T(4,128)S(1)}, f32[4,2048]{1,0:T(4,128)S(1)}, u32[]{:S(2)}, u32[]{:S(2)}) collective-permute-start(f32[4,2048]{1,0:T(4,128)S(1)} %add.452), channel_id=1, source_target_pairs={{0,6},{1,7},{2,4},{3,5},{4,2},{5,3},{6,0},{7,1},{8,14},{9,15},{10,... | collective-permute-start | bytes 98312 | tf_op jit(solution)/shard_map/ppermute | solution.py:24
  73.6 4.9 %collective-permute-start.18 = (f32[4,2048]{1,0:T(4,128)S(1)}, f32[4,2048]{1,0:T(4,128)S(1)}, u32[]{:S(2)}, u32[]{:S(2)}) collective-permute-start(f32[4,2048]{1,0:T(4,128)S(1)} %add.452), channel_id=1, source_target_pairs={{0,4},{1,5},{2,6},{3,7},{4,0},{5,1},{6,2},{7,3},{8,12},{9,13},{10,... | collective-permute-start | bytes 98312 | tf_op jit(solution)/shard_map/ppermute | solution.py:24
  78.9 5.2 %collective-permute-start.22 = (f32[4,2048]{1,0:T(4,128)S(1)}, f32[4,2048]{1,0:T(4,128)}, u32[]{:S(2)}, u32[]{:S(2)}) collective-permute-start(f32[4,2048]{1,0:T(4,128)S(1)} %add_add_fusion.3), channel_id=1, source_target_pairs={{0,24},{8,16},{16,8},{24,0},{1,25},{9,17},{17,9},{25,1},{2,26},{10... | collective-permute-start | bytes 98312 | tf_op jit(solution)/shard_map/ppermute | solution.py:24
  94.8 5.9 %collective-permute-start.26 = (f32[3,2048]{1,0:T(4,128)S(1)}, f32[3,2048]{1,0:T(4,128)S(1)}, u32[]{:S(2)}, u32[]{:S(2)}) collective-permute-start(f32[3,2048]{1,0:T(4,128)S(1)} %add.463), channel_id=1, source_target_pairs={{0,6},{1,7},{2,4},{3,5},{4,2},{5,3},{6,0},{7,1},{8,14},{9,15},{10,... | collective-permute-start | bytes 73736 | tf_op jit(solution)/shard_map/ppermute | solution.py:24
  96.6 5.2 %collective-permute-start.25 = (f32[3,2048]{1,0:T(4,128)S(1)}, f32[3,2048]{1,0:T(4,128)S(1)}, u32[]{:S(2)}, u32[]{:S(2)}) collective-permute-start(f32[3,2048]{1,0:T(4,128)S(1)} %add.463), channel_id=1, source_target_pairs={{0,4},{1,5},{2,6},{3,7},{4,0},{5,1},{6,2},{7,3},{8,12},{9,13},{10,... | collective-permute-start | bytes 73736 | tf_op jit(solution)/shard_map/ppermute | solution.py:24
  102.1 5.0 %collective-permute-start.29 = (f32[3,2048]{1,0:T(4,128)S(1)}, f32[3,2048]{1,0:T(4,128)S(1)}, u32[]{:S(2)}, u32[]{:S(2)}) collective-permute-start(f32[3,2048]{1,0:T(4,128)S(1)} %add_add_fusion.1), channel_id=1, source_target_pairs={{0,24},{8,16},{16,8},{24,0},{1,25},{9,17},{17,9},{25,1},{2,26},{10... | collective-permute-start | bytes 73736 | tf_op jit(solution)/shard_map/ppermute | solution.py:24
  118.4 11.8 %collective-permute-start.33 = (bf16[16,32,2048]{2,1,0:T(8,128)(2,1)S(1)}, bf16[16,32,2048]{2,1,0:T(8,128)(2,1)}, u32[]{:S(2)}, u32[]{:S(2)}) collective-permute-start(bf16[16,32,2048]{2,1,0:T(8,128)(2,1)S(1)} %get-tuple-element.141), channel_id=1, source_target_pairs={{0,1},{1,0},{2,3},{3,2},{4,5},{5,4},{6,7},{7,6},{8,9},{9,8},{10,11... | collective-permute-start | bytes 6291464 | tf_op jit(solution)/shard_map/ppermute | solution.py:24
  118.4 11.9 %collective-permute-start.34 = (bf16[16,32,2048]{2,1,0:T(8,128)(2,1)S(1)}, bf16[16,32,2048]{2,1,0:T(8,128)(2,1)S(1)}, u32[]{:S(2)}, u32[]{:S(2)}) collective-permute-start(bf16[16,32,2048]{2,1,0:T(8,128)(2,1)S(1)} %get-tuple-element.142), channel_id=1, source_target_pairs={{0,1},{1,0},{2,3},{3,2},{4,5},{5,4},{6,7},{7,6},{8,9},{9,8},{10,11... | collective-permute-start | bytes 6291464 | tf_op jit(solution)/shard_map/ppermute | solution.py:24
  131.6 8.7 %collective-permute-start.36 = (bf16[128,1024]{1,0:T(8,128)(2,1)S(1)}, bf16[128,1024]{1,0:T(8,128)(2,1)S(1)}, u32[]{:S(2)}, u32[]{:S(2)}) collective-permute-start(bf16[128,1024]{1,0:T(8,128)(2,1)S(1)} %get-tuple-element.144), channel_id=1, source_target_pairs={{8,0},{16,8},{24,16},{9,1},{17,9},{25,17},{10,2},{18,10},{26,18},{... | collective-permute-start | bytes 786440 | tf_op jit(solution)/shard_map/ppermute | solution.py:19
  145.3 23.1 %collective-permute-start.41 = (bf16[8,32,2048]{2,1,0:T(8,128)(2,1)S(1)}, bf16[8,32,2048]{2,1,0:T(8,128)(2,1)S(1)}, u32[]{:S(2)}, u32[]{:S(2)}) collective-permute-start(bf16[8,32,2048]{2,1,0:T(8,128)(2,1)S(1)} %slice.158), channel_id=1, source_target_pairs={{0,16},{8,24},{16,0},{24,8},{1,17},{9,25},{17,1},{25,9},{2,18},{10... | collective-permute-start | bytes 3145736 | tf_op jit(solution)/shard_map/ppermute | solution.py:24
  146.7 23.1 %collective-permute-start.40 = (bf16[8,32,2048]{2,1,0:T(8,128)(2,1)S(1)}, bf16[8,32,2048]{2,1,0:T(8,128)(2,1)S(1)}, u32[]{:S(2)}, u32[]{:S(2)}) collective-permute-start(bf16[8,32,2048]{2,1,0:T(8,128)(2,1)S(1)} %slice.157), channel_id=1, source_target_pairs={{0,8},{8,0},{16,24},{24,16},{1,9},{9,1},{17,25},{25,17},{2,10},{10... | collective-permute-start | bytes 3145736 | tf_op jit(solution)/shard_map/ppermute | solution.py:24
  146.7 5.4 %collective-permute-start.39 = (f32[2,1024]{1,0:T(2,128)S(1)}, f32[2,1024]{1,0:T(2,128)S(1)}, u32[]{:S(2)}, u32[]{:S(2)}) collective-permute-start(f32[2,1024]{1,0:T(2,128)S(1)} %add.473), channel_id=1, source_target_pairs={{0,6},{1,7},{2,4},{3,5},{4,2},{5,3},{6,0},{7,1},{8,14},{9,15},{10,... | collective-permute-start | bytes 24584 | tf_op jit(solution)/shard_map/ppermute | solution.py:24
  177.6 11.4 %collective-permute-start.50 = (bf16[4,32,2048]{2,1,0:T(8,128)(2,1)S(1)}, bf16[4,32,2048]{2,1,0:T(8,128)(2,1)S(1)}, u32[]{:S(2)}, u32[]{:S(2)}) collective-permute-start(bf16[4,32,2048]{2,1,0:T(8,128)(2,1)S(1)} %slice.162), channel_id=1, source_target_pairs={{0,8},{8,0},{16,24},{24,16},{1,9},{9,1},{17,25},{25,17},{2,10},{10... | collective-permute-start | bytes 1572872 | tf_op jit(solution)/shard_map/ppermute | solution.py:24
  177.9 11.1 %collective-permute-start.49 = (bf16[4,32,2048]{2,1,0:T(8,128)(2,1)S(1)}, bf16[4,32,2048]{2,1,0:T(8,128)(2,1)S(1)}, u32[]{:S(2)}, u32[]{:S(2)}) collective-permute-start(bf16[4,32,2048]{2,1,0:T(8,128)(2,1)S(1)} %slice.160), channel_id=1, source_target_pairs={{0,16},{8,24},{16,0},{24,8},{1,17},{9,25},{17,1},{25,9},{2,18},{10... | collective-permute-start | bytes 1572872 | tf_op jit(solution)/shard_map/ppermute | solution.py:24
  179.8 8.1 %collective-permute-start.48 = (f32[2,1024]{1,0:T(2,128)S(1)}, f32[2,1024]{1,0:T(2,128)S(1)}, u32[]{:S(2)}, u32[]{:S(2)}) collective-permute-start(f32[2,1024]{1,0:T(2,128)S(1)} %add.482), channel_id=1, source_target_pairs={{0,6},{1,7},{2,4},{3,5},{4,2},{5,3},{6,0},{7,1},{8,14},{9,15},{10,... | collective-permute-start | bytes 24584 | tf_op jit(solution)/shard_map/ppermute | solution.py:24
  181.7 6.2 %collective-permute-start.47 = (f32[2,1024]{1,0:T(2,128)S(1)}, f32[2,1024]{1,0:T(2,128)S(1)}, u32[]{:S(2)}, u32[]{:S(2)}) collective-permute-start(f32[2,1024]{1,0:T(2,128)S(1)} %add.482), channel_id=1, source_target_pairs={{0,4},{1,5},{2,6},{3,7},{4,0},{5,1},{6,2},{7,3},{8,12},{9,13},{10,... | collective-permute-start | bytes 24584 | tf_op jit(solution)/shard_map/ppermute | solution.py:24
  182.8 5.1 %collective-permute-start.46 = (f32[2,1024]{1,0:T(2,128)S(1)}, f32[2,1024]{1,0:T(2,128)S(1)}, u32[]{:S(2)}, u32[]{:S(2)}) collective-permute-start(f32[2,1024]{1,0:T(2,128)S(1)} %add.482), channel_id=1, source_target_pairs={{0,2},{1,3},{2,0},{3,1},{4,6},{5,7},{6,4},{7,5},{8,10},{9,11},{10,... | collective-permute-start | bytes 24584 | tf_op jit(solution)/shard_map/ppermute | solution.py:24
  189.4 18.9 %collective-permute-start.51 = (bf16[1,64,2048]{2,1,0:T(8,128)(2,1)S(1)}, bf16[1,64,2048]{2,1,0:T(8,128)(2,1)S(1)}, u32[]{:S(2)}, u32[]{:S(2)}) collective-permute-start(bf16[1,64,2048]{2,1,0:T(8,128)(2,1)S(1)} %pad_maximum_fusion.8), channel_id=1, source_target_pairs={{0,4},{1,5},{2,6},{3,7},{4,0},{5,1},{6,2},{7,3},{8,12},{9,13},{10,... | collective-permute-start | bytes 786440 | tf_op jit(solution)/shard_map/ppermute | solution.py:24
  190.6 17.7 %collective-permute-start.52 = (bf16[1,64,2048]{2,1,0:T(8,128)(2,1)S(1)}, bf16[1,64,2048]{2,1,0:T(8,128)(2,1)S(1)}, u32[]{:S(2)}, u32[]{:S(2)}) collective-permute-start(bf16[1,64,2048]{2,1,0:T(8,128)(2,1)S(1)} %pad_maximum_fusion.9), channel_id=1, source_target_pairs={{0,2},{1,3},{2,0},{3,1},{4,6},{5,7},{6,4},{7,5},{8,10},{9,11},{10,... | collective-permute-start | bytes 786440 | tf_op jit(solution)/shard_map/ppermute | solution.py:24
  191.5 16.7 %collective-permute-start.53 = (bf16[1,64,2048]{2,1,0:T(8,128)(2,1)S(1)}, bf16[1,64,2048]{2,1,0:T(8,128)(2,1)S(1)}, u32[]{:S(2)}, u32[]{:S(2)}) collective-permute-start(bf16[1,64,2048]{2,1,0:T(8,128)(2,1)S(1)} %pad_maximum_fusion.10), channel_id=1, source_target_pairs={{0,6},{1,7},{2,4},{3,5},{4,2},{5,3},{6,0},{7,1},{8,14},{9,15},{10,... | collective-permute-start | bytes 786440 | tf_op jit(solution)/shard_map/ppermute | solution.py:24
  212.7 21.0 %collective-permute-start.57 = (bf16[4,48,1024]{2,1,0:T(8,128)(2,1)S(1)}, bf16[4,48,1024]{2,1,0:T(8,128)(2,1)S(1)}, u32[]{:S(2)}, u32[]{:S(2)}) collective-permute-start(bf16[4,48,1024]{2,1,0:T(8,128)(2,1)S(1)} %get-tuple-element.224), channel_id=1, source_target_pairs={{0,16},{8,24},{16,0},{24,8},{1,17},{9,25},{17,1},{25,9},{2,18},{10... | collective-permute-start | bytes 1179656 | tf_op jit(solution)/shard_map/ppermute | solution.py:24
  214.0 19.7 %collective-permute-start.56 = (bf16[4,48,1024]{2,1,0:T(8,128)(2,1)S(1)}, bf16[4,48,1024]{2,1,0:T(8,128)(2,1)S(1)}, u32[]{:S(2)}, u32[]{:S(2)}) collective-permute-start(bf16[4,48,1024]{2,1,0:T(8,128)(2,1)S(1)} %get-tuple-element.225), channel_id=1, source_target_pairs={{0,8},{8,0},{16,24},{24,16},{1,9},{9,1},{17,25},{25,17},{2,10},{10... | collective-permute-start | bytes 1179656 | tf_op jit(solution)/shard_map/ppermute | solution.py:24
  215.6 18.1 %collective-permute-start.54 = (bf16[1,64,2048]{2,1,0:T(8,128)(2,1)S(1)}, bf16[1,64,2048]{2,1,0:T(8,128)(2,1)S(1)}, u32[]{:S(2)}, u32[]{:S(2)}) collective-permute-start(bf16[1,64,2048]{2,1,0:T(8,128)(2,1)S(1)} %add_convert_fusion.8), channel_id=1, source_target_pairs={{0,4},{1,5},{2,6},{3,7},{4,0},{5,1},{6,2},{7,3},{8,12},{9,13},{10,... | collective-permute-start | bytes 786440 | tf_op jit(solution)/shard_map/ppermute | solution.py:24
  233.8 12.9 %collective-permute-start.58 = (bf16[2,64,2048]{2,1,0:T(8,128)(2,1)S(1)}, bf16[2,64,2048]{2,1,0:T(8,128)(2,1)S(1)}, u32[]{:S(2)}, u32[]{:S(2)}) collective-permute-start(bf16[2,64,2048]{2,1,0:T(8,128)(2,1)S(1)} %pad_maximum_fusion.6), channel_id=1, source_target_pairs={{0,2},{1,3},{2,0},{3,1},{4,6},{5,7},{6,4},{7,5},{8,10},{9,11},{10,... | collective-permute-start | bytes 1572872 | tf_op jit(solution)/shard_map/ppermute | solution.py:24
  233.8 11.0 %collective-permute-start.59 = (bf16[4,48,1024]{2,1,0:T(8,128)(2,1)S(1)}, bf16[4,48,1024]{2,1,0:T(8,128)(2,1)S(1)}, u32[]{:S(2)}, u32[]{:S(2)}) collective-permute-start(bf16[4,48,1024]{2,1,0:T(8,128)(2,1)S(1)} %get-tuple-element.223), channel_id=1, source_target_pairs={{0,24},{8,16},{16,8},{24,0},{1,25},{9,17},{17,9},{25,1},{2,26},{10... | collective-permute-start | bytes 1179656 | tf_op jit(solution)/shard_map/ppermute | solution.py:24
  246.8 12.0 %collective-permute-start.61 = (bf16[4,32,2048]{2,1,0:T(8,128)(2,1)S(1)}, bf16[4,32,2048]{2,1,0:T(8,128)(2,1)S(1)}, u32[]{:S(2)}, u32[]{:S(2)}) collective-permute-start(bf16[4,32,2048]{2,1,0:T(8,128)(2,1)S(1)} %get-tuple-element.226), channel_id=1, source_target_pairs={{0,8},{8,0},{16,24},{24,16},{1,9},{9,1},{17,25},{25,17},{2,10},{10... | collective-permute-start | bytes 1572872 | tf_op jit(solution)/shard_map/ppermute | solution.py:24
  247.4 11.8 %collective-permute-start.60 = (bf16[4,32,2048]{2,1,0:T(8,128)(2,1)S(1)}, bf16[4,32,2048]{2,1,0:T(8,128)(2,1)S(1)}, u32[]{:S(2)}, u32[]{:S(2)}) collective-permute-start(bf16[4,32,2048]{2,1,0:T(8,128)(2,1)S(1)} %get-tuple-element.227), channel_id=1, source_target_pairs={{0,16},{8,24},{16,0},{24,8},{1,17},{9,25},{17,1},{25,9},{2,18},{10... | collective-permute-start | bytes 1572872 | tf_op jit(solution)/shard_map/ppermute | solution.py:24
  248.5 6.6 %collective-permute-start.64 = (bf16[1,48,1024]{2,1,0:T(8,128)(2,1)S(1)}, bf16[1,48,1024]{2,1,0:T(8,128)(2,1)S(1)}, u32[]{:S(2)}, u32[]{:S(2)}) collective-permute-start(bf16[1,48,1024]{2,1,0:T(8,128)(2,1)S(1)} %get-tuple-element.238), channel_id=1, source_target_pairs={{0,6},{1,7},{2,4},{3,5},{4,2},{5,3},{6,0},{7,1},{8,14},{9,15},{10,... | collective-permute-start | bytes 294920 | tf_op jit(solution)/shard_map/ppermute | solution.py:24
  250.6 6.5 %collective-permute-start.63 = (bf16[1,48,1024]{2,1,0:T(8,128)(2,1)S(1)}, bf16[1,48,1024]{2,1,0:T(8,128)(2,1)S(1)}, u32[]{:S(2)}, u32[]{:S(2)}) collective-permute-start(bf16[1,48,1024]{2,1,0:T(8,128)(2,1)S(1)} %get-tuple-element.239), channel_id=1, source_target_pairs={{0,2},{1,3},{2,0},{3,1},{4,6},{5,7},{6,4},{7,5},{8,10},{9,11},{10,... | collective-permute-start | bytes 294920 | tf_op jit(solution)/shard_map/ppermute | solution.py:24
  250.7 7.3 %collective-permute-start.62 = (bf16[1,48,1024]{2,1,0:T(8,128)(2,1)S(1)}, bf16[1,48,1024]{2,1,0:T(8,128)(2,1)S(1)}, u32[]{:S(2)}, u32[]{:S(2)}) collective-permute-start(bf16[1,48,1024]{2,1,0:T(8,128)(2,1)S(1)} %get-tuple-element.240), channel_id=1, source_target_pairs={{0,4},{1,5},{2,6},{3,7},{4,0},{5,1},{6,2},{7,3},{8,12},{9,13},{10,... | collective-permute-start | bytes 294920 | tf_op jit(solution)/shard_map/ppermute | solution.py:24
  259.4 22.1 %collective-permute-start.66 = (bf16[8,32,2048]{2,1,0:T(8,128)(2,1)S(1)}, bf16[8,32,2048]{2,1,0:T(8,128)(2,1)S(1)}, u32[]{:S(2)}, u32[]{:S(2)}) collective-permute-start(bf16[8,32,2048]{2,1,0:T(8,128)(2,1)S(1)} %pad_maximum_fusion.5), channel_id=1, source_target_pairs={{0,16},{8,24},{16,0},{24,8},{1,17},{9,25},{17,1},{25,9},{2,18},{10... | collective-permute-start | bytes 3145736 | tf_op jit(solution)/shard_map/ppermute | solution.py:24
  260.3 21.4 %collective-permute-start.65 = (bf16[8,32,2048]{2,1,0:T(8,128)(2,1)S(1)}, bf16[8,32,2048]{2,1,0:T(8,128)(2,1)S(1)}, u32[]{:S(2)}, u32[]{:S(2)}) collective-permute-start(bf16[8,32,2048]{2,1,0:T(8,128)(2,1)S(1)} %pad_maximum_fusion.4), channel_id=1, source_target_pairs={{0,8},{8,0},{16,24},{24,16},{1,9},{9,1},{17,25},{25,17},{2,10},{10... | collective-permute-start | bytes 3145736 | tf_op jit(solution)/shard_map/ppermute | solution.py:24
  261.8 13.3 %collective-permute-start.69 = (bf16[1,48,1024]{2,1,0:T(8,128)(2,1)S(1)}, bf16[1,48,1024]{2,1,0:T(8,128)(2,1)S(1)}, u32[]{:S(2)}, u32[]{:S(2)}) collective-permute-start(bf16[1,48,1024]{2,1,0:T(8,128)(2,1)S(1)} %get-tuple-element.215), channel_id=1, source_target_pairs={{0,6},{1,7},{2,4},{3,5},{4,2},{5,3},{6,0},{7,1},{8,14},{9,15},{10,... | collective-permute-start | bytes 294920 | tf_op jit(solution)/shard_map/ppermute | solution.py:24
  264.0 11.1 %collective-permute-start.68 = (bf16[1,48,1024]{2,1,0:T(8,128)(2,1)S(1)}, bf16[1,48,1024]{2,1,0:T(8,128)(2,1)S(1)}, u32[]{:S(2)}, u32[]{:S(2)}) collective-permute-start(bf16[1,48,1024]{2,1,0:T(8,128)(2,1)S(1)} %get-tuple-element.215), channel_id=1, source_target_pairs={{0,2},{1,3},{2,0},{3,1},{4,6},{5,7},{6,4},{7,5},{8,10},{9,11},{10,... | collective-permute-start | bytes 294920 | tf_op jit(solution)/shard_map/ppermute | solution.py:24
  264.0 11.1 %collective-permute-start.67 = (bf16[1,48,1024]{2,1,0:T(8,128)(2,1)S(1)}, bf16[1,48,1024]{2,1,0:T(8,128)(2,1)S(1)}, u32[]{:S(2)}, u32[]{:S(2)}) collective-permute-start(bf16[1,48,1024]{2,1,0:T(8,128)(2,1)S(1)} %get-tuple-element.215), channel_id=1, source_target_pairs={{0,4},{1,5},{2,6},{3,7},{4,0},{5,1},{6,2},{7,3},{8,12},{9,13},{10,... | collective-permute-start | bytes 294920 | tf_op jit(solution)/shard_map/ppermute | solution.py:24
  282.3 8.0 %collective-permute-start.71 = (bf16[16,32,2048]{2,1,0:T(8,128)(2,1)S(1)}, bf16[16,32,2048]{2,1,0:T(8,128)(2,1)S(1)}, u32[]{:S(2)}, u32[]{:S(2)}) collective-permute-start(bf16[16,32,2048]{2,1,0:T(8,128)(2,1)S(1)} %pad_maximum_fusion.low_ref), channel_id=1, source_target_pairs={{0,1},{1,0},{2,3},{3,2},{4,5},{5,4},{6,7},{7,6},{8,9},{9,8},{10,11... | collective-permute-start | bytes 6291464 | tf_op jit(solution)/shard_map/ppermute | solution.py:24
  282.9 13.0 %collective-permute-start.74 = (bf16[4,48,1024]{2,1,0:T(8,128)(2,1)S(1)}, bf16[4,48,1024]{2,1,0:T(8,128)(2,1)S(1)}, u32[]{:S(2)}, u32[]{:S(2)}) collective-permute-start(bf16[4,48,1024]{2,1,0:T(8,128)(2,1)S(1)} %pad_maximum_fusion.7), channel_id=1, source_target_pairs={{0,24},{8,16},{16,8},{24,0},{1,25},{9,17},{17,9},{25,1},{2,26},{10... | collective-permute-start | bytes 1179656 | tf_op jit(solution)/shard_map/ppermute | solution.py:24
  285.1 18.2 %collective-permute-start.73 = (bf16[4,48,1024]{2,1,0:T(8,128)(2,1)S(1)}, bf16[4,48,1024]{2,1,0:T(8,128)(2,1)S(1)}, u32[]{:S(2)}, u32[]{:S(2)}) collective-permute-start(bf16[4,48,1024]{2,1,0:T(8,128)(2,1)S(1)} %pad_maximum_fusion.7), channel_id=1, source_target_pairs={{0,16},{8,24},{16,0},{24,8},{1,17},{9,25},{17,1},{25,9},{2,18},{10... | collective-permute-start | bytes 1179656 | tf_op jit(solution)/shard_map/ppermute | solution.py:24
  285.8 17.5 %collective-permute-start.72 = (bf16[4,48,1024]{2,1,0:T(8,128)(2,1)S(1)}, bf16[4,48,1024]{2,1,0:T(8,128)(2,1)S(1)}, u32[]{:S(2)}, u32[]{:S(2)}) collective-permute-start(bf16[4,48,1024]{2,1,0:T(8,128)(2,1)S(1)} %pad_maximum_fusion.7), channel_id=1, source_target_pairs={{0,8},{8,0},{16,24},{24,16},{1,9},{9,1},{17,25},{25,17},{2,10},{10... | collective-permute-start | bytes 1179656 | tf_op jit(solution)/shard_map/ppermute | solution.py:24
  (57 other events, 473.6 us)

commit v7 on v6

--- a/solution.py
+++ b/solution.py
@@ -10,7 +10,7 @@
 
 GW = 32
 EPS = 1e-05
-VMEM_LIMIT = 36 * 1024 * 1024
+VMEM_LIMIT = 40 * 1024 * 1024
 
 
 def shifted(value, axis, by):
@@ -908,7 +908,7 @@
     pixels = images * image_rows * cols
     block = 256
     steps = mid // block
-    strip = 512
+    strip = 1024
     strips = wide // strip
 
     valid = valid_mask.astype(WIDE)

time: 311 us -> 312 us (level)
    unnamed x64 -> x62, local copies, waits for them, and re-layouts: 7.11 us -> 7.11 us
  transfers between devices with their start and end apart: 76 -> 76, of which waited for: 48 -> 49; matrix products, arithmetic and copies ran while one was open for 1% -> 1% of each run, Pallas kernels for 23% -> 23%
where the time goes in v7:
time: 312 us; the launch traced here: 311 us
  Pallas kernels  106 us (34%)
  waiting for transfers between devices  91.4 us (29%)
  starting transfers between devices  90.7 us (29%)
  local copies, waits for them, and re-layouts  11.7 us (4%)
  other arithmetic  9.14 us (3%)
    ppermute x73, waiting for transfers between devices, exchange(): return lax.ppermute(value, axis, [(i, i ^ mask) for i in range(peers)])  88.6 us
    ppermute x73, starting transfers between devices, exchange(): return lax.ppermute(value, axis, [(i, i ^ mask) for i in range(peers)])  82.6 us
    pallas_call x1, Pallas kernels, per_device(): call(functools.partial(conv_back_kernel, (images, tall, half_cols)), step...  15 us
    pallas_call x1, Pallas kernels, per_device(): call(functools.partial(reduce_kernel, (images, image_rows, cols), lead),...  11.6 us
    pallas_call x1, Pallas kernels, per_device(): call(functools.partial(weights_kernel, 16), strips, [SCALARS, SCALARS, wi...  10.5 us
    pallas_call x3, Pallas kernels, plain_order(): pl.pallas_call(functools.partial(spread_kernel, order), grid=(cols // wid...  10.5 us
    pallas_call x1, Pallas kernels, per_device(): call(functools.partial(reduced_back_kernel, 16), steps, [SCALARS, SCALARS...  9.61 us
    pallas_call x1, Pallas kernels, images_back(): call(functools.partial(images_back_kernel, (image_rows, cols)), images, [...  8.85 us
  transfers between devices with their start and end apart: 76, of which 49 were waited for; matrix products, arithmetic and copies ran while one was open for 1% of the time, Pallas kernels for 23%

profile of v7, /device:TPU:0, one launch (start us, length us, event | category | flops | bytes accessed | tf_op | source)
XLA Modules:
  0.0 311.1 jit_solution(3310408209899304407)
XLA Ops:
  1.7 4.9 %collective-permute-start = (bf16[8,32,1024]{2,1,0:T(8,128)(2,1)S(1)}, bf16[8,32,1024]{2,1,0:T(8,128)(2,1)S(1)}, u32[]{:S(2)}, u32[]{:S(2)}) collective-permute-start(bf16[8,32,1024]{2,1,0:T(8,128)(2,1)S(1)} %slice_bitcast_fusion), channel_id=1, source_target_pairs={{0,8},{8,16},{16,24},{1,9},{9,17},{17,25},{2,10},{10,18},{18,26},{... | collective-permute-start | bytes 1572872 | tf_op jit(solution)/shard_map/ppermute | solution.py:19
  7.3 11.6 %shard_map.254 = (bf16[4,8,64,1024]{3,2,1,0:T(8,128)(2,1)}, f32[2048,1024]{1,0:T(8,128)}, f32[3,1024]{1,0:T(4,128)S(1)}, f32[1,1024]{1,0:T(1,128)S(1)}) custom-call(f32[8]{0:T(128)S(1)} %convert_element_type.123.valid_ref, bf16[2048,1024]{1,0:T(8,128)(2,1)} %bitcast.52, bf16[1024,1024]{1,0:T(8,128)(2,1)} %w_ref.11), custom_call_target="tpu_custom_call" | custom-call | flops 5368709120 | bytes 20971520 | tf_op jit(solution)/shard_map/pallas_call | solution.py:932
  20.3 3.7 %collective-permute-start.4 = (f32[4,1024]{1,0:T(4,128)S(1)}, f32[4,1024]{1,0:T(4,128)S(1)}, u32[]{:S(2)}, u32[]{:S(2)}) collective-permute-start(f32[4,1024]{1,0:T(4,128)S(1)} %pad_maximum_fusion.13), channel_id=1, source_target_pairs={{0,6},{1,7},{2,4},{3,5},{4,2},{5,3},{6,0},{7,1},{8,14},{9,15},{10,... | collective-permute-start | bytes 49160 | tf_op jit(solution)/shard_map/ppermute | solution.py:24
  25.9 2.7 collective-permute-done.3
  28.8 2.2 collective-permute-start.7
  37.6 8.4 %shard_map.256 = (f32[512,1024]{1,0:T(8,128)S(1)}, f32[2,1024]{1,0:T(2,128)S(1)}, f32[1,1024]{1,0:T(1,128)S(1)}, bf16[128,1024]{1,0:T(8,128)(2,1)S(1)}, bf16[256,1024]{1,0:T(8,128)(2,1)S(1)}) custom-call(f32[4]{0:T(128)S(1)} %pad_maximum_fusion.18.scalar_ref, f32[8]{0:T(128)S(1)} %convert_element_type.123.valid_ref, ...), custom_call_target="tpu_custom_call" | custom-call | flops 2415919104 | bytes 14680064 | tf_op jit(solution)/shard_map/pallas_call | solution.py:970
  49.3 2.3 collective-permute-start.9
  53.4 3.2 %collective-permute-start.14 = (f32[2,1024]{1,0:T(2,128)S(1)}, f32[2,1024]{1,0:T(2,128)S(1)}, u32[]{:S(2)}, u32[]{:S(2)}) collective-permute-start(f32[2,1024]{1,0:T(2,128)S(1)} %add_add_fusion.9), channel_id=1, source_target_pairs={{0,24},{8,16},{16,8},{24,0},{1,25},{9,17},{17,9},{25,1},{2,26},{10... | collective-permute-start | bytes 24584 | tf_op jit(solution)/shard_map/ppermute | solution.py:24
  57.4 5.9 %shard_map.257 = (f32[512,2048]{1,0:T(8,128)}, f32[3,2048]{1,0:T(4,128)S(1)}) custom-call(f32[8]{0:T(128)S(1)} %convert_element_type.123.valid_ref, bf16[2048,1024]{1,0:T(8,128)(2,1)} %bitcast.45, bf16[1024,2048]{1,0:T(8,128)(2,1)S(1)} %copy-done, f32[1,1024]{1,0:T(1,128)S(1)} %slice.121.sampled_ref), custom_call_target="tpu_custom_call" | custom-call | flops 2147483648 | bytes 10485760 | tf_op jit(solution)/shard_map/pallas_call | solution.py:1003
  63.5 5.8 %shard_map.258 = (bf16[512,1024]{1,0:T(8,128)(2,1)S(1)}, f32[512,2048]{1,0:T(8,128)}, f32[4,2048]{1,0:T(4,128)S(1)}, f32[2,2048]{1,0:T(2,128)S(1)}) custom-call(f32[4]{0:T(128)S(1)} %pad_maximum_fusion.18.scalar_ref, f32[8]{0:T(128)S(1)} %convert_element_type.123.valid_ref, f32[512,1024]{1,0:T(8,128)S(1)} %get-tuple-element.121.grouped_ref, ...), custom_call_target="tpu_custom_call" | custom-call | flops 2147483648 | bytes 12582912 | tf_op jit(solution)/shard_map/pallas_call | solution.py:1012
  71.4 2.0 collective-permute-start.19
  78.7 2.4 collective-permute-start.22
  86.7 6.5 %shard_map.260 = (bf16[512,2048]{1,0:T(8,128)(2,1)}, f32[3,2048]{1,0:T(4,128)S(1)}) custom-call(f32[4]{0:T(128)S(1)} %pad_maximum_fusion.18.scalar_ref, f32[8]{0:T(128)S(1)} %convert_element_type.123.valid_ref, f32[512,2048]{1,0:T(8,128)} %get-tuple-element.127.expanded_ref, f32[512,2048]{1,0:T(8,128)} %get-tuple-element.128.projected_ref, ...), custom_call_target="tpu_custom_call" | custom-call | flops 20971520 | bytes 12582912 | tf_op jit(solution)/shard_map/pallas_call | solution.py:1033
  94.4 1.8 collective-permute-start.26
  103.3 1.9 collective-permute-start.27
  107.3 10.5 %shard_map.261 = (bf16[512,2048]{1,0:T(8,128)(2,1)S(1)}, bf16[512,2048]{1,0:T(8,128)(2,1)S(1)}, bf16[16,32,2048]{2,1,0:T(8,128)(2,1)S(1)}, bf16[16,32,2048]{2,1,...) custom-call(f32[4]{0:T(128)S(1)} %pad_maximum_fusion.18.scalar_ref, ...), custom_call_target="tpu_custom_call" | custom-call | flops 4294967296 | bytes 25165824 | tf_op jit(solution)/shard_map/pallas_call | solution.py:1058
  119.6 4.2 %shard_map.262 = (f32[512,1024]{1,0:T(8,128)S(1)}, f32[2,1024]{1,0:T(2,128)S(1)}, bf16[128,1024]{1,0:T(8,128)(2,1)S(1)}) custom-call(f32[4]{0:T(128)S(1)} %pad_maximum_fusion.18.scalar_ref, bf16[512,2048]{1,0:T(8,128)(2,1)S(1)} %get-tuple-element.137.d_ref, bf16[1024,2048]{1,0:T(8,128)(2,1)S(1)} %copy-done.3, f32[512,1024]{1,0:T(8,128)S(1)} %copy-done.7, ...), custom_call_target="tpu_custom_call" | custom-call | flops 2147483648 | bytes 10485760 | tf_op jit(solution)/shard_map/pallas_call | solution.py:1096
  123.9 2.7 collective-permute-start.32
  132.4 1.8 collective-permute-start.36
  135.8 2.4 shard_map.263.side_ref
  138.2 2.8 collective-permute-done.36.below_grad_ref
  141.0 2.4 add_convert_fusion.1
  149.9 1.8 collective-permute-start.37
  153.7 15.0 %shard_map.265 = (f32[2048,1024]{1,0:T(8,128)}, f32[2,1024]{1,0:T(2,128)S(1)}, bf16[9,32,1024]{2,1,0:T(8,128)(2,1)S(1)}) custom-call(f32[4]{0:T(128)S(1)} %pad_maximum_fusion.18.scalar_ref, s32[1]{0:T(128)} %bitcast.3.own_ref, f32[8]{0:T(128)S(1)} %convert_element_type.123.valid_ref, f32[512,1024]{1,0:T(8,128)S(1)} %get-tuple-element.138.grad_ref, ...), custom_call_target="tpu_custom_call" | custom-call | flops 4831838208 | bytes 25165824 | tf_op jit(solution)/shard_map/pallas_call | solution.py:1131
  170.6 1.9 collective-permute-start.44
  183.2 1.9 collective-permute-start.46
  192.9 2.2 collective-permute-start.53
  195.1 9.6 %shard_map.268 = (bf16[2048,1024]{1,0:T(8,128)(2,1)}, bf16[16,32,1024]{2,1,0:T(8,128)(2,1)S(1)}, bf16[16,32,1024]{2,1,0:T(8,128)(2,1)S(1)}) custom-call(f32[4]{0:T(128)S(1)} %pad_maximum_fusion.18.scalar_ref, f32[8]{0:T(128)S(1)} %convert_element_type.123.valid_ref, f32[2048,1024]{1,0:T(8,128)} %get-tuple-element.154.grad_ref, ...), custom_call_target="tpu_custom_call" | custom-call | flops 4294967296 | bytes 27262976 | tf_op jit(solution)/shard_map/pallas_call | solution.py:1188
  204.8 4.3 %collective-permute-done.51 = bf16[1,64,2048]{2,1,0:T(8,128)(2,1)S(1)} collective-permute-done((bf16[1,64,2048]{2,1,0:T(8,128)(2,1)S(1)}, bf16[1,64,2048]{2,1,0:T(8,128)(2,1)S(1)}, u32[]{:S(2)}, u32[]{:S(2)}) %collective-permute-start.51) | collective-permute-done | bytes 262176 | tf_op jit(solution)/shard_map/ppermute | solution.py:24
  209.3 3.4 %collective-permute-done.55 = bf16[16,48,1024]{2,1,0:T(8,128)(2,1)S(1)} collective-permute-done((bf16[16,48,1024]{2,1,0:T(8,128)(2,1)S(1)}, bf16[16,48,1024]{2,1,0:T(8,128)(2,1)S(1)}, u32[]{:S(2)}, u32[]{:S(2)}) %collective-permute-start.55) | collective-permute-done | bytes 1572896 | tf_op jit(solution)/shard_map/ppermute | solution.py:24
  216.4 6.4 %collective-permute-start.54 = (bf16[1,64,2048]{2,1,0:T(8,128)(2,1)S(1)}, bf16[1,64,2048]{2,1,0:T(8,128)(2,1)S(1)}, u32[]{:S(2)}, u32[]{:S(2)}) collective-permute-start(bf16[1,64,2048]{2,1,0:T(8,128)(2,1)S(1)} %add_convert_fusion.8), channel_id=1, source_target_pairs={{0,4},{1,5},{2,6},{3,7},{4,0},{5,1},{6,2},{7,3},{8,12},{9,13},{10,... | collective-permute-start | bytes 786440 | tf_op jit(solution)/shard_map/ppermute | solution.py:24
  222.8 11.7 %collective-permute-done.54 = bf16[1,64,2048]{2,1,0:T(8,128)(2,1)S(1)} collective-permute-done((bf16[1,64,2048]{2,1,0:T(8,128)(2,1)S(1)}, bf16[1,64,2048]{2,1,0:T(8,128)(2,1)S(1)}, u32[]{:S(2)}, u32[]{:S(2)}) %collective-permute-start.54) | collective-permute-done | bytes 262176 | tf_op jit(solution)/shard_map/ppermute | solution.py:24
  235.1 10.4 %collective-permute-done.59 = bf16[4,48,1024]{2,1,0:T(8,128)(2,1)S(1)} collective-permute-done((bf16[4,48,1024]{2,1,0:T(8,128)(2,1)S(1)}, bf16[4,48,1024]{2,1,0:T(8,128)(2,1)S(1)}, u32[]{:S(2)}, u32[]{:S(2)}) %collective-permute-start.59) | collective-permute-done | bytes 393248 | tf_op jit(solution)/shard_map/ppermute | solution.py:24
  245.6 1.8 collective-permute-done.58
  249.0 2.2 collective-permute-start.64
  251.2 2.3 collective-permute-start.62
  253.5 2.1 collective-permute-done.64
  255.6 2.2 collective-permute-done.63
  260.7 1.9 collective-permute-start.65
  262.6 2.2 collective-permute-start.69
  264.8 2.3 collective-permute-start.67
  267.1 8.9 %shard_map.269 = bf16[8,256,1024]{2,1,0:T(8,128)(2,1)} custom-call(bf16[4,8,64,1024]{3,2,1,0:T(8,128)(2,1)S(1)} %bitcast.43, bf16[1024,1024]{1,0:T(8,128)(2,1)S(1)} %copy-done.5, f32[512,1024]{1,0:T(8,128)S(1)} %shard_map.263.side_ref), custom_call_target="tpu_custom_call" | custom-call | flops 4294967296 | bytes 16777216 | tf_op jit(solution)/shard_map/pallas_call | solution.py:1212
  275.9 6.4 %collective-permute-done.66 = bf16[8,32,2048]{2,1,0:T(8,128)(2,1)S(1)} collective-permute-done((bf16[8,32,2048]{2,1,0:T(8,128)(2,1)S(1)}, bf16[8,32,2048]{2,1,0:T(8,128)(2,1)S(1)}, u32[]{:S(2)}, u32[]{:S(2)}) %collective-permute-start.66) | collective-permute-done | bytes 1048608 | tf_op jit(solution)/shard_map/ppermute | solution.py:24
  283.6 2.3 collective-permute-start.74
  287.2 3.8 %shard_map.270 = f32[32,32,2048]{2,1,0:T(8,128)} custom-call(s32[1]{0:T(128)} %bitcast.14.own_ref, bf16[16,32,2048]{2,1,0:T(8,128)(2,1)S(1)} %pad_maximum_fusion.1.low_ref, bf16[16,32,2048]{2,1,0:T(8,128)(2,1)S(1)} %collective-permute-done.70.high_ref), custom_call_target="tpu_custom_call" | custom-call | bytes 12582912 | tf_op jit(solution)/shard_map/pallas_call | solution.py:119
  291.0 3.8 %shard_map.271 = f32[32,32,2048]{2,1,0:T(8,128)} custom-call(s32[1]{0:T(128)} %bitcast.3.own_ref, bf16[16,32,2048]{2,1,0:T(8,128)(2,1)S(1)} %pad_maximum_fusion.low_ref, bf16[16,32,2048]{2,1,0:T(8,128)(2,1)S(1)} %collective-permute-done.71.high_ref), custom_call_target="tpu_custom_call" | custom-call | bytes 12582912 | tf_op jit(solution)/shard_map/pallas_call | solution.py:119
  296.6 7.4 %collective-permute-done.73 = bf16[4,48,1024]{2,1,0:T(8,128)(2,1)S(1)} collective-permute-done((bf16[4,48,1024]{2,1,0:T(8,128)(2,1)S(1)}, bf16[4,48,1024]{2,1,0:T(8,128)(2,1)S(1)}, u32[]{:S(2)}, u32[]{:S(2)}) %collective-permute-start.73) | collective-permute-done | bytes 393248 | tf_op jit(solution)/shard_map/ppermute | solution.py:24
  307.6 2.9 shard_map.272
  (257 shorter events, 95.8 us)
Async XLA Ops:
  1.7 17.2 %collective-permute-start = (bf16[8,32,1024]{2,1,0:T(8,128)(2,1)S(1)}, bf16[8,32,1024]{2,1,0:T(8,128)(2,1)S(1)}, u32[]{:S(2)}, u32[]{:S(2)}) collective-permute-start(bf16[8,32,1024]{2,1,0:T(8,128)(2,1)S(1)} %slice_bitcast_fusion), channel_id=1, source_target_pairs={{0,8},{8,16},{16,24},{1,9},{9,17},{17,25},{2,10},{10,18},{18,26},{... | collective-permute-start | bytes 1572872 | tf_op jit(solution)/shard_map/ppermute | solution.py:19
  20.3 5.6 %collective-permute-start.4 = (f32[4,1024]{1,0:T(4,128)S(1)}, f32[4,1024]{1,0:T(4,128)S(1)}, u32[]{:S(2)}, u32[]{:S(2)}) collective-permute-start(f32[4,1024]{1,0:T(4,128)S(1)} %pad_maximum_fusion.13), channel_id=1, source_target_pairs={{0,6},{1,7},{2,4},{3,5},{4,2},{5,3},{6,0},{7,1},{8,14},{9,15},{10,... | collective-permute-start | bytes 49160 | tf_op jit(solution)/shard_map/ppermute | solution.py:24
  24.0 4.6 %collective-permute-start.3 = (f32[4,1024]{1,0:T(4,128)S(1)}, f32[4,1024]{1,0:T(4,128)S(1)}, u32[]{:S(2)}, u32[]{:S(2)}) collective-permute-start(f32[4,1024]{1,0:T(4,128)S(1)} %pad_maximum_fusion.13), channel_id=1, source_target_pairs={{0,4},{1,5},{2,6},{3,7},{4,0},{5,1},{6,2},{7,3},{8,12},{9,13},{10,... | collective-permute-start | bytes 49160 | tf_op jit(solution)/shard_map/ppermute | solution.py:24
  28.8 5.4 %collective-permute-start.7 = (f32[4,1024]{1,0:T(4,128)S(1)}, f32[4,1024]{1,0:T(4,128)S(1)}, u32[]{:S(2)}, u32[]{:S(2)}) collective-permute-start(f32[4,1024]{1,0:T(4,128)S(1)} %pad_maximum_fusion.14), channel_id=1, source_target_pairs={{0,24},{8,16},{16,8},{24,0},{1,25},{9,17},{17,9},{25,1},{2,26},{10... | collective-permute-start | bytes 49160 | tf_op jit(solution)/shard_map/ppermute | solution.py:24
  47.2 5.9 %collective-permute-start.11 = (f32[2,1024]{1,0:T(2,128)S(1)}, f32[2,1024]{1,0:T(2,128)S(1)}, u32[]{:S(2)}, u32[]{:S(2)}) collective-permute-start(f32[2,1024]{1,0:T(2,128)S(1)} %add.445), channel_id=1, source_target_pairs={{0,6},{1,7},{2,4},{3,5},{4,2},{5,3},{6,0},{7,1},{8,14},{9,15},{10,... | collective-permute-start | bytes 24584 | tf_op jit(solution)/shard_map/ppermute | solution.py:24
  51.6 11.8 %collective-permute-start.15 = (bf16[128,1024]{1,0:T(8,128)(2,1)S(1)}, bf16[128,1024]{1,0:T(8,128)(2,1)S(1)}, u32[]{:S(2)}, u32[]{:S(2)}) collective-permute-start(bf16[128,1024]{1,0:T(8,128)(2,1)S(1)} %get-tuple-element.123), channel_id=1, source_target_pairs={{8,0},{16,8},{24,16},{9,1},{17,9},{25,17},{10,2},{18,10},{26,18},{... | collective-permute-start | bytes 786440 | tf_op jit(solution)/shard_map/ppermute | solution.py:19
  53.4 10.0 %collective-permute-start.14 = (f32[2,1024]{1,0:T(2,128)S(1)}, f32[2,1024]{1,0:T(2,128)S(1)}, u32[]{:S(2)}, u32[]{:S(2)}) collective-permute-start(f32[2,1024]{1,0:T(2,128)S(1)} %add_add_fusion.9), channel_id=1, source_target_pairs={{0,24},{8,16},{16,8},{24,0},{1,25},{9,17},{17,9},{25,1},{2,26},{10... | collective-permute-start | bytes 24584 | tf_op jit(solution)/shard_map/ppermute | solution.py:24
  56.6 6.8 %collective-permute-start.13 = (f32[2,1024]{1,0:T(2,128)S(1)}, f32[2,1024]{1,0:T(2,128)S(1)}, u32[]{:S(2)}, u32[]{:S(2)}) collective-permute-start(f32[2,1024]{1,0:T(2,128)S(1)} %add_add_fusion.9), channel_id=1, source_target_pairs={{0,16},{8,24},{16,0},{24,8},{1,17},{9,25},{17,1},{25,9},{2,18},{10... | collective-permute-start | bytes 24584 | tf_op jit(solution)/shard_map/ppermute | solution.py:24
  57.3 6.0 %collective-permute-start.12 = (f32[2,1024]{1,0:T(2,128)S(1)}, f32[2,1024]{1,0:T(2,128)S(1)}, u32[]{:S(2)}, u32[]{:S(2)}) collective-permute-start(f32[2,1024]{1,0:T(2,128)S(1)} %add_add_fusion.9), channel_id=1, source_target_pairs={{0,8},{8,0},{16,24},{24,16},{1,9},{9,1},{17,25},{25,17},{2,10},{10... | collective-permute-start | bytes 24584 | tf_op jit(solution)/shard_map/ppermute | solution.py:24
  71.4 5.9 %collective-permute-start.19 = (f32[4,2048]{1,0:T(4,128)S(1)}, f32[4,2048]{1,0:T(4,128)S(1)}, u32[]{:S(2)}, u32[]{:S(2)}) collective-permute-start(f32[4,2048]{1,0:T(4,128)S(1)} %add.452), channel_id=1, source_target_pairs={{0,6},{1,7},{2,4},{3,5},{4,2},{5,3},{6,0},{7,1},{8,14},{9,15},{10,... | collective-permute-start | bytes 98312 | tf_op jit(solution)/shard_map/ppermute | solution.py:24
  73.4 5.0 %collective-permute-start.18 = (f32[4,2048]{1,0:T(4,128)S(1)}, f32[4,2048]{1,0:T(4,128)S(1)}, u32[]{:S(2)}, u32[]{:S(2)}) collective-permute-start(f32[4,2048]{1,0:T(4,128)S(1)} %add.452), channel_id=1, source_target_pairs={{0,4},{1,5},{2,6},{3,7},{4,0},{5,1},{6,2},{7,3},{8,12},{9,13},{10,... | collective-permute-start | bytes 98312 | tf_op jit(solution)/shard_map/ppermute | solution.py:24
  78.7 5.2 %collective-permute-start.22 = (f32[4,2048]{1,0:T(4,128)S(1)}, f32[4,2048]{1,0:T(4,128)}, u32[]{:S(2)}, u32[]{:S(2)}) collective-permute-start(f32[4,2048]{1,0:T(4,128)S(1)} %add_add_fusion.3), channel_id=1, source_target_pairs={{0,24},{8,16},{16,8},{24,0},{1,25},{9,17},{17,9},{25,1},{2,26},{10... | collective-permute-start | bytes 98312 | tf_op jit(solution)/shard_map/ppermute | solution.py:24
  94.4 5.9 %collective-permute-start.26 = (f32[3,2048]{1,0:T(4,128)S(1)}, f32[3,2048]{1,0:T(4,128)S(1)}, u32[]{:S(2)}, u32[]{:S(2)}) collective-permute-start(f32[3,2048]{1,0:T(4,128)S(1)} %add.463), channel_id=1, source_target_pairs={{0,6},{1,7},{2,4},{3,5},{4,2},{5,3},{6,0},{7,1},{8,14},{9,15},{10,... | collective-permute-start | bytes 73736 | tf_op jit(solution)/shard_map/ppermute | solution.py:24
  96.2 5.2 %collective-permute-start.25 = (f32[3,2048]{1,0:T(4,128)S(1)}, f32[3,2048]{1,0:T(4,128)S(1)}, u32[]{:S(2)}, u32[]{:S(2)}) collective-permute-start(f32[3,2048]{1,0:T(4,128)S(1)} %add.463), channel_id=1, source_target_pairs={{0,4},{1,5},{2,6},{3,7},{4,0},{5,1},{6,2},{7,3},{8,12},{9,13},{10,... | collective-permute-start | bytes 73736 | tf_op jit(solution)/shard_map/ppermute | solution.py:24
  101.7 5.0 %collective-permute-start.29 = (f32[3,2048]{1,0:T(4,128)S(1)}, f32[3,2048]{1,0:T(4,128)S(1)}, u32[]{:S(2)}, u32[]{:S(2)}) collective-permute-start(f32[3,2048]{1,0:T(4,128)S(1)} %add_add_fusion.1), channel_id=1, source_target_pairs={{0,24},{8,16},{16,8},{24,0},{1,25},{9,17},{17,9},{25,1},{2,26},{10... | collective-permute-start | bytes 73736 | tf_op jit(solution)/shard_map/ppermute | solution.py:24
  119.1 11.9 %collective-permute-start.33 = (bf16[16,32,2048]{2,1,0:T(8,128)(2,1)S(1)}, bf16[16,32,2048]{2,1,0:T(8,128)(2,1)}, u32[]{:S(2)}, u32[]{:S(2)}) collective-permute-start(bf16[16,32,2048]{2,1,0:T(8,128)(2,1)S(1)} %get-tuple-element.141), channel_id=1, source_target_pairs={{0,1},{1,0},{2,3},{3,2},{4,5},{5,4},{6,7},{7,6},{8,9},{9,8},{10,11... | collective-permute-start | bytes 6291464 | tf_op jit(solution)/shard_map/ppermute | solution.py:24
  119.1 11.9 %collective-permute-start.34 = (bf16[16,32,2048]{2,1,0:T(8,128)(2,1)}, bf16[16,32,2048]{2,1,0:T(8,128)(2,1)S(1)}, u32[]{:S(2)}, u32[]{:S(2)}) collective-permute-start(bf16[16,32,2048]{2,1,0:T(8,128)(2,1)} %get-tuple-element.142), channel_id=1, source_target_pairs={{0,1},{1,0},{2,3},{3,2},{4,5},{5,4},{6,7},{7,6},{8,9},{9,8},{10,11... | collective-permute-start | bytes 6291464 | tf_op jit(solution)/shard_map/ppermute | solution.py:24
  132.4 8.7 %collective-permute-start.36 = (bf16[128,1024]{1,0:T(8,128)(2,1)S(1)}, bf16[128,1024]{1,0:T(8,128)(2,1)S(1)}, u32[]{:S(2)}, u32[]{:S(2)}) collective-permute-start(bf16[128,1024]{1,0:T(8,128)(2,1)S(1)} %get-tuple-element.144), channel_id=1, source_target_pairs={{8,0},{16,8},{24,16},{9,1},{17,9},{25,17},{10,2},{18,10},{26,18},{... | collective-permute-start | bytes 786440 | tf_op jit(solution)/shard_map/ppermute | solution.py:19
  145.9 23.3 %collective-permute-start.41 = (bf16[8,32,2048]{2,1,0:T(8,128)(2,1)S(1)}, bf16[8,32,2048]{2,1,0:T(8,128)(2,1)S(1)}, u32[]{:S(2)}, u32[]{:S(2)}) collective-permute-start(bf16[8,32,2048]{2,1,0:T(8,128)(2,1)S(1)} %slice.158), channel_id=1, source_target_pairs={{0,16},{8,24},{16,0},{24,8},{1,17},{9,25},{17,1},{25,9},{2,18},{10... | collective-permute-start | bytes 3145736 | tf_op jit(solution)/shard_map/ppermute | solution.py:24
  147.3 23.4 %collective-permute-start.40 = (bf16[8,32,2048]{2,1,0:T(8,128)(2,1)S(1)}, bf16[8,32,2048]{2,1,0:T(8,128)(2,1)S(1)}, u32[]{:S(2)}, u32[]{:S(2)}) collective-permute-start(bf16[8,32,2048]{2,1,0:T(8,128)(2,1)S(1)} %slice.157), channel_id=1, source_target_pairs={{0,8},{8,0},{16,24},{24,16},{1,9},{9,1},{17,25},{25,17},{2,10},{10... | collective-permute-start | bytes 3145736 | tf_op jit(solution)/shard_map/ppermute | solution.py:24
  147.3 5.4 %collective-permute-start.39 = (f32[2,1024]{1,0:T(2,128)S(1)}, f32[2,1024]{1,0:T(2,128)S(1)}, u32[]{:S(2)}, u32[]{:S(2)}) collective-permute-start(f32[2,1024]{1,0:T(2,128)S(1)} %add.473), channel_id=1, source_target_pairs={{0,6},{1,7},{2,4},{3,5},{4,2},{5,3},{6,0},{7,1},{8,14},{9,15},{10,... | collective-permute-start | bytes 24584 | tf_op jit(solution)/shard_map/ppermute | solution.py:24
  178.4 11.6 %collective-permute-start.50 = (bf16[4,32,2048]{2,1,0:T(8,128)(2,1)S(1)}, bf16[4,32,2048]{2,1,0:T(8,128)(2,1)S(1)}, u32[]{:S(2)}, u32[]{:S(2)}) collective-permute-start(bf16[4,32,2048]{2,1,0:T(8,128)(2,1)S(1)} %slice.162), channel_id=1, source_target_pairs={{0,8},{8,0},{16,24},{24,16},{1,9},{9,1},{17,25},{25,17},{2,10},{10... | collective-permute-start | bytes 1572872 | tf_op jit(solution)/shard_map/ppermute | solution.py:24
  178.7 11.4 %collective-permute-start.49 = (bf16[4,32,2048]{2,1,0:T(8,128)(2,1)S(1)}, bf16[4,32,2048]{2,1,0:T(8,128)(2,1)S(1)}, u32[]{:S(2)}, u32[]{:S(2)}) collective-permute-start(bf16[4,32,2048]{2,1,0:T(8,128)(2,1)S(1)} %slice.160), channel_id=1, source_target_pairs={{0,16},{8,24},{16,0},{24,8},{1,17},{9,25},{17,1},{25,9},{2,18},{10... | collective-permute-start | bytes 1572872 | tf_op jit(solution)/shard_map/ppermute | solution.py:24
  180.7 8.1 %collective-permute-start.48 = (f32[2,1024]{1,0:T(2,128)S(1)}, f32[2,1024]{1,0:T(2,128)S(1)}, u32[]{:S(2)}, u32[]{:S(2)}) collective-permute-start(f32[2,1024]{1,0:T(2,128)S(1)} %add.482), channel_id=1, source_target_pairs={{0,6},{1,7},{2,4},{3,5},{4,2},{5,3},{6,0},{7,1},{8,14},{9,15},{10,... | collective-permute-start | bytes 24584 | tf_op jit(solution)/shard_map/ppermute | solution.py:24
  182.4 6.4 %collective-permute-start.47 = (f32[2,1024]{1,0:T(2,128)S(1)}, f32[2,1024]{1,0:T(2,128)S(1)}, u32[]{:S(2)}, u32[]{:S(2)}) collective-permute-start(f32[2,1024]{1,0:T(2,128)S(1)} %add.482), channel_id=1, source_target_pairs={{0,4},{1,5},{2,6},{3,7},{4,0},{5,1},{6,2},{7,3},{8,12},{9,13},{10,... | collective-permute-start | bytes 24584 | tf_op jit(solution)/shard_map/ppermute | solution.py:24
  183.2 5.6 %collective-permute-start.46 = (f32[2,1024]{1,0:T(2,128)S(1)}, f32[2,1024]{1,0:T(2,128)S(1)}, u32[]{:S(2)}, u32[]{:S(2)}) collective-permute-start(f32[2,1024]{1,0:T(2,128)S(1)} %add.482), channel_id=1, source_target_pairs={{0,2},{1,3},{2,0},{3,1},{4,6},{5,7},{6,4},{7,5},{8,10},{9,11},{10,... | collective-permute-start | bytes 24584 | tf_op jit(solution)/shard_map/ppermute | solution.py:24
  190.5 18.6 %collective-permute-start.51 = (bf16[1,64,2048]{2,1,0:T(8,128)(2,1)S(1)}, bf16[1,64,2048]{2,1,0:T(8,128)(2,1)S(1)}, u32[]{:S(2)}, u32[]{:S(2)}) collective-permute-start(bf16[1,64,2048]{2,1,0:T(8,128)(2,1)S(1)} %pad_maximum_fusion.8), channel_id=1, source_target_pairs={{0,4},{1,5},{2,6},{3,7},{4,0},{5,1},{6,2},{7,3},{8,12},{9,13},{10,... | collective-permute-start | bytes 786440 | tf_op jit(solution)/shard_map/ppermute | solution.py:24
  191.9 17.3 %collective-permute-start.52 = (bf16[1,64,2048]{2,1,0:T(8,128)(2,1)S(1)}, bf16[1,64,2048]{2,1,0:T(8,128)(2,1)S(1)}, u32[]{:S(2)}, u32[]{:S(2)}) collective-permute-start(bf16[1,64,2048]{2,1,0:T(8,128)(2,1)S(1)} %pad_maximum_fusion.9), channel_id=1, source_target_pairs={{0,2},{1,3},{2,0},{3,1},{4,6},{5,7},{6,4},{7,5},{8,10},{9,11},{10,... | collective-permute-start | bytes 786440 | tf_op jit(solution)/shard_map/ppermute | solution.py:24
  192.9 16.2 %collective-permute-start.53 = (bf16[1,64,2048]{2,1,0:T(8,128)(2,1)S(1)}, bf16[1,64,2048]{2,1,0:T(8,128)(2,1)S(1)}, u32[]{:S(2)}, u32[]{:S(2)}) collective-permute-start(bf16[1,64,2048]{2,1,0:T(8,128)(2,1)S(1)} %pad_maximum_fusion.10), channel_id=1, source_target_pairs={{0,6},{1,7},{2,4},{3,5},{4,2},{5,3},{6,0},{7,1},{8,14},{9,15},{10,... | collective-permute-start | bytes 786440 | tf_op jit(solution)/shard_map/ppermute | solution.py:24
  213.6 20.9 %collective-permute-start.57 = (bf16[4,48,1024]{2,1,0:T(8,128)(2,1)S(1)}, bf16[4,48,1024]{2,1,0:T(8,128)(2,1)S(1)}, u32[]{:S(2)}, u32[]{:S(2)}) collective-permute-start(bf16[4,48,1024]{2,1,0:T(8,128)(2,1)S(1)} %get-tuple-element.224), channel_id=1, source_target_pairs={{0,16},{8,24},{16,0},{24,8},{1,17},{9,25},{17,1},{25,9},{2,18},{10... | collective-permute-start | bytes 1179656 | tf_op jit(solution)/shard_map/ppermute | solution.py:24
  214.8 19.7 %collective-permute-start.56 = (bf16[4,48,1024]{2,1,0:T(8,128)(2,1)S(1)}, bf16[4,48,1024]{2,1,0:T(8,128)(2,1)S(1)}, u32[]{:S(2)}, u32[]{:S(2)}) collective-permute-start(bf16[4,48,1024]{2,1,0:T(8,128)(2,1)S(1)} %get-tuple-element.225), channel_id=1, source_target_pairs={{0,8},{8,0},{16,24},{24,16},{1,9},{9,1},{17,25},{25,17},{2,10},{10... | collective-permute-start | bytes 1179656 | tf_op jit(solution)/shard_map/ppermute | solution.py:24
  216.4 18.1 %collective-permute-start.54 = (bf16[1,64,2048]{2,1,0:T(8,128)(2,1)S(1)}, bf16[1,64,2048]{2,1,0:T(8,128)(2,1)S(1)}, u32[]{:S(2)}, u32[]{:S(2)}) collective-permute-start(bf16[1,64,2048]{2,1,0:T(8,128)(2,1)S(1)} %add_convert_fusion.8), channel_id=1, source_target_pairs={{0,4},{1,5},{2,6},{3,7},{4,0},{5,1},{6,2},{7,3},{8,12},{9,13},{10,... | collective-permute-start | bytes 786440 | tf_op jit(solution)/shard_map/ppermute | solution.py:24
  234.5 12.9 %collective-permute-start.58 = (bf16[2,64,2048]{2,1,0:T(8,128)(2,1)S(1)}, bf16[2,64,2048]{2,1,0:T(8,128)(2,1)S(1)}, u32[]{:S(2)}, u32[]{:S(2)}) collective-permute-start(bf16[2,64,2048]{2,1,0:T(8,128)(2,1)S(1)} %pad_maximum_fusion.6), channel_id=1, source_target_pairs={{0,2},{1,3},{2,0},{3,1},{4,6},{5,7},{6,4},{7,5},{8,10},{9,11},{10,... | collective-permute-start | bytes 1572872 | tf_op jit(solution)/shard_map/ppermute | solution.py:24
  234.6 11.0 %collective-permute-start.59 = (bf16[4,48,1024]{2,1,0:T(8,128)(2,1)S(1)}, bf16[4,48,1024]{2,1,0:T(8,128)(2,1)S(1)}, u32[]{:S(2)}, u32[]{:S(2)}) collective-permute-start(bf16[4,48,1024]{2,1,0:T(8,128)(2,1)S(1)} %get-tuple-element.223), channel_id=1, source_target_pairs={{0,24},{8,16},{16,8},{24,0},{1,25},{9,17},{17,9},{25,1},{2,26},{10... | collective-permute-start | bytes 1179656 | tf_op jit(solution)/shard_map/ppermute | solution.py:24
  247.6 12.0 %collective-permute-start.61 = (bf16[4,32,2048]{2,1,0:T(8,128)(2,1)S(1)}, bf16[4,32,2048]{2,1,0:T(8,128)(2,1)S(1)}, u32[]{:S(2)}, u32[]{:S(2)}) collective-permute-start(bf16[4,32,2048]{2,1,0:T(8,128)(2,1)S(1)} %get-tuple-element.226), channel_id=1, source_target_pairs={{0,8},{8,0},{16,24},{24,16},{1,9},{9,1},{17,25},{25,17},{2,10},{10... | collective-permute-start | bytes 1572872 | tf_op jit(solution)/shard_map/ppermute | solution.py:24
  248.2 11.8 %collective-permute-start.60 = (bf16[4,32,2048]{2,1,0:T(8,128)(2,1)S(1)}, bf16[4,32,2048]{2,1,0:T(8,128)(2,1)S(1)}, u32[]{:S(2)}, u32[]{:S(2)}) collective-permute-start(bf16[4,32,2048]{2,1,0:T(8,128)(2,1)S(1)} %get-tuple-element.227), channel_id=1, source_target_pairs={{0,16},{8,24},{16,0},{24,8},{1,17},{9,25},{17,1},{25,9},{2,18},{10... | collective-permute-start | bytes 1572872 | tf_op jit(solution)/shard_map/ppermute | solution.py:24
  249.0 6.6 %collective-permute-start.64 = (bf16[1,48,1024]{2,1,0:T(8,128)(2,1)S(1)}, bf16[1,48,1024]{2,1,0:T(8,128)(2,1)S(1)}, u32[]{:S(2)}, u32[]{:S(2)}) collective-permute-start(bf16[1,48,1024]{2,1,0:T(8,128)(2,1)S(1)} %get-tuple-element.238), channel_id=1, source_target_pairs={{0,6},{1,7},{2,4},{3,5},{4,2},{5,3},{6,0},{7,1},{8,14},{9,15},{10,... | collective-permute-start | bytes 294920 | tf_op jit(solution)/shard_map/ppermute | solution.py:24
  251.2 6.5 %collective-permute-start.63 = (bf16[1,48,1024]{2,1,0:T(8,128)(2,1)S(1)}, bf16[1,48,1024]{2,1,0:T(8,128)(2,1)S(1)}, u32[]{:S(2)}, u32[]{:S(2)}) collective-permute-start(bf16[1,48,1024]{2,1,0:T(8,128)(2,1)S(1)} %get-tuple-element.239), channel_id=1, source_target_pairs={{0,2},{1,3},{2,0},{3,1},{4,6},{5,7},{6,4},{7,5},{8,10},{9,11},{10,... | collective-permute-start | bytes 294920 | tf_op jit(solution)/shard_map/ppermute | solution.py:24
  251.2 7.2 %collective-permute-start.62 = (bf16[1,48,1024]{2,1,0:T(8,128)(2,1)S(1)}, bf16[1,48,1024]{2,1,0:T(8,128)(2,1)S(1)}, u32[]{:S(2)}, u32[]{:S(2)}) collective-permute-start(bf16[1,48,1024]{2,1,0:T(8,128)(2,1)S(1)} %get-tuple-element.240), channel_id=1, source_target_pairs={{0,4},{1,5},{2,6},{3,7},{4,0},{5,1},{6,2},{7,3},{8,12},{9,13},{10,... | collective-permute-start | bytes 294920 | tf_op jit(solution)/shard_map/ppermute | solution.py:24
  260.2 22.1 %collective-permute-start.66 = (bf16[8,32,2048]{2,1,0:T(8,128)(2,1)S(1)}, bf16[8,32,2048]{2,1,0:T(8,128)(2,1)S(1)}, u32[]{:S(2)}, u32[]{:S(2)}) collective-permute-start(bf16[8,32,2048]{2,1,0:T(8,128)(2,1)S(1)} %pad_maximum_fusion.5), channel_id=1, source_target_pairs={{0,16},{8,24},{16,0},{24,8},{1,17},{9,25},{17,1},{25,9},{2,18},{10... | collective-permute-start | bytes 3145736 | tf_op jit(solution)/shard_map/ppermute | solution.py:24
  260.7 21.8 %collective-permute-start.65 = (bf16[8,32,2048]{2,1,0:T(8,128)(2,1)S(1)}, bf16[8,32,2048]{2,1,0:T(8,128)(2,1)S(1)}, u32[]{:S(2)}, u32[]{:S(2)}) collective-permute-start(bf16[8,32,2048]{2,1,0:T(8,128)(2,1)S(1)} %pad_maximum_fusion.4), channel_id=1, source_target_pairs={{0,8},{8,0},{16,24},{24,16},{1,9},{9,1},{17,25},{25,17},{2,10},{10... | collective-permute-start | bytes 3145736 | tf_op jit(solution)/shard_map/ppermute | solution.py:24
  262.6 13.3 %collective-permute-start.69 = (bf16[1,48,1024]{2,1,0:T(8,128)(2,1)S(1)}, bf16[1,48,1024]{2,1,0:T(8,128)(2,1)S(1)}, u32[]{:S(2)}, u32[]{:S(2)}) collective-permute-start(bf16[1,48,1024]{2,1,0:T(8,128)(2,1)S(1)} %get-tuple-element.215), channel_id=1, source_target_pairs={{0,6},{1,7},{2,4},{3,5},{4,2},{5,3},{6,0},{7,1},{8,14},{9,15},{10,... | collective-permute-start | bytes 294920 | tf_op jit(solution)/shard_map/ppermute | solution.py:24
  264.8 11.1 %collective-permute-start.68 = (bf16[1,48,1024]{2,1,0:T(8,128)(2,1)S(1)}, bf16[1,48,1024]{2,1,0:T(8,128)(2,1)S(1)}, u32[]{:S(2)}, u32[]{:S(2)}) collective-permute-start(bf16[1,48,1024]{2,1,0:T(8,128)(2,1)S(1)} %get-tuple-element.215), channel_id=1, source_target_pairs={{0,2},{1,3},{2,0},{3,1},{4,6},{5,7},{6,4},{7,5},{8,10},{9,11},{10,... | collective-permute-start | bytes 294920 | tf_op jit(solution)/shard_map/ppermute | solution.py:24
  264.8 11.1 %collective-permute-start.67 = (bf16[1,48,1024]{2,1,0:T(8,128)(2,1)S(1)}, bf16[1,48,1024]{2,1,0:T(8,128)(2,1)S(1)}, u32[]{:S(2)}, u32[]{:S(2)}) collective-permute-start(bf16[1,48,1024]{2,1,0:T(8,128)(2,1)S(1)} %get-tuple-element.215), channel_id=1, source_target_pairs={{0,4},{1,5},{2,6},{3,7},{4,0},{5,1},{6,2},{7,3},{8,12},{9,13},{10,... | collective-permute-start | bytes 294920 | tf_op jit(solution)/shard_map/ppermute | solution.py:24
  283.0 8.0 %collective-permute-start.71 = (bf16[16,32,2048]{2,1,0:T(8,128)(2,1)S(1)}, bf16[16,32,2048]{2,1,0:T(8,128)(2,1)S(1)}, u32[]{:S(2)}, u32[]{:S(2)}) collective-permute-start(bf16[16,32,2048]{2,1,0:T(8,128)(2,1)S(1)} %pad_maximum_fusion.low_ref), channel_id=1, source_target_pairs={{0,1},{1,0},{2,3},{3,2},{4,5},{5,4},{6,7},{7,6},{8,9},{9,8},{10,11... | collective-permute-start | bytes 6291464 | tf_op jit(solution)/shard_map/ppermute | solution.py:24
  283.6 13.0 %collective-permute-start.74 = (bf16[4,48,1024]{2,1,0:T(8,128)(2,1)S(1)}, bf16[4,48,1024]{2,1,0:T(8,128)(2,1)S(1)}, u32[]{:S(2)}, u32[]{:S(2)}) collective-permute-start(bf16[4,48,1024]{2,1,0:T(8,128)(2,1)S(1)} %pad_maximum_fusion.7), channel_id=1, source_target_pairs={{0,24},{8,16},{16,8},{24,0},{1,25},{9,17},{17,9},{25,1},{2,26},{10... | collective-permute-start | bytes 1179656 | tf_op jit(solution)/shard_map/ppermute | solution.py:24
  285.9 18.2 %collective-permute-start.73 = (bf16[4,48,1024]{2,1,0:T(8,128)(2,1)S(1)}, bf16[4,48,1024]{2,1,0:T(8,128)(2,1)S(1)}, u32[]{:S(2)}, u32[]{:S(2)}) collective-permute-start(bf16[4,48,1024]{2,1,0:T(8,128)(2,1)S(1)} %pad_maximum_fusion.7), channel_id=1, source_target_pairs={{0,16},{8,24},{16,0},{24,8},{1,17},{9,25},{17,1},{25,9},{2,18},{10... | collective-permute-start | bytes 1179656 | tf_op jit(solution)/shard_map/ppermute | solution.py:24
  286.6 17.4 %collective-permute-start.72 = (bf16[4,48,1024]{2,1,0:T(8,128)(2,1)S(1)}, bf16[4,48,1024]{2,1,0:T(8,128)(2,1)S(1)}, u32[]{:S(2)}, u32[]{:S(2)}) collective-permute-start(bf16[4,48,1024]{2,1,0:T(8,128)(2,1)S(1)} %pad_maximum_fusion.7), channel_id=1, source_target_pairs={{0,8},{8,0},{16,24},{24,16},{1,9},{9,1},{17,25},{25,17},{2,10},{10... | collective-permute-start | bytes 1179656 | tf_op jit(solution)/shard_map/ppermute | solution.py:24
  (56 other events, 466.8 us)
